TPU v7x, 256 devices: a whole 4x4x8 slice. The times are simulated.
256 devices in a mesh: seq: 64 (over z, y, core), mp: 4 (over x).
Axes of the slice: x: 4, y: 4, z: 8, core: 2. Of those that a mesh axis runs over, the one named last changes fastest.
Arguments:
- latents: bfloat16 [16384, 1536], P('seq'), may hold values from -6 to 6
- w_query: bfloat16 [1536, 1536], P(None, 'mp'), may hold values from -0.15625 to 0.15625
- w_key: bfloat16 [1536, 1536], P(None, 'mp'), may hold values from -0.15625 to 0.15625
- w_value: bfloat16 [1536, 1536], P(None, 'mp'), may hold values from -0.15625 to 0.15625
- w_out: bfloat16 [1536, 1536], P('mp'), may hold values from -0.15625 to 0.15625
- head_gain: float32 [1536], P('mp'), may hold values from 0.25 to 1.75
- grad_out: bfloat16 [16384, 1536], P('seq', 'mp'), may hold values from -6 to 6
Outputs:
- branch: bfloat16 [16384, 1536], P('seq', 'mp')
- d_latents: bfloat16 [16384, 1536], P('seq', 'mp')
All inputs are finite; a program needn't handle non-finite values.
Results may differ from a plain program's by a relative error of at most 0.013.
Values may be sent and summed in bfloat16 or wider, within the bound.
No kernel may reach another device: no remote copies, remote signals or barrier semaphores. Data moves between devices by JAX's collectives and lax.ppermute only.
A program may use at most 64 MiB of HBM per device.

v0:
```python
import jax
import jax.numpy as jnp
from jax import lax
from jax.sharding import Mesh
from jax.sharding import PartitionSpec as P

HD = 64
SEQ = ("seq_0", "seq_1", "seq_2")


epsilon = 1e-06


def nothing_yet(x, identity):
    return jnp.broadcast_to(jnp.asarray(identity, x.dtype), x.shape)


def prefix_by_axis(x, axes, combine, identity):
    before = start = nothing_yet(x, identity)
    running = x
    for axis in reversed(axes):
        devices, mine = (lax.axis_size(axis), lax.axis_index(axis))
        pieces = lax.all_gather(running.astype(jnp.bfloat16), axis)
        inside, running = (start, start)
        for k in range(devices):
            passed = k < mine
            running = combine(running, pieces[k].astype(x.dtype))
            inside = jnp.where(passed, running, inside)
        before = combine(inside, before)
    return before


def split_up(x, dim, devices):
    before, after = (x.shape[:dim], x.shape[dim + 1 :])
    return jnp.moveaxis(x.reshape(*before, devices, -1, *after), dim, 0)


def sum_at_owner(x, axis, dim):
    devices = lax.axis_size(axis)
    parts = lax.all_to_all(split_up(x, dim, devices), axis, 0, 0, tiled=True)
    return jnp.sum(parts.astype(jnp.float32), axis=0)


def copy_for_each(x, axis):
    devices = lax.axis_size(axis)
    return lax.all_to_all(jnp.broadcast_to(x[None], (devices, *x.shape)), axis, 0, 0, tiled=True)


def in_order(parts, dim):
    parts = jnp.moveaxis(parts, 0, dim)
    dims = parts.shape
    return parts.reshape(*dims[:dim], dims[dim] * dims[dim + 1], *dims[dim + 2 :])


def gathered_copies(x, axis, dim):
    parts = copy_for_each(x, axis)
    return in_order(parts, dim)


def carried_in(x, axes, combine, identity):
    before = start = nothing_yet(x, identity)
    running = x
    for axis in reversed(axes):
        devices, mine = (lax.axis_size(axis), lax.axis_index(axis))
        pieces = lax.all_gather(
            running.astype(jnp.bfloat16 if x.dtype == jnp.float32 else x.dtype), axis
        )
        inside, running = (start, start)
        for k in reversed(range(devices)):
            passed = k > mine
            running = combine(running, pieces[k].astype(x.dtype))
            inside = jnp.where(passed, running, inside)
        before = combine(inside, before)
    return before


def feature_map(inputs):
    return jnp.where(inputs > 0, inputs + 1.0, jnp.exp(jnp.minimum(inputs, 0.0)))


def feature_slope(inputs):
    return jnp.where(inputs > 0, jnp.ones_like(inputs), jnp.exp(jnp.minimum(inputs, 0.0)))


def causal_table(block_rows):
    return (jnp.arange(block_rows)[:, None] >= jnp.arange(block_rows)[None, :]).astype(jnp.float32)


def add_states(earlier, later):
    return earlier + later


def per_device(latents, w_query, w_key, w_value, w_out, head_gain, grad_out):
    row_count = latents.shape[0]
    local_width = w_query.shape[1]
    local_heads = local_width // HD
    query_raw = jnp.dot(latents, w_query, preferred_element_type=jnp.float32).reshape(
        row_count, local_heads, HD
    )
    key_raw = jnp.dot(latents, w_key, preferred_element_type=jnp.float32).reshape(
        row_count, local_heads, HD
    )
    value_matrix = jnp.dot(latents, w_value, preferred_element_type=jnp.float32).reshape(
        row_count, local_heads, HD
    )
    mapped_query = feature_map(query_raw)
    mapped_key = feature_map(key_raw)
    forward_state_local = jnp.einsum("omw,omd->mwd", mapped_key, value_matrix)
    prefix_state = prefix_by_axis(
        forward_state_local, SEQ, add_states, jnp.zeros_like(forward_state_local)
    )
    block_rows = min(512, row_count)
    block_count = row_count // block_rows
    causal_mask = causal_table(block_rows)

    def blocked(array):
        return array.reshape(block_count, block_rows, local_heads, HD)

    def forward_step(running_state, inputs):
        mapped_query_block, mapped_key_block, value_block = inputs
        score_matrix = (
            jnp.einsum("thk,shk->hts", mapped_query_block, mapped_key_block) * causal_mask
        )
        unnormed_block = jnp.einsum("hts,shv->thv", score_matrix, value_block)
        unnormed_block = unnormed_block + jnp.einsum(
            "lsd,sdq->lsq", mapped_query_block, running_state
        )
        updated_state = running_state + jnp.einsum("omw,omd->mwd", mapped_key_block, value_block)
        return (updated_state, (unnormed_block, running_state))

    _, forward_out = lax.scan(
        forward_step,
        prefix_state,
        (blocked(mapped_query), blocked(mapped_key), blocked(value_matrix)),
    )
    raw = forward_out[0].reshape(row_count, local_heads, HD)
    befores = forward_out[1]
    inv_scale = lax.rsqrt(jnp.mean(raw * raw, axis=-1, keepdims=True) + epsilon)
    gain_rows = head_gain.reshape(local_heads, HD)
    attn = (raw * inv_scale * gain_rows).astype(jnp.bfloat16).reshape(row_count, local_width)
    partial_out = jnp.dot(attn, w_out, preferred_element_type=jnp.float32)
    branch = sum_at_owner(partial_out.astype(jnp.bfloat16), "mp", 1).astype(jnp.bfloat16)
    contract = (((1,), (1,)), ((), ()))
    d_attn = lax.dot_general(
        gathered_copies(grad_out, "mp", 1), w_out, contract, preferred_element_type=jnp.float32
    )
    upstream = d_attn.reshape(row_count, local_heads, HD) * gain_rows
    row_stat = jnp.mean(raw * upstream, axis=-1, keepdims=True)
    unnormed_gradient = inv_scale * upstream - inv_scale * inv_scale * inv_scale * raw * row_stat
    reverse_state_local = jnp.einsum("wei,wej->eij", mapped_query, unnormed_gradient)
    suffix_state = carried_in(
        reverse_state_local, SEQ, add_states, jnp.zeros_like(reverse_state_local)
    )

    def backward_step(running_state, inputs):
        (
            mapped_query_block,
            mapped_key_block,
            value_block,
            unnormed_block_gradient,
            prior_state_sum,
        ) = inputs
        score_matrix = (
            jnp.einsum("thk,shk->hts", mapped_query_block, mapped_key_block) * causal_mask
        )
        mixed_output = (
            jnp.einsum("thv,shv->hts", unnormed_block_gradient, value_block) * causal_mask
        )
        feature_query_gradient = jnp.einsum(
            "fui,ifc->ufc", mixed_output, mapped_key_block
        ) + jnp.einsum("pue,ure->pur", unnormed_block_gradient, prior_state_sum)
        feature_key_gradient = jnp.einsum(
            "xbc,bxj->cxj", mixed_output, mapped_query_block
        ) + jnp.einsum("wqj,qtj->wqt", value_block, running_state)
        value_gradient = jnp.einsum(
            "fud,ufx->dfx", score_matrix, unnormed_block_gradient
        ) + jnp.einsum("eul,ulw->euw", mapped_key_block, running_state)
        updated_state = running_state + jnp.einsum(
            "wei,wej->eij", mapped_query_block, unnormed_block_gradient
        )
        return (updated_state, (feature_query_gradient, feature_key_gradient, value_gradient))

    backward_in = (
        blocked(mapped_query),
        blocked(mapped_key),
        blocked(value_matrix),
        blocked(unnormed_gradient),
        befores,
    )
    _, (feature_query_gradient, feature_key_gradient, value_gradient) = lax.scan(
        backward_step, suffix_state, backward_in, reverse=True
    )
    d_query = (
        (feature_query_gradient.reshape(row_count, local_heads, HD) * feature_slope(query_raw))
        .astype(jnp.bfloat16)
        .reshape(row_count, local_width)
    )
    d_key = (
        (feature_key_gradient.reshape(row_count, local_heads, HD) * feature_slope(key_raw))
        .astype(jnp.bfloat16)
        .reshape(row_count, local_width)
    )
    d_value = value_gradient.reshape(row_count, local_width).astype(jnp.bfloat16)
    partial_in = lax.dot_general(d_query, w_query, contract, preferred_element_type=jnp.float32)
    partial_in = partial_in + lax.dot_general(
        d_key, w_key, contract, preferred_element_type=jnp.float32
    )
    partial_in = partial_in + lax.dot_general(
        d_value, w_value, contract, preferred_element_type=jnp.float32
    )
    d_latents = sum_at_owner(partial_in.astype(jnp.bfloat16), "mp", 1).astype(jnp.bfloat16)
    return (branch, d_latents)


def solution(mesh):
    split = Mesh(mesh.devices.reshape(8, 4, 2, mesh.shape["mp"]), ("seq_0", "seq_1", "seq_2", "mp"))
    in_specs = (
        P(SEQ, None),
        P(None, "mp"),
        P(None, "mp"),
        P(None, "mp"),
        P("mp", None),
        P("mp"),
        P(SEQ, "mp"),
    )
    out_specs = (P(SEQ, "mp"), P(SEQ, "mp"))
    return jax.shard_map(
        per_device, mesh=split, in_specs=in_specs, out_specs=out_specs, check_vma=False
    )
```

profile of v0, /device:TPU:8, one launch (start us, length us, event | category | flops | bytes accessed | tf_op | source)
XLA Modules:
  0.0 145.1 jit_solution(12479894322549822337)
XLA Ops:
  0.7 2.0 %broadcast_in_dim.28 = bf16[4,256,384]{2,1,0:T(8,128)(2,1)} broadcast(bf16[256,384]{1,0:T(8,128)(2,1)} %param.13), dimensions={1,2} | broadcast | bytes 983040 | tf_op jit(solution)/shard_map/broadcast_in_dim | solution.py:46
  2.7 4.3 %all-to-all-start.1 = ((bf16[4,256,384]{2,1,0:T(8,128)(2,1)}), bf16[4,256,384]{2,1,0:T(8,128)(2,1)}, u32[]{:S(2)}, u32[]{:S(2)}) async-start(bf16[4,256,384]{2,1,0:T(8,128)(2,1)} %broadcast_in_dim.28), calls=%async_computation.1 | async-start | bytes 1572864 | tf_op jit(solution)/shard_map/all_to_all | solution.py:46
  7.0 2.7 %add_select_fusion = (bf16[256,384]{1,0:T(8,128)(2,1)S(1)}, f32[256,384]{1,0:T(8,128)}) fusion(bf16[256,1536]{1,0:T(8,128)(2,1)S(1)} %copy-done.11, bf16[1536,384]{1,0:T(8,128)(2,1)} %param.9), kind=kOutput, calls=%fused_computation.24 | convolution fusion | flops 302383104 | bytes 2555904 | tf_op jit(solution)/shard_map/dot_general | solution.py:100
  10.7 2.1 %all-gather = bf16[12,64,64]{2,1,0:T(8,128)(2,1)S(1)} all-gather(bf16[6,64,64]{2,1,0:T(8,128)(2,1)S(1)} %fusion.55), channel_id=2, replica_groups=mesh['seq_0'=8,'seq_1'=4,'seq_2'=2,'mp'=4] {'seq_2'}, dimensions={0}, use_global_device_ids=true | all-gather | bytes 147456 | tf_op jit(solution)/shard_map/all_gather | solution.py:23
  12.8 12.7 %all_gather.30 = bf16[4,6,64,64]{3,2,1,0:T(8,128)(2,1)S(1)} all-gather(bf16[1,6,64,64]{3,2,1,0:T(8,128)(2,1)S(1)} %fusion.43), channel_id=1, replica_groups=mesh['seq_0'=8,'seq_1'=4,'seq_2'=2,'mp'=4] {'seq_1'}, dimensions={0}, use_global_device_ids=true | all-gather | bytes 245760 | tf_op jit(solution)/shard_map/all_gather | solution.py:23
  25.6 29.9 %all_gather.31 = bf16[8,6,64,64]{3,2,1,0:T(8,128)(2,1)S(1)} all-gather(bf16[1,6,64,64]{3,2,1,0:T(8,128)(2,1)S(1)} %fusion.38), channel_id=1, replica_groups=mesh['seq_0'=8,'seq_1'=4,'seq_2'=2,'mp'=4] {'seq_0'}, dimensions={0}, use_global_device_ids=true | all-gather | bytes 442368 | tf_op jit(solution)/shard_map/all_gather | solution.py:23
  55.5 1.3 add_select_fusion.1
  57.4 1.0 fusion.50
  58.8 1.7 %copy.37 = bf16[256,4,384]{2,1,0:T(4,128)(2,1)S(1)} copy(bf16[256,4,384]{2,0,1:T(8,128)(2,1)} %bitcast.9) | data formatting | bytes 1572864 | tf_op jit(solution)/shard_map/transpose | solution.py:50
  60.6 1.2 reshape.268
  61.8 1.7 %convolution_multiply_fusion.2 = f32[256,6,64]{0,2,1:T(8,128)S(1)} fusion(bf16[256,1536,1]{1,0,2:T(8,128)(2,1)} %reshape.268, bf16[6,64,1536]{2,1,0:T(8,128)(2,1)S(1)} %bitcast.85, f32[6,64]{1,0:T(8,128)S(1)} %mul.110), kind=kOutput, calls=%fused_computation.9 | convolution fusion | flops 302088192 | bytes 2360832 | tf_op jit(solution)/shard_map/dot_general | solution.py:144
  64.2 1.9 %all-gather.1 = bf16[12,64,64]{2,1,0:T(8,128)(2,1)S(1)} all-gather(bf16[6,64,64]{2,1,0:T(8,128)(2,1)S(1)} %fusion.54), channel_id=3, replica_groups=mesh['seq_0'=8,'seq_1'=4,'seq_2'=2,'mp'=4] {'seq_2'}, dimensions={0}, use_global_device_ids=true | all-gather | bytes 147456 | tf_op jit(solution)/shard_map/all_gather | solution.py:65
  66.2 12.9 %all_gather.34 = bf16[4,6,64,64]{3,2,1,0:T(8,128)(2,1)S(1)} all-gather(bf16[1,6,64,64]{3,2,1,0:T(8,128)(2,1)S(1)} %fusion.44), channel_id=1, replica_groups=mesh['seq_0'=8,'seq_1'=4,'seq_2'=2,'mp'=4] {'seq_1'}, dimensions={0}, use_global_device_ids=true | all-gather | bytes 245760 | tf_op jit(solution)/shard_map/all_gather | solution.py:65
  79.1 26.1 %all_gather.35 = bf16[8,6,64,64]{3,2,1,0:T(8,128)(2,1)S(1)} all-gather(bf16[1,6,64,64]{3,2,1,0:T(8,128)(2,1)S(1)} %fusion.37), channel_id=1, replica_groups=mesh['seq_0'=8,'seq_1'=4,'seq_2'=2,'mp'=4] {'seq_0'}, dimensions={0}, use_global_device_ids=true | all-gather | bytes 442368 | tf_op jit(solution)/shard_map/all_gather | solution.py:65
  106.6 1.0 fusion.51
  109.4 2.1 %fusion.34 = f32[256,1536]{1,0:T(8,128)S(1)} fusion(bf16[1536,384]{1,0:T(8,128)(2,1)} %param.8, f32[256,384]{1,0:T(8,128)S(1)} %copy.38, f32[256,384]{1,0:T(8,128)} %get-tuple-element.55), kind=kOutput, calls=%fused_computation.71 | convolution fusion | flops 302481408 | bytes 3538944 | tf_op jit(solution)/shard_map/dot_general | solution.py:204
  113.4 1.0 copy.49
  114.4 5.1 %all-to-all-start.2 = ((bf16[4,256,384]{2,1,0:T(8,128)(2,1)}), bf16[4,256,384]{2,1,0:T(8,128)(2,1)S(1)}, u32[]{:S(2)}, u32[]{:S(2)}) async-start(bf16[4,256,384]{2,1,0:T(8,128)(2,1)} %bitcast.82), calls=%async_computation.2 | async-start | bytes 1572864 | tf_op jit(solution)/shard_map/all_to_all | solution.py:40
  120.2 1.0 copy.50
  121.2 10.1 %all-to-all-done.2 = bf16[4,256,384]{2,1,0:T(8,128)(2,1)S(1)} async-done(((bf16[4,256,384]{2,1,0:T(8,128)(2,1)}), bf16[4,256,384]{2,1,0:T(8,128)(2,1)S(1)}, u32[]{:S(2)}, u32[]{:S(2)}) %all-to-all-start.2) | async-done | bytes 786464 | tf_op jit(solution)/shard_map/all_to_all | solution.py:40
  131.3 3.5 %all-to-all-start = ((bf16[4,256,384]{2,1,0:T(8,128)(2,1)}), bf16[4,256,384]{2,1,0:T(8,128)(2,1)S(1)}, u32[]{:S(2)}, u32[]{:S(2)}) async-start(bf16[4,256,384]{2,1,0:T(8,128)(2,1)} %bitcast.84), calls=%async_computation | async-start | bytes 1572864 | tf_op jit(solution)/shard_map/all_to_all | solution.py:40
  134.8 0.8 reduce_sum.45
  135.6 8.6 %all-to-all-done = bf16[4,256,384]{2,1,0:T(8,128)(2,1)S(1)} async-done(((bf16[4,256,384]{2,1,0:T(8,128)(2,1)}), bf16[4,256,384]{2,1,0:T(8,128)(2,1)S(1)}, u32[]{:S(2)}, u32[]{:S(2)}) %all-to-all-start) | async-done | bytes 786464 | tf_op jit(solution)/shard_map/all_to_all | solution.py:40
  144.3 0.8 reduce_sum.43
  (60 shorter events, 8.5 us)
Async XLA Ops:
  0.6 61.2 %copy-start = (bf16[384,1536]{1,0:T(8,128)(2,1)S(1)}, bf16[384,1536]{1,0:T(8,128)(2,1)}, u32[]{:S(2)}) copy-start(bf16[384,1536]{1,0:T(8,128)(2,1)} %param.11) | copy-start | bytes 3538948
  0.6 6.4 %copy-start.11 = (bf16[256,1536]{1,0:T(8,128)(2,1)S(1)}, bf16[256,1536]{1,0:T(8,128)(2,1)}, u32[]{:S(2)}) copy-start(bf16[256,1536]{1,0:T(8,128)(2,1)} %param.7) | copy-start | bytes 2359300
  2.7 56.1 %all-to-all-start.1 = ((bf16[4,256,384]{2,1,0:T(8,128)(2,1)}), bf16[4,256,384]{2,1,0:T(8,128)(2,1)}, u32[]{:S(2)}, u32[]{:S(2)}) async-start(bf16[4,256,384]{2,1,0:T(8,128)(2,1)} %broadcast_in_dim.28), calls=%async_computation.1 | async-start | bytes 1572864 | tf_op jit(solution)/shard_map/all_to_all | solution.py:46
  7.0 2.8 %copy-start.1 = (bf16[1536,384]{1,0:T(8,128)(2,1)S(1)}, bf16[1536,384]{1,0:T(8,128)(2,1)}, u32[]{:S(2)}) copy-start(bf16[1536,384]{1,0:T(8,128)(2,1)} %param.10) | copy-start | bytes 3538948
  10.6 44.9 %copy-start.9 = (bf16[1536,384]{1,0:T(8,128)(2,1)S(1)}, bf16[1536,384]{1,0:T(8,128)(2,1)}, u32[]{:S(2)}) copy-start(bf16[1536,384]{1,0:T(8,128)(2,1)} %param.8) | copy-start | bytes 3538948
  10.7 44.9 %copy-start.12 = (bf16[256,1536]{1,0:T(8,128)(2,1)S(1)}, bf16[256,1536]{1,0:T(8,128)(2,1)}, u32[]{:S(2)}) copy-start(bf16[256,1536]{1,0:T(8,128)(2,1)} %param.7) | copy-start | bytes 2359300
  55.5 1.5 %copy-start.14 = (f32[384]{0:T(512)S(1)}, f32[384]{0:T(512)}, u32[]{:S(2)}) copy-start(f32[384]{0:T(512)} %param.12) | copy-start | bytes 4612
  57.4 1.4 copy-start.5
  61.8 1.7 %copy-start.8 = (f32[6,64,256]{2,1,0:T(8,128)S(1)}, f32[6,64,256]{2,1,0:T(8,128)}, u32[]{:S(2)}) copy-start(f32[6,64,256]{2,1,0:T(8,128)} %fusion.50) | copy-start | bytes 1179652
  63.9 2.3 %copy-start.3 = (f32[256,6,64]{0,2,1:T(8,128)}, f32[256,6,64]{0,2,1:T(8,128)S(1)}, u32[]{:S(2)}) copy-start(f32[256,6,64]{0,2,1:T(8,128)S(1)} %get-tuple-element.56) | copy-start | bytes 1179652
  105.2 1.0 copy-start.6
  107.8 1.0 copy-start.7
  109.3 2.1 %copy-start.10 = (bf16[1536,384]{1,0:T(8,128)(2,1)S(1)}, bf16[1536,384]{1,0:T(8,128)(2,1)}, u32[]{:S(2)}) copy-start(bf16[1536,384]{1,0:T(8,128)(2,1)} %param.9) | copy-start | bytes 3538948
  109.3 2.1 %copy-start.13 = (f32[256,384]{1,0:T(8,128)S(1)}, f32[256,384]{1,0:T(8,128)}, u32[]{:S(2)}) copy-start(f32[256,384]{1,0:T(8,128)} %get-tuple-element.42) | copy-start | bytes 1179652
  111.5 1.3 copy-start.2
  114.4 5.1 %copy-start.4 = (f32[256,6,64]{0,2,1:T(8,128)S(1)}, f32[256,6,64]{0,2,1:T(8,128)}, u32[]{:S(2)}) copy-start(f32[256,6,64]{0,2,1:T(8,128)} %copy-done.3) | copy-start | bytes 1179652
  114.4 16.9 %all-to-all-start.2 = ((bf16[4,256,384]{2,1,0:T(8,128)(2,1)}), bf16[4,256,384]{2,1,0:T(8,128)(2,1)S(1)}, u32[]{:S(2)}, u32[]{:S(2)}) async-start(bf16[4,256,384]{2,1,0:T(8,128)(2,1)} %bitcast.82), calls=%async_computation.2 | async-start | bytes 1572864 | tf_op jit(solution)/shard_map/all_to_all | solution.py:40
  131.3 13.0 %all-to-all-start = ((bf16[4,256,384]{2,1,0:T(8,128)(2,1)}), bf16[4,256,384]{2,1,0:T(8,128)(2,1)S(1)}, u32[]{:S(2)}, u32[]{:S(2)}) async-start(bf16[4,256,384]{2,1,0:T(8,128)(2,1)} %bitcast.84), calls=%async_computation | async-start | bytes 1572864 | tf_op jit(solution)/shard_map/all_to_all | solution.py:40
where the time goes:
time: 146 us; the launch traced here: 145 us
  blocking collectives  85.7 us (59%)
  waiting for transfers between devices  18.8 us (13%)
  matrix products  15.1 us (10%)
  starting transfers between devices  12.9 us (9%)
  local copies, waits for them, and re-layouts  9.15 us (6%)
  other arithmetic  2.6 us (2%)
    all_gather x3, blocking collectives, prefix_by_axis(): pieces = lax.all_gather(running.astype(jnp.bfloat16), axis)  44.8 us
    all_gather x3, blocking collectives, carried_in(): lax.all_gather(running.astype(jnp.bfloat16 if x.dtype == jnp.float32 else...  40.9 us
    all_to_all x2, waiting for transfers between devices, sum_at_owner(): parts = lax.all_to_all(split_up(x, dim, devices), axis, 0, 0, tiled=True)  18.8 us
    all_to_all x2, starting transfers between devices, sum_at_owner(): parts = lax.all_to_all(split_up(x, dim, devices), axis, 0, 0, tiled=True)  8.57 us
    all_to_all x1, starting transfers between devices, copy_for_each(): lax.all_to_all(jnp.broadcast_to(x[None], (devices, *x.shape)), axis, 0, 0...  4.29 us
  transfers between devices with their start and end apart: 3, of which 2 were waited for; matrix products, arithmetic and copies ran while one was open for 7% of the time, Pallas kernels for 0%

commit v1 on v0

--- a/solution.py
+++ b/solution.py
@@ -11,23 +11,48 @@
 epsilon = 1e-06
 
 
-def nothing_yet(x, identity):
-    return jnp.broadcast_to(jnp.asarray(identity, x.dtype), x.shape)
-
-
-def prefix_by_axis(x, axes, combine, identity):
-    before = start = nothing_yet(x, identity)
-    running = x
-    for axis in reversed(axes):
-        devices, mine = (lax.axis_size(axis), lax.axis_index(axis))
-        pieces = lax.all_gather(running.astype(jnp.bfloat16), axis)
-        inside, running = (start, start)
-        for k in range(devices):
-            passed = k < mine
-            running = combine(running, pieces[k].astype(x.dtype))
-            inside = jnp.where(passed, running, inside)
-        before = combine(inside, before)
-    return before
+def shifts(count, step):
+    return [(i, (i + step) % count) for i in range(count)]
+
+
+SWAP = [(0, 1), (1, 0)]
+
+
+def seq_before(state, later):
+    z, y, c = (lax.axis_index(a) for a in SEQ)
+    if later:
+        z, y, c = (7 - z, 3 - y, 1 - c)
+    side = lax.axis_index("seq_2")
+    half = state.shape[0] // 2
+    low, high = (state[:half], state[half:])
+    own = jnp.where(side == 0, low, high)
+    other = jnp.where(side == 0, high, low)
+    pair = lax.ppermute(other.astype(jnp.bfloat16), "seq_2", SWAP).astype(jnp.float32)
+    chip = own + pair
+    chip16 = chip.astype(jnp.bfloat16)
+    plane, inside = (chip, jnp.zeros_like(chip))
+    for k in (1, 2, 3):
+        step = -k if later else k
+        got = lax.ppermute(chip16, "seq_1", shifts(4, step)).astype(jnp.float32)
+        plane = plane + got
+        inside = inside + jnp.where(y >= k, got, 0.0)
+    planes = lax.all_to_all(
+        jnp.broadcast_to(plane.astype(jnp.bfloat16)[None], (8, *plane.shape)), "seq_0", 0, 0, tiled=True
+    ).astype(jnp.float32)
+    order = jnp.arange(8)
+    order = 7 - order if later else order
+    inside = inside + jnp.sum(jnp.where((order < z)[:, None, None], planes, 0.0), axis=0)
+    send = inside + jnp.where(c == 0, own, 0.0)
+    got = lax.ppermute(send.astype(jnp.bfloat16), "seq_2", SWAP).astype(jnp.float32)
+    mine = inside + jnp.where(c == 1, pair, 0.0)
+    first, second = (jnp.where(side == 0, mine, got), jnp.where(side == 0, got, mine))
+    return jnp.concatenate([first, second], axis=0)
+
+
+def packed_scan(state, later):
+    heads = state.shape[0]
+    flat = state.reshape(heads * HD * HD // 128, 128)
+    return seq_before(flat, later).reshape(state.shape)
 
 
 def split_up(x, dim, devices):
@@ -57,23 +82,6 @@
     return in_order(parts, dim)
 
 
-def carried_in(x, axes, combine, identity):
-    before = start = nothing_yet(x, identity)
-    running = x
-    for axis in reversed(axes):
-        devices, mine = (lax.axis_size(axis), lax.axis_index(axis))
-        pieces = lax.all_gather(
-            running.astype(jnp.bfloat16 if x.dtype == jnp.float32 else x.dtype), axis
-        )
-        inside, running = (start, start)
-        for k in reversed(range(devices)):
-            passed = k > mine
-            running = combine(running, pieces[k].astype(x.dtype))
-            inside = jnp.where(passed, running, inside)
-        before = combine(inside, before)
-    return before
-
-
 def feature_map(inputs):
     return jnp.where(inputs > 0, inputs + 1.0, jnp.exp(jnp.minimum(inputs, 0.0)))
 
@@ -84,10 +92,6 @@
 
 def causal_table(block_rows):
     return (jnp.arange(block_rows)[:, None] >= jnp.arange(block_rows)[None, :]).astype(jnp.float32)
-
-
-def add_states(earlier, later):
-    return earlier + later
 
 
 def per_device(latents, w_query, w_key, w_value, w_out, head_gain, grad_out):
@@ -106,9 +110,7 @@
     mapped_query = feature_map(query_raw)
     mapped_key = feature_map(key_raw)
     forward_state_local = jnp.einsum("omw,omd->mwd", mapped_key, value_matrix)
-    prefix_state = prefix_by_axis(
-        forward_state_local, SEQ, add_states, jnp.zeros_like(forward_state_local)
-    )
+    prefix_state = packed_scan(forward_state_local, False)
     block_rows = min(512, row_count)
     block_count = row_count // block_rows
     causal_mask = causal_table(block_rows)
@@ -148,9 +150,7 @@
     row_stat = jnp.mean(raw * upstream, axis=-1, keepdims=True)
     unnormed_gradient = inv_scale * upstream - inv_scale * inv_scale * inv_scale * raw * row_stat
     reverse_state_local = jnp.einsum("wei,wej->eij", mapped_query, unnormed_gradient)
-    suffix_state = carried_in(
-        reverse_state_local, SEQ, add_states, jnp.zeros_like(reverse_state_local)
-    )
+    suffix_state = packed_scan(reverse_state_local, True)
 
     def backward_step(running_state, inputs):
         (

time: 146 us -> 129 us (0.88)
  the two profiles are of different devices: /device:TPU:8 before, /device:TPU:1 now
where the time goes in v1:
time: 129 us; the launch traced here: 127 us
  starting transfers between devices  45.8 us (36%)
  waiting for transfers between devices  25.7 us (20%)
  matrix products  22.9 us (18%)
  local copies, waits for them, and re-layouts  17.9 us (14%)
  other arithmetic  13.6 us (11%)
    all_to_all x2, starting transfers between devices, seq_before(): lax.all_to_all(jnp.broadcast_to(plane.astype(jnp.bfloat16)[None], (8, *pl...  12.2 us
    all_to_all x2, waiting for transfers between devices, seq_before(): lax.all_to_all(jnp.broadcast_to(plane.astype(jnp.bfloat16)[None], (8, *pl...  10.2 us
    all_to_all x2, waiting for transfers between devices, sum_at_owner(): parts = lax.all_to_all(split_up(x, dim, devices), axis, 0, 0, tiled=True)  10.1 us
    all_to_all x2, starting transfers between devices, sum_at_owner(): parts = lax.all_to_all(split_up(x, dim, devices), axis, 0, 0, tiled=True)  8.68 us
    ppermute x2, starting transfers between devices, seq_before(): lax.ppermute(other.astype(jnp.bfloat16), 'seq_2', SWAP).astype(jnp.float32)  7.78 us
    ppermute x2, starting transfers between devices, seq_before(): lax.ppermute(send.astype(jnp.bfloat16), 'seq_2', SWAP).astype(jnp.float32)  6.61 us
    ppermute x6, starting transfers between devices, seq_before(): got = lax.ppermute(chip16, 'seq_1', shifts(4, step)).astype(jnp.float32)  6.37 us
    all_to_all x1, starting transfers between devices, copy_for_each(): lax.all_to_all(jnp.broadcast_to(x[None], (devices, *x.shape)), axis, 0, 0...  4.15 us
  transfers between devices with their start and end apart: 15, of which 9 were waited for; matrix products, arithmetic and copies ran while one was open for 28% of the time, Pallas kernels for 0%

profile of v1, /device:TPU:1, one launch (start us, length us, event | category | flops | bytes accessed | tf_op | source)
XLA Modules:
  0.0 127.0 jit_solution(17459848678802317385)
XLA Ops:
  0.7 3.0 %add_select_fusion = (bf16[256,384]{1,0:T(8,128)(2,1)S(1)}, f32[256,384]{1,0:T(8,128)}) fusion(bf16[256,1536]{1,0:T(8,128)(2,1)} %param.7, bf16[1536,384]{1,0:T(8,128)(2,1)} %param.9), kind=kOutput, calls=%fused_computation.24 | convolution fusion | flops 302383104 | bytes 2555904 | tf_op jit(solution)/shard_map/dot_general | solution.py:104
  4.7 3.3 %collective-permute-start = (bf16[96,128]{1,0:T(8,128)(2,1)S(1)}, bf16[96,128]{1,0:T(8,128)(2,1)S(1)}, u32[]{:S(2)}, u32[]{:S(2)}) collective-permute-start(bf16[96,128]{1,0:T(8,128)(2,1)S(1)} %convert_element_type.107), channel_id=1, source_target_pairs={{0,4},{4,0},{1,5},{5,1},{2,6},{6,2},{3,7},{7,3},{8,12},{12,8},{9,1... | collective-permute-start | bytes 73736 | tf_op jit(solution)/shard_map/ppermute | solution.py:30
  8.0 2.6 %add_select_fusion.1 = (bf16[256,384]{1,0:T(8,128)(2,1)S(1)}, f32[256,384]{1,0:T(8,128)}) fusion(bf16[256,1536]{1,0:T(8,128)(2,1)S(1)} %copy-done.11, bf16[1536,384]{1,0:T(8,128)(2,1)} %param.8), kind=kOutput, calls=%fused_computation.26 | convolution fusion | flops 302383104 | bytes 2555904 | tf_op jit(solution)/shard_map/dot_general | solution.py:101
  10.8 2.2 %collective-permute-start.2 = (bf16[96,128]{1,0:T(8,128)(2,1)S(1)}, bf16[96,128]{1,0:T(8,128)(2,1)S(1)}, u32[]{:S(2)}, u32[]{:S(2)}) collective-permute-start(bf16[96,128]{1,0:T(8,128)(2,1)S(1)} %fusion.19), channel_id=1, source_target_pairs={{0,16},{8,24},{16,0},{24,8},{1,17},{9,25},{17,1},{25,9},{2,18},{10... | collective-permute-start | bytes 73736 | tf_op jit(solution)/shard_map/ppermute | solution.py:36
  16.7 8.0 %all-to-all-start = ((bf16[8,96,128]{2,1,0:T(8,128)(2,1)}), bf16[8,96,128]{2,1,0:T(8,128)(2,1)S(1)}, u32[]{:S(2)}, u32[]{:S(2)}) async-start(bf16[8,96,128]{2,1,0:T(8,128)(2,1)} %broadcast_in_dim.75), calls=%async_computation | async-start | bytes 393216 | tf_op jit(solution)/shard_map/all_to_all | solution.py:39
  25.1 8.2 %all-to-all-done = bf16[8,96,128]{2,1,0:T(8,128)(2,1)S(1)} async-done(((bf16[8,96,128]{2,1,0:T(8,128)(2,1)}), bf16[8,96,128]{2,1,0:T(8,128)(2,1)S(1)}, u32[]{:S(2)}, u32[]{:S(2)}) %all-to-all-start) | async-done | bytes 196640 | tf_op jit(solution)/shard_map/all_to_all | solution.py:39
  34.3 4.1 %all-to-all-start.2 = ((bf16[4,256,384]{2,1,0:T(8,128)(2,1)}), bf16[4,256,384]{2,1,0:T(8,128)(2,1)S(1)}, u32[]{:S(2)}, u32[]{:S(2)}) async-start(bf16[4,256,384]{2,1,0:T(8,128)(2,1)} %broadcast_in_dim.77), calls=%async_computation.2 | async-start | bytes 1572864 | tf_op jit(solution)/shard_map/all_to_all | solution.py:71
  39.4 3.5 %collective-permute-start.4 = (bf16[96,128]{1,0:T(8,128)(2,1)S(1)}, bf16[96,128]{1,0:T(8,128)(2,1)S(1)}, u32[]{:S(2)}, u32[]{:S(2)}) collective-permute-start(bf16[96,128]{1,0:T(8,128)(2,1)S(1)} %get-tuple-element.41), channel_id=1, source_target_pairs={{0,4},{4,0},{1,5},{5,1},{2,6},{6,2},{3,7},{7,3},{8,12},{12,8},{9,1... | collective-permute-start | bytes 73736 | tf_op jit(solution)/shard_map/ppermute | solution.py:46
  45.6 1.6 %all-to-all-done.2 = bf16[4,256,384]{2,1,0:T(8,128)(2,1)S(1)} async-done(((bf16[4,256,384]{2,1,0:T(8,128)(2,1)}), bf16[4,256,384]{2,1,0:T(8,128)(2,1)S(1)}, u32[]{:S(2)}, u32[]{:S(2)}) %all-to-all-start.2) | async-done | bytes 786464 | tf_op jit(solution)/shard_map/all_to_all | solution.py:71
  48.8 1.7 %reshape.147 = bf16[256,1536,1]{1,0,2:T(8,128)(2,1)S(1)} reshape(bf16[256,4,384]{2,1,0:T(4,128)(2,1)} %copy.47) | data formatting | bytes 1572864 | tf_op jit(solution)/shard_map/reshape | solution.py:77
  56.5 4.5 %collective-permute-start.5 = (bf16[96,128]{1,0:T(8,128)(2,1)}, bf16[96,128]{1,0:T(8,128)(2,1)}, u32[]{:S(2)}, u32[]{:S(2)}) collective-permute-start(bf16[96,128]{1,0:T(8,128)(2,1)} %convert_element_type.121), channel_id=1, source_target_pairs={{0,4},{4,0},{1,5},{5,1},{2,6},{6,2},{3,7},{7,3},{8,12},{12,8},{9,1... | collective-permute-start | bytes 73736 | tf_op jit(solution)/shard_map/ppermute | solution.py:30
  65.0 2.3 %collective-permute-start.6 = (bf16[96,128]{1,0:T(8,128)(2,1)S(1)}, bf16[96,128]{1,0:T(8,128)(2,1)S(1)}, u32[]{:S(2)}, u32[]{:S(2)}) collective-permute-start(bf16[96,128]{1,0:T(8,128)(2,1)S(1)} %fusion.20), channel_id=1, source_target_pairs={{0,24},{8,0},{16,8},{24,16},{1,25},{9,1},{17,9},{25,17},{2,26},{10... | collective-permute-start | bytes 73736 | tf_op jit(solution)/shard_map/ppermute | solution.py:36
  68.0 2.1 %convolution_add_fusion.4 = f32[6,64,256]{2,1,0:T(8,128)} fusion(f32[6,64,256]{2,1,0:T(8,128)} %fusion.30, bf16[256,6,64]{0,2,1:T(8,128)(2,1)S(1)} %bitcast.76, bf16[6,256,256]{2,1,0:T(8,128)(2,1)S(1)} %convolution_multiply_fusion), kind=kOutput, calls=%fused_computation.8 | convolution fusion | flops 50429952 | bytes 1769472 | tf_op jit(solution)/shard_map/while/body/eval_jaxpr/fui,ifc->ufc/dot_general | solution.py:169
  73.1 4.2 %all-to-all-start.3 = ((bf16[8,96,128]{2,1,0:T(8,128)(2,1)}), bf16[8,96,128]{2,1,0:T(8,128)(2,1)}, u32[]{:S(2)}, u32[]{:S(2)}) async-start(bf16[8,96,128]{2,1,0:T(8,128)(2,1)} %broadcast_in_dim.79), calls=%async_computation.3 | async-start | bytes 393216 | tf_op jit(solution)/shard_map/all_to_all | solution.py:39
  77.3 1.8 %multiply_convert_fusion.2 = bf16[256,6,64]{0,2,1:T(8,128)(2,1)} fusion(f32[256,6,64]{0,2,1:T(8,128)} %copy-done.3, f32[6,64]{1,0:T(8,128)S(1)} %mul.110, f32[256,6]{0,1:T(8,128)S(1)} %get-tuple-element.59), kind=kLoop, calls=%fused_computation.20 | loop fusion | flops 294912 | bytes 597504 | tf_op jit(solution)/shard_map/convert_element_type | solution.py:142
  79.1 1.9 %copy.48 = f32[256,384]{1,0:T(8,128)} copy(f32[256,384]{0,1:T(8,128)} %bitcast.86) | data formatting | bytes 786432 | tf_op jit(solution)/shard_map/reshape | solution.py:194
  83.5 2.0 %all-to-all-done.3 = bf16[8,96,128]{2,1,0:T(8,128)(2,1)} async-done(((bf16[8,96,128]{2,1,0:T(8,128)(2,1)}), bf16[8,96,128]{2,1,0:T(8,128)(2,1)}, u32[]{:S(2)}, u32[]{:S(2)}) %all-to-all-start.3) | async-done | bytes 196640 | tf_op jit(solution)/shard_map/all_to_all | solution.py:39
  85.5 4.2 %all-to-all-start.1 = ((bf16[4,256,384]{2,1,0:T(8,128)(2,1)}), bf16[4,256,384]{2,1,0:T(8,128)(2,1)}, u32[]{:S(2)}, u32[]{:S(2)}) async-start(bf16[4,256,384]{2,1,0:T(8,128)(2,1)} %bitcast.83), calls=%async_computation.1 | async-start | bytes 1572864 | tf_op jit(solution)/shard_map/all_to_all | solution.py:65
  91.6 3.1 %collective-permute-start.9 = (bf16[96,128]{1,0:T(8,128)(2,1)S(1)}, bf16[96,128]{1,0:T(8,128)(2,1)S(1)}, u32[]{:S(2)}, u32[]{:S(2)}) collective-permute-start(bf16[96,128]{1,0:T(8,128)(2,1)S(1)} %get-tuple-element.39), channel_id=1, source_target_pairs={{0,4},{4,0},{1,5},{5,1},{2,6},{6,2},{3,7},{7,3},{8,12},{12,8},{9,1... | collective-permute-start | bytes 73736 | tf_op jit(solution)/shard_map/ppermute | solution.py:46
  94.7 3.3 %fusion.4 = f32[256,1536]{1,0:T(8,128)} fusion(bf16[1536,384]{1,0:T(8,128)(2,1)} %param.8, f32[256,384]{1,0:T(8,128)} %copy.48, f32[256,384]{1,0:T(8,128)} %get-tuple-element.63), kind=kOutput, calls=%fused_computation.29 | convolution fusion | flops 302481408 | bytes 3538944 | tf_op jit(solution)/shard_map/dot_general | solution.py:204
  104.2 2.5 %convolution_add_fusion.1 = f32[256,1536]{1,0:T(8,128)S(1)} fusion(f32[256,1536]{1,0:T(8,128)} %fusion.4, bf16[1536,384]{1,0:T(8,128)(2,1)} %param.9, f32[256,384]{1,0:T(8,128)S(1)} %copy.49, f32[256,384]{1,0:T(8,128)} %get-tuple-element.61), kind=kOutput, calls=%fused_computation.1 | convolution fusion | flops 302874624 | bytes 5111808 | tf_op jit(solution)/shard_map/dot_general | solution.py:205
  109.6 4.5 %all-to-all-start.4 = ((bf16[4,256,384]{2,1,0:T(8,128)(2,1)}), bf16[4,256,384]{2,1,0:T(8,128)(2,1)S(1)}, u32[]{:S(2)}, u32[]{:S(2)}) async-start(bf16[4,256,384]{2,1,0:T(8,128)(2,1)} %bitcast.66), calls=%async_computation.4 | async-start | bytes 1572864 | tf_op jit(solution)/shard_map/all_to_all | solution.py:65
  114.1 2.0 %reduce_sum.62 = bf16[256,384]{1,0:T(8,128)(2,1)} reduce(bf16[4,256,384]{2,1,0:T(8,128)(2,1)} %all-to-all-done.1, bf16[]{:T(256)} %constant.66.clone.1), dimensions={0}, to_apply=%region_2.3 | reduce | flops 294912 | bytes 983042 | tf_op jit(solution)/shard_map/reduce_sum | solution.py:66
  116.1 10.1 %all-to-all-done.4 = bf16[4,256,384]{2,1,0:T(8,128)(2,1)S(1)} async-done(((bf16[4,256,384]{2,1,0:T(8,128)(2,1)}), bf16[4,256,384]{2,1,0:T(8,128)(2,1)S(1)}, u32[]{:S(2)}, u32[]{:S(2)}) %all-to-all-start.4) | async-done | bytes 786464 | tf_op jit(solution)/shard_map/all_to_all | solution.py:65
  (114 shorter events, 39.1 us)
Async XLA Ops:
  0.6 49.8 %copy-start = (bf16[384,1536]{1,0:T(8,128)(2,1)S(1)}, bf16[384,1536]{1,0:T(8,128)(2,1)}, u32[]{:S(2)}) copy-start(bf16[384,1536]{1,0:T(8,128)(2,1)} %param.11) | copy-start | bytes 3538948
  4.7 6.0 %collective-permute-start = (bf16[96,128]{1,0:T(8,128)(2,1)S(1)}, bf16[96,128]{1,0:T(8,128)(2,1)S(1)}, u32[]{:S(2)}, u32[]{:S(2)}) collective-permute-start(bf16[96,128]{1,0:T(8,128)(2,1)S(1)} %convert_element_type.107), channel_id=1, source_target_pairs={{0,4},{4,0},{1,5},{5,1},{2,6},{6,2},{3,7},{7,3},{8,12},{12,8},{9,1... | collective-permute-start | bytes 73736 | tf_op jit(solution)/shard_map/ppermute | solution.py:30
  10.7 13.9 %copy-start.12 = (f32[96,128]{1,0:T(8,128)}, f32[96,128]{1,0:T(8,128)S(1)}, u32[]{:S(2)}) copy-start(f32[96,128]{1,0:T(8,128)S(1)} %select_n.142) | copy-start | bytes 147460
  10.7 13.9 %copy-start.14 = (bf16[96,128]{1,0:T(8,128)(2,1)}, bf16[96,128]{1,0:T(8,128)(2,1)S(1)}, u32[]{:S(2)}) copy-start(bf16[96,128]{1,0:T(8,128)(2,1)S(1)} %collective-permute-done) | copy-start | bytes 73732
  10.7 4.0 %collective-permute-start.1 = (bf16[96,128]{1,0:T(8,128)(2,1)S(1)}, bf16[96,128]{1,0:T(8,128)(2,1)S(1)}, u32[]{:S(2)}, u32[]{:S(2)}) collective-permute-start(bf16[96,128]{1,0:T(8,128)(2,1)S(1)} %fusion.19), channel_id=1, source_target_pairs={{0,8},{8,16},{16,24},{24,0},{1,9},{9,17},{17,25},{25,1},{2,10},{10... | collective-permute-start | bytes 73736 | tf_op jit(solution)/shard_map/ppermute | solution.py:36
  10.8 4.3 %collective-permute-start.2 = (bf16[96,128]{1,0:T(8,128)(2,1)S(1)}, bf16[96,128]{1,0:T(8,128)(2,1)S(1)}, u32[]{:S(2)}, u32[]{:S(2)}) collective-permute-start(bf16[96,128]{1,0:T(8,128)(2,1)S(1)} %fusion.19), channel_id=1, source_target_pairs={{0,16},{8,24},{16,0},{24,8},{1,17},{9,25},{17,1},{25,9},{2,18},{10... | collective-permute-start | bytes 73736 | tf_op jit(solution)/shard_map/ppermute | solution.py:36
  13.0 2.9 %collective-permute-start.3 = (bf16[96,128]{1,0:T(8,128)(2,1)S(1)}, bf16[96,128]{1,0:T(8,128)(2,1)S(1)}, u32[]{:S(2)}, u32[]{:S(2)}) collective-permute-start(bf16[96,128]{1,0:T(8,128)(2,1)S(1)} %fusion.19), channel_id=1, source_target_pairs={{0,24},{8,0},{16,8},{24,16},{1,25},{9,1},{17,9},{25,17},{2,26},{10... | collective-permute-start | bytes 73736 | tf_op jit(solution)/shard_map/ppermute | solution.py:36
  14.1 11.0 %copy-start.4 = (f32[256,256]{1,0:T(8,128)}, f32[256,256]{1,0:T(8,128)S(1)}, u32[]{:S(2)}) copy-start(f32[256,256]{1,0:T(8,128)S(1)} %fusion.3) | copy-start | bytes 786436
  14.3 19.1 %copy-start.15 = (bf16[256,384]{1,0:T(8,128)(2,1)S(1)}, bf16[256,384]{1,0:T(8,128)(2,1)}, u32[]{:S(2)}) copy-start(bf16[256,384]{1,0:T(8,128)(2,1)} %param.13) | copy-start | bytes 589828
  14.7 9.9 %copy-start.16 = (bf16[96,128]{1,0:T(8,128)(2,1)}, bf16[96,128]{1,0:T(8,128)(2,1)S(1)}, u32[]{:S(2)}) copy-start(bf16[96,128]{1,0:T(8,128)(2,1)S(1)} %collective-permute-done.1) | copy-start | bytes 73732
  15.1 9.5 %copy-start.17 = (bf16[96,128]{1,0:T(8,128)(2,1)}, bf16[96,128]{1,0:T(8,128)(2,1)S(1)}, u32[]{:S(2)}) copy-start(bf16[96,128]{1,0:T(8,128)(2,1)S(1)} %collective-permute-done.2) | copy-start | bytes 73732
  15.9 8.8 %copy-start.18 = (bf16[96,128]{1,0:T(8,128)(2,1)}, bf16[96,128]{1,0:T(8,128)(2,1)S(1)}, u32[]{:S(2)}) copy-start(bf16[96,128]{1,0:T(8,128)(2,1)S(1)} %collective-permute-done.3) | copy-start | bytes 73732
  16.7 16.7 %all-to-all-start = ((bf16[8,96,128]{2,1,0:T(8,128)(2,1)}), bf16[8,96,128]{2,1,0:T(8,128)(2,1)S(1)}, u32[]{:S(2)}, u32[]{:S(2)}) async-start(bf16[8,96,128]{2,1,0:T(8,128)(2,1)} %broadcast_in_dim.75), calls=%async_computation | async-start | bytes 393216 | tf_op jit(solution)/shard_map/all_to_all | solution.py:39
  34.3 8.5 %copy-start.22 = (f32[384]{0:T(512)S(1)}, f32[384]{0:T(512)}, u32[]{:S(2)}) copy-start(f32[384]{0:T(512)} %param.12) | copy-start | bytes 4612
  34.3 12.9 %all-to-all-start.2 = ((bf16[4,256,384]{2,1,0:T(8,128)(2,1)}), bf16[4,256,384]{2,1,0:T(8,128)(2,1)S(1)}, u32[]{:S(2)}, u32[]{:S(2)}) async-start(bf16[4,256,384]{2,1,0:T(8,128)(2,1)} %broadcast_in_dim.77), calls=%async_computation.2 | async-start | bytes 1572864 | tf_op jit(solution)/shard_map/all_to_all | solution.py:71
  39.4 4.3 %collective-permute-start.4 = (bf16[96,128]{1,0:T(8,128)(2,1)S(1)}, bf16[96,128]{1,0:T(8,128)(2,1)S(1)}, u32[]{:S(2)}, u32[]{:S(2)}) collective-permute-start(bf16[96,128]{1,0:T(8,128)(2,1)S(1)} %get-tuple-element.41), channel_id=1, source_target_pairs={{0,4},{4,0},{1,5},{5,1},{2,6},{6,2},{3,7},{7,3},{8,12},{12,8},{9,1... | collective-permute-start | bytes 73736 | tf_op jit(solution)/shard_map/ppermute | solution.py:46
  56.5 7.7 %collective-permute-start.5 = (bf16[96,128]{1,0:T(8,128)(2,1)}, bf16[96,128]{1,0:T(8,128)(2,1)}, u32[]{:S(2)}, u32[]{:S(2)}) collective-permute-start(bf16[96,128]{1,0:T(8,128)(2,1)} %convert_element_type.121), channel_id=1, source_target_pairs={{0,4},{4,0},{1,5},{5,1},{2,6},{6,2},{3,7},{7,3},{8,12},{12,8},{9,1... | collective-permute-start | bytes 73736 | tf_op jit(solution)/shard_map/ppermute | solution.py:30
  65.0 5.2 %collective-permute-start.6 = (bf16[96,128]{1,0:T(8,128)(2,1)S(1)}, bf16[96,128]{1,0:T(8,128)(2,1)S(1)}, u32[]{:S(2)}, u32[]{:S(2)}) collective-permute-start(bf16[96,128]{1,0:T(8,128)(2,1)S(1)} %fusion.20), channel_id=1, source_target_pairs={{0,24},{8,0},{16,8},{24,16},{1,25},{9,1},{17,9},{25,17},{2,26},{10... | collective-permute-start | bytes 73736 | tf_op jit(solution)/shard_map/ppermute | solution.py:36
  67.4 4.2 %collective-permute-start.7 = (bf16[96,128]{1,0:T(8,128)(2,1)S(1)}, bf16[96,128]{1,0:T(8,128)(2,1)S(1)}, u32[]{:S(2)}, u32[]{:S(2)}) collective-permute-start(bf16[96,128]{1,0:T(8,128)(2,1)S(1)} %fusion.20), channel_id=1, source_target_pairs={{0,16},{8,24},{16,0},{24,8},{1,17},{9,25},{17,1},{25,9},{2,18},{10... | collective-permute-start | bytes 73736 | tf_op jit(solution)/shard_map/ppermute | solution.py:36
  67.4 4.2 %collective-permute-start.8 = (bf16[96,128]{1,0:T(8,128)(2,1)S(1)}, bf16[96,128]{1,0:T(8,128)(2,1)S(1)}, u32[]{:S(2)}, u32[]{:S(2)}) collective-permute-start(bf16[96,128]{1,0:T(8,128)(2,1)S(1)} %fusion.20), channel_id=1, source_target_pairs={{0,8},{8,16},{16,24},{24,0},{1,9},{9,17},{17,25},{25,1},{2,10},{10... | collective-permute-start | bytes 73736 | tf_op jit(solution)/shard_map/ppermute | solution.py:36
  73.1 12.4 %all-to-all-start.3 = ((bf16[8,96,128]{2,1,0:T(8,128)(2,1)}), bf16[8,96,128]{2,1,0:T(8,128)(2,1)}, u32[]{:S(2)}, u32[]{:S(2)}) async-start(bf16[8,96,128]{2,1,0:T(8,128)(2,1)} %broadcast_in_dim.79), calls=%async_computation.3 | async-start | bytes 393216 | tf_op jit(solution)/shard_map/all_to_all | solution.py:39
  85.5 24.2 %all-to-all-start.1 = ((bf16[4,256,384]{2,1,0:T(8,128)(2,1)}), bf16[4,256,384]{2,1,0:T(8,128)(2,1)}, u32[]{:S(2)}, u32[]{:S(2)}) async-start(bf16[4,256,384]{2,1,0:T(8,128)(2,1)} %bitcast.83), calls=%async_computation.1 | async-start | bytes 1572864 | tf_op jit(solution)/shard_map/all_to_all | solution.py:65
  91.6 6.5 %collective-permute-start.9 = (bf16[96,128]{1,0:T(8,128)(2,1)S(1)}, bf16[96,128]{1,0:T(8,128)(2,1)S(1)}, u32[]{:S(2)}, u32[]{:S(2)}) collective-permute-start(bf16[96,128]{1,0:T(8,128)(2,1)S(1)} %get-tuple-element.39), channel_id=1, source_target_pairs={{0,4},{4,0},{1,5},{5,1},{2,6},{6,2},{3,7},{7,3},{8,12},{12,8},{9,1... | collective-permute-start | bytes 73736 | tf_op jit(solution)/shard_map/ppermute | solution.py:46
  109.6 16.6 %all-to-all-start.4 = ((bf16[4,256,384]{2,1,0:T(8,128)(2,1)}), bf16[4,256,384]{2,1,0:T(8,128)(2,1)S(1)}, u32[]{:S(2)}, u32[]{:S(2)}) async-start(bf16[4,256,384]{2,1,0:T(8,128)(2,1)} %bitcast.66), calls=%async_computation.4 | async-start | bytes 1572864 | tf_op jit(solution)/shard_map/all_to_all | solution.py:65
  (14 other events, 33.6 us)

commit v2 on v1

v2 whole, which is shorter than its diff:
```python
import functools

import jax
import jax.numpy as jnp
from jax import lax
from jax.experimental import pallas as pl
from jax.experimental.pallas import tpu as pltpu
from jax.sharding import Mesh
from jax.sharding import PartitionSpec as P

HD = 64
LANES = 128
SEQ = ("seq_0", "seq_1", "seq_2")
SWAP = [(0, 1), (1, 0)]
epsilon = 1e-06
f32, bf16 = (jnp.float32, jnp.bfloat16)
NT = (((1,), (1,)), ((), ()))
TN = (((0,), (0,)), ((), ()))
VMEM = pl.BlockSpec(memory_space=pltpu.VMEM)


def shifts(count, step):
    return [(i, (i + step) % count) for i in range(count)]


def mm(a, b, contract=(((1,), (0,)), ((), ()))):
    return lax.dot_general(a, b, contract, preferred_element_type=f32)


def call(body, outs, flops, moved, **extra):
    return pl.pallas_call(
        body,
        out_shape=[jax.ShapeDtypeStruct(s, d) for s, d in outs],
        cost_estimate=pl.CostEstimate(flops=flops, bytes_accessed=moved, transcendentals=0),
        compiler_params=pltpu.CompilerParams(vmem_limit_bytes=20 * 1024 * 1024),
        **extra,
    )


def plain(body, outs, flops, moved, *args):
    return call(
        body, outs, flops, moved, in_specs=[VMEM] * len(args), out_specs=[VMEM] * len(outs)
    )(*args)


def feature_map(u):
    return jnp.where(u > 0, u + 1.0, jnp.exp(jnp.minimum(u, 0.0)))


def low_lanes(shape):
    return lax.broadcasted_iota(jnp.int32, shape, len(shape) - 1) < HD


def one_head(x, head):
    low = low_lanes(x.shape)
    keep = low if head == 0 else jnp.logical_not(low)
    return jnp.where(keep, x, jnp.zeros_like(x))


def pack(full):
    return jnp.where(low_lanes((HD, LANES)), full[:HD], full[HD:])


def unpack(rows):
    low = low_lanes((HD, LANES))
    zero = jnp.zeros_like(rows)
    return jnp.concatenate([jnp.where(low, rows, zero), jnp.where(low, zero, rows)], axis=0)


def head_ones():
    r = lax.broadcasted_iota(jnp.int32, (LANES, LANES), 0) < HD
    c = lax.broadcasted_iota(jnp.int32, (LANES, LANES), 1) < HD
    return jnp.where(r == c, 1.0, 0.0).astype(bf16)


def split_state(state_ref, own_ref, other_ref):
    half = own_ref.shape[0]
    side = lax.axis_index("seq_2")
    own_ref[...] = state_ref[pl.ds(pl.multiple_of(side * half, 16), half), :]
    other_ref[...] = state_ref[pl.ds(pl.multiple_of((1 - side) * half, 16), half), :].astype(bf16)


def whole_state(later, inside_ref, pair_ref, got_ref, state_ref):
    half = inside_ref.shape[0]
    side = lax.axis_index("seq_2")
    last = side == (0 if later else 1)
    mine = inside_ref[...] + jnp.where(last, pair_ref[...].astype(f32), 0.0)
    state_ref[pl.ds(pl.multiple_of(side * half, 16), half), :] = mine
    state_ref[pl.ds(pl.multiple_of((1 - side) * half, 16), half), :] = got_ref[...].astype(f32)


def seq_before(later, own, other):
    half = own.shape[0]
    pair = lax.ppermute(other, "seq_2", SWAP)

    def add_pair(own_ref, pair_ref, chip_ref):
        chip_ref[...] = (own_ref[...] + pair_ref[...].astype(f32)).astype(bf16)

    (chip,) = plain(add_pair, [((half, LANES), bf16)], 1, half * 1024, own, pair)
    got = [lax.ppermute(chip, "seq_1", shifts(4, -k if later else k)) for k in (1, 2, 3)]

    def add_plane(own_ref, pair_ref, g1, g2, g3, inside_ref, planes_ref):
        y = lax.axis_index("seq_1")
        y = 3 - y if later else y
        total = own_ref[...] + pair_ref[...].astype(f32)
        inside = jnp.zeros_like(total)
        for k, ref in ((1, g1), (2, g2), (3, g3)):
            piece = ref[...].astype(f32)
            total = total + piece
            inside = inside + jnp.where(y >= k, piece, 0.0)
        inside_ref[...] = inside
        planes_ref[...] = jnp.broadcast_to(total.astype(bf16)[None], planes_ref.shape)

    in_plane, planes = plain(
        add_plane,
        [((half, LANES), f32), ((8, half, LANES), bf16)],
        1,
        half * 4096,
        own,
        pair,
        *got,
    )
    planes = lax.all_to_all(planes, "seq_0", 0, 0, tiled=True)

    def add_planes(inside_ref, own_ref, planes_ref, out_ref, send_ref):
        z = lax.axis_index("seq_0")
        first = lax.axis_index("seq_2") == (1 if later else 0)
        total = inside_ref[...]
        for k in range(8):
            take = (k > z) if later else (k < z)
            total = total + jnp.where(take, planes_ref[k].astype(f32), 0.0)
        out_ref[...] = total
        send_ref[...] = (total + jnp.where(first, own_ref[...], 0.0)).astype(bf16)

    inside, send = plain(
        add_planes,
        [((half, LANES), f32), ((half, LANES), bf16)],
        1,
        half * 4096,
        in_plane,
        own,
        planes,
    )
    return inside, pair, lax.ppermute(send, "seq_2", SWAP), in_plane, chip


def key_value(latents, w_key, w_value):
    rows, width = (latents.shape[0], w_key.shape[1])
    half = width * HD // LANES // 2
    steps = 3
    depth = latents.shape[1] // steps

    def body(x_ref, wk_ref, wv_ref, fk_ref, v_ref, own_ref, other_ref, k_acc, v_acc, state):
        step = pl.program_id(0)

        @pl.when(step == 0)
        def _():
            k_acc[...] = jnp.zeros_like(k_acc)
            v_acc[...] = jnp.zeros_like(v_acc)

        x = x_ref[...]
        k_acc[...] += mm(x, wk_ref[...])
        v_acc[...] += mm(x, wv_ref[...])

        @pl.when(step == steps - 1)
        def _():
            fk_ref[...] = feature_map(k_acc[...]).astype(bf16)
            v_ref[...] = v_acc[...].astype(bf16)
            for p in range(width // LANES):
                cols = slice(p * LANES, (p + 1) * LANES)
                state[p * HD : (p + 1) * HD, :] = pack(mm(fk_ref[:, cols], v_ref[:, cols], TN))
            split_state(state, own_ref, other_ref)

    fixed = lambda i: (0, 0)
    return call(
        body,
        [((rows, width), bf16), ((rows, width), bf16), ((half, LANES), f32), ((half, LANES), bf16)],
        4 * rows * width * latents.shape[1],
        3 * 1024 * 1024,
        grid=(steps,),
        in_specs=[
            pl.BlockSpec((rows, depth), lambda i: (0, i)),
            pl.BlockSpec((depth, width), lambda i: (i, 0)),
            pl.BlockSpec((depth, width), lambda i: (i, 0)),
        ],
        out_specs=[
            pl.BlockSpec((rows, width), fixed),
            pl.BlockSpec((rows, width), fixed),
            pl.BlockSpec((half, LANES), fixed),
            pl.BlockSpec((half, LANES), fixed),
        ],
        scratch_shapes=[
            pltpu.VMEM((rows, width), f32),
            pltpu.VMEM((rows, width), f32),
            pltpu.VMEM((2 * half, LANES), f32),
        ],
    )(latents, w_key, w_value)


def tri(rows, upper):
    t = lax.broadcasted_iota(jnp.int32, (rows, rows), 0)
    s = lax.broadcasted_iota(jnp.int32, (rows, rows), 1)
    return (t <= s) if upper else (t >= s)


def masked(scores, keep):
    return jnp.where(keep, scores, 0.0).astype(bf16)


def query_local(latents, w_query, fk, v):
    rows, width = fk.shape

    def body(x_ref, wq_ref, fk_ref, v_ref, fq_ref, raw_ref):
        fq_ref[...] = feature_map(mm(x_ref[...], wq_ref[...])).astype(bf16)
        keep = tri(rows, False)
        for p in range(width // LANES):
            cols = slice(p * LANES, (p + 1) * LANES)
            q, k, val = (fq_ref[:, cols], fk_ref[:, cols], v_ref[:, cols])
            total = None
            for h in (0, 1):
                score = masked(mm(q, one_head(k, h), NT), keep)
                part = mm(score, one_head(val, h))
                total = part if total is None else total + part
            raw_ref[:, cols] = total

    return plain(
        body,
        [((rows, width), bf16), ((rows, width), f32)],
        2 * rows * width * (latents.shape[1] + 4 * rows),
        3 * 1024 * 1024,
        latents,
        w_query,
        fk,
        v,
    )


def upstream_of(grads, w_out, gain):
    rows, width = grads[0].shape

    def body(g0, g1, g2, g3, w_ref, gain_ref, up_ref):
        m = lax.axis_index("mp")
        total = jnp.zeros((rows, width), f32)
        for k, ref in enumerate((g0, g1, g2, g3)):
            at = lax.rem(m + 4 - k, 4) * width
            total = total + mm(ref[...], w_ref[:, pl.ds(pl.multiple_of(at, LANES), width)], NT)
        up_ref[...] = total * gain_ref[...]

    return plain(
        body,
        [((rows, width), f32)],
        8 * rows * width * width,
        3 * 1024 * 1024,
        *grads,
        w_out,
        gain,
    )[0]


def normed(inside, pair, got, fq, raw_local, up, gain):
    rows, width = fq.shape
    half = inside.shape[0]

    def body(
        inside_ref,
        pair_ref,
        got_ref,
        fq_ref,
        raw_ref,
        up_ref,
        gain_ref,
        attn_ref,
        draw_ref,
        before_ref,
        own_ref,
        other_ref,
        state,
    ):
        whole_state(False, inside_ref, pair_ref, got_ref, state)
        before_ref[...] = state[...].astype(bf16)
        ones = head_ones()
        for p in range(width // LANES):
            cols = slice(p * LANES, (p + 1) * LANES)
            q = fq_ref[:, cols]
            raw = raw_ref[:, cols] + mm(q, unpack(before_ref[p * HD : (p + 1) * HD, :]))
            upstream = up_ref[:, cols]
            square = mm((raw * raw).astype(bf16), ones) * (1.0 / HD)
            cross = mm((raw * upstream).astype(bf16), ones) * (1.0 / HD)
            inv = lax.rsqrt(square + epsilon)
            unit = raw * inv
            attn_ref[:, cols] = (unit * gain_ref[:, cols]).astype(bf16)
            draw = (inv * upstream - inv * inv * unit * cross).astype(bf16)
            draw_ref[:, cols] = draw
            state[p * HD : (p + 1) * HD, :] = pack(mm(q, draw, TN))
        split_state(state, own_ref, other_ref)

    return call(
        body,
        [
            ((rows, width), bf16),
            ((rows, width), bf16),
            ((2 * half, LANES), bf16),
            ((half, LANES), f32),
            ((half, LANES), bf16),
        ],
        8 * rows * width * LANES,
        2 * 1024 * 1024,
        in_specs=[VMEM] * 7,
        out_specs=[VMEM] * 5,
        scratch_shapes=[pltpu.VMEM((2 * half, LANES), f32)],
    )(inside, pair, got, fq, raw_local, up, gain)


def branch_parts(attn, w_out):
    rows, width = attn.shape

    def body(attn_ref, w_ref, *outs):
        m = lax.axis_index("mp")
        for k, ref in zip((2, 1, 3, 0), outs):
            at = lax.rem(m + k, 4) * width
            ref[...] = mm(
                attn_ref[...], w_ref[:, pl.ds(pl.multiple_of(at, LANES), width)]
            ).astype(bf16)

    return plain(
        body,
        [((rows, width), bf16)] * 4,
        8 * rows * width * width,
        2 * 1024 * 1024,
        attn,
        w_out,
    )


def local_grads(fq, fk, v, draw, before):
    rows, width = fq.shape

    def body(fq_ref, fk_ref, v_ref, draw_ref, before_ref, dq_ref, dk_ref, dv_ref):
        lower, upper = (tri(rows, False), tri(rows, True))
        for p in range(width // LANES):
            cols = slice(p * LANES, (p + 1) * LANES)
            q, k, val, dr = (fq_ref[:, cols], fk_ref[:, cols], v_ref[:, cols], draw_ref[:, cols])
            dq = mm(dr, unpack(before_ref[p * HD : (p + 1) * HD, :]), NT)
            dk, dv = (None, None)
            for h in (0, 1):
                val_h, k_h, q_h, dr_h = (one_head(a, h) for a in (val, k, q, dr))
                dq = dq + mm(masked(mm(dr, val_h, NT), lower), k_h)
                dk_h = mm(masked(mm(val_h, dr, NT), upper), q_h)
                dv_h = mm(masked(mm(k_h, q, NT), upper), dr_h)
                dk = dk_h if dk is None else dk + dk_h
                dv = dv_h if dv is None else dv + dv_h
            dq_ref[:, cols] = (dq * jnp.minimum(q.astype(f32), 1.0)).astype(bf16)
            dk_ref[:, cols] = dk
            dv_ref[:, cols] = dv

    return plain(
        body,
        [((rows, width), bf16), ((rows, width), f32), ((rows, width), f32)],
        24 * rows * rows * width,
        3 * 1024 * 1024,
        fq,
        fk,
        v,
        draw,
        before,
    )


def latent_part(m, k, width, triples):
    rows = pl.ds(pl.multiple_of(lax.rem(m + k, 4) * width, LANES), width)
    total = None
    for grad_ref, w_ref in triples:
        part = mm(grad_ref[...], w_ref[rows, :], NT)
        total = part if total is None else total + part
    return total.astype(bf16)


def first_part(inside, pair, got, fk, v, dq, dk, dv, w_query, w_key, w_value):
    rows, width = fk.shape
    half = inside.shape[0]

    def body(
        inside_ref,
        pair_ref,
        got_ref,
        fk_ref,
        v_ref,
        dq_ref,
        dkl_ref,
        dvl_ref,
        wq_ref,
        wk_ref,
        wv_ref,
        dk_ref,
        dv_ref,
        part_ref,
        state,
    ):
        whole_state(True, inside_ref, pair_ref, got_ref, state)
        for p in range(width // LANES):
            cols = slice(p * LANES, (p + 1) * LANES)
            after = unpack(state[p * HD : (p + 1) * HD, :].astype(bf16))
            k = fk_ref[:, cols]
            dk = dkl_ref[:, cols] + mm(v_ref[:, cols], after, NT)
            dk_ref[:, cols] = (dk * jnp.minimum(k.astype(f32), 1.0)).astype(bf16)
            dv_ref[:, cols] = (dvl_ref[:, cols] + mm(k, after)).astype(bf16)
        m = lax.axis_index("mp")
        part_ref[...] = latent_part(
            m, 2, width, ((dq_ref, wq_ref), (dk_ref, wk_ref), (dv_ref, wv_ref))
        )

    return call(
        body,
        [((rows, width), bf16)] * 3,
        6 * rows * width * width,
        5 * 1024 * 1024,
        in_specs=[VMEM] * 11,
        out_specs=[VMEM] * 3,
        scratch_shapes=[pltpu.VMEM((2 * half, LANES), f32)],
    )(inside, pair, got, fk, v, dq, dk, dv, w_query, w_key, w_value)


def other_parts(which, dq, dk, dv, w_query, w_key, w_value):
    rows, width = dq.shape

    def body(dq_ref, dk_ref, dv_ref, wq_ref, wk_ref, wv_ref, *outs):
        m = lax.axis_index("mp")
        for k, ref in zip(which, outs):
            ref[...] = latent_part(
                m, k, width, ((dq_ref, wq_ref), (dk_ref, wk_ref), (dv_ref, wv_ref))
            )

    return plain(
        body,
        [((rows, width), bf16)] * len(which),
        6 * rows * width * width * len(which),
        5 * 1024 * 1024,
        dq,
        dk,
        dv,
        w_query,
        w_key,
        w_value,
    )


def add_up(parts):
    total = parts[0].astype(f32)
    for part in parts[1:]:
        total = total + part.astype(f32)
    return total.astype(bf16)


def to_owner(part, k):
    return lax.ppermute(part, "mp", shifts(4, k))


def per_device(latents, w_query, w_key, w_value, w_out, head_gain, grad_out):
    gain = head_gain.reshape(1, -1)
    fk, v, own, other = key_value(latents, w_key, w_value)
    inside, pair, got, in_plane, chip = seq_before(False, own, other)
    grad_held, _ = lax.optimization_barrier((grad_out, chip))
    grads = [grad_out] + [to_owner(grad_held, k) for k in (1, 2, 3)]
    latents_held, _ = lax.optimization_barrier((latents, in_plane))
    fq, raw_local = query_local(latents_held, w_query, fk, v)
    up = upstream_of(grads, w_out, gain)
    attn, draw, before, own_r, other_r = normed(inside, pair, got, fq, raw_local, up, gain)
    inside_r, pair_r, got_r, in_plane_r, chip_r = seq_before(True, own_r, other_r)
    attn_held, _ = lax.optimization_barrier((attn, chip_r))
    b2, b1, b3, b0 = branch_parts(attn_held, w_out)
    branch = add_up([b0, to_owner(b2, 2), to_owner(b1, 1), to_owner(b3, 3)])
    draw_held, _ = lax.optimization_barrier((draw, in_plane_r))
    dq, dk_local, dv_local = local_grads(fq, fk, v, draw_held, before)
    dk, dv, l2 = first_part(
        inside_r, pair_r, got_r, fk, v, dq, dk_local, dv_local, w_query, w_key, w_value
    )
    l1, l3 = other_parts((1, 3), dq, dk, dv, w_query, w_key, w_value)
    (l0,) = other_parts((0,), dq, dk, dv, w_query, w_key, w_value)
    d_latents = add_up([l0, to_owner(l2, 2), to_owner(l1, 1), to_owner(l3, 3)])
    return (branch, d_latents)


def solution(mesh):
    split = Mesh(mesh.devices.reshape(8, 4, 2, mesh.shape["mp"]), (*SEQ, "mp"))
    in_specs = (
        P(SEQ, None),
        P(None, "mp"),
        P(None, "mp"),
        P(None, "mp"),
        P("mp", None),
        P("mp"),
        P(SEQ, "mp"),
    )
    out_specs = (P(SEQ, "mp"), P(SEQ, "mp"))
    return jax.shard_map(
        per_device, mesh=split, in_specs=in_specs, out_specs=out_specs, check_vma=False
    )
```

time: 129 us -> 88.2 us (0.68); the launches traced: 127 us -> 87.6 us
  matrix products: 22.9 us -> 0 us
  Pallas kernels: 0 us -> 13.6 us
  other arithmetic: 13.6 us -> 1.56 us
  local copies, waits for them, and re-layouts: 17.9 us -> 10.7 us
  waiting for transfers between devices: 25.7 us -> 20 us
  starting transfers between devices: 45.8 us -> 40.8 us
    dot_general x20 -> x0, matrix products: 22.9 us -> none  [the longest x1 3.31 us: per_device(): lax.dot_general(d_query, w_query, contract, preferred_element_type=jnp.fl...]
    all_to_all x5 -> x2, waiting for transfers between devices: 22 us -> 5.68 us  [seq_before(): planes = lax.all_to_all(planes, 'seq_0', 0, 0, tiled=True)]
    pallas_call x0 -> x15, Pallas kernels: none -> 13.6 us  [the longest x12 10.1 us: plain(): call(body, outs, flops, moved, in_specs=[VMEM] * len(args), out_specs=[VM...]
    ppermute x10 -> x19, waiting for transfers between devices: 3.76 us -> 14.3 us  [the longest x9 7.73 us: to_owner(): return lax.ppermute(part, 'mp', shifts(4, k))]
    all_to_all x5 -> x2, starting transfers between devices: 25 us -> 14.8 us  [seq_before(): planes = lax.all_to_all(planes, 'seq_0', 0, 0, tiled=True)]
    unnamed x46 -> x52, local copies, waits for them, and re-layouts: 2.09 us -> 10.7 us
    reshape x7 -> x1, local copies, waits for them, and re-layouts: 8.31 us -> 0.01 us  [per_device(): gain = head_gain.reshape(1, -1)]
    ppermute x10 -> x19, starting transfers between devices: 20.8 us -> 26 us  [the longest x9 9.55 us: to_owner(): return lax.ppermute(part, 'mp', shifts(4, k))]
  transfers between devices with their start and end apart: 15 -> 21, of which waited for: 9 -> 11; matrix products, arithmetic and copies ran while one was open for 28% -> 1% of each run, Pallas kernels for 0% -> 11%
where the time goes in v2:
time: 88.2 us; the launch traced here: 87.6 us
  starting transfers between devices  40.8 us (46%)
  waiting for transfers between devices  20 us (23%)
  Pallas kernels  13.6 us (15%)
  local copies, waits for them, and re-layouts  10.7 us (12%)
  other arithmetic  1.56 us (2%)
  between operations  0.9 us (1%)
    all_to_all x2, starting transfers between devices, seq_before(): planes = lax.all_to_all(planes, 'seq_0', 0, 0, tiled=True)  14.8 us
    unnamed x52, local copies, waits for them, and re-layouts  10.7 us
    pallas_call x12, Pallas kernels, plain(): call(body, outs, flops, moved, in_specs=[VMEM] * len(args), out_specs=[VM...  10.1 us
    ppermute x9, starting transfers between devices, to_owner(): return lax.ppermute(part, 'mp', shifts(4, k))  9.55 us
    ppermute x9, waiting for transfers between devices, to_owner(): return lax.ppermute(part, 'mp', shifts(4, k))  7.73 us
    ppermute x2, starting transfers between devices, seq_before(): return (inside, pair, lax.ppermute(send, 'seq_2', SWAP), in_plane, chip)  6.29 us
    ppermute x6, starting transfers between devices, seq_before(): lax.ppermute(chip, 'seq_1', shifts(4, -k if later else k))  5.74 us
    all_to_all x2, waiting for transfers between devices, seq_before(): planes = lax.all_to_all(planes, 'seq_0', 0, 0, tiled=True)  5.68 us
  transfers between devices with their start and end apart: 21, of which 11 were waited for; matrix products, arithmetic and copies ran while one was open for 1% of the time, Pallas kernels for 11%

profile of v2, /device:TPU:1, one launch (start us, length us, event | category | flops | bytes accessed | tf_op | source)
XLA Modules:
  0.0 87.6 jit_solution(10697273795130277701)
XLA Ops:
  0.6 1.3 %copy-done = bf16[1536,384]{1,0:T(8,128)(2,1)S(1)} copy-done((bf16[1536,384]{1,0:T(8,128)(2,1)S(1)}, bf16[1536,384]{1,0:T(8,128)(2,1)}, u32[]{:S(2)}) %copy-start) | copy-done | bytes 1179672
  1.9 1.3 %copy-done.2 = bf16[1536,384]{1,0:T(8,128)(2,1)S(1)} copy-done((bf16[1536,384]{1,0:T(8,128)(2,1)S(1)}, bf16[1536,384]{1,0:T(8,128)(2,1)}, u32[]{:S(2)}) %copy-start.2) | copy-done | bytes 1179672
  3.2 1.1 %copy-done.6 = bf16[256,1536]{1,0:T(8,128)(2,1)S(1)} copy-done((bf16[256,1536]{1,0:T(8,128)(2,1)S(1)}, bf16[256,1536]{1,0:T(8,128)(2,1)}, u32[]{:S(2)}) %copy-start.6) | copy-done | bytes 786456
  4.3 1.8 %shard_map.86 = (bf16[256,384]{1,0:T(8,128)(2,1)S(1)}, bf16[256,384]{1,0:T(8,128)(2,1)S(1)}, f32[96,128]{1,0:T(8,128)S(1)}, bf16[96,128]{1,0:T(8,128)(2,1)S(1)}) custom-call(bf16[256,1536]{1,0:T(8,128)(2,1)S(1)} %copy-done.6, bf16[1536,384]{1,0:T(8,128)(2,1)S(1)} %copy-done, bf16[1536,384]{1,0:T(8,128)(2,1)S(1)} %copy-done.2), custom_call_target="tpu_custom_call" | custom-call | flops 603979776 | bytes 3145728 | tf_op jit(solution)/shard_map/pallas_call | solution.py:175
  6.1 3.3 %collective-permute-start = (bf16[96,128]{1,0:T(8,128)(2,1)S(1)}, bf16[96,128]{1,0:T(8,128)(2,1)S(1)}, u32[]{:S(2)}, u32[]{:S(2)}) collective-permute-start(bf16[96,128]{1,0:T(8,128)(2,1)S(1)} %get-tuple-element.38), channel_id=1, source_target_pairs={{0,4},{4,0},{1,5},{5,1},{2,6},{6,2},{3,7},{7,3},{8,12},{12,8},{9,1... | collective-permute-start | bytes 73736 | tf_op jit(solution)/shard_map/ppermute | solution.py:94
  10.3 1.1 %collective-permute-start.3 = (bf16[96,128]{1,0:T(8,128)(2,1)S(1)}, bf16[96,128]{1,0:T(8,128)(2,1)S(1)}, u32[]{:S(2)}, u32[]{:S(2)}) collective-permute-start(bf16[96,128]{1,0:T(8,128)(2,1)S(1)} %shard_map.87), channel_id=1, source_target_pairs={{0,24},{8,0},{16,8},{24,16},{1,25},{9,1},{17,9},{25,17},{2,26},{10... | collective-permute-start | bytes 73736 | tf_op jit(solution)/shard_map/ppermute | solution.py:100
  13.0 2.6 %collective-permute-done.2.g2 = bf16[96,128]{1,0:T(8,128)(2,1)S(1)} collective-permute-done((bf16[96,128]{1,0:T(8,128)(2,1)S(1)}, bf16[96,128]{1,0:T(8,128)(2,1)S(1)}, u32[]{:S(2)}, u32[]{:S(2)}) %collective-permute-start.2) | collective-permute-done | bytes 24608 | tf_op jit(solution)/shard_map/ppermute | solution.py:100
  17.2 8.2 %all-to-all-start = ((bf16[8,96,128]{2,1,0:T(8,128)(2,1)}), bf16[8,96,128]{2,1,0:T(8,128)(2,1)}, u32[]{:S(2)}, u32[]{:S(2)}) async-start(bf16[8,96,128]{2,1,0:T(8,128)(2,1)} %get-tuple-element.40), calls=%async_computation | async-start | bytes 393216 | tf_op jit(solution)/shard_map/all_to_all | solution.py:123
  25.3 2.5 %collective-permute-start.7 = (bf16[256,384]{1,0:T(8,128)(2,1)}, bf16[256,384]{1,0:T(8,128)(2,1)}, u32[]{:S(2)}, u32[]{:S(2)}) collective-permute-start(bf16[256,384]{1,0:T(8,128)(2,1)} %g0.1), channel_id=1, source_target_pairs={{0,3},{1,0},{2,1},{3,2},{4,7},{5,4},{6,5},{7,6},{8,11},{9,8},{10,9... | collective-permute-start | bytes 589832 | tf_op jit(solution)/shard_map/ppermute | solution.py:455
  29.0 1.3 %shard_map.90 = (bf16[256,384]{1,0:T(8,128)(2,1)S(1)}, f32[256,384]{1,0:T(8,128)S(1)}) custom-call(bf16[256,1536]{1,0:T(8,128)(2,1)S(1)} %copy-done.7, bf16[1536,384]{1,0:T(8,128)(2,1)S(1)} %copy-done.4, bf16[256,384]{1,0:T(8,128)(2,1)S(1)} %get-tuple-element.44.fk_ref, bf16[256,384]{1,0:T(8,128)(2,1)S(1)} %get-tuple-element.45.v_ref), custom_call_target="tpu_custom_call" | custom-call | flops 503316480 | bytes 3145728 | tf_op jit(solution)/shard_map/pallas_call | solution.py:41
  31.7 2.4 %all-to-all-done.planes_ref = bf16[8,96,128]{2,1,0:T(8,128)(2,1)} async-done(((bf16[8,96,128]{2,1,0:T(8,128)(2,1)}), bf16[8,96,128]{2,1,0:T(8,128)(2,1)}, u32[]{:S(2)}, u32[]{:S(2)}) %all-to-all-start) | async-done | bytes 196640 | tf_op jit(solution)/shard_map/all_to_all | solution.py:123
  36.7 3.3 %collective-permute-start.4 = (bf16[96,128]{1,0:T(8,128)(2,1)S(1)}, bf16[96,128]{1,0:T(8,128)(2,1)S(1)}, u32[]{:S(2)}, u32[]{:S(2)}) collective-permute-start(bf16[96,128]{1,0:T(8,128)(2,1)S(1)} %get-tuple-element.42), channel_id=1, source_target_pairs={{0,4},{4,0},{1,5},{5,1},{2,6},{6,2},{3,7},{7,3},{8,12},{12,8},{9,1... | collective-permute-start | bytes 73736 | tf_op jit(solution)/shard_map/ppermute | solution.py:144
  40.1 1.9 %shard_map.91.up_ref = f32[256,384]{1,0:T(8,128)S(1)} custom-call(bf16[256,384]{1,0:T(8,128)(2,1)} %g0.1, bf16[256,384]{1,0:T(8,128)(2,1)} %collective-permute-done.5.g1, bf16[256,384]{1,0:T(8,128)(2,1)} %collective-permute-done.6.g2, bf16[256,384]{1,0:T(8,128)(2,1)} %collective-permute-done.7.g3, bf16[384,1536]{1,0:T(8,128)(2,1)S(1)} %copy-done.5, ...), custom_call_target="tpu_custom_call" | custom-call | flops 301989888 | bytes 3145728 | tf_op jit(solution)/shard_map/pallas_call | solution.py:41
  43.7 1.1 %collective-permute-start.8 = (bf16[96,128]{1,0:T(8,128)(2,1)S(1)}, bf16[96,128]{1,0:T(8,128)(2,1)S(1)}, u32[]{:S(2)}, u32[]{:S(2)}) collective-permute-start(bf16[96,128]{1,0:T(8,128)(2,1)S(1)} %get-tuple-element.51), channel_id=1, source_target_pairs={{0,4},{4,0},{1,5},{5,1},{2,6},{6,2},{3,7},{7,3},{8,12},{12,8},{9,1... | collective-permute-start | bytes 73736 | tf_op jit(solution)/shard_map/ppermute | solution.py:94
  45.7 1.7 %collective-permute-start.13 = (bf16[96,128]{1,0:T(8,128)(2,1)S(1)}, bf16[96,128]{1,0:T(8,128)(2,1)S(1)}, u32[]{:S(2)}, u32[]{:S(2)}) collective-permute-start(bf16[96,128]{1,0:T(8,128)(2,1)S(1)} %shard_map.93), channel_id=1, source_target_pairs={{0,16},{8,24},{16,0},{24,8},{1,17},{9,25},{17,1},{25,9},{2,18},{10... | collective-permute-start | bytes 73736 | tf_op jit(solution)/shard_map/ppermute | solution.py:100
  47.5 1.8 %collective-permute-start.12 = (bf16[96,128]{1,0:T(8,128)(2,1)S(1)}, bf16[96,128]{1,0:T(8,128)(2,1)S(1)}, u32[]{:S(2)}, u32[]{:S(2)}) collective-permute-start(bf16[96,128]{1,0:T(8,128)(2,1)S(1)} %shard_map.93), channel_id=1, source_target_pairs={{0,24},{8,0},{16,8},{24,16},{1,25},{9,1},{17,9},{25,17},{2,26},{10... | collective-permute-start | bytes 73736 | tf_op jit(solution)/shard_map/ppermute | solution.py:100
  51.4 6.6 %all-to-all-start.1 = ((bf16[8,96,128]{2,1,0:T(8,128)(2,1)}), bf16[8,96,128]{2,1,0:T(8,128)(2,1)S(1)}, u32[]{:S(2)}, u32[]{:S(2)}) async-start(bf16[8,96,128]{2,1,0:T(8,128)(2,1)} %get-tuple-element.62), calls=%async_computation.1 | async-start | bytes 393216 | tf_op jit(solution)/shard_map/all_to_all | solution.py:123
  59.0 1.3 %shard_map.94 = (bf16[256,384]{1,0:T(8,128)(2,1)}, bf16[256,384]{1,0:T(8,128)(2,1)}, bf16[256,384]{1,0:T(8,128)(2,1)}, bf16[256,384]{1,0:T(8,128)(2,1)S(1)}) custom-call(bf16[256,384]{1,0:T(8,128)(2,1)S(1)} %copy-done.18, bf16[384,1536]{1,0:T(8,128)(2,1)S(1)} %copy-done.5), custom_call_target="tpu_custom_call" | custom-call | flops 301989888 | bytes 2097152 | tf_op jit(solution)/shard_map/pallas_call | solution.py:41
  61.2 2.3 %collective-permute-start.11 = (bf16[256,384]{1,0:T(8,128)(2,1)}, bf16[256,384]{1,0:T(8,128)(2,1)S(1)}, u32[]{:S(2)}, u32[]{:S(2)}) collective-permute-start(bf16[256,384]{1,0:T(8,128)(2,1)} %get-tuple-element.56), channel_id=1, source_target_pairs={{0,3},{1,0},{2,1},{3,2},{4,7},{5,4},{6,5},{7,6},{8,11},{9,8},{10,9... | collective-permute-start | bytes 589832 | tf_op jit(solution)/shard_map/ppermute | solution.py:455
  63.5 3.3 %all-to-all-done.1.planes_ref = bf16[8,96,128]{2,1,0:T(8,128)(2,1)S(1)} async-done(((bf16[8,96,128]{2,1,0:T(8,128)(2,1)}), bf16[8,96,128]{2,1,0:T(8,128)(2,1)S(1)}, u32[]{:S(2)}, u32[]{:S(2)}) %all-to-all-start.1) | async-done | bytes 196640 | tf_op jit(solution)/shard_map/all_to_all | solution.py:123
  66.8 3.0 %collective-permute-start.15 = (bf16[96,128]{1,0:T(8,128)(2,1)S(1)}, bf16[96,128]{1,0:T(8,128)(2,1)S(1)}, u32[]{:S(2)}, u32[]{:S(2)}) collective-permute-start(bf16[96,128]{1,0:T(8,128)(2,1)S(1)} %get-tuple-element.64), channel_id=1, source_target_pairs={{0,4},{4,0},{1,5},{5,1},{2,6},{6,2},{3,7},{7,3},{8,12},{12,8},{9,1... | collective-permute-start | bytes 73736 | tf_op jit(solution)/shard_map/ppermute | solution.py:144
  71.5 1.8 %shard_map.96 = (bf16[256,384]{1,0:T(8,128)(2,1)S(1)}, f32[256,384]{1,0:T(8,128)S(1)}, f32[256,384]{1,0:T(8,128)S(1)}) custom-call(bf16[256,384]{1,0:T(8,128)(2,1)S(1)} %copy-done.16, bf16[256,384]{1,0:T(8,128)(2,1)S(1)} %get-tuple-element.44.fk_ref, bf16[256,384]{1,0:T(8,128)(2,1)S(1)} %get-tuple-element.45.v_ref, bf16[256,384]{1,0:T(8,128)(2,1)S(1)} %copy-done.22, ...), custom_call_target="tpu_custom_call" | custom-call | flops 603979776 | bytes 3145728 | tf_op jit(solution)/shard_map/pallas_call | solution.py:41
  75.1 2.7 %collective-permute-start.18 = (bf16[256,384]{1,0:T(8,128)(2,1)S(1)}, bf16[256,384]{1,0:T(8,128)(2,1)S(1)}, u32[]{:S(2)}, u32[]{:S(2)}) collective-permute-start(bf16[256,384]{1,0:T(8,128)(2,1)S(1)} %get-tuple-element.71), channel_id=1, source_target_pairs={{0,3},{1,0},{2,1},{3,2},{4,7},{5,4},{6,5},{7,6},{8,11},{9,8},{10,9... | collective-permute-start | bytes 589832 | tf_op jit(solution)/shard_map/ppermute | solution.py:455
  79.1 7.7 %collective-permute-done.17 = bf16[256,384]{1,0:T(8,128)(2,1)S(1)} collective-permute-done((bf16[256,384]{1,0:T(8,128)(2,1)S(1)}, bf16[256,384]{1,0:T(8,128)(2,1)S(1)}, u32[]{:S(2)}, u32[]{:S(2)}) %collective-permute-start.17) | collective-permute-done | bytes 196640 | tf_op jit(solution)/shard_map/ppermute | solution.py:455
  (88 shorter events, 21.5 us)
Async XLA Ops:
  4.3 24.6 %copy-start.4 = (bf16[1536,384]{1,0:T(8,128)(2,1)S(1)}, bf16[1536,384]{1,0:T(8,128)(2,1)}, u32[]{:S(2)}) copy-start(bf16[1536,384]{1,0:T(8,128)(2,1)} %wq_ref.7) | copy-start | bytes 3538948
  4.3 24.6 %copy-start.7 = (bf16[256,1536]{1,0:T(8,128)(2,1)S(1)}, bf16[256,1536]{1,0:T(8,128)(2,1)}, u32[]{:S(2)}) copy-start(bf16[256,1536]{1,0:T(8,128)(2,1)} %x_ref.2) | copy-start | bytes 2359300
  6.1 4.1 %collective-permute-start = (bf16[96,128]{1,0:T(8,128)(2,1)S(1)}, bf16[96,128]{1,0:T(8,128)(2,1)S(1)}, u32[]{:S(2)}, u32[]{:S(2)}) collective-permute-start(bf16[96,128]{1,0:T(8,128)(2,1)S(1)} %get-tuple-element.38), channel_id=1, source_target_pairs={{0,4},{4,0},{1,5},{5,1},{2,6},{6,2},{3,7},{7,3},{8,12},{12,8},{9,1... | collective-permute-start | bytes 73736 | tf_op jit(solution)/shard_map/ppermute | solution.py:94
  10.3 2.8 %collective-permute-start.3 = (bf16[96,128]{1,0:T(8,128)(2,1)S(1)}, bf16[96,128]{1,0:T(8,128)(2,1)S(1)}, u32[]{:S(2)}, u32[]{:S(2)}) collective-permute-start(bf16[96,128]{1,0:T(8,128)(2,1)S(1)} %shard_map.87), channel_id=1, source_target_pairs={{0,24},{8,0},{16,8},{24,16},{1,25},{9,1},{17,9},{25,17},{2,26},{10... | collective-permute-start | bytes 73736 | tf_op jit(solution)/shard_map/ppermute | solution.py:100
  11.4 4.2 %collective-permute-start.2 = (bf16[96,128]{1,0:T(8,128)(2,1)S(1)}, bf16[96,128]{1,0:T(8,128)(2,1)S(1)}, u32[]{:S(2)}, u32[]{:S(2)}) collective-permute-start(bf16[96,128]{1,0:T(8,128)(2,1)S(1)} %shard_map.87), channel_id=1, source_target_pairs={{0,16},{8,24},{16,0},{24,8},{1,17},{9,25},{17,1},{25,9},{2,18},{10... | collective-permute-start | bytes 73736 | tf_op jit(solution)/shard_map/ppermute | solution.py:100
  11.7 4.1 %collective-permute-start.1 = (bf16[96,128]{1,0:T(8,128)(2,1)S(1)}, bf16[96,128]{1,0:T(8,128)(2,1)S(1)}, u32[]{:S(2)}, u32[]{:S(2)}) collective-permute-start(bf16[96,128]{1,0:T(8,128)(2,1)S(1)} %shard_map.87), channel_id=1, source_target_pairs={{0,8},{8,16},{16,24},{24,0},{1,9},{9,17},{17,25},{25,1},{2,10},{10... | collective-permute-start | bytes 73736 | tf_op jit(solution)/shard_map/ppermute | solution.py:100
  17.2 17.0 %all-to-all-start = ((bf16[8,96,128]{2,1,0:T(8,128)(2,1)}), bf16[8,96,128]{2,1,0:T(8,128)(2,1)}, u32[]{:S(2)}, u32[]{:S(2)}) async-start(bf16[8,96,128]{2,1,0:T(8,128)(2,1)} %get-tuple-element.40), calls=%async_computation | async-start | bytes 393216 | tf_op jit(solution)/shard_map/all_to_all | solution.py:123
  25.3 14.7 %collective-permute-start.7 = (bf16[256,384]{1,0:T(8,128)(2,1)}, bf16[256,384]{1,0:T(8,128)(2,1)}, u32[]{:S(2)}, u32[]{:S(2)}) collective-permute-start(bf16[256,384]{1,0:T(8,128)(2,1)} %g0.1), channel_id=1, source_target_pairs={{0,3},{1,0},{2,1},{3,2},{4,7},{5,4},{6,5},{7,6},{8,11},{9,8},{10,9... | collective-permute-start | bytes 589832 | tf_op jit(solution)/shard_map/ppermute | solution.py:455
  27.8 12.2 %collective-permute-start.6 = (bf16[256,384]{1,0:T(8,128)(2,1)}, bf16[256,384]{1,0:T(8,128)(2,1)}, u32[]{:S(2)}, u32[]{:S(2)}) collective-permute-start(bf16[256,384]{1,0:T(8,128)(2,1)} %g0.1), channel_id=1, source_target_pairs={{0,2},{1,3},{2,0},{3,1},{4,6},{5,7},{6,4},{7,5},{8,10},{9,11},{10,... | collective-permute-start | bytes 589832 | tf_op jit(solution)/shard_map/ppermute | solution.py:455
  28.3 11.7 %collective-permute-start.5 = (bf16[256,384]{1,0:T(8,128)(2,1)}, bf16[256,384]{1,0:T(8,128)(2,1)}, u32[]{:S(2)}, u32[]{:S(2)}) collective-permute-start(bf16[256,384]{1,0:T(8,128)(2,1)} %g0.1), channel_id=1, source_target_pairs={{0,1},{1,2},{2,3},{3,0},{4,5},{5,6},{6,7},{7,4},{8,9},{9,10},{10,1... | collective-permute-start | bytes 589832 | tf_op jit(solution)/shard_map/ppermute | solution.py:455
  36.7 5.2 %collective-permute-start.4 = (bf16[96,128]{1,0:T(8,128)(2,1)S(1)}, bf16[96,128]{1,0:T(8,128)(2,1)S(1)}, u32[]{:S(2)}, u32[]{:S(2)}) collective-permute-start(bf16[96,128]{1,0:T(8,128)(2,1)S(1)} %get-tuple-element.42), channel_id=1, source_target_pairs={{0,4},{4,0},{1,5},{5,1},{2,6},{6,2},{3,7},{7,3},{8,12},{12,8},{9,1... | collective-permute-start | bytes 73736 | tf_op jit(solution)/shard_map/ppermute | solution.py:144
  43.7 26.1 %copy-start.16 = (bf16[256,384]{1,0:T(8,128)(2,1)S(1)}, bf16[256,384]{1,0:T(8,128)(2,1)}, u32[]{:S(2)}) copy-start(bf16[256,384]{1,0:T(8,128)(2,1)} %copy-done.14) | copy-start | bytes 589828
  43.7 2.0 %collective-permute-start.8 = (bf16[96,128]{1,0:T(8,128)(2,1)S(1)}, bf16[96,128]{1,0:T(8,128)(2,1)S(1)}, u32[]{:S(2)}, u32[]{:S(2)}) collective-permute-start(bf16[96,128]{1,0:T(8,128)(2,1)S(1)} %get-tuple-element.51), channel_id=1, source_target_pairs={{0,4},{4,0},{1,5},{5,1},{2,6},{6,2},{3,7},{7,3},{8,12},{12,8},{9,1... | collective-permute-start | bytes 73736 | tf_op jit(solution)/shard_map/ppermute | solution.py:94
  45.6 4.0 %collective-permute-start.14 = (bf16[96,128]{1,0:T(8,128)(2,1)S(1)}, bf16[96,128]{1,0:T(8,128)(2,1)S(1)}, u32[]{:S(2)}, u32[]{:S(2)}) collective-permute-start(bf16[96,128]{1,0:T(8,128)(2,1)S(1)} %shard_map.93), channel_id=1, source_target_pairs={{0,8},{8,16},{16,24},{24,0},{1,9},{9,17},{17,25},{25,1},{2,10},{10... | collective-permute-start | bytes 73736 | tf_op jit(solution)/shard_map/ppermute | solution.py:100
  45.7 4.3 %collective-permute-start.13 = (bf16[96,128]{1,0:T(8,128)(2,1)S(1)}, bf16[96,128]{1,0:T(8,128)(2,1)S(1)}, u32[]{:S(2)}, u32[]{:S(2)}) collective-permute-start(bf16[96,128]{1,0:T(8,128)(2,1)S(1)} %shard_map.93), channel_id=1, source_target_pairs={{0,16},{8,24},{16,0},{24,8},{1,17},{9,25},{17,1},{25,9},{2,18},{10... | collective-permute-start | bytes 73736 | tf_op jit(solution)/shard_map/ppermute | solution.py:100
  47.5 3.3 %collective-permute-start.12 = (bf16[96,128]{1,0:T(8,128)(2,1)S(1)}, bf16[96,128]{1,0:T(8,128)(2,1)S(1)}, u32[]{:S(2)}, u32[]{:S(2)}) collective-permute-start(bf16[96,128]{1,0:T(8,128)(2,1)S(1)} %shard_map.93), channel_id=1, source_target_pairs={{0,24},{8,0},{16,8},{24,16},{1,25},{9,1},{17,9},{25,17},{2,26},{10... | collective-permute-start | bytes 73736 | tf_op jit(solution)/shard_map/ppermute | solution.py:100
  51.4 15.3 %all-to-all-start.1 = ((bf16[8,96,128]{2,1,0:T(8,128)(2,1)}), bf16[8,96,128]{2,1,0:T(8,128)(2,1)S(1)}, u32[]{:S(2)}, u32[]{:S(2)}) async-start(bf16[8,96,128]{2,1,0:T(8,128)(2,1)} %get-tuple-element.62), calls=%async_computation.1 | async-start | bytes 393216 | tf_op jit(solution)/shard_map/all_to_all | solution.py:123
  60.3 17.5 %collective-permute-start.9 = (bf16[256,384]{1,0:T(8,128)(2,1)}, bf16[256,384]{1,0:T(8,128)(2,1)S(1)}, u32[]{:S(2)}, u32[]{:S(2)}) collective-permute-start(bf16[256,384]{1,0:T(8,128)(2,1)} %get-tuple-element.54), channel_id=1, source_target_pairs={{0,2},{1,3},{2,0},{3,1},{4,6},{5,7},{6,4},{7,5},{8,10},{9,11},{10,... | collective-permute-start | bytes 589832 | tf_op jit(solution)/shard_map/ppermute | solution.py:455
  60.8 17.0 %collective-permute-start.10 = (bf16[256,384]{1,0:T(8,128)(2,1)}, bf16[256,384]{1,0:T(8,128)(2,1)S(1)}, u32[]{:S(2)}, u32[]{:S(2)}) collective-permute-start(bf16[256,384]{1,0:T(8,128)(2,1)} %get-tuple-element.55), channel_id=1, source_target_pairs={{0,1},{1,2},{2,3},{3,0},{4,5},{5,6},{6,7},{7,4},{8,9},{9,10},{10,1... | collective-permute-start | bytes 589832 | tf_op jit(solution)/shard_map/ppermute | solution.py:455
  61.2 16.6 %collective-permute-start.11 = (bf16[256,384]{1,0:T(8,128)(2,1)}, bf16[256,384]{1,0:T(8,128)(2,1)S(1)}, u32[]{:S(2)}, u32[]{:S(2)}) collective-permute-start(bf16[256,384]{1,0:T(8,128)(2,1)} %get-tuple-element.56), channel_id=1, source_target_pairs={{0,3},{1,0},{2,1},{3,2},{4,7},{5,4},{6,5},{7,6},{8,11},{9,8},{10,9... | collective-permute-start | bytes 589832 | tf_op jit(solution)/shard_map/ppermute | solution.py:455
  66.8 6.5 %collective-permute-start.15 = (bf16[96,128]{1,0:T(8,128)(2,1)S(1)}, bf16[96,128]{1,0:T(8,128)(2,1)S(1)}, u32[]{:S(2)}, u32[]{:S(2)}) collective-permute-start(bf16[96,128]{1,0:T(8,128)(2,1)S(1)} %get-tuple-element.64), channel_id=1, source_target_pairs={{0,4},{4,0},{1,5},{5,1},{2,6},{6,2},{3,7},{7,3},{8,12},{12,8},{9,1... | collective-permute-start | bytes 73736 | tf_op jit(solution)/shard_map/ppermute | solution.py:144
  75.0 11.8 %collective-permute-start.17 = (bf16[256,384]{1,0:T(8,128)(2,1)S(1)}, bf16[256,384]{1,0:T(8,128)(2,1)S(1)}, u32[]{:S(2)}, u32[]{:S(2)}) collective-permute-start(bf16[256,384]{1,0:T(8,128)(2,1)S(1)} %get-tuple-element.70), channel_id=1, source_target_pairs={{0,1},{1,2},{2,3},{3,0},{4,5},{5,6},{6,7},{7,4},{8,9},{9,10},{10,1... | collective-permute-start | bytes 589832 | tf_op jit(solution)/shard_map/ppermute | solution.py:455
  75.1 11.7 %collective-permute-start.18 = (bf16[256,384]{1,0:T(8,128)(2,1)S(1)}, bf16[256,384]{1,0:T(8,128)(2,1)S(1)}, u32[]{:S(2)}, u32[]{:S(2)}) collective-permute-start(bf16[256,384]{1,0:T(8,128)(2,1)S(1)} %get-tuple-element.71), channel_id=1, source_target_pairs={{0,3},{1,0},{2,1},{3,2},{4,7},{5,4},{6,5},{7,6},{8,11},{9,8},{10,9... | collective-permute-start | bytes 589832 | tf_op jit(solution)/shard_map/ppermute | solution.py:455
  77.8 9.1 %collective-permute-start.16 = (bf16[256,384]{1,0:T(8,128)(2,1)S(1)}, bf16[256,384]{1,0:T(8,128)(2,1)S(1)}, u32[]{:S(2)}, u32[]{:S(2)}) collective-permute-start(bf16[256,384]{1,0:T(8,128)(2,1)S(1)} %get-tuple-element.69), channel_id=1, source_target_pairs={{0,2},{1,3},{2,0},{3,1},{4,6},{5,7},{6,4},{7,5},{8,10},{9,11},{10,... | collective-permute-start | bytes 589832 | tf_op jit(solution)/shard_map/ppermute | solution.py:455
  (23 other events, 106.8 us)

commit v3 on v2

v3 whole, which is shorter than its diff:
```python
import jax
import jax.numpy as jnp
from jax import lax
from jax.experimental import pallas as pl
from jax.experimental.pallas import tpu as pltpu
from jax.sharding import Mesh
from jax.sharding import PartitionSpec as P


HD = 64
LANES = 128
SEQ = ("seq_0", "seq_1", "seq_2")
SWAP = [(0, 1), (1, 0)]
epsilon = 1e-06
f32, bf16 = (jnp.float32, jnp.bfloat16)
NT = (((1,), (1,)), ((), ()))
TN = (((0,), (0,)), ((), ()))
VMEM = pl.BlockSpec(memory_space=pltpu.VMEM)


def shifts(count, step):
    return [(i, (i + step) % count) for i in range(count)]


def mm(a, b, contract=(((1,), (0,)), ((), ()))):
    return lax.dot_general(a, b, contract, preferred_element_type=f32)


def relay(near, *args):
    def body(*refs):
        sources, targets, sem = (refs[: len(args)], refs[len(args) : -1], refs[-1])
        copies = [
            pltpu.make_async_copy(a, b, sem.at[i]) for i, (a, b) in enumerate(zip(sources, targets))
        ]
        for copy in copies:
            copy.start()
        for copy in copies:
            copy.wait()

    hbm = pl.BlockSpec(memory_space=pltpu.HBM)
    make = pltpu.VMEM if near else pltpu.HBM
    return pl.pallas_call(
        body,
        out_shape=[make(a.shape, a.dtype) for a in args],
        in_specs=[hbm if near else VMEM] * len(args),
        out_specs=[VMEM if near else hbm] * len(args),
        scratch_shapes=[pltpu.SemaphoreType.DMA((len(args),))],
        cost_estimate=pl.CostEstimate(flops=1, bytes_accessed=1024 * 1024, transcendentals=0),
    )(*(pltpu.with_memory_space_constraint(a, pltpu.HBM if near else pltpu.VMEM) for a in args))


def in_hbm(x):
    return pltpu.with_memory_space_constraint(x, pltpu.HBM)


def shape_of(shape, kind, far=False):
    return pltpu.HBM(shape, kind) if far else jax.ShapeDtypeStruct(shape, kind)


def call(body, outs, flops, moved, **extra):
    return pl.pallas_call(
        body,
        out_shape=[shape_of(*out) for out in outs],
        cost_estimate=pl.CostEstimate(flops=flops, bytes_accessed=moved, transcendentals=0),
        compiler_params=pltpu.CompilerParams(vmem_limit_bytes=20 * 1024 * 1024),
        **extra,
    )


def plain(body, outs, flops, moved, *args):
    return call(
        body, outs, flops, moved, in_specs=[VMEM] * len(args), out_specs=[VMEM] * len(outs)
    )(*args)


def feature_map(u):
    return jnp.where(u > 0, u + 1.0, jnp.exp(jnp.minimum(u, 0.0)))


def low_lanes(shape):
    return lax.broadcasted_iota(jnp.int32, shape, len(shape) - 1) < HD


def one_head(x, head):
    low = low_lanes(x.shape)
    keep = low if head == 0 else jnp.logical_not(low)
    return jnp.where(keep, x, jnp.zeros_like(x))


def pack(full):
    return jnp.where(low_lanes((HD, LANES)), full[:HD], full[HD:])


def unpack(rows):
    low = low_lanes((HD, LANES))
    zero = jnp.zeros_like(rows)
    return jnp.concatenate([jnp.where(low, rows, zero), jnp.where(low, zero, rows)], axis=0)


def head_ones():
    r = lax.broadcasted_iota(jnp.int32, (LANES, LANES), 0) < HD
    c = lax.broadcasted_iota(jnp.int32, (LANES, LANES), 1) < HD
    return jnp.where(r == c, 1.0, 0.0).astype(bf16)


def half_at(other, half):
    side = lax.axis_index("seq_2")
    side = 1 - side if other else side
    return pl.ds(pl.multiple_of(side * half, 16), half)


def whole_state(later, mine_ref, got_ref, pair_ref, state_ref):
    half = mine_ref.shape[0]
    last = lax.axis_index("seq_2") == (0 if later else 1)
    state_ref[half_at(False, half), :] = mine_ref[...].astype(f32)
    state_ref[half_at(True, half), :] = got_ref[...].astype(f32)
    state_ref[...] += jnp.where(last, pair_ref[...].astype(f32), 0.0)


def pair_sum(state, pair):
    half = state.shape[0] // 2

    def body(state_ref, pair_ref, chip_ref):
        own = half_at(False, half)
        chip_ref[...] = (state_ref[own, :].astype(f32) + pair_ref[own, :].astype(f32)).astype(bf16)

    return plain(body, [((half, LANES), bf16)], 1, half * 1024, state, pair)[0]


def plane_sums(later, chip, got, pair):
    half = chip.shape[0]

    def body(chip_ref, g1, g2, g3, pair_ref, planes_ref, kept_ref):
        y = lax.axis_index("seq_1")
        y = 3 - y if later else y
        total = chip_ref[...].astype(f32)
        inside = jnp.zeros_like(total)
        for k, ref in ((1, g1), (2, g2), (3, g3)):
            piece = ref[...].astype(f32)
            total = total + piece
            inside = inside + jnp.where(y >= k, piece, 0.0)
        planes_ref[...] = jnp.broadcast_to(total.astype(bf16)[None], planes_ref.shape)
        planes_ref[pl.ds(lax.axis_index("seq_0"), 1)] = inside.astype(bf16)[None]
        kept_ref[...] = pair_ref[...]

    outs = [((8, half, LANES), bf16, True), ((2 * half, LANES), bf16, True)]
    return plain(body, outs, 1, half * 4096, chip, *got, pair)


def before_chip(later, planes):
    half = planes.shape[1]

    def body(planes_ref, send_ref):
        z = lax.axis_index("seq_0")
        total = jnp.zeros((half, LANES), f32)
        for k in range(8):
            take = (z <= k) if later else (z >= k)
            total = total + jnp.where(take, planes_ref[k].astype(f32), 0.0)
        send_ref[...] = total.astype(bf16)

    return plain(body, [((half, LANES), bf16)], 1, half * 4096, planes)[0]


def plane_exchange(planes):
    return lax.all_to_all(planes, "seq_0", 0, 0, tiled=True)


def swap(x):
    return lax.ppermute(x, "seq_2", SWAP)


def y_gather(later, chip):
    got = []
    for k in (2, 1, 3):
        got.append(lax.ppermute(chip, "seq_1", shifts(4, -k if later else k)))
    return got[1], got[0], got[2]


def key_value(latents, w_key, w_value):
    rows, width = (latents.shape[0], w_key.shape[1])
    steps = 4
    depth = latents.shape[1] // steps

    def body(x_hbm, wk_hbm, wv_hbm, fk_ref, v_ref, state_ref, x_ref, w_ref, sem):
        copies = []
        for i in range(steps):
            span = pl.ds(i * depth, depth)
            copies.append(
                [
                    pltpu.make_async_copy(src, dst, sem.at[3 * i + j])
                    for j, (src, dst) in enumerate(
                        (
                            (x_hbm.at[:, span], x_ref.at[:, span]),
                            (wk_hbm.at[span, :], w_ref.at[span, pl.ds(0, width)]),
                            (wv_hbm.at[span, :], w_ref.at[span, pl.ds(width, width)]),
                        )
                    )
                ]
            )
        for group in copies:
            for copy in group:
                copy.start()
        total = None
        for i, group in enumerate(copies):
            for copy in group:
                copy.wait()
            span = slice(i * depth, (i + 1) * depth)
            part = mm(x_ref[:, span], w_ref[span, :])
            total = part if total is None else total + part
        fk_ref[...] = feature_map(total[:, :width]).astype(bf16)
        v_ref[...] = total[:, width:].astype(bf16)
        for p in range(width // LANES):
            cols = slice(p * LANES, (p + 1) * LANES)
            state_ref[p * HD : (p + 1) * HD, :] = pack(
                mm(fk_ref[:, cols], v_ref[:, cols], TN)
            ).astype(bf16)

    hbm = pl.BlockSpec(memory_space=pltpu.HBM)
    return call(
        body,
        [
            ((rows, width), bf16),
            ((rows, width), bf16),
            ((width * HD // LANES, LANES), bf16),
        ],
        4 * rows * width * latents.shape[1],
        3 * 1024 * 1024,
        in_specs=[hbm] * 3,
        out_specs=[VMEM] * 3,
        scratch_shapes=[
            pltpu.VMEM(latents.shape, bf16),
            pltpu.VMEM((latents.shape[1], 2 * width), bf16),
            pltpu.SemaphoreType.DMA((3 * steps,)),
        ],
    )(in_hbm(latents), in_hbm(w_key), in_hbm(w_value))


def tri(rows, upper):
    t = lax.broadcasted_iota(jnp.int32, (rows, rows), 0)
    s = lax.broadcasted_iota(jnp.int32, (rows, rows), 1)
    return (t <= s) if upper else (t >= s)


def masked(scores, keep):
    return jnp.where(keep, scores, 0.0).astype(bf16)


def query_local(latents, w_query, fk, v):
    rows, width = fk.shape

    def body(x_ref, wq_ref, fk_ref, v_ref, fq_ref, raw_ref):
        fq_ref[...] = feature_map(mm(x_ref[...], wq_ref[...])).astype(bf16)
        keep = tri(rows, False)
        for p in range(width // LANES):
            cols = slice(p * LANES, (p + 1) * LANES)
            q, k, val = (fq_ref[:, cols], fk_ref[:, cols], v_ref[:, cols])
            total = None
            for h in (0, 1):
                score = masked(mm(q, one_head(k, h), NT), keep)
                part = mm(score, one_head(val, h))
                total = part if total is None else total + part
            raw_ref[:, cols] = total.astype(bf16)

    return plain(
        body,
        [((rows, width), bf16, True)] * 2,
        2 * rows * width * (latents.shape[1] + 4 * rows),
        3 * 1024 * 1024,
        latents,
        w_query,
        in_hbm(fk),
        in_hbm(v),
    )


def upstream_of(grads, w_out, gain):
    rows, width = grads[0].shape

    def body(g0, g1, g2, g3, w_ref, gain_ref, up_ref):
        m = lax.axis_index("mp")
        total = jnp.zeros((rows, width), f32)
        for k, ref in enumerate((g0, g1, g2, g3)):
            at = lax.rem(m + 4 - k, 4) * width
            total = total + mm(ref[...], w_ref[:, pl.ds(pl.multiple_of(at, LANES), width)], NT)
        up_ref[...] = (total * gain_ref[...]).astype(bf16)

    return plain(
        body,
        [((rows, width), bf16, True)],
        8 * rows * width * width,
        3 * 1024 * 1024,
        *grads,
        w_out,
        gain,
    )[0]


def normed(mine, got, pair, fq, raw_local, up, gain):
    rows, width = fq.shape
    half = mine.shape[0]

    def body(
        mine_ref,
        got_ref,
        pair_ref,
        fq_ref,
        raw_ref,
        up_ref,
        gain_ref,
        attn_ref,
        draw_ref,
        before_ref,
        after_ref,
        state,
    ):
        whole_state(False, mine_ref, got_ref, pair_ref, state)
        before_ref[...] = state[...].astype(bf16)
        ones = head_ones()
        for p in range(width // LANES):
            cols = slice(p * LANES, (p + 1) * LANES)
            q = fq_ref[:, cols]
            raw = raw_ref[:, cols].astype(f32) + mm(q, unpack(before_ref[p * HD : (p + 1) * HD, :]))
            upstream = up_ref[:, cols].astype(f32)
            square = mm((raw * raw).astype(bf16), ones) * (1.0 / HD)
            cross = mm((raw * upstream).astype(bf16), ones) * (1.0 / HD)
            inv = lax.rsqrt(square + epsilon)
            unit = raw * inv
            attn_ref[:, cols] = (unit * gain_ref[:, cols]).astype(bf16)
            draw = (inv * upstream - inv * inv * unit * cross).astype(bf16)
            draw_ref[:, cols] = draw
            after_ref[p * HD : (p + 1) * HD, :] = pack(mm(q, draw, TN)).astype(bf16)

    return call(
        body,
        [
            ((rows, width), bf16),
            ((rows, width), bf16),
            ((2 * half, LANES), bf16),
            ((2 * half, LANES), bf16),
        ],
        8 * rows * width * LANES,
        2 * 1024 * 1024,
        in_specs=[VMEM] * 7,
        out_specs=[VMEM] * 4,
        scratch_shapes=[pltpu.VMEM((2 * half, LANES), f32)],
    )(mine, got, pair, fq, raw_local, up, gain)


def branch_parts(attn, w_out, draw, before):
    rows, width = attn.shape

    def body(attn_ref, w_ref, draw_ref, before_ref, *refs):
        outs, kept, sem = (refs[:4], refs[4:6], refs[6])
        copies = [
            pltpu.make_async_copy(a, b, sem.at[i])
            for i, (a, b) in enumerate(zip((draw_ref, before_ref), kept))
        ]
        for copy in copies:
            copy.start()
        m = lax.axis_index("mp")
        for k, ref in zip((2, 1, 3, 0), outs):
            at = lax.rem(m + k, 4) * width
            ref[...] = mm(
                attn_ref[...], w_ref[:, pl.ds(pl.multiple_of(at, LANES), width)]
            ).astype(bf16)
        for copy in copies:
            copy.wait()

    return call(
        body,
        [((rows, width), bf16, True)] * 5 + [(before.shape, bf16, True)],
        8 * rows * width * width,
        2 * 1024 * 1024,
        in_specs=[VMEM] * 4,
        out_specs=[VMEM] * 4 + [pl.BlockSpec(memory_space=pltpu.HBM)] * 2,
        scratch_shapes=[pltpu.SemaphoreType.DMA((2,))],
    )(attn, w_out, draw, before)


def local_grads(fq, fk, v, draw, before):
    rows, width = fq.shape

    def body(fq_ref, fk_ref, v_ref, draw_ref, before_ref, dq_ref, dk_ref, dv_ref):
        lower, upper = (tri(rows, False), tri(rows, True))
        for p in range(width // LANES):
            cols = slice(p * LANES, (p + 1) * LANES)
            q, k, val, dr = (fq_ref[:, cols], fk_ref[:, cols], v_ref[:, cols], draw_ref[:, cols])
            dq = mm(dr, unpack(before_ref[p * HD : (p + 1) * HD, :]), NT)
            dk, dv = (None, None)
            for h in (0, 1):
                val_h, k_h, q_h, dr_h = (one_head(a, h) for a in (val, k, q, dr))
                dq = dq + mm(masked(mm(dr, val_h, NT), lower), k_h)
                dk_h = mm(masked(mm(val_h, dr, NT), upper), q_h)
                dv_h = mm(masked(mm(k_h, q, NT), upper), dr_h)
                dk = dk_h if dk is None else dk + dk_h
                dv = dv_h if dv is None else dv + dv_h
            dq_ref[:, cols] = (dq * jnp.minimum(q.astype(f32), 1.0)).astype(bf16)
            dk_ref[:, cols] = dk.astype(bf16)
            dv_ref[:, cols] = dv.astype(bf16)

    return plain(
        body,
        [((rows, width), bf16, True)] * 3,
        400 * rows * rows * width,
        3 * 1024 * 1024,
        *(in_hbm(a) for a in (fq, fk, v, draw, before)),
    )


def latent_part(m, k, width, triples):
    rows = pl.ds(pl.multiple_of(lax.rem(m + k, 4) * width, LANES), width)
    total = None
    for grad_ref, w_ref in triples:
        part = mm(grad_ref[...], w_ref[rows, :], NT)
        total = part if total is None else total + part
    return total.astype(bf16)


def first_part(mine, got, pair, fk, v, dq, dk, dv, w_query, w_key, w_value):
    rows, width = fk.shape
    half = mine.shape[0]

    def body(
        mine_ref,
        got_ref,
        pair_ref,
        fk_ref,
        v_ref,
        dq_ref,
        dkl_ref,
        dvl_ref,
        wq_ref,
        wk_ref,
        wv_ref,
        dk_ref,
        dv_ref,
        part_ref,
        state,
    ):
        whole_state(True, mine_ref, got_ref, pair_ref, state)
        for p in range(width // LANES):
            cols = slice(p * LANES, (p + 1) * LANES)
            after = unpack(state[p * HD : (p + 1) * HD, :].astype(bf16))
            k = fk_ref[:, cols]
            dk = dkl_ref[:, cols].astype(f32) + mm(v_ref[:, cols], after, NT)
            dk_ref[:, cols] = (dk * jnp.minimum(k.astype(f32), 1.0)).astype(bf16)
            dv_ref[:, cols] = (dvl_ref[:, cols].astype(f32) + mm(k, after)).astype(bf16)
        m = lax.axis_index("mp")
        part_ref[...] = latent_part(
            m, 2, width, ((dq_ref, wq_ref), (dk_ref, wk_ref), (dv_ref, wv_ref))
        )

    return call(
        body,
        [((rows, width), bf16)] * 3,
        6 * rows * width * width,
        5 * 1024 * 1024,
        in_specs=[VMEM] * 11,
        out_specs=[VMEM] * 3,
        scratch_shapes=[pltpu.VMEM((2 * half, LANES), f32)],
    )(mine, got, pair, fk, v, dq, dk, dv, w_query, w_key, w_value)


def other_parts(which, dq, dk, dv, w_query, w_key, w_value):
    rows, width = dq.shape

    def body(dq_ref, dk_ref, dv_ref, wq_ref, wk_ref, wv_ref, *outs):
        m = lax.axis_index("mp")
        for k, ref in zip(which, outs):
            ref[...] = latent_part(
                m, k, width, ((dq_ref, wq_ref), (dk_ref, wk_ref), (dv_ref, wv_ref))
            )

    return plain(
        body,
        [((rows, width), bf16)] * len(which),
        6 * rows * width * width * len(which),
        5 * 1024 * 1024,
        dq,
        dk,
        dv,
        w_query,
        w_key,
        w_value,
    )


def add_up(parts):
    total = parts[0].astype(f32)
    for part in parts[1:]:
        total = total + part.astype(f32)
    return total.astype(bf16)


def to_owner(part, k):
    return lax.ppermute(part, "mp", shifts(4, k))


def hold(x, anchor):
    return lax.optimization_barrier((x, anchor))[0]


def per_device(latents, w_query, w_key, w_value, w_out, head_gain, grad_out):
    gain = head_gain.reshape(1, -1)
    fk, v, state = key_value(latents, w_key, w_value)
    pair = swap(state)
    fk, v = relay(False, fk, v)
    chip = pair_sum(state, pair)
    got = y_gather(False, chip)
    grad_held = hold(grad_out, chip)
    grads = [grad_out] + [to_owner(grad_held, k) for k in (1, 2, 3)]
    planes, pair = plane_sums(False, chip, got, pair)
    fq, raw_local = query_local(hold(latents, planes), w_query, fk, v)
    up = upstream_of(grads, w_out, gain)
    planes = plane_exchange(planes)
    mine = before_chip(False, planes)
    got = swap(mine)
    near = relay(True, pair, fq, raw_local, up)
    attn, draw, before, state = normed(mine, got, *near, gain)
    pair = swap(state)
    b2, b1, b3, b0, draw, before = branch_parts(attn, w_out, draw, before)
    chip = pair_sum(state, pair)
    got = y_gather(True, chip)
    b2, b1, b3 = (hold(b, chip) for b in (b2, b1, b3))
    branch = [b0, to_owner(b2, 2), to_owner(b1, 1), to_owner(b3, 3)]
    planes, pair = plane_sums(True, chip, got, pair)
    dq, dk_local, dv_local = local_grads(fq, fk, v, hold(draw, planes), before)
    (w_query,) = relay(True, hold(w_query, dq))
    planes = plane_exchange(planes)
    mine = before_chip(True, planes)
    got = swap(mine)
    near = relay(True, pair, fk, v, dq, dk_local, dv_local)
    dq = near[3]
    weights = (w_query, w_key, w_value)
    dk, dv, l2 = first_part(mine, got, *near, *weights)
    l2 = to_owner(l2, 2)
    l1, l3 = other_parts((1, 3), dq, dk, dv, *weights)
    l1, l3 = (to_owner(l1, 1), to_owner(l3, 3))
    (l0,) = other_parts((0,), dq, dk, dv, *weights)
    return (add_up(branch), add_up([l0, l2, l1, l3]))


def solution(mesh):
    split = Mesh(mesh.devices.reshape(8, 4, 2, mesh.shape["mp"]), (*SEQ, "mp"))
    in_specs = (
        P(SEQ, None),
        P(None, "mp"),
        P(None, "mp"),
        P(None, "mp"),
        P("mp", None),
        P("mp"),
        P(SEQ, "mp"),
    )
    out_specs = (P(SEQ, "mp"), P(SEQ, "mp"))
    return jax.shard_map(
        per_device, mesh=split, in_specs=in_specs, out_specs=out_specs, check_vma=False
    )
```

time: 88.2 us -> 92.8 us (1.052)
  Pallas kernels: 13.6 us -> 24.8 us
  local copies, waits for them, and re-layouts: 10.7 us -> 3.46 us
  other arithmetic: 1.56 us -> 2.68 us
    pallas_call x1 -> x6, Pallas kernels: 1.8 us -> 9.51 us  [the longest x4 4.71 us: relay(): pl.pallas_call(body, out_shape=[make(a.shape, a.dtype) for a in args], in...]
    unnamed x52 -> x22, local copies, waits for them, and re-layouts: 10.7 us -> 3.45 us
    pallas_call x12 -> x11, Pallas kernels: 10.1 us -> 12.7 us  [plain(): call(body, outs, flops, moved, in_specs=[VMEM] * len(args), out_specs=[VM...]
    ppermute x9, waiting for transfers between devices: 7.73 us -> 9 us  [to_owner(): return lax.ppermute(part, 'mp', shifts(4, k))]
    convert_element_type x2, other arithmetic: 1.56 us -> 2.68 us  [add_up(): return total.astype(bf16)]
    ppermute x9, starting transfers between devices: 9.55 us -> 8.47 us  [to_owner(): return lax.ppermute(part, 'mp', shifts(4, k))]
  transfers between devices with their start and end apart: 21 -> 21, of which waited for: 11 -> 11; matrix products, arithmetic and copies ran while one was open for 1% -> 2% of each run, Pallas kernels for 11% -> 21%
where the time goes in v3:
time: 92.8 us; the launch traced here: 92.3 us
  starting transfers between devices  39.9 us (43%)
  Pallas kernels  24.8 us (27%)
  waiting for transfers between devices  20.5 us (22%)
  local copies, waits for them, and re-layouts  3.46 us (4%)
  other arithmetic  2.68 us (3%)
    all_to_all x2, starting transfers between devices, plane_exchange(): return lax.all_to_all(planes, 'seq_0', 0, 0, tiled=True)  14.8 us
    pallas_call x11, Pallas kernels, plain(): call(body, outs, flops, moved, in_specs=[VMEM] * len(args), out_specs=[VM...  12.7 us
    ppermute x4, starting transfers between devices, swap(): return lax.ppermute(x, 'seq_2', SWAP)  10.9 us
    ppermute x9, waiting for transfers between devices, to_owner(): return lax.ppermute(part, 'mp', shifts(4, k))  9 us
    ppermute x9, starting transfers between devices, to_owner(): return lax.ppermute(part, 'mp', shifts(4, k))  8.47 us
    ppermute x6, starting transfers between devices, y_gather(): got.append(lax.ppermute(chip, 'seq_1', shifts(4, -k if later else k)))  5.76 us
    all_to_all x2, waiting for transfers between devices, plane_exchange(): return lax.all_to_all(planes, 'seq_0', 0, 0, tiled=True)  4.89 us
    ppermute x6, waiting for transfers between devices, y_gather(): got.append(lax.ppermute(chip, 'seq_1', shifts(4, -k if later else k)))  4.88 us
  transfers between devices with their start and end apart: 21, of which 11 were waited for; matrix products, arithmetic and copies ran while one was open for 2% of the time, Pallas kernels for 21%

profile of v3, /device:TPU:1, one launch (start us, length us, event | category | flops | bytes accessed | tf_op | source)
XLA Modules:
  0.0 92.3 jit_solution(6742941645163359166)
XLA Ops:
  0.7 3.1 %shard_map.86 = (bf16[256,384]{1,0:T(8,128)(2,1)S(1)}, bf16[256,384]{1,0:T(8,128)(2,1)S(1)}, bf16[192,128]{1,0:T(8,128)(2,1)S(1)}) custom-call(bf16[256,1536]{1,0:T(8,128)(2,1)} %x_ref, bf16[1536,384]{1,0:T(8,128)(2,1)} %wk_ref.5, bf16[1536,384]{1,0:T(8,128)(2,1)} %wv_ref.5), custom_call_target="tpu_custom_call" | custom-call | flops 603979776 | bytes 3145728 | tf_op jit(solution)/shard_map/pallas_call | solution.py:219
  3.8 3.3 %collective-permute-start = (bf16[192,128]{1,0:T(8,128)(2,1)S(1)}, bf16[192,128]{1,0:T(8,128)(2,1)S(1)}, u32[]{:S(2)}, u32[]{:S(2)}) collective-permute-start(bf16[192,128]{1,0:T(8,128)(2,1)S(1)} %get-tuple-element.48.state_ref), channel_id=1, source_target_pairs={{0,4},{4,0},{1,5},{5,1},{2,6},{6,2},{3,7},{7,3},{8,12},{12,8},{9,1... | collective-permute-start | bytes 147464 | tf_op jit(solution)/shard_map/ppermute | solution.py:169
  10.7 2.5 %collective-permute-done.2.g2 = bf16[96,128]{1,0:T(8,128)(2,1)S(1)} collective-permute-done((bf16[96,128]{1,0:T(8,128)(2,1)S(1)}, bf16[96,128]{1,0:T(8,128)(2,1)S(1)}, u32[]{:S(2)}, u32[]{:S(2)}) %collective-permute-start.2) | collective-permute-done | bytes 24608 | tf_op jit(solution)/shard_map/ppermute | solution.py:175
  14.2 8.2 %all-to-all-start = ((bf16[8,96,128]{2,1,0:T(8,128)(2,1)}), bf16[8,96,128]{2,1,0:T(8,128)(2,1)S(1)}, u32[]{:S(2)}, u32[]{:S(2)}) async-start(bf16[8,96,128]{2,1,0:T(8,128)(2,1)} %get-tuple-element.49), calls=%async_computation | async-start | bytes 393216 | tf_op jit(solution)/shard_map/all_to_all | solution.py:165
  22.4 2.6 %collective-permute-start.7 = (bf16[256,384]{1,0:T(8,128)(2,1)S(1)}, bf16[256,384]{1,0:T(8,128)(2,1)S(1)}, u32[]{:S(2)}, u32[]{:S(2)}) collective-permute-start(bf16[256,384]{1,0:T(8,128)(2,1)S(1)} %copy-done.8), channel_id=1, source_target_pairs={{0,3},{1,0},{2,1},{3,2},{4,7},{5,4},{6,5},{7,6},{8,11},{9,8},{10,9... | collective-permute-start | bytes 589832 | tf_op jit(solution)/shard_map/ppermute | solution.py:496
  28.0 3.1 %shard_map.91 = (bf16[256,384]{1,0:T(8,128)(2,1)}, bf16[256,384]{1,0:T(8,128)(2,1)}) custom-call(bf16[256,1536]{1,0:T(8,128)(2,1)S(1)} %copy-done.7, bf16[1536,384]{1,0:T(8,128)(2,1)S(1)} %copy-done.6, bf16[256,384]{1,0:T(8,128)(2,1)} %get-tuple-element.54.fk_ref.refs_1_, bf16[256,384]{1,0:T(8,128)(2,1)} %get-tuple-element.55.v_ref.refs_2_), custom_call_target="tpu_custom_call" | custom-call | flops 503316480 | bytes 3145728 | tf_op jit(solution)/shard_map/pallas_call | solution.py:71
  31.2 3.3 %collective-permute-start.4 = (bf16[96,128]{1,0:T(8,128)(2,1)S(1)}, bf16[96,128]{1,0:T(8,128)(2,1)S(1)}, u32[]{:S(2)}, u32[]{:S(2)}) collective-permute-start(bf16[96,128]{1,0:T(8,128)(2,1)S(1)} %shard_map.89.mine_ref), channel_id=1, source_target_pairs={{0,4},{4,0},{1,5},{5,1},{2,6},{6,2},{3,7},{7,3},{8,12},{12,8},{9,1... | collective-permute-start | bytes 73736 | tf_op jit(solution)/shard_map/ppermute | solution.py:169
  34.5 2.2 %collective-permute-done.5.g1 = bf16[256,384]{1,0:T(8,128)(2,1)} collective-permute-done((bf16[256,384]{1,0:T(8,128)(2,1)S(1)}, bf16[256,384]{1,0:T(8,128)(2,1)}, u32[]{:S(2)}, u32[]{:S(2)}) %collective-permute-start.5) | collective-permute-done | bytes 196640 | tf_op jit(solution)/shard_map/ppermute | solution.py:496
  36.7 2.4 %shard_map.92.refs_3_ = bf16[256,384]{1,0:T(8,128)(2,1)} custom-call(bf16[256,384]{1,0:T(8,128)(2,1)S(1)} %copy-done.8, bf16[256,384]{1,0:T(8,128)(2,1)} %collective-permute-done.5.g1, bf16[256,384]{1,0:T(8,128)(2,1)} %collective-permute-done.6.g2, bf16[256,384]{1,0:T(8,128)(2,1)S(1)} %collective-permute-done.7.g3, bf16[384,1536]{1,0:T(8,128)(2,1)S(1)} %copy-done.5, ...), custom_call_target="tpu_custom_call" | custom-call | flops 301989888 | bytes 3145728 | tf_op jit(solution)/shard_map/pallas_call | solution.py:71
  41.3 1.5 %collective-permute-start.8 = (bf16[192,128]{1,0:T(8,128)(2,1)S(1)}, bf16[192,128]{1,0:T(8,128)(2,1)S(1)}, u32[]{:S(2)}, u32[]{:S(2)}) collective-permute-start(bf16[192,128]{1,0:T(8,128)(2,1)S(1)} %get-tuple-element.68.state_ref), channel_id=1, source_target_pairs={{0,4},{4,0},{1,5},{5,1},{2,6},{6,2},{3,7},{7,3},{8,12},{12,8},{9,1... | collective-permute-start | bytes 147464 | tf_op jit(solution)/shard_map/ppermute | solution.py:169
  43.7 1.7 %collective-permute-start.13 = (bf16[96,128]{1,0:T(8,128)(2,1)S(1)}, bf16[96,128]{1,0:T(8,128)(2,1)S(1)}, u32[]{:S(2)}, u32[]{:S(2)}) collective-permute-start(bf16[96,128]{1,0:T(8,128)(2,1)S(1)} %shard_map.96.chip_ref), channel_id=1, source_target_pairs={{0,16},{8,24},{16,0},{24,8},{1,17},{9,25},{17,1},{25,9},{2,18},{10... | collective-permute-start | bytes 73736 | tf_op jit(solution)/shard_map/ppermute | solution.py:175
  45.5 1.8 %collective-permute-start.12 = (bf16[96,128]{1,0:T(8,128)(2,1)S(1)}, bf16[96,128]{1,0:T(8,128)(2,1)S(1)}, u32[]{:S(2)}, u32[]{:S(2)}) collective-permute-start(bf16[96,128]{1,0:T(8,128)(2,1)S(1)} %shard_map.96.chip_ref), channel_id=1, source_target_pairs={{0,24},{8,0},{16,8},{24,16},{1,25},{9,1},{17,9},{25,17},{2,26},{10... | collective-permute-start | bytes 73736 | tf_op jit(solution)/shard_map/ppermute | solution.py:175
  49.5 6.6 %all-to-all-start.1 = ((bf16[8,96,128]{2,1,0:T(8,128)(2,1)}), bf16[8,96,128]{2,1,0:T(8,128)(2,1)S(1)}, u32[]{:S(2)}, u32[]{:S(2)}) async-start(bf16[8,96,128]{2,1,0:T(8,128)(2,1)} %get-tuple-element.76), calls=%async_computation.1 | async-start | bytes 393216 | tf_op jit(solution)/shard_map/all_to_all | solution.py:165
  56.0 1.7 %shard_map.95 = (bf16[256,384]{1,0:T(8,128)(2,1)}, bf16[256,384]{1,0:T(8,128)(2,1)}, bf16[256,384]{1,0:T(8,128)(2,1)}, bf16[256,384]{1,0:T(8,128)(2,1)}, bf16[25...) custom-call(bf16[256,384]{1,0:T(8,128)(2,1)S(1)} %get-tuple-element.63.attn_ref, bf16[384,1536]{1,0:T(8,128)(2,1)S(1)} %copy-done.5, ...), custom_call_target="tpu_custom_call" | custom-call | flops 301989888 | bytes 2097152 | tf_op jit(solution)/shard_map/pallas_call | solution.py:369
  59.8 4.9 %all-to-all-done.1.planes_ref = bf16[8,96,128]{2,1,0:T(8,128)(2,1)S(1)} async-done(((bf16[8,96,128]{2,1,0:T(8,128)(2,1)}), bf16[8,96,128]{2,1,0:T(8,128)(2,1)S(1)}, u32[]{:S(2)}, u32[]{:S(2)}) %all-to-all-start.1) | async-done | bytes 196640 | tf_op jit(solution)/shard_map/all_to_all | solution.py:165
  65.3 2.9 %collective-permute-start.15 = (bf16[96,128]{1,0:T(8,128)(2,1)}, bf16[96,128]{1,0:T(8,128)(2,1)}, u32[]{:S(2)}, u32[]{:S(2)}) collective-permute-start(bf16[96,128]{1,0:T(8,128)(2,1)} %shard_map.100.mine_ref), channel_id=1, source_target_pairs={{0,4},{4,0},{1,5},{5,1},{2,6},{6,2},{3,7},{7,3},{8,12},{12,8},{9,1... | collective-permute-start | bytes 73736 | tf_op jit(solution)/shard_map/ppermute | solution.py:169
  68.2 3.7 %shard_map.98 = (bf16[256,384]{1,0:T(8,128)(2,1)}, bf16[256,384]{1,0:T(8,128)(2,1)}, bf16[256,384]{1,0:T(8,128)(2,1)}) custom-call(bf16[256,384]{1,0:T(8,128)(2,1)} %get-tuple-element.56.refs_1_.fq_ref, bf16[256,384]{1,0:T(8,128)(2,1)} %get-tuple-element.54.fk_ref.refs_1_, bf16[256,384]{1,0:T(8,128)(2,1)} %get-tuple-element.55.v_ref.refs_2_, ...), custom_call_target="tpu_custom_call" | custom-call | flops 10066329600 | bytes 3145728 | tf_op jit(solution)/shard_map/pallas_call | solution.py:71
  71.9 1.4 %shard_map.101.wq_ref = bf16[1536,384]{1,0:T(8,128)(2,1)S(1)} custom-call(bf16[1536,384]{1,0:T(8,128)(2,1)} %refs_0_), custom_call_target="tpu_custom_call" | custom-call | flops 1 | bytes 1048576 | tf_op jit(solution)/shard_map/pallas_call | solution.py:42
  74.4 1.4 %shard_map.99 = (bf16[192,128]{1,0:T(8,128)(2,1)S(1)}, bf16[256,384]{1,0:T(8,128)(2,1)S(1)}, bf16[256,384]{1,0:T(8,128)(2,1)S(1)}, bf16[256,384]{1,0:T(8,128)(2,...) custom-call(bf16[192,128]{1,0:T(8,128)(2,1)} %get-tuple-element.74.refs_0_, ...), custom_call_target="tpu_custom_call" | custom-call | flops 1 | bytes 1048576 | tf_op jit(solution)/shard_map/pallas_call | solution.py:42
  75.8 1.3 %copy-done.3 = bf16[1536,384]{1,0:T(8,128)(2,1)S(1)} copy-done((bf16[1536,384]{1,0:T(8,128)(2,1)S(1)}, bf16[1536,384]{1,0:T(8,128)(2,1)}, u32[]{:S(2)}) %copy-start.3) | copy-done | bytes 1179672
  77.1 1.6 %shard_map.102 = (bf16[256,384]{1,0:T(8,128)(2,1)S(1)}, bf16[256,384]{1,0:T(8,128)(2,1)S(1)}, bf16[256,384]{1,0:T(8,128)(2,1)S(1)}) custom-call(bf16[96,128]{1,0:T(8,128)(2,1)} %shard_map.100.mine_ref, bf16[96,128]{1,0:T(8,128)(2,1)} %collective-permute-done.15.got_ref, bf16[192,128]{1,0:T(8,128)(2,1)S(1)} %get-tuple-element.83.pair_ref, ...), custom_call_target="tpu_custom_call" | custom-call | flops 226492416 | bytes 5242880 | tf_op jit(solution)/shard_map/pallas_call | solution.py:453
  79.7 2.7 %collective-permute-start.18 = (bf16[256,384]{1,0:T(8,128)(2,1)S(1)}, bf16[256,384]{1,0:T(8,128)(2,1)S(1)}, u32[]{:S(2)}, u32[]{:S(2)}) collective-permute-start(bf16[256,384]{1,0:T(8,128)(2,1)S(1)} %get-tuple-element.93), channel_id=1, source_target_pairs={{0,3},{1,0},{2,1},{3,2},{4,7},{5,4},{6,5},{7,6},{8,11},{9,8},{10,9... | collective-permute-start | bytes 589832 | tf_op jit(solution)/shard_map/ppermute | solution.py:496
  82.4 1.9 %add_convert_fusion.1 = bf16[256,384]{1,0:T(8,128)(2,1)} fusion(bf16[256,384]{1,0:T(8,128)(2,1)} %collective-permute-done.11, bf16[256,384]{1,0:T(8,128)(2,1)} %collective-permute-done.10, bf16[256,384]{1,0:T(8,128)(2,1)} %collective-permute-done.9, bf16[256,384]{1,0:T(8,128)(2,1)S(1)} %copy-done.9), kind=kLoop, calls=%fused_computation.1 | loop fusion | flops 786432 | bytes 983040 | tf_op jit(solution)/shard_map/convert_element_type | solution.py:492
  84.8 6.7 %collective-permute-done.17 = bf16[256,384]{1,0:T(8,128)(2,1)S(1)} collective-permute-done((bf16[256,384]{1,0:T(8,128)(2,1)S(1)}, bf16[256,384]{1,0:T(8,128)(2,1)S(1)}, u32[]{:S(2)}, u32[]{:S(2)}) %collective-permute-start.17) | collective-permute-done | bytes 196640 | tf_op jit(solution)/shard_map/ppermute | solution.py:496
  (62 shorter events, 19.1 us)
Async XLA Ops:
  0.6 21.8 %copy-start.8 = (bf16[256,384]{1,0:T(8,128)(2,1)S(1)}, bf16[256,384]{1,0:T(8,128)(2,1)}, u32[]{:S(2)}) copy-start(bf16[256,384]{1,0:T(8,128)(2,1)} %g0.1) | copy-start | bytes 589828
  0.6 26.2 %copy-start.10 = (f32[384]{0:T(512)S(1)}, f32[384]{0:T(512)}, u32[]{:S(2)}) copy-start(f32[384]{0:T(512)} %param.12) | copy-start | bytes 4612
  0.6 26.2 %copy-start.6 = (bf16[1536,384]{1,0:T(8,128)(2,1)S(1)}, bf16[1536,384]{1,0:T(8,128)(2,1)}, u32[]{:S(2)}) copy-start(bf16[1536,384]{1,0:T(8,128)(2,1)} %refs_0_) | copy-start | bytes 3538948
  3.8 4.2 %collective-permute-start = (bf16[192,128]{1,0:T(8,128)(2,1)S(1)}, bf16[192,128]{1,0:T(8,128)(2,1)S(1)}, u32[]{:S(2)}, u32[]{:S(2)}) collective-permute-start(bf16[192,128]{1,0:T(8,128)(2,1)S(1)} %get-tuple-element.48.state_ref), channel_id=1, source_target_pairs={{0,4},{4,0},{1,5},{5,1},{2,6},{6,2},{3,7},{7,3},{8,12},{12,8},{9,1... | collective-permute-start | bytes 147464 | tf_op jit(solution)/shard_map/ppermute | solution.py:169
  8.0 2.8 %collective-permute-start.3 = (bf16[96,128]{1,0:T(8,128)(2,1)S(1)}, bf16[96,128]{1,0:T(8,128)(2,1)S(1)}, u32[]{:S(2)}, u32[]{:S(2)}) collective-permute-start(bf16[96,128]{1,0:T(8,128)(2,1)S(1)} %shard_map.87.chip_ref), channel_id=1, source_target_pairs={{0,24},{8,0},{16,8},{24,16},{1,25},{9,1},{17,9},{25,17},{2,26},{10... | collective-permute-start | bytes 73736 | tf_op jit(solution)/shard_map/ppermute | solution.py:175
  9.1 4.2 %collective-permute-start.2 = (bf16[96,128]{1,0:T(8,128)(2,1)S(1)}, bf16[96,128]{1,0:T(8,128)(2,1)S(1)}, u32[]{:S(2)}, u32[]{:S(2)}) collective-permute-start(bf16[96,128]{1,0:T(8,128)(2,1)S(1)} %shard_map.87.chip_ref), channel_id=1, source_target_pairs={{0,16},{8,24},{16,0},{24,8},{1,17},{9,25},{17,1},{25,9},{2,18},{10... | collective-permute-start | bytes 73736 | tf_op jit(solution)/shard_map/ppermute | solution.py:175
  9.4 4.1 %collective-permute-start.1 = (bf16[96,128]{1,0:T(8,128)(2,1)S(1)}, bf16[96,128]{1,0:T(8,128)(2,1)S(1)}, u32[]{:S(2)}, u32[]{:S(2)}) collective-permute-start(bf16[96,128]{1,0:T(8,128)(2,1)S(1)} %shard_map.87.chip_ref), channel_id=1, source_target_pairs={{0,8},{8,16},{16,24},{24,0},{1,9},{9,17},{17,25},{25,1},{2,10},{10... | collective-permute-start | bytes 73736 | tf_op jit(solution)/shard_map/ppermute | solution.py:175
  14.2 16.9 %all-to-all-start = ((bf16[8,96,128]{2,1,0:T(8,128)(2,1)}), bf16[8,96,128]{2,1,0:T(8,128)(2,1)S(1)}, u32[]{:S(2)}, u32[]{:S(2)}) async-start(bf16[8,96,128]{2,1,0:T(8,128)(2,1)} %get-tuple-element.49), calls=%async_computation | async-start | bytes 393216 | tf_op jit(solution)/shard_map/all_to_all | solution.py:165
  22.4 12.1 %collective-permute-start.7 = (bf16[256,384]{1,0:T(8,128)(2,1)S(1)}, bf16[256,384]{1,0:T(8,128)(2,1)S(1)}, u32[]{:S(2)}, u32[]{:S(2)}) collective-permute-start(bf16[256,384]{1,0:T(8,128)(2,1)S(1)} %copy-done.8), channel_id=1, source_target_pairs={{0,3},{1,0},{2,1},{3,2},{4,7},{5,4},{6,5},{7,6},{8,11},{9,8},{10,9... | collective-permute-start | bytes 589832 | tf_op jit(solution)/shard_map/ppermute | solution.py:496
  25.0 9.5 %collective-permute-start.6 = (bf16[256,384]{1,0:T(8,128)(2,1)S(1)}, bf16[256,384]{1,0:T(8,128)(2,1)}, u32[]{:S(2)}, u32[]{:S(2)}) collective-permute-start(bf16[256,384]{1,0:T(8,128)(2,1)S(1)} %copy-done.8), channel_id=1, source_target_pairs={{0,2},{1,3},{2,0},{3,1},{4,6},{5,7},{6,4},{7,5},{8,10},{9,11},{10,... | collective-permute-start | bytes 589832 | tf_op jit(solution)/shard_map/ppermute | solution.py:496
  25.5 11.2 %collective-permute-start.5 = (bf16[256,384]{1,0:T(8,128)(2,1)S(1)}, bf16[256,384]{1,0:T(8,128)(2,1)}, u32[]{:S(2)}, u32[]{:S(2)}) collective-permute-start(bf16[256,384]{1,0:T(8,128)(2,1)S(1)} %copy-done.8), channel_id=1, source_target_pairs={{0,1},{1,2},{2,3},{3,0},{4,5},{5,6},{6,7},{7,4},{8,9},{9,10},{10,1... | collective-permute-start | bytes 589832 | tf_op jit(solution)/shard_map/ppermute | solution.py:496
  31.2 9.1 %collective-permute-start.4 = (bf16[96,128]{1,0:T(8,128)(2,1)S(1)}, bf16[96,128]{1,0:T(8,128)(2,1)S(1)}, u32[]{:S(2)}, u32[]{:S(2)}) collective-permute-start(bf16[96,128]{1,0:T(8,128)(2,1)S(1)} %shard_map.89.mine_ref), channel_id=1, source_target_pairs={{0,4},{4,0},{1,5},{5,1},{2,6},{6,2},{3,7},{7,3},{8,12},{12,8},{9,1... | collective-permute-start | bytes 73736 | tf_op jit(solution)/shard_map/ppermute | solution.py:169
  41.3 2.4 %collective-permute-start.8 = (bf16[192,128]{1,0:T(8,128)(2,1)S(1)}, bf16[192,128]{1,0:T(8,128)(2,1)S(1)}, u32[]{:S(2)}, u32[]{:S(2)}) collective-permute-start(bf16[192,128]{1,0:T(8,128)(2,1)S(1)} %get-tuple-element.68.state_ref), channel_id=1, source_target_pairs={{0,4},{4,0},{1,5},{5,1},{2,6},{6,2},{3,7},{7,3},{8,12},{12,8},{9,1... | collective-permute-start | bytes 147464 | tf_op jit(solution)/shard_map/ppermute | solution.py:169
  43.6 4.0 %collective-permute-start.14 = (bf16[96,128]{1,0:T(8,128)(2,1)S(1)}, bf16[96,128]{1,0:T(8,128)(2,1)S(1)}, u32[]{:S(2)}, u32[]{:S(2)}) collective-permute-start(bf16[96,128]{1,0:T(8,128)(2,1)S(1)} %shard_map.96.chip_ref), channel_id=1, source_target_pairs={{0,8},{8,16},{16,24},{24,0},{1,9},{9,17},{17,25},{25,1},{2,10},{10... | collective-permute-start | bytes 73736 | tf_op jit(solution)/shard_map/ppermute | solution.py:175
  43.7 4.3 %collective-permute-start.13 = (bf16[96,128]{1,0:T(8,128)(2,1)S(1)}, bf16[96,128]{1,0:T(8,128)(2,1)S(1)}, u32[]{:S(2)}, u32[]{:S(2)}) collective-permute-start(bf16[96,128]{1,0:T(8,128)(2,1)S(1)} %shard_map.96.chip_ref), channel_id=1, source_target_pairs={{0,16},{8,24},{16,0},{24,8},{1,17},{9,25},{17,1},{25,9},{2,18},{10... | collective-permute-start | bytes 73736 | tf_op jit(solution)/shard_map/ppermute | solution.py:175
  45.5 3.3 %collective-permute-start.12 = (bf16[96,128]{1,0:T(8,128)(2,1)S(1)}, bf16[96,128]{1,0:T(8,128)(2,1)S(1)}, u32[]{:S(2)}, u32[]{:S(2)}) collective-permute-start(bf16[96,128]{1,0:T(8,128)(2,1)S(1)} %shard_map.96.chip_ref), channel_id=1, source_target_pairs={{0,24},{8,0},{16,8},{24,16},{1,25},{9,1},{17,9},{25,17},{2,26},{10... | collective-permute-start | bytes 73736 | tf_op jit(solution)/shard_map/ppermute | solution.py:175
  49.5 15.2 %all-to-all-start.1 = ((bf16[8,96,128]{2,1,0:T(8,128)(2,1)}), bf16[8,96,128]{2,1,0:T(8,128)(2,1)S(1)}, u32[]{:S(2)}, u32[]{:S(2)}) async-start(bf16[8,96,128]{2,1,0:T(8,128)(2,1)} %get-tuple-element.76), calls=%async_computation.1 | async-start | bytes 393216 | tf_op jit(solution)/shard_map/all_to_all | solution.py:165
  57.8 24.6 %collective-permute-start.11 = (bf16[256,384]{1,0:T(8,128)(2,1)}, bf16[256,384]{1,0:T(8,128)(2,1)}, u32[]{:S(2)}, u32[]{:S(2)}) collective-permute-start(bf16[256,384]{1,0:T(8,128)(2,1)} %get-tuple-element.73), channel_id=1, source_target_pairs={{0,3},{1,0},{2,1},{3,2},{4,7},{5,4},{6,5},{7,6},{8,11},{9,8},{10,9... | collective-permute-start | bytes 589832 | tf_op jit(solution)/shard_map/ppermute | solution.py:496
  58.2 24.2 %collective-permute-start.10 = (bf16[256,384]{1,0:T(8,128)(2,1)}, bf16[256,384]{1,0:T(8,128)(2,1)}, u32[]{:S(2)}, u32[]{:S(2)}) collective-permute-start(bf16[256,384]{1,0:T(8,128)(2,1)} %get-tuple-element.71), channel_id=1, source_target_pairs={{0,1},{1,2},{2,3},{3,0},{4,5},{5,6},{6,7},{7,4},{8,9},{9,10},{10,1... | collective-permute-start | bytes 589832 | tf_op jit(solution)/shard_map/ppermute | solution.py:496
  59.3 23.0 %collective-permute-start.9 = (bf16[256,384]{1,0:T(8,128)(2,1)}, bf16[256,384]{1,0:T(8,128)(2,1)}, u32[]{:S(2)}, u32[]{:S(2)}) collective-permute-start(bf16[256,384]{1,0:T(8,128)(2,1)} %get-tuple-element.69), channel_id=1, source_target_pairs={{0,2},{1,3},{2,0},{3,1},{4,6},{5,7},{6,4},{7,5},{8,10},{9,11},{10,... | collective-permute-start | bytes 589832 | tf_op jit(solution)/shard_map/ppermute | solution.py:496
  65.3 10.4 %collective-permute-start.15 = (bf16[96,128]{1,0:T(8,128)(2,1)}, bf16[96,128]{1,0:T(8,128)(2,1)}, u32[]{:S(2)}, u32[]{:S(2)}) collective-permute-start(bf16[96,128]{1,0:T(8,128)(2,1)} %shard_map.100.mine_ref), channel_id=1, source_target_pairs={{0,4},{4,0},{1,5},{5,1},{2,6},{6,2},{3,7},{7,3},{8,12},{12,8},{9,1... | collective-permute-start | bytes 73736 | tf_op jit(solution)/shard_map/ppermute | solution.py:169
  79.6 12.0 %collective-permute-start.17 = (bf16[256,384]{1,0:T(8,128)(2,1)S(1)}, bf16[256,384]{1,0:T(8,128)(2,1)S(1)}, u32[]{:S(2)}, u32[]{:S(2)}) collective-permute-start(bf16[256,384]{1,0:T(8,128)(2,1)S(1)} %get-tuple-element.92), channel_id=1, source_target_pairs={{0,1},{1,2},{2,3},{3,0},{4,5},{5,6},{6,7},{7,4},{8,9},{9,10},{10,1... | collective-permute-start | bytes 589832 | tf_op jit(solution)/shard_map/ppermute | solution.py:496
  79.7 11.9 %collective-permute-start.18 = (bf16[256,384]{1,0:T(8,128)(2,1)S(1)}, bf16[256,384]{1,0:T(8,128)(2,1)S(1)}, u32[]{:S(2)}, u32[]{:S(2)}) collective-permute-start(bf16[256,384]{1,0:T(8,128)(2,1)S(1)} %get-tuple-element.93), channel_id=1, source_target_pairs={{0,3},{1,0},{2,1},{3,2},{4,7},{5,4},{6,5},{7,6},{8,11},{9,8},{10,9... | collective-permute-start | bytes 589832 | tf_op jit(solution)/shard_map/ppermute | solution.py:496
  82.3 9.2 %collective-permute-start.16 = (bf16[256,384]{1,0:T(8,128)(2,1)S(1)}, bf16[256,384]{1,0:T(8,128)(2,1)S(1)}, u32[]{:S(2)}, u32[]{:S(2)}) collective-permute-start(bf16[256,384]{1,0:T(8,128)(2,1)S(1)} %get-tuple-element.91), channel_id=1, source_target_pairs={{0,2},{1,3},{2,0},{3,1},{4,6},{5,7},{6,4},{7,5},{8,10},{9,11},{10,... | collective-permute-start | bytes 589832 | tf_op jit(solution)/shard_map/ppermute | solution.py:496
  (8 other events, 25.1 us)

commit v4 on v3

--- a/solution.py
+++ b/solution.py
@@ -26,35 +26,12 @@
     return lax.dot_general(a, b, contract, preferred_element_type=f32)
 
 
-def relay(near, *args):
-    def body(*refs):
-        sources, targets, sem = (refs[: len(args)], refs[len(args) : -1], refs[-1])
-        copies = [
-            pltpu.make_async_copy(a, b, sem.at[i]) for i, (a, b) in enumerate(zip(sources, targets))
-        ]
-        for copy in copies:
-            copy.start()
-        for copy in copies:
-            copy.wait()
-
-    hbm = pl.BlockSpec(memory_space=pltpu.HBM)
-    make = pltpu.VMEM if near else pltpu.HBM
-    return pl.pallas_call(
-        body,
-        out_shape=[make(a.shape, a.dtype) for a in args],
-        in_specs=[hbm if near else VMEM] * len(args),
-        out_specs=[VMEM if near else hbm] * len(args),
-        scratch_shapes=[pltpu.SemaphoreType.DMA((len(args),))],
-        cost_estimate=pl.CostEstimate(flops=1, bytes_accessed=1024 * 1024, transcendentals=0),
-    )(*(pltpu.with_memory_space_constraint(a, pltpu.HBM if near else pltpu.VMEM) for a in args))
-
-
 def in_hbm(x):
     return pltpu.with_memory_space_constraint(x, pltpu.HBM)
 
 
-def shape_of(shape, kind, far=False):
-    return pltpu.HBM(shape, kind) if far else jax.ShapeDtypeStruct(shape, kind)
+def shape_of(shape, kind, where=pltpu.VMEM):
+    return where(shape, kind)
 
 
 def call(body, outs, flops, moved, **extra):
@@ -127,10 +104,10 @@
     return plain(body, [((half, LANES), bf16)], 1, half * 1024, state, pair)[0]
 
 
-def plane_sums(later, chip, got, pair):
+def plane_sums(later, chip, got):
     half = chip.shape[0]
 
-    def body(chip_ref, g1, g2, g3, pair_ref, planes_ref, kept_ref):
+    def body(chip_ref, g1, g2, g3, planes_ref):
         y = lax.axis_index("seq_1")
         y = 3 - y if later else y
         total = chip_ref[...].astype(f32)
@@ -141,10 +118,9 @@
             inside = inside + jnp.where(y >= k, piece, 0.0)
         planes_ref[...] = jnp.broadcast_to(total.astype(bf16)[None], planes_ref.shape)
         planes_ref[pl.ds(lax.axis_index("seq_0"), 1)] = inside.astype(bf16)[None]
-        kept_ref[...] = pair_ref[...]
-
-    outs = [((8, half, LANES), bf16, True), ((2 * half, LANES), bf16, True)]
-    return plain(body, outs, 1, half * 4096, chip, *got, pair)
+
+    outs = [((8, half, LANES), bf16, pltpu.HBM)]
+    return plain(body, outs, 1, half * 4096, chip, *got)[0]
 
 
 def before_chip(later, planes):
@@ -263,36 +239,44 @@
 
     return plain(
         body,
-        [((rows, width), bf16, True)] * 2,
+        [((rows, width), bf16)] * 2,
         2 * rows * width * (latents.shape[1] + 4 * rows),
         3 * 1024 * 1024,
         latents,
         w_query,
-        in_hbm(fk),
-        in_hbm(v),
+        fk,
+        v,
     )
 
 
 def upstream_of(grads, w_out, gain):
     rows, width = grads[0].shape
 
-    def body(g0, g1, g2, g3, w_ref, gain_ref, up_ref):
+    def body(g0, g1, g2, g3, w_hbm, gain_ref, up_ref, w_ref, sem):
         m = lax.axis_index("mp")
+        copies = []
+        for k in range(4):
+            at = pl.multiple_of(lax.rem(m + 4 - k, 4) * width, LANES)
+            copies.append(
+                pltpu.make_async_copy(w_hbm.at[:, pl.ds(at, width)], w_ref.at[k], sem.at[k])
+            )
+        for copy in copies:
+            copy.start()
         total = jnp.zeros((rows, width), f32)
         for k, ref in enumerate((g0, g1, g2, g3)):
-            at = lax.rem(m + 4 - k, 4) * width
-            total = total + mm(ref[...], w_ref[:, pl.ds(pl.multiple_of(at, LANES), width)], NT)
+            copies[k].wait()
+            total = total + mm(ref[...], w_ref[k], NT)
         up_ref[...] = (total * gain_ref[...]).astype(bf16)
 
-    return plain(
-        body,
-        [((rows, width), bf16, True)],
+    return call(
+        body,
+        [((rows, width), bf16)],
         8 * rows * width * width,
         3 * 1024 * 1024,
-        *grads,
-        w_out,
-        gain,
-    )[0]
+        in_specs=[VMEM] * 4 + [pl.BlockSpec(memory_space=pltpu.HBM), VMEM],
+        out_specs=[VMEM],
+        scratch_shapes=[pltpu.VMEM((4, width, width), bf16), pltpu.SemaphoreType.DMA((4,))],
+    )(*grads, in_hbm(w_out), gain)[0]
 
 
 def normed(mine, got, pair, fq, raw_local, up, gain):
@@ -346,35 +330,30 @@
     )(mine, got, pair, fq, raw_local, up, gain)
 
 
-def branch_parts(attn, w_out, draw, before):
+def branch_parts(attn, w_out):
     rows, width = attn.shape
 
-    def body(attn_ref, w_ref, draw_ref, before_ref, *refs):
-        outs, kept, sem = (refs[:4], refs[4:6], refs[6])
-        copies = [
-            pltpu.make_async_copy(a, b, sem.at[i])
-            for i, (a, b) in enumerate(zip((draw_ref, before_ref), kept))
-        ]
+    def body(attn_ref, w_hbm, *refs):
+        outs, w_ref, sem = (refs[:4], refs[4], refs[5])
+        copies = []
+        for i, k in enumerate((2, 1, 3, 0)):
+            source = w_hbm.at[:, block_rows(k, width)]
+            copies.append(pltpu.make_async_copy(source, w_ref.at[i], sem.at[i]))
         for copy in copies:
             copy.start()
-        m = lax.axis_index("mp")
-        for k, ref in zip((2, 1, 3, 0), outs):
-            at = lax.rem(m + k, 4) * width
-            ref[...] = mm(
-                attn_ref[...], w_ref[:, pl.ds(pl.multiple_of(at, LANES), width)]
-            ).astype(bf16)
-        for copy in copies:
-            copy.wait()
-
-    return call(
-        body,
-        [((rows, width), bf16, True)] * 5 + [(before.shape, bf16, True)],
+        for i, ref in enumerate(outs):
+            copies[i].wait()
+            ref[...] = mm(attn_ref[...], w_ref[i]).astype(bf16)
+
+    return call(
+        body,
+        [((rows, width), bf16, pltpu.HBM)] * 4,
         8 * rows * width * width,
         2 * 1024 * 1024,
-        in_specs=[VMEM] * 4,
-        out_specs=[VMEM] * 4 + [pl.BlockSpec(memory_space=pltpu.HBM)] * 2,
-        scratch_shapes=[pltpu.SemaphoreType.DMA((2,))],
-    )(attn, w_out, draw, before)
+        in_specs=[VMEM, pl.BlockSpec(memory_space=pltpu.HBM)],
+        out_specs=[VMEM] * 4,
+        scratch_shapes=[pltpu.VMEM((4, width, width), bf16), pltpu.SemaphoreType.DMA((4,))],
+    )(attn, in_hbm(w_out))
 
 
 def local_grads(fq, fk, v, draw, before):
@@ -400,23 +379,52 @@
 
     return plain(
         body,
-        [((rows, width), bf16, True)] * 3,
-        400 * rows * rows * width,
+        [((rows, width), bf16)] * 3,
+        24 * rows * rows * width,
         3 * 1024 * 1024,
-        *(in_hbm(a) for a in (fq, fk, v, draw, before)),
+        fq,
+        fk,
+        v,
+        draw,
+        before,
     )
 
 
-def latent_part(m, k, width, triples):
-    rows = pl.ds(pl.multiple_of(lax.rem(m + k, 4) * width, LANES), width)
-    total = None
-    for grad_ref, w_ref in triples:
-        part = mm(grad_ref[...], w_ref[rows, :], NT)
-        total = part if total is None else total + part
-    return total.astype(bf16)
-
-
-def first_part(mine, got, pair, fk, v, dq, dk, dv, w_query, w_key, w_value):
+def block_rows(k, width):
+    at = lax.rem(lax.axis_index("mp") + k, 4) * width
+    return pl.ds(pl.multiple_of(at, LANES), width)
+
+
+def block_copies(k, sources, targets, sem, first):
+    width = sources[0].shape[1]
+    return [
+        pltpu.make_async_copy(src.at[block_rows(k, width), :], dst, sem.at[first + i])
+        for i, (src, dst) in enumerate(zip(sources, targets))
+    ]
+
+
+def weight_blocks(k, weights):
+    width = weights[0].shape[1]
+
+    def body(*refs):
+        copies = block_copies(k, refs[:3], refs[3:6], refs[6], 0)
+        for copy in copies:
+            copy.start()
+        for copy in copies:
+            copy.wait()
+
+    return call(
+        body,
+        [((width, width), bf16)] * 3,
+        1,
+        1024 * 1024,
+        in_specs=[pl.BlockSpec(memory_space=pltpu.HBM)] * 3,
+        out_specs=[VMEM] * 3,
+        scratch_shapes=[pltpu.SemaphoreType.DMA((3,))],
+    )(*(in_hbm(w) for w in weights))
+
+
+def first_part(mine, got, pair, fk, v, dq, dk, dv, blocks):
     rows, width = fk.shape
     half = mine.shape[0]
 
@@ -445,44 +453,58 @@
             dk = dkl_ref[:, cols].astype(f32) + mm(v_ref[:, cols], after, NT)
             dk_ref[:, cols] = (dk * jnp.minimum(k.astype(f32), 1.0)).astype(bf16)
             dv_ref[:, cols] = (dvl_ref[:, cols].astype(f32) + mm(k, after)).astype(bf16)
-        m = lax.axis_index("mp")
-        part_ref[...] = latent_part(
-            m, 2, width, ((dq_ref, wq_ref), (dk_ref, wk_ref), (dv_ref, wv_ref))
-        )
+        total = mm(dq_ref[...], wq_ref[...], NT)
+        total = total + mm(dk_ref[...], wk_ref[...], NT)
+        part_ref[...] = (total + mm(dv_ref[...], wv_ref[...], NT)).astype(bf16)
 
     return call(
         body,
         [((rows, width), bf16)] * 3,
         6 * rows * width * width,
-        5 * 1024 * 1024,
+        2 * 1024 * 1024,
         in_specs=[VMEM] * 11,
         out_specs=[VMEM] * 3,
         scratch_shapes=[pltpu.VMEM((2 * half, LANES), f32)],
-    )(mine, got, pair, fk, v, dq, dk, dv, w_query, w_key, w_value)
-
-
-def other_parts(which, dq, dk, dv, w_query, w_key, w_value):
+    )(mine, got, pair, fk, v, dq, dk, dv, *blocks)
+
+
+def other_parts(which, dq, dk, dv, weights):
     rows, width = dq.shape
-
-    def body(dq_ref, dk_ref, dv_ref, wq_ref, wk_ref, wv_ref, *outs):
-        m = lax.axis_index("mp")
-        for k, ref in zip(which, outs):
-            ref[...] = latent_part(
-                m, k, width, ((dq_ref, wq_ref), (dk_ref, wk_ref), (dv_ref, wv_ref))
+    count = len(which)
+
+    def body(dq_ref, dk_ref, dv_ref, wq_hbm, wk_hbm, wv_hbm, *refs):
+        outs, blocks, sem = (refs[:count], refs[count], refs[count + 1])
+        copies = [
+            block_copies(
+                k, (wq_hbm, wk_hbm, wv_hbm), [blocks.at[3 * i + j] for j in range(3)], sem, 3 * i
             )
-
-    return plain(
-        body,
-        [((rows, width), bf16)] * len(which),
-        6 * rows * width * width * len(which),
-        5 * 1024 * 1024,
-        dq,
-        dk,
-        dv,
-        w_query,
-        w_key,
-        w_value,
-    )
+            for i, k in enumerate(which)
+        ]
+        for group in copies:
+            for copy in group:
+                copy.start()
+        for i, (group, ref) in enumerate(zip(copies, outs)):
+            for copy in group:
+                copy.wait()
+            total = None
+            for j, grad_ref in enumerate((dq_ref, dk_ref, dv_ref)):
+                part = mm(grad_ref[...], blocks[3 * i + j], NT)
+                total = part if total is None else total + part
+            ref[...] = total.astype(bf16)
+
+    hbm = pl.BlockSpec(memory_space=pltpu.HBM)
+    return call(
+        body,
+        [((rows, width), bf16)] * count,
+        6 * rows * width * width * count,
+        1024 * 1024 * count,
+        in_specs=[VMEM] * 3 + [hbm] * 3,
+        out_specs=[VMEM] * count,
+        scratch_shapes=[
+            pltpu.VMEM((3 * count, width, width), bf16),
+            pltpu.SemaphoreType.DMA((3 * count,)),
+        ],
+    )(dq, dk, dv, *(in_hbm(w) for w in weights))
 
 
 def add_up(parts):
@@ -504,39 +526,35 @@
     gain = head_gain.reshape(1, -1)
     fk, v, state = key_value(latents, w_key, w_value)
     pair = swap(state)
-    fk, v = relay(False, fk, v)
     chip = pair_sum(state, pair)
     got = y_gather(False, chip)
     grad_held = hold(grad_out, chip)
     grads = [grad_out] + [to_owner(grad_held, k) for k in (1, 2, 3)]
-    planes, pair = plane_sums(False, chip, got, pair)
+    planes = plane_sums(False, chip, got)
     fq, raw_local = query_local(hold(latents, planes), w_query, fk, v)
     up = upstream_of(grads, w_out, gain)
     planes = plane_exchange(planes)
     mine = before_chip(False, planes)
     got = swap(mine)
-    near = relay(True, pair, fq, raw_local, up)
-    attn, draw, before, state = normed(mine, got, *near, gain)
+    attn, draw, before, state = normed(mine, got, pair, fq, raw_local, up, gain)
     pair = swap(state)
-    b2, b1, b3, b0, draw, before = branch_parts(attn, w_out, draw, before)
     chip = pair_sum(state, pair)
     got = y_gather(True, chip)
-    b2, b1, b3 = (hold(b, chip) for b in (b2, b1, b3))
+    b2, b1, b3, b0 = branch_parts(hold(attn, chip), w_out)
+    planes = plane_sums(True, chip, got)
+    b2, b1, b3 = (hold(b, planes) for b in (b2, b1, b3))
     branch = [b0, to_owner(b2, 2), to_owner(b1, 1), to_owner(b3, 3)]
-    planes, pair = plane_sums(True, chip, got, pair)
     dq, dk_local, dv_local = local_grads(fq, fk, v, hold(draw, planes), before)
-    (w_query,) = relay(True, hold(w_query, dq))
+    weights = (w_query, w_key, w_value)
+    blocks = weight_blocks(2, (hold(w_query, dq), w_key, w_value))
     planes = plane_exchange(planes)
     mine = before_chip(True, planes)
     got = swap(mine)
-    near = relay(True, pair, fk, v, dq, dk_local, dv_local)
-    dq = near[3]
-    weights = (w_query, w_key, w_value)
-    dk, dv, l2 = first_part(mine, got, *near, *weights)
+    dk, dv, l2 = first_part(mine, got, pair, fk, v, dq, dk_local, dv_local, blocks)
     l2 = to_owner(l2, 2)
-    l1, l3 = other_parts((1, 3), dq, dk, dv, *weights)
+    l1, l3 = other_parts((1, 3), dq, dk, dv, weights)
     l1, l3 = (to_owner(l1, 1), to_owner(l3, 3))
-    (l0,) = other_parts((0,), dq, dk, dv, *weights)
+    (l0,) = other_parts((0,), dq, dk, dv, weights)
     return (add_up(branch), add_up([l0, l2, l1, l3]))
 
 

time: 92.8 us -> 85.6 us (0.922)
  Pallas kernels: 24.8 us -> 19.9 us
  local copies, waits for them, and re-layouts: 3.46 us -> 1.37 us
  other arithmetic: 2.68 us -> 1.56 us
  waiting for transfers between devices: 20.5 us -> 21.5 us
    pallas_call x11 -> x8, Pallas kernels: 12.7 us -> 4.62 us  [plain(): call(body, outs, flops, moved, in_specs=[VMEM] * len(args), out_specs=[VM...]
    pallas_call x6, Pallas kernels: 7.97 us -> 11.1 us  [the longest x2 4.24 us: other_parts(): call(body, [((rows, width), bf16)] * count, 6 * rows * width * width * co...]
    unnamed x22 -> x18, local copies, waits for them, and re-layouts: 3.45 us -> 1.37 us
    all_to_all x2, waiting for transfers between devices: 4.89 us -> 6.05 us  [plane_exchange(): return lax.all_to_all(planes, 'seq_0', 0, 0, tiled=True)]
    convert_element_type x2, other arithmetic: 2.68 us -> 1.56 us  [add_up(): return total.astype(bf16)]
  transfers between devices with their start and end apart: 21 -> 21, of which waited for: 11 -> 12; matrix products, arithmetic and copies ran while one was open for 2% -> 1% of each run, Pallas kernels for 21% -> 17%
where the time goes in v4:
time: 85.6 us; the launch traced here: 85.3 us
  starting transfers between devices  40.1 us (47%)
  waiting for transfers between devices  21.5 us (25%)
  Pallas kernels  19.9 us (23%)
  other arithmetic  1.56 us (2%)
  local copies, waits for them, and re-layouts  1.37 us (2%)
  between operations  0.87 us (1%)
    all_to_all x2, starting transfers between devices, plane_exchange(): return lax.all_to_all(planes, 'seq_0', 0, 0, tiled=True)  14.8 us
    ppermute x4, starting transfers between devices, swap(): return lax.ppermute(x, 'seq_2', SWAP)  11.1 us
    ppermute x9, waiting for transfers between devices, to_owner(): return lax.ppermute(part, 'mp', shifts(4, k))  8.81 us
    ppermute x9, starting transfers between devices, to_owner(): return lax.ppermute(part, 'mp', shifts(4, k))  8.48 us
    all_to_all x2, waiting for transfers between devices, plane_exchange(): return lax.all_to_all(planes, 'seq_0', 0, 0, tiled=True)  6.05 us
    ppermute x6, starting transfers between devices, y_gather(): got.append(lax.ppermute(chip, 'seq_1', shifts(4, -k if later else k)))  5.75 us
    ppermute x6, waiting for transfers between devices, y_gather(): got.append(lax.ppermute(chip, 'seq_1', shifts(4, -k if later else k)))  4.88 us
    pallas_call x8, Pallas kernels, plain(): call(body, outs, flops, moved, in_specs=[VMEM] * len(args), out_specs=[VM...  4.62 us
  transfers between devices with their start and end apart: 21, of which 12 were waited for; matrix products, arithmetic and copies ran while one was open for 1% of the time, Pallas kernels for 17%

profile of v4, /device:TPU:1, one launch (start us, length us, event | category | flops | bytes accessed | tf_op | source)
XLA Modules:
  0.0 85.3 jit_solution(9835249271246029770)
XLA Ops:
  0.7 3.1 %shard_map.86 = (bf16[256,384]{1,0:T(8,128)(2,1)S(1)}, bf16[256,384]{1,0:T(8,128)(2,1)S(1)}, bf16[192,128]{1,0:T(8,128)(2,1)S(1)}) custom-call(bf16[256,1536]{1,0:T(8,128)(2,1)} %x_ref, bf16[1536,384]{1,0:T(8,128)(2,1)} %wk_hbm.5, bf16[1536,384]{1,0:T(8,128)(2,1)} %wv_hbm.5), custom_call_target="tpu_custom_call" | custom-call | flops 603979776 | bytes 3145728 | tf_op jit(solution)/shard_map/pallas_call | solution.py:195
  3.8 3.3 %collective-permute-start = (bf16[192,128]{1,0:T(8,128)(2,1)S(1)}, bf16[192,128]{1,0:T(8,128)(2,1)S(1)}, u32[]{:S(2)}, u32[]{:S(2)}) collective-permute-start(bf16[192,128]{1,0:T(8,128)(2,1)S(1)} %get-tuple-element.34.state_ref), channel_id=1, source_target_pairs={{0,4},{4,0},{1,5},{5,1},{2,6},{6,2},{3,7},{7,3},{8,12},{12,8},{9,1... | collective-permute-start | bytes 147464 | tf_op jit(solution)/shard_map/ppermute | solution.py:145
  10.7 2.5 %collective-permute-done.2.g2 = bf16[96,128]{1,0:T(8,128)(2,1)S(1)} collective-permute-done((bf16[96,128]{1,0:T(8,128)(2,1)S(1)}, bf16[96,128]{1,0:T(8,128)(2,1)S(1)}, u32[]{:S(2)}, u32[]{:S(2)}) %collective-permute-start.2) | collective-permute-done | bytes 24608 | tf_op jit(solution)/shard_map/ppermute | solution.py:151
  14.2 8.2 %all-to-all-start = ((bf16[8,96,128]{2,1,0:T(8,128)(2,1)}), bf16[8,96,128]{2,1,0:T(8,128)(2,1)S(1)}, u32[]{:S(2)}, u32[]{:S(2)}) async-start(bf16[8,96,128]{2,1,0:T(8,128)(2,1)} %shard_map.88), calls=%async_computation | async-start | bytes 393216 | tf_op jit(solution)/shard_map/all_to_all | solution.py:141
  22.4 2.6 %collective-permute-start.7 = (bf16[256,384]{1,0:T(8,128)(2,1)S(1)}, bf16[256,384]{1,0:T(8,128)(2,1)S(1)}, u32[]{:S(2)}, u32[]{:S(2)}) collective-permute-start(bf16[256,384]{1,0:T(8,128)(2,1)S(1)} %copy-done.2), channel_id=1, source_target_pairs={{0,3},{1,0},{2,1},{3,2},{4,7},{5,4},{6,5},{7,6},{8,11},{9,8},{10,9... | collective-permute-start | bytes 589832 | tf_op jit(solution)/shard_map/ppermute | solution.py:518
  26.1 1.3 %shard_map.90 = (bf16[256,384]{1,0:T(8,128)(2,1)S(1)}, bf16[256,384]{1,0:T(8,128)(2,1)S(1)}) custom-call(bf16[256,1536]{1,0:T(8,128)(2,1)S(1)} %copy-done.1, bf16[1536,384]{1,0:T(8,128)(2,1)S(1)} %copy-done, bf16[256,384]{1,0:T(8,128)(2,1)S(1)} %get-tuple-element.36.fk_ref, bf16[256,384]{1,0:T(8,128)(2,1)S(1)} %get-tuple-element.37.v_ref), custom_call_target="tpu_custom_call" | custom-call | flops 503316480 | bytes 3145728 | tf_op jit(solution)/shard_map/pallas_call | solution.py:48
  28.8 2.3 %all-to-all-done.planes_ref = bf16[8,96,128]{2,1,0:T(8,128)(2,1)S(1)} async-done(((bf16[8,96,128]{2,1,0:T(8,128)(2,1)}), bf16[8,96,128]{2,1,0:T(8,128)(2,1)S(1)}, u32[]{:S(2)}, u32[]{:S(2)}) %all-to-all-start) | async-done | bytes 196640 | tf_op jit(solution)/shard_map/all_to_all | solution.py:141
  31.2 3.3 %collective-permute-start.4 = (bf16[96,128]{1,0:T(8,128)(2,1)S(1)}, bf16[96,128]{1,0:T(8,128)(2,1)S(1)}, u32[]{:S(2)}, u32[]{:S(2)}) collective-permute-start(bf16[96,128]{1,0:T(8,128)(2,1)S(1)} %shard_map.89.mine_ref), channel_id=1, source_target_pairs={{0,4},{4,0},{1,5},{5,1},{2,6},{6,2},{3,7},{7,3},{8,12},{12,8},{9,1... | collective-permute-start | bytes 73736 | tf_op jit(solution)/shard_map/ppermute | solution.py:145
  34.5 2.1 %collective-permute-done.5.g1 = bf16[256,384]{1,0:T(8,128)(2,1)S(1)} collective-permute-done((bf16[256,384]{1,0:T(8,128)(2,1)S(1)}, bf16[256,384]{1,0:T(8,128)(2,1)S(1)}, u32[]{:S(2)}, u32[]{:S(2)}) %collective-permute-start.5) | collective-permute-done | bytes 196640 | tf_op jit(solution)/shard_map/ppermute | solution.py:518
  36.6 2.1 %shard_map.91.up_ref = bf16[256,384]{1,0:T(8,128)(2,1)S(1)} custom-call(bf16[256,384]{1,0:T(8,128)(2,1)S(1)} %copy-done.2, bf16[256,384]{1,0:T(8,128)(2,1)S(1)} %collective-permute-done.5.g1, bf16[256,384]{1,0:T(8,128)(2,1)S(1)} %collective-permute-done.6.g2, bf16[256,384]{1,0:T(8,128)(2,1)S(1)} %collective-permute-done.7.g3, bf16[384,1536]{1,0:T(8,128)(2,1)} %w_hbm.3, ...), custom_call_target="tpu_custom_call" | custom-call | flops 301989888 | bytes 3145728 | tf_op jit(solution)/shard_map/pallas_call | solution.py:271
  39.8 1.5 %collective-permute-start.8 = (bf16[192,128]{1,0:T(8,128)(2,1)S(1)}, bf16[192,128]{1,0:T(8,128)(2,1)S(1)}, u32[]{:S(2)}, u32[]{:S(2)}) collective-permute-start(bf16[192,128]{1,0:T(8,128)(2,1)S(1)} %get-tuple-element.42.state_ref), channel_id=1, source_target_pairs={{0,4},{4,0},{1,5},{5,1},{2,6},{6,2},{3,7},{7,3},{8,12},{12,8},{9,1... | collective-permute-start | bytes 147464 | tf_op jit(solution)/shard_map/ppermute | solution.py:145
  42.3 1.8 %collective-permute-start.10 = (bf16[96,128]{1,0:T(8,128)(2,1)S(1)}, bf16[96,128]{1,0:T(8,128)(2,1)S(1)}, u32[]{:S(2)}, u32[]{:S(2)}) collective-permute-start(bf16[96,128]{1,0:T(8,128)(2,1)S(1)} %shard_map.93.chip_ref), channel_id=1, source_target_pairs={{0,16},{8,24},{16,0},{24,8},{1,17},{9,25},{17,1},{25,9},{2,18},{10... | collective-permute-start | bytes 73736 | tf_op jit(solution)/shard_map/ppermute | solution.py:151
  44.0 1.8 %collective-permute-start.9 = (bf16[96,128]{1,0:T(8,128)(2,1)S(1)}, bf16[96,128]{1,0:T(8,128)(2,1)S(1)}, u32[]{:S(2)}, u32[]{:S(2)}) collective-permute-start(bf16[96,128]{1,0:T(8,128)(2,1)S(1)} %shard_map.93.chip_ref), channel_id=1, source_target_pairs={{0,24},{8,0},{16,8},{24,16},{1,25},{9,1},{17,9},{25,17},{2,26},{10... | collective-permute-start | bytes 73736 | tf_op jit(solution)/shard_map/ppermute | solution.py:151
  48.0 6.6 %all-to-all-start.1 = ((bf16[8,96,128]{2,1,0:T(8,128)(2,1)}), bf16[8,96,128]{2,1,0:T(8,128)(2,1)S(1)}, u32[]{:S(2)}, u32[]{:S(2)}) async-start(bf16[8,96,128]{2,1,0:T(8,128)(2,1)} %shard_map.95), calls=%async_computation.1 | async-start | bytes 393216 | tf_op jit(solution)/shard_map/all_to_all | solution.py:141
  54.6 2.9 %shard_map.94 = (bf16[256,384]{1,0:T(8,128)(2,1)}, bf16[256,384]{1,0:T(8,128)(2,1)}, bf16[256,384]{1,0:T(8,128)(2,1)}, bf16[256,384]{1,0:T(8,128)(2,1)}) custom-call(bf16[256,384]{1,0:T(8,128)(2,1)S(1)} %get-tuple-element.43.attn_ref, bf16[384,1536]{1,0:T(8,128)(2,1)} %w_hbm.3), custom_call_target="tpu_custom_call" | custom-call | flops 301989888 | bytes 2097152 | tf_op jit(solution)/shard_map/pallas_call | solution.py:348
  57.8 1.1 %collective-permute-start.13 = (bf16[256,384]{1,0:T(8,128)(2,1)}, bf16[256,384]{1,0:T(8,128)(2,1)S(1)}, u32[]{:S(2)}, u32[]{:S(2)}) collective-permute-start(bf16[256,384]{1,0:T(8,128)(2,1)} %get-tuple-element.48), channel_id=1, source_target_pairs={{0,1},{1,2},{2,3},{3,0},{4,5},{5,6},{6,7},{7,4},{8,9},{9,10},{10,1... | collective-permute-start | bytes 589832 | tf_op jit(solution)/shard_map/ppermute | solution.py:518
  59.5 3.7 %all-to-all-done.1.planes_ref = bf16[8,96,128]{2,1,0:T(8,128)(2,1)S(1)} async-done(((bf16[8,96,128]{2,1,0:T(8,128)(2,1)}), bf16[8,96,128]{2,1,0:T(8,128)(2,1)S(1)}, u32[]{:S(2)}, u32[]{:S(2)}) %all-to-all-start.1) | async-done | bytes 196640 | tf_op jit(solution)/shard_map/all_to_all | solution.py:141
  63.3 3.0 %collective-permute-start.15 = (bf16[96,128]{1,0:T(8,128)(2,1)S(1)}, bf16[96,128]{1,0:T(8,128)(2,1)S(1)}, u32[]{:S(2)}, u32[]{:S(2)}) collective-permute-start(bf16[96,128]{1,0:T(8,128)(2,1)S(1)} %shard_map.97.mine_ref), channel_id=1, source_target_pairs={{0,4},{4,0},{1,5},{5,1},{2,6},{6,2},{3,7},{7,3},{8,12},{12,8},{9,1... | collective-permute-start | bytes 73736 | tf_op jit(solution)/shard_map/ppermute | solution.py:145
  66.2 1.8 %shard_map.96 = (bf16[256,384]{1,0:T(8,128)(2,1)S(1)}, bf16[256,384]{1,0:T(8,128)(2,1)S(1)}, bf16[256,384]{1,0:T(8,128)(2,1)S(1)}) custom-call(bf16[256,384]{1,0:T(8,128)(2,1)S(1)} %copy-done.4, bf16[256,384]{1,0:T(8,128)(2,1)S(1)} %get-tuple-element.36.fk_ref, bf16[256,384]{1,0:T(8,128)(2,1)S(1)} %get-tuple-element.37.v_ref, ...), custom_call_target="tpu_custom_call" | custom-call | flops 603979776 | bytes 3145728 | tf_op jit(solution)/shard_map/pallas_call | solution.py:48
  68.0 1.2 %shard_map.98 = (bf16[384,384]{1,0:T(8,128)(2,1)S(1)}, bf16[384,384]{1,0:T(8,128)(2,1)S(1)}, bf16[384,384]{1,0:T(8,128)(2,1)S(1)}) custom-call(bf16[1536,384]{1,0:T(8,128)(2,1)} %wq_hbm.3, bf16[1536,384]{1,0:T(8,128)(2,1)} %wk_hbm.5, bf16[1536,384]{1,0:T(8,128)(2,1)} %wv_hbm.5), custom_call_target="tpu_custom_call" | custom-call | flops 1 | bytes 1048576 | tf_op jit(solution)/shard_map/pallas_call | solution.py:416
  70.0 2.5 %shard_map.101 = (bf16[256,384]{1,0:T(8,128)(2,1)S(1)}, bf16[256,384]{1,0:T(8,128)(2,1)S(1)}) custom-call(bf16[256,384]{1,0:T(8,128)(2,1)S(1)} %get-tuple-element.54.dq_ref, bf16[256,384]{1,0:T(8,128)(2,1)S(1)} %get-tuple-element.61.dk_ref, bf16[256,384]{1,0:T(8,128)(2,1)S(1)} %get-tuple-element.62.dv_ref, bf16[1536,384]{1,0:T(8,128)(2,1)} %wq_hbm.3, ...), custom_call_target="tpu_custom_call" | custom-call | flops 452984832 | bytes 2097152 | tf_op jit(solution)/shard_map/pallas_call | solution.py:496
  72.6 2.7 %collective-permute-start.18 = (bf16[256,384]{1,0:T(8,128)(2,1)S(1)}, bf16[256,384]{1,0:T(8,128)(2,1)S(1)}, u32[]{:S(2)}, u32[]{:S(2)}) collective-permute-start(bf16[256,384]{1,0:T(8,128)(2,1)S(1)} %get-tuple-element.65), channel_id=1, source_target_pairs={{0,3},{1,0},{2,1},{3,2},{4,7},{5,4},{6,5},{7,6},{8,11},{9,8},{10,9... | collective-permute-start | bytes 589832 | tf_op jit(solution)/shard_map/ppermute | solution.py:518
  76.1 1.7 %shard_map.100 = bf16[256,384]{1,0:T(8,128)(2,1)S(1)} custom-call(bf16[256,384]{1,0:T(8,128)(2,1)S(1)} %get-tuple-element.54.dq_ref, bf16[256,384]{1,0:T(8,128)(2,1)S(1)} %get-tuple-element.61.dk_ref, bf16[256,384]{1,0:T(8,128)(2,1)S(1)} %get-tuple-element.62.dv_ref, bf16[1536,384]{1,0:T(8,128)(2,1)} %wq_hbm.3, bf16[1536,384]{1,0:T(8,128)(2,1)} %wk_hbm.5, ...), custom_call_target="tpu_custom_call" | custom-call | flops 226492416 | bytes 1048576 | tf_op jit(solution)/shard_map/pallas_call | solution.py:496
  77.8 6.7 %collective-permute-done.17 = bf16[256,384]{1,0:T(8,128)(2,1)S(1)} collective-permute-done((bf16[256,384]{1,0:T(8,128)(2,1)S(1)}, bf16[256,384]{1,0:T(8,128)(2,1)S(1)}, u32[]{:S(2)}, u32[]{:S(2)}) %collective-permute-start.17) | collective-permute-done | bytes 196640 | tf_op jit(solution)/shard_map/ppermute | solution.py:518
  (55 shorter events, 14.7 us)
Async XLA Ops:
  0.6 25.5 %copy-start.8 = (f32[384]{0:T(512)S(1)}, f32[384]{0:T(512)}, u32[]{:S(2)}) copy-start(f32[384]{0:T(512)} %param.12) | copy-start | bytes 4612
  0.6 25.4 %copy-start = (bf16[1536,384]{1,0:T(8,128)(2,1)S(1)}, bf16[1536,384]{1,0:T(8,128)(2,1)}, u32[]{:S(2)}) copy-start(bf16[1536,384]{1,0:T(8,128)(2,1)} %wq_hbm.3) | copy-start | bytes 3538948
  3.8 22.3 %copy-start.1 = (bf16[256,1536]{1,0:T(8,128)(2,1)S(1)}, bf16[256,1536]{1,0:T(8,128)(2,1)}, u32[]{:S(2)}) copy-start(bf16[256,1536]{1,0:T(8,128)(2,1)} %x_ref) | copy-start | bytes 2359300
  3.8 4.2 %collective-permute-start = (bf16[192,128]{1,0:T(8,128)(2,1)S(1)}, bf16[192,128]{1,0:T(8,128)(2,1)S(1)}, u32[]{:S(2)}, u32[]{:S(2)}) collective-permute-start(bf16[192,128]{1,0:T(8,128)(2,1)S(1)} %get-tuple-element.34.state_ref), channel_id=1, source_target_pairs={{0,4},{4,0},{1,5},{5,1},{2,6},{6,2},{3,7},{7,3},{8,12},{12,8},{9,1... | collective-permute-start | bytes 147464 | tf_op jit(solution)/shard_map/ppermute | solution.py:145
  8.0 2.8 %collective-permute-start.3 = (bf16[96,128]{1,0:T(8,128)(2,1)S(1)}, bf16[96,128]{1,0:T(8,128)(2,1)S(1)}, u32[]{:S(2)}, u32[]{:S(2)}) collective-permute-start(bf16[96,128]{1,0:T(8,128)(2,1)S(1)} %shard_map.87.chip_ref), channel_id=1, source_target_pairs={{0,24},{8,0},{16,8},{24,16},{1,25},{9,1},{17,9},{25,17},{2,26},{10... | collective-permute-start | bytes 73736 | tf_op jit(solution)/shard_map/ppermute | solution.py:151
  9.1 4.2 %collective-permute-start.2 = (bf16[96,128]{1,0:T(8,128)(2,1)S(1)}, bf16[96,128]{1,0:T(8,128)(2,1)S(1)}, u32[]{:S(2)}, u32[]{:S(2)}) collective-permute-start(bf16[96,128]{1,0:T(8,128)(2,1)S(1)} %shard_map.87.chip_ref), channel_id=1, source_target_pairs={{0,16},{8,24},{16,0},{24,8},{1,17},{9,25},{17,1},{25,9},{2,18},{10... | collective-permute-start | bytes 73736 | tf_op jit(solution)/shard_map/ppermute | solution.py:151
  9.4 4.1 %collective-permute-start.1 = (bf16[96,128]{1,0:T(8,128)(2,1)S(1)}, bf16[96,128]{1,0:T(8,128)(2,1)S(1)}, u32[]{:S(2)}, u32[]{:S(2)}) collective-permute-start(bf16[96,128]{1,0:T(8,128)(2,1)S(1)} %shard_map.87.chip_ref), channel_id=1, source_target_pairs={{0,8},{8,16},{16,24},{24,0},{1,9},{9,17},{17,25},{25,1},{2,10},{10... | collective-permute-start | bytes 73736 | tf_op jit(solution)/shard_map/ppermute | solution.py:151
  14.2 16.9 %all-to-all-start = ((bf16[8,96,128]{2,1,0:T(8,128)(2,1)}), bf16[8,96,128]{2,1,0:T(8,128)(2,1)S(1)}, u32[]{:S(2)}, u32[]{:S(2)}) async-start(bf16[8,96,128]{2,1,0:T(8,128)(2,1)} %shard_map.88), calls=%async_computation | async-start | bytes 393216 | tf_op jit(solution)/shard_map/all_to_all | solution.py:141
  22.4 12.1 %collective-permute-start.7 = (bf16[256,384]{1,0:T(8,128)(2,1)S(1)}, bf16[256,384]{1,0:T(8,128)(2,1)S(1)}, u32[]{:S(2)}, u32[]{:S(2)}) collective-permute-start(bf16[256,384]{1,0:T(8,128)(2,1)S(1)} %copy-done.2), channel_id=1, source_target_pairs={{0,3},{1,0},{2,1},{3,2},{4,7},{5,4},{6,5},{7,6},{8,11},{9,8},{10,9... | collective-permute-start | bytes 589832 | tf_op jit(solution)/shard_map/ppermute | solution.py:518
  25.0 9.5 %collective-permute-start.6 = (bf16[256,384]{1,0:T(8,128)(2,1)S(1)}, bf16[256,384]{1,0:T(8,128)(2,1)S(1)}, u32[]{:S(2)}, u32[]{:S(2)}) collective-permute-start(bf16[256,384]{1,0:T(8,128)(2,1)S(1)} %copy-done.2), channel_id=1, source_target_pairs={{0,2},{1,3},{2,0},{3,1},{4,6},{5,7},{6,4},{7,5},{8,10},{9,11},{10,... | collective-permute-start | bytes 589832 | tf_op jit(solution)/shard_map/ppermute | solution.py:518
  25.5 11.1 %collective-permute-start.5 = (bf16[256,384]{1,0:T(8,128)(2,1)S(1)}, bf16[256,384]{1,0:T(8,128)(2,1)S(1)}, u32[]{:S(2)}, u32[]{:S(2)}) collective-permute-start(bf16[256,384]{1,0:T(8,128)(2,1)S(1)} %copy-done.2), channel_id=1, source_target_pairs={{0,1},{1,2},{2,3},{3,0},{4,5},{5,6},{6,7},{7,4},{8,9},{9,10},{10,1... | collective-permute-start | bytes 589832 | tf_op jit(solution)/shard_map/ppermute | solution.py:518
  31.2 7.6 %collective-permute-start.4 = (bf16[96,128]{1,0:T(8,128)(2,1)S(1)}, bf16[96,128]{1,0:T(8,128)(2,1)S(1)}, u32[]{:S(2)}, u32[]{:S(2)}) collective-permute-start(bf16[96,128]{1,0:T(8,128)(2,1)S(1)} %shard_map.89.mine_ref), channel_id=1, source_target_pairs={{0,4},{4,0},{1,5},{5,1},{2,6},{6,2},{3,7},{7,3},{8,12},{12,8},{9,1... | collective-permute-start | bytes 73736 | tf_op jit(solution)/shard_map/ppermute | solution.py:145
  39.8 2.4 %collective-permute-start.8 = (bf16[192,128]{1,0:T(8,128)(2,1)S(1)}, bf16[192,128]{1,0:T(8,128)(2,1)S(1)}, u32[]{:S(2)}, u32[]{:S(2)}) collective-permute-start(bf16[192,128]{1,0:T(8,128)(2,1)S(1)} %get-tuple-element.42.state_ref), channel_id=1, source_target_pairs={{0,4},{4,0},{1,5},{5,1},{2,6},{6,2},{3,7},{7,3},{8,12},{12,8},{9,1... | collective-permute-start | bytes 147464 | tf_op jit(solution)/shard_map/ppermute | solution.py:145
  42.2 4.0 %collective-permute-start.11 = (bf16[96,128]{1,0:T(8,128)(2,1)S(1)}, bf16[96,128]{1,0:T(8,128)(2,1)S(1)}, u32[]{:S(2)}, u32[]{:S(2)}) collective-permute-start(bf16[96,128]{1,0:T(8,128)(2,1)S(1)} %shard_map.93.chip_ref), channel_id=1, source_target_pairs={{0,8},{8,16},{16,24},{24,0},{1,9},{9,17},{17,25},{25,1},{2,10},{10... | collective-permute-start | bytes 73736 | tf_op jit(solution)/shard_map/ppermute | solution.py:151
  42.3 4.3 %collective-permute-start.10 = (bf16[96,128]{1,0:T(8,128)(2,1)S(1)}, bf16[96,128]{1,0:T(8,128)(2,1)S(1)}, u32[]{:S(2)}, u32[]{:S(2)}) collective-permute-start(bf16[96,128]{1,0:T(8,128)(2,1)S(1)} %shard_map.93.chip_ref), channel_id=1, source_target_pairs={{0,16},{8,24},{16,0},{24,8},{1,17},{9,25},{17,1},{25,9},{2,18},{10... | collective-permute-start | bytes 73736 | tf_op jit(solution)/shard_map/ppermute | solution.py:151
  44.0 3.3 %collective-permute-start.9 = (bf16[96,128]{1,0:T(8,128)(2,1)S(1)}, bf16[96,128]{1,0:T(8,128)(2,1)S(1)}, u32[]{:S(2)}, u32[]{:S(2)}) collective-permute-start(bf16[96,128]{1,0:T(8,128)(2,1)S(1)} %shard_map.93.chip_ref), channel_id=1, source_target_pairs={{0,24},{8,0},{16,8},{24,16},{1,25},{9,1},{17,9},{25,17},{2,26},{10... | collective-permute-start | bytes 73736 | tf_op jit(solution)/shard_map/ppermute | solution.py:151
  48.0 15.2 %all-to-all-start.1 = ((bf16[8,96,128]{2,1,0:T(8,128)(2,1)}), bf16[8,96,128]{2,1,0:T(8,128)(2,1)S(1)}, u32[]{:S(2)}, u32[]{:S(2)}) async-start(bf16[8,96,128]{2,1,0:T(8,128)(2,1)} %shard_map.95), calls=%async_computation.1 | async-start | bytes 393216 | tf_op jit(solution)/shard_map/all_to_all | solution.py:141
  57.4 17.9 %collective-permute-start.14 = (bf16[256,384]{1,0:T(8,128)(2,1)}, bf16[256,384]{1,0:T(8,128)(2,1)S(1)}, u32[]{:S(2)}, u32[]{:S(2)}) collective-permute-start(bf16[256,384]{1,0:T(8,128)(2,1)} %get-tuple-element.50), channel_id=1, source_target_pairs={{0,3},{1,0},{2,1},{3,2},{4,7},{5,4},{6,5},{7,6},{8,11},{9,8},{10,9... | collective-permute-start | bytes 589832 | tf_op jit(solution)/shard_map/ppermute | solution.py:518
  57.8 17.5 %collective-permute-start.13 = (bf16[256,384]{1,0:T(8,128)(2,1)}, bf16[256,384]{1,0:T(8,128)(2,1)S(1)}, u32[]{:S(2)}, u32[]{:S(2)}) collective-permute-start(bf16[256,384]{1,0:T(8,128)(2,1)} %get-tuple-element.48), channel_id=1, source_target_pairs={{0,1},{1,2},{2,3},{3,0},{4,5},{5,6},{6,7},{7,4},{8,9},{9,10},{10,1... | collective-permute-start | bytes 589832 | tf_op jit(solution)/shard_map/ppermute | solution.py:518
  59.0 16.3 %collective-permute-start.12 = (bf16[256,384]{1,0:T(8,128)(2,1)}, bf16[256,384]{1,0:T(8,128)(2,1)S(1)}, u32[]{:S(2)}, u32[]{:S(2)}) collective-permute-start(bf16[256,384]{1,0:T(8,128)(2,1)} %get-tuple-element.46), channel_id=1, source_target_pairs={{0,2},{1,3},{2,0},{3,1},{4,6},{5,7},{6,4},{7,5},{8,10},{9,11},{10,... | collective-permute-start | bytes 589832 | tf_op jit(solution)/shard_map/ppermute | solution.py:518
  63.3 5.9 %collective-permute-start.15 = (bf16[96,128]{1,0:T(8,128)(2,1)S(1)}, bf16[96,128]{1,0:T(8,128)(2,1)S(1)}, u32[]{:S(2)}, u32[]{:S(2)}) collective-permute-start(bf16[96,128]{1,0:T(8,128)(2,1)S(1)} %shard_map.97.mine_ref), channel_id=1, source_target_pairs={{0,4},{4,0},{1,5},{5,1},{2,6},{6,2},{3,7},{7,3},{8,12},{12,8},{9,1... | collective-permute-start | bytes 73736 | tf_op jit(solution)/shard_map/ppermute | solution.py:145
  72.5 11.9 %collective-permute-start.17 = (bf16[256,384]{1,0:T(8,128)(2,1)S(1)}, bf16[256,384]{1,0:T(8,128)(2,1)S(1)}, u32[]{:S(2)}, u32[]{:S(2)}) collective-permute-start(bf16[256,384]{1,0:T(8,128)(2,1)S(1)} %get-tuple-element.64), channel_id=1, source_target_pairs={{0,1},{1,2},{2,3},{3,0},{4,5},{5,6},{6,7},{7,4},{8,9},{9,10},{10,1... | collective-permute-start | bytes 589832 | tf_op jit(solution)/shard_map/ppermute | solution.py:518
  72.6 11.9 %collective-permute-start.18 = (bf16[256,384]{1,0:T(8,128)(2,1)S(1)}, bf16[256,384]{1,0:T(8,128)(2,1)S(1)}, u32[]{:S(2)}, u32[]{:S(2)}) collective-permute-start(bf16[256,384]{1,0:T(8,128)(2,1)S(1)} %get-tuple-element.65), channel_id=1, source_target_pairs={{0,3},{1,0},{2,1},{3,2},{4,7},{5,4},{6,5},{7,6},{8,11},{9,8},{10,9... | collective-permute-start | bytes 589832 | tf_op jit(solution)/shard_map/ppermute | solution.py:518
  75.3 9.2 %collective-permute-start.16 = (bf16[256,384]{1,0:T(8,128)(2,1)S(1)}, bf16[256,384]{1,0:T(8,128)(2,1)S(1)}, u32[]{:S(2)}, u32[]{:S(2)}) collective-permute-start(bf16[256,384]{1,0:T(8,128)(2,1)S(1)} %get-tuple-element.63), channel_id=1, source_target_pairs={{0,2},{1,3},{2,0},{3,1},{4,6},{5,7},{6,4},{7,5},{8,10},{9,11},{10,... | collective-permute-start | bytes 589832 | tf_op jit(solution)/shard_map/ppermute | solution.py:518
  (6 other events, 43.8 us)

commit v5 on v4

--- a/solution.py
+++ b/solution.py
@@ -223,9 +223,22 @@
 
 def query_local(latents, w_query, fk, v):
     rows, width = fk.shape
-
-    def body(x_ref, wq_ref, fk_ref, v_ref, fq_ref, raw_ref):
-        fq_ref[...] = feature_map(mm(x_ref[...], wq_ref[...])).astype(bf16)
+    steps = 2
+    depth = latents.shape[1] // steps
+
+    def body(x_hbm, wq_ref, fk_ref, v_ref, fq_ref, raw_ref, x_ref, sem):
+        spans = [pl.ds(i * depth, depth) for i in range(steps)]
+        copies = [
+            pltpu.make_async_copy(x_hbm.at[:, span], x_ref.at[:, span], sem.at[i])
+            for i, span in enumerate(spans)
+        ]
+        for copy in copies:
+            copy.start()
+        total = jnp.zeros((rows, width), f32)
+        for copy, span in zip(copies, spans):
+            copy.wait()
+            total = total + mm(x_ref[:, span], wq_ref[span, :])
+        fq_ref[...] = feature_map(total).astype(bf16)
         keep = tri(rows, False)
         for p in range(width // LANES):
             cols = slice(p * LANES, (p + 1) * LANES)
@@ -237,16 +250,15 @@
                 total = part if total is None else total + part
             raw_ref[:, cols] = total.astype(bf16)
 
-    return plain(
+    return call(
         body,
         [((rows, width), bf16)] * 2,
         2 * rows * width * (latents.shape[1] + 4 * rows),
         3 * 1024 * 1024,
-        latents,
-        w_query,
-        fk,
-        v,
-    )
+        in_specs=[pl.BlockSpec(memory_space=pltpu.HBM)] + [VMEM] * 3,
+        out_specs=[VMEM] * 2,
+        scratch_shapes=[pltpu.VMEM(latents.shape, bf16), pltpu.SemaphoreType.DMA((steps,))],
+    )(in_hbm(latents), w_query, fk, v)
 
 
 def upstream_of(grads, w_out, gain):
@@ -333,27 +345,18 @@
 def branch_parts(attn, w_out):
     rows, width = attn.shape
 
-    def body(attn_ref, w_hbm, *refs):
-        outs, w_ref, sem = (refs[:4], refs[4], refs[5])
-        copies = []
-        for i, k in enumerate((2, 1, 3, 0)):
-            source = w_hbm.at[:, block_rows(k, width)]
-            copies.append(pltpu.make_async_copy(source, w_ref.at[i], sem.at[i]))
-        for copy in copies:
-            copy.start()
-        for i, ref in enumerate(outs):
-            copies[i].wait()
-            ref[...] = mm(attn_ref[...], w_ref[i]).astype(bf16)
-
-    return call(
+    def body(attn_ref, w_ref, *outs):
+        for k, ref in zip((2, 1, 3, 0), outs):
+            ref[...] = mm(attn_ref[...], w_ref[:, block_rows(k, width)]).astype(bf16)
+
+    return plain(
         body,
         [((rows, width), bf16, pltpu.HBM)] * 4,
         8 * rows * width * width,
         2 * 1024 * 1024,
-        in_specs=[VMEM, pl.BlockSpec(memory_space=pltpu.HBM)],
-        out_specs=[VMEM] * 4,
-        scratch_shapes=[pltpu.VMEM((4, width, width), bf16), pltpu.SemaphoreType.DMA((4,))],
-    )(attn, in_hbm(w_out))
+        attn,
+        w_out,
+    )
 
 
 def local_grads(fq, fk, v, draw, before):
@@ -537,6 +540,8 @@
     mine = before_chip(False, planes)
     got = swap(mine)
     attn, draw, before, state = normed(mine, got, pair, fq, raw_local, up, gain)
+    weights = (w_query, w_key, w_value)
+    blocks = weight_blocks(2, (hold(w_query, state), w_key, w_value))
     pair = swap(state)
     chip = pair_sum(state, pair)
     got = y_gather(True, chip)
@@ -545,8 +550,6 @@
     b2, b1, b3 = (hold(b, planes) for b in (b2, b1, b3))
     branch = [b0, to_owner(b2, 2), to_owner(b1, 1), to_owner(b3, 3)]
     dq, dk_local, dv_local = local_grads(fq, fk, v, hold(draw, planes), before)
-    weights = (w_query, w_key, w_value)
-    blocks = weight_blocks(2, (hold(w_query, dq), w_key, w_value))
     planes = plane_exchange(planes)
     mine = before_chip(True, planes)
     got = swap(mine)

time: 85.6 us -> 84.4 us (0.986)
  local copies, waits for them, and re-layouts: 1.37 us -> 0.03 us
    unnamed x18 -> x10, local copies, waits for them, and re-layouts: 1.37 us -> 0.03 us
where the time goes in v5:
time: 84.4 us; the launch traced here: 84 us
  starting transfers between devices  40 us (47%)
  waiting for transfers between devices  22.2 us (26%)
  Pallas kernels  19.4 us (23%)
  other arithmetic  1.56 us (2%)
    all_to_all x2, starting transfers between devices, plane_exchange(): return lax.all_to_all(planes, 'seq_0', 0, 0, tiled=True)  14.8 us
    ppermute x4, starting transfers between devices, swap(): return lax.ppermute(x, 'seq_2', SWAP)  11.1 us
    ppermute x9, waiting for transfers between devices, to_owner(): return lax.ppermute(part, 'mp', shifts(4, k))  8.82 us
    ppermute x9, starting transfers between devices, to_owner(): return lax.ppermute(part, 'mp', shifts(4, k))  8.4 us
    all_to_all x2, waiting for transfers between devices, plane_exchange(): return lax.all_to_all(planes, 'seq_0', 0, 0, tiled=True)  6.71 us
    ppermute x6, starting transfers between devices, y_gather(): got.append(lax.ppermute(chip, 'seq_1', shifts(4, -k if later else k)))  5.75 us
    ppermute x6, waiting for transfers between devices, y_gather(): got.append(lax.ppermute(chip, 'seq_1', shifts(4, -k if later else k)))  4.88 us
    pallas_call x8, Pallas kernels, plain(): call(body, outs, flops, moved, in_specs=[VMEM] * len(args), out_specs=[VM...  4.63 us
  transfers between devices with their start and end apart: 21, of which 12 were waited for; matrix products, arithmetic and copies ran while one was open for 1% of the time, Pallas kernels for 17%

profile of v5, /device:TPU:1, one launch (start us, length us, event | category | flops | bytes accessed | tf_op | source)
XLA Modules:
  0.0 84.0 jit_solution(8621116057069968203)
XLA Ops:
  0.7 3.1 %shard_map.86 = (bf16[256,384]{1,0:T(8,128)(2,1)S(1)}, bf16[256,384]{1,0:T(8,128)(2,1)S(1)}, bf16[192,128]{1,0:T(8,128)(2,1)S(1)}) custom-call(bf16[256,1536]{1,0:T(8,128)(2,1)} %x_hbm.2, bf16[1536,384]{1,0:T(8,128)(2,1)} %wk_hbm.5, bf16[1536,384]{1,0:T(8,128)(2,1)} %wv_hbm.5), custom_call_target="tpu_custom_call" | custom-call | flops 603979776 | bytes 3145728 | tf_op jit(solution)/shard_map/pallas_call | solution.py:195
  3.8 3.3 %collective-permute-start = (bf16[192,128]{1,0:T(8,128)(2,1)S(1)}, bf16[192,128]{1,0:T(8,128)(2,1)S(1)}, u32[]{:S(2)}, u32[]{:S(2)}) collective-permute-start(bf16[192,128]{1,0:T(8,128)(2,1)S(1)} %get-tuple-element.34.state_ref), channel_id=1, source_target_pairs={{0,4},{4,0},{1,5},{5,1},{2,6},{6,2},{3,7},{7,3},{8,12},{12,8},{9,1... | collective-permute-start | bytes 147464 | tf_op jit(solution)/shard_map/ppermute | solution.py:145
  10.7 2.5 %collective-permute-done.2.g2 = bf16[96,128]{1,0:T(8,128)(2,1)S(1)} collective-permute-done((bf16[96,128]{1,0:T(8,128)(2,1)S(1)}, bf16[96,128]{1,0:T(8,128)(2,1)S(1)}, u32[]{:S(2)}, u32[]{:S(2)}) %collective-permute-start.2) | collective-permute-done | bytes 24608 | tf_op jit(solution)/shard_map/ppermute | solution.py:151
  14.2 8.2 %all-to-all-start = ((bf16[8,96,128]{2,1,0:T(8,128)(2,1)}), bf16[8,96,128]{2,1,0:T(8,128)(2,1)S(1)}, u32[]{:S(2)}, u32[]{:S(2)}) async-start(bf16[8,96,128]{2,1,0:T(8,128)(2,1)} %shard_map.88), calls=%async_computation | async-start | bytes 393216 | tf_op jit(solution)/shard_map/all_to_all | solution.py:141
  22.4 2.6 %collective-permute-start.7 = (bf16[256,384]{1,0:T(8,128)(2,1)S(1)}, bf16[256,384]{1,0:T(8,128)(2,1)S(1)}, u32[]{:S(2)}, u32[]{:S(2)}) collective-permute-start(bf16[256,384]{1,0:T(8,128)(2,1)S(1)} %copy-done.2), channel_id=1, source_target_pairs={{0,3},{1,0},{2,1},{3,2},{4,7},{5,4},{6,5},{7,6},{8,11},{9,8},{10,9... | collective-permute-start | bytes 589832 | tf_op jit(solution)/shard_map/ppermute | solution.py:521
  26.1 2.5 %shard_map.90 = (bf16[256,384]{1,0:T(8,128)(2,1)S(1)}, bf16[256,384]{1,0:T(8,128)(2,1)S(1)}) custom-call(bf16[256,1536]{1,0:T(8,128)(2,1)} %x_hbm.2, bf16[1536,384]{1,0:T(8,128)(2,1)S(1)} %copy-done, bf16[256,384]{1,0:T(8,128)(2,1)S(1)} %get-tuple-element.36.fk_ref, bf16[256,384]{1,0:T(8,128)(2,1)S(1)} %get-tuple-element.37.v_ref), custom_call_target="tpu_custom_call" | custom-call | flops 503316480 | bytes 3145728 | tf_op jit(solution)/shard_map/pallas_call | solution.py:253
  28.5 2.5 %all-to-all-done.planes_ref = bf16[8,96,128]{2,1,0:T(8,128)(2,1)S(1)} async-done(((bf16[8,96,128]{2,1,0:T(8,128)(2,1)}), bf16[8,96,128]{2,1,0:T(8,128)(2,1)S(1)}, u32[]{:S(2)}, u32[]{:S(2)}) %all-to-all-start) | async-done | bytes 196640 | tf_op jit(solution)/shard_map/all_to_all | solution.py:141
  31.1 3.3 %collective-permute-start.4 = (bf16[96,128]{1,0:T(8,128)(2,1)S(1)}, bf16[96,128]{1,0:T(8,128)(2,1)S(1)}, u32[]{:S(2)}, u32[]{:S(2)}) collective-permute-start(bf16[96,128]{1,0:T(8,128)(2,1)S(1)} %shard_map.89.mine_ref), channel_id=1, source_target_pairs={{0,4},{4,0},{1,5},{5,1},{2,6},{6,2},{3,7},{7,3},{8,12},{12,8},{9,1... | collective-permute-start | bytes 73736 | tf_op jit(solution)/shard_map/ppermute | solution.py:145
  34.5 2.1 %collective-permute-done.5.g1 = bf16[256,384]{1,0:T(8,128)(2,1)S(1)} collective-permute-done((bf16[256,384]{1,0:T(8,128)(2,1)S(1)}, bf16[256,384]{1,0:T(8,128)(2,1)S(1)}, u32[]{:S(2)}, u32[]{:S(2)}) %collective-permute-start.5) | collective-permute-done | bytes 196640 | tf_op jit(solution)/shard_map/ppermute | solution.py:521
  36.6 2.1 %shard_map.91.up_ref = bf16[256,384]{1,0:T(8,128)(2,1)S(1)} custom-call(bf16[256,384]{1,0:T(8,128)(2,1)S(1)} %copy-done.2, bf16[256,384]{1,0:T(8,128)(2,1)S(1)} %collective-permute-done.5.g1, bf16[256,384]{1,0:T(8,128)(2,1)S(1)} %collective-permute-done.6.g2, bf16[256,384]{1,0:T(8,128)(2,1)S(1)} %collective-permute-done.7.g3, bf16[384,1536]{1,0:T(8,128)(2,1)} %w_ref.1, ...), custom_call_target="tpu_custom_call" | custom-call | flops 301989888 | bytes 3145728 | tf_op jit(solution)/shard_map/pallas_call | solution.py:283
  39.8 1.5 %collective-permute-start.8 = (bf16[192,128]{1,0:T(8,128)(2,1)S(1)}, bf16[192,128]{1,0:T(8,128)(2,1)S(1)}, u32[]{:S(2)}, u32[]{:S(2)}) collective-permute-start(bf16[192,128]{1,0:T(8,128)(2,1)S(1)} %get-tuple-element.42.state_ref), channel_id=1, source_target_pairs={{0,4},{4,0},{1,5},{5,1},{2,6},{6,2},{3,7},{7,3},{8,12},{12,8},{9,1... | collective-permute-start | bytes 147464 | tf_op jit(solution)/shard_map/ppermute | solution.py:145
  42.3 1.7 %collective-permute-start.10 = (bf16[96,128]{1,0:T(8,128)(2,1)S(1)}, bf16[96,128]{1,0:T(8,128)(2,1)S(1)}, u32[]{:S(2)}, u32[]{:S(2)}) collective-permute-start(bf16[96,128]{1,0:T(8,128)(2,1)S(1)} %shard_map.93.chip_ref), channel_id=1, source_target_pairs={{0,16},{8,24},{16,0},{24,8},{1,17},{9,25},{17,1},{25,9},{2,18},{10... | collective-permute-start | bytes 73736 | tf_op jit(solution)/shard_map/ppermute | solution.py:151
  44.0 1.8 %collective-permute-start.9 = (bf16[96,128]{1,0:T(8,128)(2,1)S(1)}, bf16[96,128]{1,0:T(8,128)(2,1)S(1)}, u32[]{:S(2)}, u32[]{:S(2)}) collective-permute-start(bf16[96,128]{1,0:T(8,128)(2,1)S(1)} %shard_map.93.chip_ref), channel_id=1, source_target_pairs={{0,24},{8,0},{16,8},{24,16},{1,25},{9,1},{17,9},{25,17},{2,26},{10... | collective-permute-start | bytes 73736 | tf_op jit(solution)/shard_map/ppermute | solution.py:151
  48.0 6.6 %all-to-all-start.1 = ((bf16[8,96,128]{2,1,0:T(8,128)(2,1)}), bf16[8,96,128]{2,1,0:T(8,128)(2,1)S(1)}, u32[]{:S(2)}, u32[]{:S(2)}) async-start(bf16[8,96,128]{2,1,0:T(8,128)(2,1)} %shard_map.95), calls=%async_computation.1 | async-start | bytes 393216 | tf_op jit(solution)/shard_map/all_to_all | solution.py:141
  54.5 1.3 %shard_map.94 = (bf16[256,384]{1,0:T(8,128)(2,1)}, bf16[256,384]{1,0:T(8,128)(2,1)}, bf16[256,384]{1,0:T(8,128)(2,1)}, bf16[256,384]{1,0:T(8,128)(2,1)}) custom-call(bf16[256,384]{1,0:T(8,128)(2,1)S(1)} %get-tuple-element.43.attn_ref, bf16[384,1536]{1,0:T(8,128)(2,1)S(1)} %copy-done.1), custom_call_target="tpu_custom_call" | custom-call | flops 301989888 | bytes 2097152 | tf_op jit(solution)/shard_map/pallas_call | solution.py:48
  56.2 1.1 %collective-permute-start.13 = (bf16[256,384]{1,0:T(8,128)(2,1)}, bf16[256,384]{1,0:T(8,128)(2,1)S(1)}, u32[]{:S(2)}, u32[]{:S(2)}) collective-permute-start(bf16[256,384]{1,0:T(8,128)(2,1)} %get-tuple-element.48), channel_id=1, source_target_pairs={{0,1},{1,2},{2,3},{3,0},{4,5},{5,6},{6,7},{7,4},{8,9},{9,10},{10,1... | collective-permute-start | bytes 589832 | tf_op jit(solution)/shard_map/ppermute | solution.py:521
  57.8 1.2 %shard_map.98 = (bf16[384,384]{1,0:T(8,128)(2,1)S(1)}, bf16[384,384]{1,0:T(8,128)(2,1)S(1)}, bf16[384,384]{1,0:T(8,128)(2,1)S(1)}) custom-call(bf16[1536,384]{1,0:T(8,128)(2,1)} %wq_hbm.3, bf16[1536,384]{1,0:T(8,128)(2,1)} %wk_hbm.5, bf16[1536,384]{1,0:T(8,128)(2,1)} %wv_hbm.5), custom_call_target="tpu_custom_call" | custom-call | flops 1 | bytes 1048576 | tf_op jit(solution)/shard_map/pallas_call | solution.py:419
  59.0 4.2 %all-to-all-done.1.planes_ref = bf16[8,96,128]{2,1,0:T(8,128)(2,1)S(1)} async-done(((bf16[8,96,128]{2,1,0:T(8,128)(2,1)}), bf16[8,96,128]{2,1,0:T(8,128)(2,1)S(1)}, u32[]{:S(2)}, u32[]{:S(2)}) %all-to-all-start.1) | async-done | bytes 196640 | tf_op jit(solution)/shard_map/all_to_all | solution.py:141
  63.2 3.0 %collective-permute-start.15 = (bf16[96,128]{1,0:T(8,128)(2,1)S(1)}, bf16[96,128]{1,0:T(8,128)(2,1)S(1)}, u32[]{:S(2)}, u32[]{:S(2)}) collective-permute-start(bf16[96,128]{1,0:T(8,128)(2,1)S(1)} %shard_map.97.mine_ref), channel_id=1, source_target_pairs={{0,4},{4,0},{1,5},{5,1},{2,6},{6,2},{3,7},{7,3},{8,12},{12,8},{9,1... | collective-permute-start | bytes 73736 | tf_op jit(solution)/shard_map/ppermute | solution.py:145
  66.2 1.8 %shard_map.96 = (bf16[256,384]{1,0:T(8,128)(2,1)S(1)}, bf16[256,384]{1,0:T(8,128)(2,1)S(1)}, bf16[256,384]{1,0:T(8,128)(2,1)S(1)}) custom-call(bf16[256,384]{1,0:T(8,128)(2,1)S(1)} %get-tuple-element.38.fq_ref, bf16[256,384]{1,0:T(8,128)(2,1)S(1)} %get-tuple-element.36.fk_ref, bf16[256,384]{1,0:T(8,128)(2,1)S(1)} %get-tuple-element.37.v_ref, ...), custom_call_target="tpu_custom_call" | custom-call | flops 603979776 | bytes 3145728 | tf_op jit(solution)/shard_map/pallas_call | solution.py:48
  68.8 2.5 %shard_map.101 = (bf16[256,384]{1,0:T(8,128)(2,1)S(1)}, bf16[256,384]{1,0:T(8,128)(2,1)S(1)}) custom-call(bf16[256,384]{1,0:T(8,128)(2,1)S(1)} %get-tuple-element.54.dq_ref, bf16[256,384]{1,0:T(8,128)(2,1)S(1)} %get-tuple-element.61.dk_ref, bf16[256,384]{1,0:T(8,128)(2,1)S(1)} %get-tuple-element.62.dv_ref, bf16[1536,384]{1,0:T(8,128)(2,1)} %wq_hbm.3, ...), custom_call_target="tpu_custom_call" | custom-call | flops 452984832 | bytes 2097152 | tf_op jit(solution)/shard_map/pallas_call | solution.py:499
  71.4 2.7 %collective-permute-start.18 = (bf16[256,384]{1,0:T(8,128)(2,1)S(1)}, bf16[256,384]{1,0:T(8,128)(2,1)S(1)}, u32[]{:S(2)}, u32[]{:S(2)}) collective-permute-start(bf16[256,384]{1,0:T(8,128)(2,1)S(1)} %get-tuple-element.65), channel_id=1, source_target_pairs={{0,3},{1,0},{2,1},{3,2},{4,7},{5,4},{6,5},{7,6},{8,11},{9,8},{10,9... | collective-permute-start | bytes 589832 | tf_op jit(solution)/shard_map/ppermute | solution.py:521
  74.9 1.7 %shard_map.100 = bf16[256,384]{1,0:T(8,128)(2,1)S(1)} custom-call(bf16[256,384]{1,0:T(8,128)(2,1)S(1)} %get-tuple-element.54.dq_ref, bf16[256,384]{1,0:T(8,128)(2,1)S(1)} %get-tuple-element.61.dk_ref, bf16[256,384]{1,0:T(8,128)(2,1)S(1)} %get-tuple-element.62.dv_ref, bf16[1536,384]{1,0:T(8,128)(2,1)} %wq_hbm.3, bf16[1536,384]{1,0:T(8,128)(2,1)} %wk_hbm.5, ...), custom_call_target="tpu_custom_call" | custom-call | flops 226492416 | bytes 1048576 | tf_op jit(solution)/shard_map/pallas_call | solution.py:499
  76.6 6.7 %collective-permute-done.17 = bf16[256,384]{1,0:T(8,128)(2,1)S(1)} collective-permute-done((bf16[256,384]{1,0:T(8,128)(2,1)S(1)}, bf16[256,384]{1,0:T(8,128)(2,1)S(1)}, u32[]{:S(2)}, u32[]{:S(2)}) %collective-permute-start.17) | collective-permute-done | bytes 196640 | tf_op jit(solution)/shard_map/ppermute | solution.py:521
  (47 shorter events, 13.2 us)
Async XLA Ops:
  0.6 21.8 %copy-start.2 = (bf16[256,384]{1,0:T(8,128)(2,1)S(1)}, bf16[256,384]{1,0:T(8,128)(2,1)}, u32[]{:S(2)}) copy-start(bf16[256,384]{1,0:T(8,128)(2,1)} %g0.1) | copy-start | bytes 589828
  0.6 25.4 %copy-start.4 = (f32[384]{0:T(512)S(1)}, f32[384]{0:T(512)}, u32[]{:S(2)}) copy-start(f32[384]{0:T(512)} %param.12) | copy-start | bytes 4612
  0.6 25.4 %copy-start = (bf16[1536,384]{1,0:T(8,128)(2,1)S(1)}, bf16[1536,384]{1,0:T(8,128)(2,1)}, u32[]{:S(2)}) copy-start(bf16[1536,384]{1,0:T(8,128)(2,1)} %wq_hbm.3) | copy-start | bytes 3538948
  3.8 4.2 %collective-permute-start = (bf16[192,128]{1,0:T(8,128)(2,1)S(1)}, bf16[192,128]{1,0:T(8,128)(2,1)S(1)}, u32[]{:S(2)}, u32[]{:S(2)}) collective-permute-start(bf16[192,128]{1,0:T(8,128)(2,1)S(1)} %get-tuple-element.34.state_ref), channel_id=1, source_target_pairs={{0,4},{4,0},{1,5},{5,1},{2,6},{6,2},{3,7},{7,3},{8,12},{12,8},{9,1... | collective-permute-start | bytes 147464 | tf_op jit(solution)/shard_map/ppermute | solution.py:145
  8.0 2.8 %collective-permute-start.3 = (bf16[96,128]{1,0:T(8,128)(2,1)S(1)}, bf16[96,128]{1,0:T(8,128)(2,1)S(1)}, u32[]{:S(2)}, u32[]{:S(2)}) collective-permute-start(bf16[96,128]{1,0:T(8,128)(2,1)S(1)} %shard_map.87.chip_ref), channel_id=1, source_target_pairs={{0,24},{8,0},{16,8},{24,16},{1,25},{9,1},{17,9},{25,17},{2,26},{10... | collective-permute-start | bytes 73736 | tf_op jit(solution)/shard_map/ppermute | solution.py:151
  9.1 4.2 %collective-permute-start.2 = (bf16[96,128]{1,0:T(8,128)(2,1)S(1)}, bf16[96,128]{1,0:T(8,128)(2,1)S(1)}, u32[]{:S(2)}, u32[]{:S(2)}) collective-permute-start(bf16[96,128]{1,0:T(8,128)(2,1)S(1)} %shard_map.87.chip_ref), channel_id=1, source_target_pairs={{0,16},{8,24},{16,0},{24,8},{1,17},{9,25},{17,1},{25,9},{2,18},{10... | collective-permute-start | bytes 73736 | tf_op jit(solution)/shard_map/ppermute | solution.py:151
  9.4 4.1 %collective-permute-start.1 = (bf16[96,128]{1,0:T(8,128)(2,1)S(1)}, bf16[96,128]{1,0:T(8,128)(2,1)S(1)}, u32[]{:S(2)}, u32[]{:S(2)}) collective-permute-start(bf16[96,128]{1,0:T(8,128)(2,1)S(1)} %shard_map.87.chip_ref), channel_id=1, source_target_pairs={{0,8},{8,16},{16,24},{24,0},{1,9},{9,17},{17,25},{25,1},{2,10},{10... | collective-permute-start | bytes 73736 | tf_op jit(solution)/shard_map/ppermute | solution.py:151
  14.2 16.9 %all-to-all-start = ((bf16[8,96,128]{2,1,0:T(8,128)(2,1)}), bf16[8,96,128]{2,1,0:T(8,128)(2,1)S(1)}, u32[]{:S(2)}, u32[]{:S(2)}) async-start(bf16[8,96,128]{2,1,0:T(8,128)(2,1)} %shard_map.88), calls=%async_computation | async-start | bytes 393216 | tf_op jit(solution)/shard_map/all_to_all | solution.py:141
  22.4 12.1 %collective-permute-start.7 = (bf16[256,384]{1,0:T(8,128)(2,1)S(1)}, bf16[256,384]{1,0:T(8,128)(2,1)S(1)}, u32[]{:S(2)}, u32[]{:S(2)}) collective-permute-start(bf16[256,384]{1,0:T(8,128)(2,1)S(1)} %copy-done.2), channel_id=1, source_target_pairs={{0,3},{1,0},{2,1},{3,2},{4,7},{5,4},{6,5},{7,6},{8,11},{9,8},{10,9... | collective-permute-start | bytes 589832 | tf_op jit(solution)/shard_map/ppermute | solution.py:521
  25.0 9.5 %collective-permute-start.6 = (bf16[256,384]{1,0:T(8,128)(2,1)S(1)}, bf16[256,384]{1,0:T(8,128)(2,1)S(1)}, u32[]{:S(2)}, u32[]{:S(2)}) collective-permute-start(bf16[256,384]{1,0:T(8,128)(2,1)S(1)} %copy-done.2), channel_id=1, source_target_pairs={{0,2},{1,3},{2,0},{3,1},{4,6},{5,7},{6,4},{7,5},{8,10},{9,11},{10,... | collective-permute-start | bytes 589832 | tf_op jit(solution)/shard_map/ppermute | solution.py:521
  25.5 11.1 %collective-permute-start.5 = (bf16[256,384]{1,0:T(8,128)(2,1)S(1)}, bf16[256,384]{1,0:T(8,128)(2,1)S(1)}, u32[]{:S(2)}, u32[]{:S(2)}) collective-permute-start(bf16[256,384]{1,0:T(8,128)(2,1)S(1)} %copy-done.2), channel_id=1, source_target_pairs={{0,1},{1,2},{2,3},{3,0},{4,5},{5,6},{6,7},{7,4},{8,9},{9,10},{10,1... | collective-permute-start | bytes 589832 | tf_op jit(solution)/shard_map/ppermute | solution.py:521
  31.1 7.6 %collective-permute-start.4 = (bf16[96,128]{1,0:T(8,128)(2,1)S(1)}, bf16[96,128]{1,0:T(8,128)(2,1)S(1)}, u32[]{:S(2)}, u32[]{:S(2)}) collective-permute-start(bf16[96,128]{1,0:T(8,128)(2,1)S(1)} %shard_map.89.mine_ref), channel_id=1, source_target_pairs={{0,4},{4,0},{1,5},{5,1},{2,6},{6,2},{3,7},{7,3},{8,12},{12,8},{9,1... | collective-permute-start | bytes 73736 | tf_op jit(solution)/shard_map/ppermute | solution.py:145
  39.8 2.4 %collective-permute-start.8 = (bf16[192,128]{1,0:T(8,128)(2,1)S(1)}, bf16[192,128]{1,0:T(8,128)(2,1)S(1)}, u32[]{:S(2)}, u32[]{:S(2)}) collective-permute-start(bf16[192,128]{1,0:T(8,128)(2,1)S(1)} %get-tuple-element.42.state_ref), channel_id=1, source_target_pairs={{0,4},{4,0},{1,5},{5,1},{2,6},{6,2},{3,7},{7,3},{8,12},{12,8},{9,1... | collective-permute-start | bytes 147464 | tf_op jit(solution)/shard_map/ppermute | solution.py:145
  42.2 4.0 %collective-permute-start.11 = (bf16[96,128]{1,0:T(8,128)(2,1)S(1)}, bf16[96,128]{1,0:T(8,128)(2,1)S(1)}, u32[]{:S(2)}, u32[]{:S(2)}) collective-permute-start(bf16[96,128]{1,0:T(8,128)(2,1)S(1)} %shard_map.93.chip_ref), channel_id=1, source_target_pairs={{0,8},{8,16},{16,24},{24,0},{1,9},{9,17},{17,25},{25,1},{2,10},{10... | collective-permute-start | bytes 73736 | tf_op jit(solution)/shard_map/ppermute | solution.py:151
  42.3 4.3 %collective-permute-start.10 = (bf16[96,128]{1,0:T(8,128)(2,1)S(1)}, bf16[96,128]{1,0:T(8,128)(2,1)S(1)}, u32[]{:S(2)}, u32[]{:S(2)}) collective-permute-start(bf16[96,128]{1,0:T(8,128)(2,1)S(1)} %shard_map.93.chip_ref), channel_id=1, source_target_pairs={{0,16},{8,24},{16,0},{24,8},{1,17},{9,25},{17,1},{25,9},{2,18},{10... | collective-permute-start | bytes 73736 | tf_op jit(solution)/shard_map/ppermute | solution.py:151
  44.0 3.3 %collective-permute-start.9 = (bf16[96,128]{1,0:T(8,128)(2,1)S(1)}, bf16[96,128]{1,0:T(8,128)(2,1)S(1)}, u32[]{:S(2)}, u32[]{:S(2)}) collective-permute-start(bf16[96,128]{1,0:T(8,128)(2,1)S(1)} %shard_map.93.chip_ref), channel_id=1, source_target_pairs={{0,24},{8,0},{16,8},{24,16},{1,25},{9,1},{17,9},{25,17},{2,26},{10... | collective-permute-start | bytes 73736 | tf_op jit(solution)/shard_map/ppermute | solution.py:151
  48.0 15.2 %all-to-all-start.1 = ((bf16[8,96,128]{2,1,0:T(8,128)(2,1)}), bf16[8,96,128]{2,1,0:T(8,128)(2,1)S(1)}, u32[]{:S(2)}, u32[]{:S(2)}) async-start(bf16[8,96,128]{2,1,0:T(8,128)(2,1)} %shard_map.95), calls=%async_computation.1 | async-start | bytes 393216 | tf_op jit(solution)/shard_map/all_to_all | solution.py:141
  55.9 18.2 %collective-permute-start.14 = (bf16[256,384]{1,0:T(8,128)(2,1)}, bf16[256,384]{1,0:T(8,128)(2,1)S(1)}, u32[]{:S(2)}, u32[]{:S(2)}) collective-permute-start(bf16[256,384]{1,0:T(8,128)(2,1)} %get-tuple-element.50), channel_id=1, source_target_pairs={{0,3},{1,0},{2,1},{3,2},{4,7},{5,4},{6,5},{7,6},{8,11},{9,8},{10,9... | collective-permute-start | bytes 589832 | tf_op jit(solution)/shard_map/ppermute | solution.py:521
  56.2 17.9 %collective-permute-start.13 = (bf16[256,384]{1,0:T(8,128)(2,1)}, bf16[256,384]{1,0:T(8,128)(2,1)S(1)}, u32[]{:S(2)}, u32[]{:S(2)}) collective-permute-start(bf16[256,384]{1,0:T(8,128)(2,1)} %get-tuple-element.48), channel_id=1, source_target_pairs={{0,1},{1,2},{2,3},{3,0},{4,5},{5,6},{6,7},{7,4},{8,9},{9,10},{10,1... | collective-permute-start | bytes 589832 | tf_op jit(solution)/shard_map/ppermute | solution.py:521
  57.3 16.7 %collective-permute-start.12 = (bf16[256,384]{1,0:T(8,128)(2,1)}, bf16[256,384]{1,0:T(8,128)(2,1)S(1)}, u32[]{:S(2)}, u32[]{:S(2)}) collective-permute-start(bf16[256,384]{1,0:T(8,128)(2,1)} %get-tuple-element.46), channel_id=1, source_target_pairs={{0,2},{1,3},{2,0},{3,1},{4,6},{5,7},{6,4},{7,5},{8,10},{9,11},{10,... | collective-permute-start | bytes 589832 | tf_op jit(solution)/shard_map/ppermute | solution.py:521
  63.2 4.8 %collective-permute-start.15 = (bf16[96,128]{1,0:T(8,128)(2,1)S(1)}, bf16[96,128]{1,0:T(8,128)(2,1)S(1)}, u32[]{:S(2)}, u32[]{:S(2)}) collective-permute-start(bf16[96,128]{1,0:T(8,128)(2,1)S(1)} %shard_map.97.mine_ref), channel_id=1, source_target_pairs={{0,4},{4,0},{1,5},{5,1},{2,6},{6,2},{3,7},{7,3},{8,12},{12,8},{9,1... | collective-permute-start | bytes 73736 | tf_op jit(solution)/shard_map/ppermute | solution.py:145
  71.3 11.9 %collective-permute-start.17 = (bf16[256,384]{1,0:T(8,128)(2,1)S(1)}, bf16[256,384]{1,0:T(8,128)(2,1)S(1)}, u32[]{:S(2)}, u32[]{:S(2)}) collective-permute-start(bf16[256,384]{1,0:T(8,128)(2,1)S(1)} %get-tuple-element.64), channel_id=1, source_target_pairs={{0,1},{1,2},{2,3},{3,0},{4,5},{5,6},{6,7},{7,4},{8,9},{9,10},{10,1... | collective-permute-start | bytes 589832 | tf_op jit(solution)/shard_map/ppermute | solution.py:521
  71.4 11.9 %collective-permute-start.18 = (bf16[256,384]{1,0:T(8,128)(2,1)S(1)}, bf16[256,384]{1,0:T(8,128)(2,1)S(1)}, u32[]{:S(2)}, u32[]{:S(2)}) collective-permute-start(bf16[256,384]{1,0:T(8,128)(2,1)S(1)} %get-tuple-element.65), channel_id=1, source_target_pairs={{0,3},{1,0},{2,1},{3,2},{4,7},{5,4},{6,5},{7,6},{8,11},{9,8},{10,9... | collective-permute-start | bytes 589832 | tf_op jit(solution)/shard_map/ppermute | solution.py:521
  74.1 9.2 %collective-permute-start.16 = (bf16[256,384]{1,0:T(8,128)(2,1)S(1)}, bf16[256,384]{1,0:T(8,128)(2,1)S(1)}, u32[]{:S(2)}, u32[]{:S(2)}) collective-permute-start(bf16[256,384]{1,0:T(8,128)(2,1)S(1)} %get-tuple-element.63), channel_id=1, source_target_pairs={{0,2},{1,3},{2,0},{3,1},{4,6},{5,7},{6,4},{7,5},{8,10},{9,11},{10,... | collective-permute-start | bytes 589832 | tf_op jit(solution)/shard_map/ppermute | solution.py:521
  (2 other events, 21.1 us)

commit v6 on v5

--- a/solution.py
+++ b/solution.py
@@ -406,11 +406,15 @@
     ]
 
 
-def weight_blocks(k, weights):
+def weight_blocks(which, weights):
     width = weights[0].shape[1]
+    count = 3 * len(which)
 
     def body(*refs):
-        copies = block_copies(k, refs[:3], refs[3:6], refs[6], 0)
+        sources, targets, sem = (refs[:3], refs[3 : 3 + count], refs[3 + count])
+        copies = []
+        for i, k in enumerate(which):
+            copies += block_copies(k, sources, targets[3 * i : 3 * i + 3], sem, 3 * i)
         for copy in copies:
             copy.start()
         for copy in copies:
@@ -418,12 +422,12 @@
 
     return call(
         body,
-        [((width, width), bf16)] * 3,
+        [((width, width), bf16)] * count,
         1,
         1024 * 1024,
         in_specs=[pl.BlockSpec(memory_space=pltpu.HBM)] * 3,
-        out_specs=[VMEM] * 3,
-        scratch_shapes=[pltpu.SemaphoreType.DMA((3,))],
+        out_specs=[VMEM] * count,
+        scratch_shapes=[pltpu.SemaphoreType.DMA((count,))],
     )(*(in_hbm(w) for w in weights))
 
 
@@ -445,7 +449,8 @@
         wv_ref,
         dk_ref,
         dv_ref,
-        part_ref,
+        upper_ref,
+        lower_ref,
         state,
     ):
         whole_state(True, mine_ref, got_ref, pair_ref, state)
@@ -458,63 +463,116 @@
             dv_ref[:, cols] = (dvl_ref[:, cols].astype(f32) + mm(k, after)).astype(bf16)
         total = mm(dq_ref[...], wq_ref[...], NT)
         total = total + mm(dk_ref[...], wk_ref[...], NT)
-        part_ref[...] = (total + mm(dv_ref[...], wv_ref[...], NT)).astype(bf16)
-
-    return call(
-        body,
-        [((rows, width), bf16)] * 3,
+        total = (total + mm(dv_ref[...], wv_ref[...], NT)).astype(bf16)
+        upper_ref[...] = total[: rows // 2]
+        lower_ref[...] = total[rows // 2 :]
+
+    return call(
+        body,
+        [((rows, width), bf16)] * 2 + [((rows // 2, width), bf16)] * 2,
         6 * rows * width * width,
         2 * 1024 * 1024,
         in_specs=[VMEM] * 11,
-        out_specs=[VMEM] * 3,
+        out_specs=[VMEM] * 4,
         scratch_shapes=[pltpu.VMEM((2 * half, LANES), f32)],
     )(mine, got, pair, fk, v, dq, dk, dv, *blocks)
 
 
-def other_parts(which, dq, dk, dv, weights):
+def side_parts(dq, dk, dv, blocks):
     rows, width = dq.shape
-    count = len(which)
-
-    def body(dq_ref, dk_ref, dv_ref, wq_hbm, wk_hbm, wv_hbm, *refs):
-        outs, blocks, sem = (refs[:count], refs[count], refs[count + 1])
-        copies = [
-            block_copies(
-                k, (wq_hbm, wk_hbm, wv_hbm), [blocks.at[3 * i + j] for j in range(3)], sem, 3 * i
-            )
-            for i, k in enumerate(which)
-        ]
-        for group in copies:
-            for copy in group:
-                copy.start()
-        for i, (group, ref) in enumerate(zip(copies, outs)):
-            for copy in group:
-                copy.wait()
+    half = rows // 2
+
+    def body(dq_ref, dk_ref, dv_ref, q1, k1, v1, q3, k3, v3, soon1, soon3, late1, late3):
+        top, bottom = (slice(0, half), slice(half, rows))
+        for weights, soon, late, first in (
+            ((q1, k1, v1), soon1, late1, bottom),
+            ((q3, k3, v3), soon3, late3, top),
+        ):
             total = None
-            for j, grad_ref in enumerate((dq_ref, dk_ref, dv_ref)):
-                part = mm(grad_ref[...], blocks[3 * i + j], NT)
+            for grad_ref, w_ref in zip((dq_ref, dk_ref, dv_ref), weights):
+                part = mm(grad_ref[...], w_ref[...], NT)
                 total = part if total is None else total + part
-            ref[...] = total.astype(bf16)
+            soon[...] = total[first].astype(bf16)
+            late[...] = total[top if first is bottom else bottom]
+
+    return plain(
+        body,
+        [((half, width), bf16)] * 2 + [((half, width), f32)] * 2,
+        12 * rows * width * width,
+        2 * 1024 * 1024,
+        dq,
+        dk,
+        dv,
+        *blocks,
+    )
+
+
+def marker(x):
+    def body(x_ref, out_ref):
+        out_ref[...] = x_ref[:8, :LANES]
+
+    return plain(body, [((8, LANES), x.dtype)], 1, 1024, x)[0]
+
+
+def relayed(late1, late3, far1, far3, mark):
+    half, width = far1.shape
+
+    def body(a, b, c, d, _, out1, out3):
+        out1[...] = (a[...] + c[...].astype(f32)).astype(bf16)
+        out3[...] = (b[...] + d[...].astype(f32)).astype(bf16)
+
+    outs = [((half, width), bf16)] * 2
+    return plain(body, outs, 1, 1024 * 1024, late1, late3, far1, far3, mark)
+
+
+def finished(own, soon3, late1, soon1, late3):
+    half = soon1.shape[0]
+
+    def body(own_ref, s3, l1, s1, l3, out_ref):
+        for rows, a, b in ((slice(0, half), s3, l1), (slice(half, 2 * half), s1, l3)):
+            total = own_ref[rows, :].astype(f32) + a[...].astype(f32) + b[...].astype(f32)
+            out_ref[rows, :] = total.astype(bf16)
+
+    outs = [(own.shape, bf16, pltpu.HBM)]
+    return plain(body, outs, 1, 1024 * 1024, own, soon3, late1, soon1, late3)[0]
+
+
+def own_part(dq, dk, dv, weights):
+    rows, width = dq.shape
+
+    def body(dq_ref, dk_ref, dv_ref, wq_hbm, wk_hbm, wv_hbm, out_ref, blocks, sem):
+        copies = block_copies(0, (wq_hbm, wk_hbm, wv_hbm), [blocks.at[j] for j in range(3)], sem, 0)
+        for copy in copies:
+            copy.start()
+        total = jnp.zeros((rows, width), f32)
+        for j, grad_ref in enumerate((dq_ref, dk_ref, dv_ref)):
+            copies[j].wait()
+            total = total + mm(grad_ref[...], blocks[j], NT)
+        out_ref[...] = total.astype(bf16)
 
     hbm = pl.BlockSpec(memory_space=pltpu.HBM)
     return call(
         body,
-        [((rows, width), bf16)] * count,
-        6 * rows * width * width * count,
-        1024 * 1024 * count,
+        [((rows, width), bf16)],
+        6 * rows * width * width,
+        1024 * 1024,
         in_specs=[VMEM] * 3 + [hbm] * 3,
-        out_specs=[VMEM] * count,
+        out_specs=[VMEM],
         scratch_shapes=[
-            pltpu.VMEM((3 * count, width, width), bf16),
-            pltpu.SemaphoreType.DMA((3 * count,)),
+            pltpu.VMEM((3, width, width), bf16),
+            pltpu.SemaphoreType.DMA((3,)),
         ],
-    )(dq, dk, dv, *(in_hbm(w) for w in weights))
+    )(dq, dk, dv, *(in_hbm(w) for w in weights))[0]
 
 
 def add_up(parts):
-    total = parts[0].astype(f32)
-    for part in parts[1:]:
-        total = total + part.astype(f32)
-    return total.astype(bf16)
+    def body(*refs):
+        total = refs[0][...].astype(f32)
+        for ref in refs[1:-1]:
+            total = total + ref[...].astype(f32)
+        refs[-1][...] = total.astype(bf16)
+
+    return plain(body, [(parts[0].shape, bf16, pltpu.HBM)], 1, 1024 * 1024, *map(in_hbm, parts))[0]
 
 
 def to_owner(part, k):
@@ -541,7 +599,7 @@
     got = swap(mine)
     attn, draw, before, state = normed(mine, got, pair, fq, raw_local, up, gain)
     weights = (w_query, w_key, w_value)
-    blocks = weight_blocks(2, (hold(w_query, state), w_key, w_value))
+    blocks = weight_blocks((2,), (hold(w_query, state), w_key, w_value))
     pair = swap(state)
     chip = pair_sum(state, pair)
     got = y_gather(True, chip)
@@ -553,12 +611,17 @@
     planes = plane_exchange(planes)
     mine = before_chip(True, planes)
     got = swap(mine)
-    dk, dv, l2 = first_part(mine, got, pair, fk, v, dq, dk_local, dv_local, blocks)
-    l2 = to_owner(l2, 2)
-    l1, l3 = other_parts((1, 3), dq, dk, dv, weights)
-    l1, l3 = (to_owner(l1, 1), to_owner(l3, 3))
-    (l0,) = other_parts((0,), dq, dk, dv, weights)
-    return (add_up(branch), add_up([l0, l2, l1, l3]))
+    others = weight_blocks((1, 3), (hold(w_query, mine), w_key, w_value))
+    dk, dv, up2, down2 = first_part(mine, got, pair, fk, v, dq, dk_local, dv_local, blocks)
+    far1, far3 = (to_owner(up2, 1), to_owner(down2, 3))
+    soon1, soon3, late1, late3 = side_parts(dq, dk, dv, others)
+    soon1, soon3 = (to_owner(soon1, 1), to_owner(soon3, 3))
+    mark = marker(late1)
+    late1, late3 = relayed(late1, late3, far1, far3, mark)
+    late1, late3 = (to_owner(late1, 1), to_owner(late3, 3))
+    branch = add_up(branch)
+    own = own_part(dq, dk, dv, weights)
+    return (branch, finished(own, soon3, late1, soon1, late3))
 
 
 def solution(mesh):

time: 84.4 us -> 85.1 us (level)
  waiting for transfers between devices: 22.2 us -> 15.9 us
  starting transfers between devices: 40 us -> 44.3 us
  Pallas kernels: 19.4 us -> 22.2 us
  other arithmetic: 1.56 us -> 0 us
    ppermute x9 -> x12, waiting for transfers between devices: 8.82 us -> 2.64 us  [to_owner(): return lax.ppermute(part, 'mp', shifts(4, k))]
    ppermute x9 -> x12, starting transfers between devices: 8.4 us -> 12.7 us  [to_owner(): return lax.ppermute(part, 'mp', shifts(4, k))]
    pallas_call x8 -> x13, Pallas kernels: 4.63 us -> 8.33 us  [plain(): call(body, outs, flops, moved, in_specs=[VMEM] * len(args), out_specs=[VM...]
    convert_element_type x2 -> x0, other arithmetic: 1.56 us -> none  [add_up(): return total.astype(bf16)]
    pallas_call x4, Pallas kernels: 6.12 us -> 5.16 us  [the longest x2 2.62 us: weight_blocks(): call(body, [((width, width), bf16)] * count, 1, 1024 * 1024, in_specs=[pl...]
  transfers between devices with their start and end apart: 21 -> 24, of which waited for: 12 -> 12; matrix products, arithmetic and copies ran while one was open for 1% -> 0% of each run, Pallas kernels for 17% -> 19%
where the time goes in v6:
time: 85.1 us; the launch traced here: 84 us
  starting transfers between devices  44.3 us (52%)
  Pallas kernels  22.2 us (26%)
  waiting for transfers between devices  15.9 us (19%)
  between operations  0.91 us (1%)
    all_to_all x2, starting transfers between devices, plane_exchange(): return lax.all_to_all(planes, 'seq_0', 0, 0, tiled=True)  14.8 us
    ppermute x12, starting transfers between devices, to_owner(): return lax.ppermute(part, 'mp', shifts(4, k))  12.7 us
    ppermute x4, starting transfers between devices, swap(): return lax.ppermute(x, 'seq_2', SWAP)  11.1 us
    pallas_call x13, Pallas kernels, plain(): call(body, outs, flops, moved, in_specs=[VMEM] * len(args), out_specs=[VM...  8.33 us
    all_to_all x2, waiting for transfers between devices, plane_exchange(): return lax.all_to_all(planes, 'seq_0', 0, 0, tiled=True)  6.61 us
    ppermute x6, starting transfers between devices, y_gather(): got.append(lax.ppermute(chip, 'seq_1', shifts(4, -k if later else k)))  5.75 us
    ppermute x6, waiting for transfers between devices, y_gather(): got.append(lax.ppermute(chip, 'seq_1', shifts(4, -k if later else k)))  4.88 us
    pallas_call x1, Pallas kernels, key_value(): call(body, [((rows, width), bf16), ((rows, width), bf16), ((width * HD //...  3.1 us
  transfers between devices with their start and end apart: 24, of which 12 were waited for; matrix products, arithmetic and copies ran while one was open for 0% of the time, Pallas kernels for 19%

profile of v6, /device:TPU:1, one launch (start us, length us, event | category | flops | bytes accessed | tf_op | source)
XLA Modules:
  0.0 84.0 jit_solution(15546792154604327606)
XLA Ops:
  0.7 3.1 %shard_map.86 = (bf16[256,384]{1,0:T(8,128)(2,1)S(1)}, bf16[256,384]{1,0:T(8,128)(2,1)S(1)}, bf16[192,128]{1,0:T(8,128)(2,1)S(1)}) custom-call(bf16[256,1536]{1,0:T(8,128)(2,1)} %x_hbm.2, bf16[1536,384]{1,0:T(8,128)(2,1)} %refs_1_.3, bf16[1536,384]{1,0:T(8,128)(2,1)} %refs_2_.3), custom_call_target="tpu_custom_call" | custom-call | flops 603979776 | bytes 3145728 | tf_op jit(solution)/shard_map/pallas_call | solution.py:195
  3.8 3.3 %collective-permute-start = (bf16[192,128]{1,0:T(8,128)(2,1)S(1)}, bf16[192,128]{1,0:T(8,128)(2,1)S(1)}, u32[]{:S(2)}, u32[]{:S(2)}) collective-permute-start(bf16[192,128]{1,0:T(8,128)(2,1)S(1)} %get-tuple-element.46.state_ref), channel_id=1, source_target_pairs={{0,4},{4,0},{1,5},{5,1},{2,6},{6,2},{3,7},{7,3},{8,12},{12,8},{9,1... | collective-permute-start | bytes 147464 | tf_op jit(solution)/shard_map/ppermute | solution.py:145
  10.7 2.5 %collective-permute-done.2.g2 = bf16[96,128]{1,0:T(8,128)(2,1)S(1)} collective-permute-done((bf16[96,128]{1,0:T(8,128)(2,1)S(1)}, bf16[96,128]{1,0:T(8,128)(2,1)S(1)}, u32[]{:S(2)}, u32[]{:S(2)}) %collective-permute-start.2) | collective-permute-done | bytes 24608 | tf_op jit(solution)/shard_map/ppermute | solution.py:151
  14.2 8.2 %all-to-all-start = ((bf16[8,96,128]{2,1,0:T(8,128)(2,1)}), bf16[8,96,128]{2,1,0:T(8,128)(2,1)S(1)}, u32[]{:S(2)}, u32[]{:S(2)}) async-start(bf16[8,96,128]{2,1,0:T(8,128)(2,1)} %shard_map.88), calls=%async_computation | async-start | bytes 393216 | tf_op jit(solution)/shard_map/all_to_all | solution.py:141
  22.4 2.6 %collective-permute-start.7 = (bf16[256,384]{1,0:T(8,128)(2,1)S(1)}, bf16[256,384]{1,0:T(8,128)(2,1)S(1)}, u32[]{:S(2)}, u32[]{:S(2)}) collective-permute-start(bf16[256,384]{1,0:T(8,128)(2,1)S(1)} %copy-done.2), channel_id=1, source_target_pairs={{0,3},{1,0},{2,1},{3,2},{4,7},{5,4},{6,5},{7,6},{8,11},{9,8},{10,9... | collective-permute-start | bytes 589832 | tf_op jit(solution)/shard_map/ppermute | solution.py:579
  26.1 2.5 %shard_map.90 = (bf16[256,384]{1,0:T(8,128)(2,1)S(1)}, bf16[256,384]{1,0:T(8,128)(2,1)S(1)}) custom-call(bf16[256,1536]{1,0:T(8,128)(2,1)} %x_hbm.2, bf16[1536,384]{1,0:T(8,128)(2,1)S(1)} %copy-done, bf16[256,384]{1,0:T(8,128)(2,1)S(1)} %get-tuple-element.48.fk_ref, bf16[256,384]{1,0:T(8,128)(2,1)S(1)} %get-tuple-element.49.v_ref), custom_call_target="tpu_custom_call" | custom-call | flops 503316480 | bytes 3145728 | tf_op jit(solution)/shard_map/pallas_call | solution.py:253
  28.5 2.5 %all-to-all-done.planes_ref = bf16[8,96,128]{2,1,0:T(8,128)(2,1)S(1)} async-done(((bf16[8,96,128]{2,1,0:T(8,128)(2,1)}), bf16[8,96,128]{2,1,0:T(8,128)(2,1)S(1)}, u32[]{:S(2)}, u32[]{:S(2)}) %all-to-all-start) | async-done | bytes 196640 | tf_op jit(solution)/shard_map/all_to_all | solution.py:141
  31.1 3.3 %collective-permute-start.4 = (bf16[96,128]{1,0:T(8,128)(2,1)S(1)}, bf16[96,128]{1,0:T(8,128)(2,1)S(1)}, u32[]{:S(2)}, u32[]{:S(2)}) collective-permute-start(bf16[96,128]{1,0:T(8,128)(2,1)S(1)} %shard_map.89.mine_ref), channel_id=1, source_target_pairs={{0,4},{4,0},{1,5},{5,1},{2,6},{6,2},{3,7},{7,3},{8,12},{12,8},{9,1... | collective-permute-start | bytes 73736 | tf_op jit(solution)/shard_map/ppermute | solution.py:145
  34.5 2.1 %collective-permute-done.5.g1 = bf16[256,384]{1,0:T(8,128)(2,1)S(1)} collective-permute-done((bf16[256,384]{1,0:T(8,128)(2,1)S(1)}, bf16[256,384]{1,0:T(8,128)(2,1)S(1)}, u32[]{:S(2)}, u32[]{:S(2)}) %collective-permute-start.5) | collective-permute-done | bytes 196640 | tf_op jit(solution)/shard_map/ppermute | solution.py:579
  36.6 2.1 %shard_map.91.up_ref = bf16[256,384]{1,0:T(8,128)(2,1)S(1)} custom-call(bf16[256,384]{1,0:T(8,128)(2,1)S(1)} %copy-done.2, bf16[256,384]{1,0:T(8,128)(2,1)S(1)} %collective-permute-done.5.g1, bf16[256,384]{1,0:T(8,128)(2,1)S(1)} %collective-permute-done.6.g2, bf16[256,384]{1,0:T(8,128)(2,1)S(1)} %collective-permute-done.7.g3, bf16[384,1536]{1,0:T(8,128)(2,1)} %w_ref.1, ...), custom_call_target="tpu_custom_call" | custom-call | flops 301989888 | bytes 3145728 | tf_op jit(solution)/shard_map/pallas_call | solution.py:283
  39.8 1.5 %collective-permute-start.8 = (bf16[192,128]{1,0:T(8,128)(2,1)S(1)}, bf16[192,128]{1,0:T(8,128)(2,1)S(1)}, u32[]{:S(2)}, u32[]{:S(2)}) collective-permute-start(bf16[192,128]{1,0:T(8,128)(2,1)S(1)} %get-tuple-element.54.state_ref), channel_id=1, source_target_pairs={{0,4},{4,0},{1,5},{5,1},{2,6},{6,2},{3,7},{7,3},{8,12},{12,8},{9,1... | collective-permute-start | bytes 147464 | tf_op jit(solution)/shard_map/ppermute | solution.py:145
  42.3 1.7 %collective-permute-start.10 = (bf16[96,128]{1,0:T(8,128)(2,1)S(1)}, bf16[96,128]{1,0:T(8,128)(2,1)S(1)}, u32[]{:S(2)}, u32[]{:S(2)}) collective-permute-start(bf16[96,128]{1,0:T(8,128)(2,1)S(1)} %shard_map.93.chip_ref), channel_id=1, source_target_pairs={{0,16},{8,24},{16,0},{24,8},{1,17},{9,25},{17,1},{25,9},{2,18},{10... | collective-permute-start | bytes 73736 | tf_op jit(solution)/shard_map/ppermute | solution.py:151
  44.0 1.8 %collective-permute-start.9 = (bf16[96,128]{1,0:T(8,128)(2,1)S(1)}, bf16[96,128]{1,0:T(8,128)(2,1)S(1)}, u32[]{:S(2)}, u32[]{:S(2)}) collective-permute-start(bf16[96,128]{1,0:T(8,128)(2,1)S(1)} %shard_map.93.chip_ref), channel_id=1, source_target_pairs={{0,24},{8,0},{16,8},{24,16},{1,25},{9,1},{17,9},{25,17},{2,26},{10... | collective-permute-start | bytes 73736 | tf_op jit(solution)/shard_map/ppermute | solution.py:151
  48.0 6.6 %all-to-all-start.1 = ((bf16[8,96,128]{2,1,0:T(8,128)(2,1)}), bf16[8,96,128]{2,1,0:T(8,128)(2,1)S(1)}, u32[]{:S(2)}, u32[]{:S(2)}) async-start(bf16[8,96,128]{2,1,0:T(8,128)(2,1)} %shard_map.95), calls=%async_computation.1 | async-start | bytes 393216 | tf_op jit(solution)/shard_map/all_to_all | solution.py:141
  54.5 1.3 %shard_map.94 = (bf16[256,384]{1,0:T(8,128)(2,1)}, bf16[256,384]{1,0:T(8,128)(2,1)}, bf16[256,384]{1,0:T(8,128)(2,1)}, bf16[256,384]{1,0:T(8,128)(2,1)}) custom-call(bf16[256,384]{1,0:T(8,128)(2,1)S(1)} %get-tuple-element.55.attn_ref, bf16[384,1536]{1,0:T(8,128)(2,1)S(1)} %copy-done.1), custom_call_target="tpu_custom_call" | custom-call | flops 301989888 | bytes 2097152 | tf_op jit(solution)/shard_map/pallas_call | solution.py:48
  59.1 4.1 %all-to-all-done.1.planes_ref = bf16[8,96,128]{2,1,0:T(8,128)(2,1)S(1)} async-done(((bf16[8,96,128]{2,1,0:T(8,128)(2,1)}), bf16[8,96,128]{2,1,0:T(8,128)(2,1)S(1)}, u32[]{:S(2)}, u32[]{:S(2)}) %all-to-all-start.1) | async-done | bytes 196640 | tf_op jit(solution)/shard_map/all_to_all | solution.py:141
  63.3 3.0 %collective-permute-start.15 = (bf16[96,128]{1,0:T(8,128)(2,1)S(1)}, bf16[96,128]{1,0:T(8,128)(2,1)S(1)}, u32[]{:S(2)}, u32[]{:S(2)}) collective-permute-start(bf16[96,128]{1,0:T(8,128)(2,1)S(1)} %shard_map.98.mine_ref), channel_id=1, source_target_pairs={{0,4},{4,0},{1,5},{5,1},{2,6},{6,2},{3,7},{7,3},{8,12},{12,8},{9,1... | collective-permute-start | bytes 73736 | tf_op jit(solution)/shard_map/ppermute | solution.py:145
  66.2 1.8 %shard_map.97 = (bf16[256,384]{1,0:T(8,128)(2,1)S(1)}, bf16[256,384]{1,0:T(8,128)(2,1)S(1)}, bf16[256,384]{1,0:T(8,128)(2,1)S(1)}) custom-call(bf16[256,384]{1,0:T(8,128)(2,1)S(1)} %get-tuple-element.50.fq_ref, bf16[256,384]{1,0:T(8,128)(2,1)S(1)} %get-tuple-element.48.fk_ref, bf16[256,384]{1,0:T(8,128)(2,1)S(1)} %get-tuple-element.49.v_ref, ...), custom_call_target="tpu_custom_call" | custom-call | flops 603979776 | bytes 3145728 | tf_op jit(solution)/shard_map/pallas_call | solution.py:48
  68.8 2.7 %collective-permute-start.18 = (bf16[128,384]{1,0:T(8,128)(2,1)S(1)}, bf16[128,384]{1,0:T(8,128)(2,1)S(1)}, u32[]{:S(2)}, u32[]{:S(2)}) collective-permute-start(bf16[128,384]{1,0:T(8,128)(2,1)S(1)} %get-tuple-element.86), channel_id=1, source_target_pairs={{0,3},{1,0},{2,1},{3,2},{4,7},{5,4},{6,5},{7,6},{8,11},{9,8},{10,9... | collective-permute-start | bytes 294920 | tf_op jit(solution)/shard_map/ppermute | solution.py:579
  71.5 1.5 %shard_map.102 = (bf16[384,384]{1,0:T(8,128)(2,1)S(1)}, bf16[384,384]{1,0:T(8,128)(2,1)S(1)}, bf16[384,384]{1,0:T(8,128)(2,1)S(1)}, bf16[384,384]{1,0:T(8,128)(2...) custom-call(bf16[1536,384]{1,0:T(8,128)(2,1)} %refs_0_.1, bf16[1536,384]{1,0:T(8,128)(2,1)} %refs_1_.3, ...), custom_call_target="tpu_custom_call" | custom-call | flops 1 | bytes 1048576 | tf_op jit(solution)/shard_map/pallas_call | solution.py:423
  74.4 1.5 %collective-permute-start.20 = (bf16[128,384]{1,0:T(8,128)(2,1)S(1)}, bf16[128,384]{1,0:T(8,128)(2,1)S(1)}, u32[]{:S(2)}, u32[]{:S(2)}) collective-permute-start(bf16[128,384]{1,0:T(8,128)(2,1)S(1)} %get-tuple-element.88), channel_id=1, source_target_pairs={{0,1},{1,2},{2,3},{3,0},{4,5},{5,6},{6,7},{7,4},{8,9},{9,10},{10,1... | collective-permute-start | bytes 294920 | tf_op jit(solution)/shard_map/ppermute | solution.py:579
  76.0 2.6 %collective-permute-start.21 = (bf16[128,384]{1,0:T(8,128)(2,1)S(1)}, bf16[128,384]{1,0:T(8,128)(2,1)S(1)}, u32[]{:S(2)}, u32[]{:S(2)}) collective-permute-start(bf16[128,384]{1,0:T(8,128)(2,1)S(1)} %get-tuple-element.89), channel_id=1, source_target_pairs={{0,3},{1,0},{2,1},{3,2},{4,7},{5,4},{6,5},{7,6},{8,11},{9,8},{10,9... | collective-permute-start | bytes 294920 | tf_op jit(solution)/shard_map/ppermute | solution.py:579
  79.4 2.0 %shard_map.96 = bf16[256,384]{1,0:T(8,128)(2,1)} custom-call(bf16[256,384]{1,0:T(8,128)(2,1)} %get-tuple-element.56.refs_0_, bf16[256,384]{1,0:T(8,128)(2,1)} %copy-done.5, bf16[256,384]{1,0:T(8,128)(2,1)} %copy-done.4, bf16[256,384]{1,0:T(8,128)(2,1)} %copy-done.3), custom_call_target="tpu_custom_call" | custom-call | flops 1 | bytes 1048576 | tf_op jit(solution)/shard_map/pallas_call | solution.py:48
  81.4 1.8 %shard_map.101.own_ref = bf16[256,384]{1,0:T(8,128)(2,1)S(1)} custom-call(bf16[256,384]{1,0:T(8,128)(2,1)S(1)} %get-tuple-element.66.dq_ref, bf16[256,384]{1,0:T(8,128)(2,1)S(1)} %get-tuple-element.73.dk_ref, bf16[256,384]{1,0:T(8,128)(2,1)S(1)} %get-tuple-element.74.dv_ref, bf16[1536,384]{1,0:T(8,128)(2,1)} %refs_0_.1, bf16[1536,384]{1,0:T(8,128)(2,1)} %refs_1_.3, ...), custom_call_target="tpu_custom_call" | custom-call | flops 226492416 | bytes 1048576 | tf_op jit(solution)/shard_map/pallas_call | solution.py:554
  (62 shorter events, 17.0 us)
Async XLA Ops:
  3.8 4.2 %collective-permute-start = (bf16[192,128]{1,0:T(8,128)(2,1)S(1)}, bf16[192,128]{1,0:T(8,128)(2,1)S(1)}, u32[]{:S(2)}, u32[]{:S(2)}) collective-permute-start(bf16[192,128]{1,0:T(8,128)(2,1)S(1)} %get-tuple-element.46.state_ref), channel_id=1, source_target_pairs={{0,4},{4,0},{1,5},{5,1},{2,6},{6,2},{3,7},{7,3},{8,12},{12,8},{9,1... | collective-permute-start | bytes 147464 | tf_op jit(solution)/shard_map/ppermute | solution.py:145
  8.0 2.8 %collective-permute-start.3 = (bf16[96,128]{1,0:T(8,128)(2,1)S(1)}, bf16[96,128]{1,0:T(8,128)(2,1)S(1)}, u32[]{:S(2)}, u32[]{:S(2)}) collective-permute-start(bf16[96,128]{1,0:T(8,128)(2,1)S(1)} %shard_map.87.chip_ref), channel_id=1, source_target_pairs={{0,24},{8,0},{16,8},{24,16},{1,25},{9,1},{17,9},{25,17},{2,26},{10... | collective-permute-start | bytes 73736 | tf_op jit(solution)/shard_map/ppermute | solution.py:151
  9.1 4.2 %collective-permute-start.2 = (bf16[96,128]{1,0:T(8,128)(2,1)S(1)}, bf16[96,128]{1,0:T(8,128)(2,1)S(1)}, u32[]{:S(2)}, u32[]{:S(2)}) collective-permute-start(bf16[96,128]{1,0:T(8,128)(2,1)S(1)} %shard_map.87.chip_ref), channel_id=1, source_target_pairs={{0,16},{8,24},{16,0},{24,8},{1,17},{9,25},{17,1},{25,9},{2,18},{10... | collective-permute-start | bytes 73736 | tf_op jit(solution)/shard_map/ppermute | solution.py:151
  9.4 4.1 %collective-permute-start.1 = (bf16[96,128]{1,0:T(8,128)(2,1)S(1)}, bf16[96,128]{1,0:T(8,128)(2,1)S(1)}, u32[]{:S(2)}, u32[]{:S(2)}) collective-permute-start(bf16[96,128]{1,0:T(8,128)(2,1)S(1)} %shard_map.87.chip_ref), channel_id=1, source_target_pairs={{0,8},{8,16},{16,24},{24,0},{1,9},{9,17},{17,25},{25,1},{2,10},{10... | collective-permute-start | bytes 73736 | tf_op jit(solution)/shard_map/ppermute | solution.py:151
  14.2 16.9 %all-to-all-start = ((bf16[8,96,128]{2,1,0:T(8,128)(2,1)}), bf16[8,96,128]{2,1,0:T(8,128)(2,1)S(1)}, u32[]{:S(2)}, u32[]{:S(2)}) async-start(bf16[8,96,128]{2,1,0:T(8,128)(2,1)} %shard_map.88), calls=%async_computation | async-start | bytes 393216 | tf_op jit(solution)/shard_map/all_to_all | solution.py:141
  22.4 12.1 %collective-permute-start.7 = (bf16[256,384]{1,0:T(8,128)(2,1)S(1)}, bf16[256,384]{1,0:T(8,128)(2,1)S(1)}, u32[]{:S(2)}, u32[]{:S(2)}) collective-permute-start(bf16[256,384]{1,0:T(8,128)(2,1)S(1)} %copy-done.2), channel_id=1, source_target_pairs={{0,3},{1,0},{2,1},{3,2},{4,7},{5,4},{6,5},{7,6},{8,11},{9,8},{10,9... | collective-permute-start | bytes 589832 | tf_op jit(solution)/shard_map/ppermute | solution.py:579
  25.0 9.5 %collective-permute-start.6 = (bf16[256,384]{1,0:T(8,128)(2,1)S(1)}, bf16[256,384]{1,0:T(8,128)(2,1)S(1)}, u32[]{:S(2)}, u32[]{:S(2)}) collective-permute-start(bf16[256,384]{1,0:T(8,128)(2,1)S(1)} %copy-done.2), channel_id=1, source_target_pairs={{0,2},{1,3},{2,0},{3,1},{4,6},{5,7},{6,4},{7,5},{8,10},{9,11},{10,... | collective-permute-start | bytes 589832 | tf_op jit(solution)/shard_map/ppermute | solution.py:579
  25.5 11.1 %collective-permute-start.5 = (bf16[256,384]{1,0:T(8,128)(2,1)S(1)}, bf16[256,384]{1,0:T(8,128)(2,1)S(1)}, u32[]{:S(2)}, u32[]{:S(2)}) collective-permute-start(bf16[256,384]{1,0:T(8,128)(2,1)S(1)} %copy-done.2), channel_id=1, source_target_pairs={{0,1},{1,2},{2,3},{3,0},{4,5},{5,6},{6,7},{7,4},{8,9},{9,10},{10,1... | collective-permute-start | bytes 589832 | tf_op jit(solution)/shard_map/ppermute | solution.py:579
  31.1 7.6 %collective-permute-start.4 = (bf16[96,128]{1,0:T(8,128)(2,1)S(1)}, bf16[96,128]{1,0:T(8,128)(2,1)S(1)}, u32[]{:S(2)}, u32[]{:S(2)}) collective-permute-start(bf16[96,128]{1,0:T(8,128)(2,1)S(1)} %shard_map.89.mine_ref), channel_id=1, source_target_pairs={{0,4},{4,0},{1,5},{5,1},{2,6},{6,2},{3,7},{7,3},{8,12},{12,8},{9,1... | collective-permute-start | bytes 73736 | tf_op jit(solution)/shard_map/ppermute | solution.py:145
  39.8 2.4 %collective-permute-start.8 = (bf16[192,128]{1,0:T(8,128)(2,1)S(1)}, bf16[192,128]{1,0:T(8,128)(2,1)S(1)}, u32[]{:S(2)}, u32[]{:S(2)}) collective-permute-start(bf16[192,128]{1,0:T(8,128)(2,1)S(1)} %get-tuple-element.54.state_ref), channel_id=1, source_target_pairs={{0,4},{4,0},{1,5},{5,1},{2,6},{6,2},{3,7},{7,3},{8,12},{12,8},{9,1... | collective-permute-start | bytes 147464 | tf_op jit(solution)/shard_map/ppermute | solution.py:145
  42.2 4.0 %collective-permute-start.11 = (bf16[96,128]{1,0:T(8,128)(2,1)S(1)}, bf16[96,128]{1,0:T(8,128)(2,1)S(1)}, u32[]{:S(2)}, u32[]{:S(2)}) collective-permute-start(bf16[96,128]{1,0:T(8,128)(2,1)S(1)} %shard_map.93.chip_ref), channel_id=1, source_target_pairs={{0,8},{8,16},{16,24},{24,0},{1,9},{9,17},{17,25},{25,1},{2,10},{10... | collective-permute-start | bytes 73736 | tf_op jit(solution)/shard_map/ppermute | solution.py:151
  42.3 4.3 %collective-permute-start.10 = (bf16[96,128]{1,0:T(8,128)(2,1)S(1)}, bf16[96,128]{1,0:T(8,128)(2,1)S(1)}, u32[]{:S(2)}, u32[]{:S(2)}) collective-permute-start(bf16[96,128]{1,0:T(8,128)(2,1)S(1)} %shard_map.93.chip_ref), channel_id=1, source_target_pairs={{0,16},{8,24},{16,0},{24,8},{1,17},{9,25},{17,1},{25,9},{2,18},{10... | collective-permute-start | bytes 73736 | tf_op jit(solution)/shard_map/ppermute | solution.py:151
  44.0 3.3 %collective-permute-start.9 = (bf16[96,128]{1,0:T(8,128)(2,1)S(1)}, bf16[96,128]{1,0:T(8,128)(2,1)S(1)}, u32[]{:S(2)}, u32[]{:S(2)}) collective-permute-start(bf16[96,128]{1,0:T(8,128)(2,1)S(1)} %shard_map.93.chip_ref), channel_id=1, source_target_pairs={{0,24},{8,0},{16,8},{24,16},{1,25},{9,1},{17,9},{25,17},{2,26},{10... | collective-permute-start | bytes 73736 | tf_op jit(solution)/shard_map/ppermute | solution.py:151
  48.0 15.2 %all-to-all-start.1 = ((bf16[8,96,128]{2,1,0:T(8,128)(2,1)}), bf16[8,96,128]{2,1,0:T(8,128)(2,1)S(1)}, u32[]{:S(2)}, u32[]{:S(2)}) async-start(bf16[8,96,128]{2,1,0:T(8,128)(2,1)} %shard_map.95), calls=%async_computation.1 | async-start | bytes 393216 | tf_op jit(solution)/shard_map/all_to_all | solution.py:141
  55.9 20.0 %collective-permute-start.14 = (bf16[256,384]{1,0:T(8,128)(2,1)}, bf16[256,384]{1,0:T(8,128)(2,1)S(1)}, u32[]{:S(2)}, u32[]{:S(2)}) collective-permute-start(bf16[256,384]{1,0:T(8,128)(2,1)} %get-tuple-element.62), channel_id=1, source_target_pairs={{0,3},{1,0},{2,1},{3,2},{4,7},{5,4},{6,5},{7,6},{8,11},{9,8},{10,9... | collective-permute-start | bytes 589832 | tf_op jit(solution)/shard_map/ppermute | solution.py:579
  56.2 19.8 %collective-permute-start.13 = (bf16[256,384]{1,0:T(8,128)(2,1)}, bf16[256,384]{1,0:T(8,128)(2,1)S(1)}, u32[]{:S(2)}, u32[]{:S(2)}) collective-permute-start(bf16[256,384]{1,0:T(8,128)(2,1)} %get-tuple-element.60), channel_id=1, source_target_pairs={{0,1},{1,2},{2,3},{3,0},{4,5},{5,6},{6,7},{7,4},{8,9},{9,10},{10,1... | collective-permute-start | bytes 589832 | tf_op jit(solution)/shard_map/ppermute | solution.py:579
  58.5 20.2 %collective-permute-start.12 = (bf16[256,384]{1,0:T(8,128)(2,1)S(1)}, bf16[256,384]{1,0:T(8,128)(2,1)S(1)}, u32[]{:S(2)}, u32[]{:S(2)}) collective-permute-start(bf16[256,384]{1,0:T(8,128)(2,1)S(1)} %copy-done.7), channel_id=1, source_target_pairs={{0,2},{1,3},{2,0},{3,1},{4,6},{5,7},{6,4},{7,5},{8,10},{9,11},{10,... | collective-permute-start | bytes 589832 | tf_op jit(solution)/shard_map/ppermute | solution.py:579
  63.3 4.8 %collective-permute-start.15 = (bf16[96,128]{1,0:T(8,128)(2,1)S(1)}, bf16[96,128]{1,0:T(8,128)(2,1)S(1)}, u32[]{:S(2)}, u32[]{:S(2)}) collective-permute-start(bf16[96,128]{1,0:T(8,128)(2,1)S(1)} %shard_map.98.mine_ref), channel_id=1, source_target_pairs={{0,4},{4,0},{1,5},{5,1},{2,6},{6,2},{3,7},{7,3},{8,12},{12,8},{9,1... | collective-permute-start | bytes 73736 | tf_op jit(solution)/shard_map/ppermute | solution.py:145
  68.8 5.6 %collective-permute-start.17 = (bf16[128,384]{1,0:T(8,128)(2,1)S(1)}, bf16[128,384]{1,0:T(8,128)(2,1)S(1)}, u32[]{:S(2)}, u32[]{:S(2)}) collective-permute-start(bf16[128,384]{1,0:T(8,128)(2,1)S(1)} %get-tuple-element.85), channel_id=1, source_target_pairs={{0,1},{1,2},{2,3},{3,0},{4,5},{5,6},{6,7},{7,4},{8,9},{9,10},{10,1... | collective-permute-start | bytes 294920 | tf_op jit(solution)/shard_map/ppermute | solution.py:579
  68.8 5.5 %collective-permute-start.18 = (bf16[128,384]{1,0:T(8,128)(2,1)S(1)}, bf16[128,384]{1,0:T(8,128)(2,1)S(1)}, u32[]{:S(2)}, u32[]{:S(2)}) collective-permute-start(bf16[128,384]{1,0:T(8,128)(2,1)S(1)} %get-tuple-element.86), channel_id=1, source_target_pairs={{0,3},{1,0},{2,1},{3,2},{4,7},{5,4},{6,5},{7,6},{8,11},{9,8},{10,9... | collective-permute-start | bytes 294920 | tf_op jit(solution)/shard_map/ppermute | solution.py:579
  74.4 8.8 %collective-permute-start.16 = (bf16[128,384]{1,0:T(8,128)(2,1)S(1)}, bf16[128,384]{1,0:T(8,128)(2,1)S(1)}, u32[]{:S(2)}, u32[]{:S(2)}) collective-permute-start(bf16[128,384]{1,0:T(8,128)(2,1)S(1)} %get-tuple-element.82), channel_id=1, source_target_pairs={{0,3},{1,0},{2,1},{3,2},{4,7},{5,4},{6,5},{7,6},{8,11},{9,8},{10,9... | collective-permute-start | bytes 294920 | tf_op jit(solution)/shard_map/ppermute | solution.py:579
  74.4 8.8 %collective-permute-start.20 = (bf16[128,384]{1,0:T(8,128)(2,1)S(1)}, bf16[128,384]{1,0:T(8,128)(2,1)S(1)}, u32[]{:S(2)}, u32[]{:S(2)}) collective-permute-start(bf16[128,384]{1,0:T(8,128)(2,1)S(1)} %get-tuple-element.88), channel_id=1, source_target_pairs={{0,1},{1,2},{2,3},{3,0},{4,5},{5,6},{6,7},{7,4},{8,9},{9,10},{10,1... | collective-permute-start | bytes 294920 | tf_op jit(solution)/shard_map/ppermute | solution.py:579
  75.9 7.3 %collective-permute-start.19 = (bf16[128,384]{1,0:T(8,128)(2,1)S(1)}, bf16[128,384]{1,0:T(8,128)(2,1)S(1)}, u32[]{:S(2)}, u32[]{:S(2)}) collective-permute-start(bf16[128,384]{1,0:T(8,128)(2,1)S(1)} %get-tuple-element.87), channel_id=1, source_target_pairs={{0,1},{1,2},{2,3},{3,0},{4,5},{5,6},{6,7},{7,4},{8,9},{9,10},{10,1... | collective-permute-start | bytes 294920 | tf_op jit(solution)/shard_map/ppermute | solution.py:579
  76.0 7.2 %collective-permute-start.21 = (bf16[128,384]{1,0:T(8,128)(2,1)S(1)}, bf16[128,384]{1,0:T(8,128)(2,1)S(1)}, u32[]{:S(2)}, u32[]{:S(2)}) collective-permute-start(bf16[128,384]{1,0:T(8,128)(2,1)S(1)} %get-tuple-element.89), channel_id=1, source_target_pairs={{0,3},{1,0},{2,1},{3,2},{4,7},{5,4},{6,5},{7,6},{8,11},{9,8},{10,9... | collective-permute-start | bytes 294920 | tf_op jit(solution)/shard_map/ppermute | solution.py:579
  (8 other events, 97.2 us)

commit v7 on v5

--- a/solution.py
+++ b/solution.py
@@ -407,10 +407,10 @@
 
 
 def weight_blocks(k, weights):
-    width = weights[0].shape[1]
+    width, count = (weights[0].shape[1], len(weights))
 
     def body(*refs):
-        copies = block_copies(k, refs[:3], refs[3:6], refs[6], 0)
+        copies = block_copies(k, refs[:count], refs[count : 2 * count], refs[2 * count], 0)
         for copy in copies:
             copy.start()
         for copy in copies:
@@ -418,12 +418,12 @@
 
     return call(
         body,
-        [((width, width), bf16)] * 3,
+        [((width, width), bf16)] * count,
         1,
         1024 * 1024,
-        in_specs=[pl.BlockSpec(memory_space=pltpu.HBM)] * 3,
-        out_specs=[VMEM] * 3,
-        scratch_shapes=[pltpu.SemaphoreType.DMA((3,))],
+        in_specs=[pl.BlockSpec(memory_space=pltpu.HBM)] * count,
+        out_specs=[VMEM] * count,
+        scratch_shapes=[pltpu.SemaphoreType.DMA((count,))],
     )(*(in_hbm(w) for w in weights))
 
 
@@ -527,21 +527,21 @@
 
 def per_device(latents, w_query, w_key, w_value, w_out, head_gain, grad_out):
     gain = head_gain.reshape(1, -1)
+    grads = [grad_out] + [to_owner(grad_out, k) for k in (1, 2, 3)]
     fk, v, state = key_value(latents, w_key, w_value)
     pair = swap(state)
     chip = pair_sum(state, pair)
     got = y_gather(False, chip)
-    grad_held = hold(grad_out, chip)
-    grads = [grad_out] + [to_owner(grad_held, k) for k in (1, 2, 3)]
     planes = plane_sums(False, chip, got)
     fq, raw_local = query_local(hold(latents, planes), w_query, fk, v)
     up = upstream_of(grads, w_out, gain)
     planes = plane_exchange(planes)
     mine = before_chip(False, planes)
     got = swap(mine)
+    blocks = weight_blocks(2, (hold(w_query, mine), w_key))
     attn, draw, before, state = normed(mine, got, pair, fq, raw_local, up, gain)
     weights = (w_query, w_key, w_value)
-    blocks = weight_blocks(2, (hold(w_query, state), w_key, w_value))
+    blocks = blocks + weight_blocks(2, (hold(w_value, state),))
     pair = swap(state)
     chip = pair_sum(state, pair)
     got = y_gather(True, chip)

time: 84.4 us -> 83.5 us (0.989)
  waiting for transfers between devices: 22.2 us -> 15.5 us
  starting transfers between devices: 40 us -> 44.9 us
  Pallas kernels: 19.4 us -> 20.3 us
    ppermute x9, starting transfers between devices: 8.4 us -> 13.3 us  [to_owner(): return lax.ppermute(part, 'mp', shifts(4, k))]
    all_to_all x2, waiting for transfers between devices: 6.71 us -> 2.11 us  [plane_exchange(): return lax.all_to_all(planes, 'seq_0', 0, 0, tiled=True)]
    ppermute x9, waiting for transfers between devices: 8.82 us -> 6.71 us  [to_owner(): return lax.ppermute(part, 'mp', shifts(4, k))]
    pallas_call x1 -> x2, Pallas kernels: 1.16 us -> 2.05 us  [weight_blocks(): call(body, [((width, width), bf16)] * count, 1, 1024 * 1024, in_specs=[pl...]
  transfers between devices with their start and end apart: 21 -> 21, of which waited for: 12 -> 12; matrix products, arithmetic and copies ran while one was open for 1% -> 1% of each run, Pallas kernels for 17% -> 18%
where the time goes in v7:
time: 83.5 us; the launch traced here: 83.1 us
  starting transfers between devices  44.9 us (54%)
  Pallas kernels  20.3 us (24%)
  waiting for transfers between devices  15.5 us (19%)
  other arithmetic  1.56 us (2%)
    all_to_all x2, starting transfers between devices, plane_exchange(): return lax.all_to_all(planes, 'seq_0', 0, 0, tiled=True)  14.8 us
    ppermute x9, starting transfers between devices, to_owner(): return lax.ppermute(part, 'mp', shifts(4, k))  13.3 us
    ppermute x4, starting transfers between devices, swap(): return lax.ppermute(x, 'seq_2', SWAP)  11.1 us
    ppermute x9, waiting for transfers between devices, to_owner(): return lax.ppermute(part, 'mp', shifts(4, k))  6.71 us
    ppermute x6, starting transfers between devices, y_gather(): got.append(lax.ppermute(chip, 'seq_1', shifts(4, -k if later else k)))  5.75 us
    ppermute x6, waiting for transfers between devices, y_gather(): got.append(lax.ppermute(chip, 'seq_1', shifts(4, -k if later else k)))  4.88 us
    pallas_call x8, Pallas kernels, plain(): call(body, outs, flops, moved, in_specs=[VMEM] * len(args), out_specs=[VM...  4.63 us
    pallas_call x2, Pallas kernels, other_parts(): call(body, [((rows, width), bf16)] * count, 6 * rows * width * width * co...  4.24 us
  transfers between devices with their start and end apart: 21, of which 12 were waited for; matrix products, arithmetic and copies ran while one was open for 1% of the time, Pallas kernels for 18%

profile of v7, /device:TPU:1, one launch (start us, length us, event | category | flops | bytes accessed | tf_op | source)
XLA Modules:
  0.0 83.1 jit_solution(15420311510794978258)
XLA Ops:
  0.7 3.1 %shard_map.86 = (bf16[256,384]{1,0:T(8,128)(2,1)S(1)}, bf16[256,384]{1,0:T(8,128)(2,1)S(1)}, bf16[192,128]{1,0:T(8,128)(2,1)S(1)}) custom-call(bf16[256,1536]{1,0:T(8,128)(2,1)} %x_hbm.2, bf16[1536,384]{1,0:T(8,128)(2,1)} %wk_hbm.5, bf16[1536,384]{1,0:T(8,128)(2,1)} %wv_hbm.5), custom_call_target="tpu_custom_call" | custom-call | flops 603979776 | bytes 3145728 | tf_op jit(solution)/shard_map/pallas_call | solution.py:195
  3.8 3.3 %collective-permute-start = (bf16[192,128]{1,0:T(8,128)(2,1)S(1)}, bf16[192,128]{1,0:T(8,128)(2,1)S(1)}, u32[]{:S(2)}, u32[]{:S(2)}) collective-permute-start(bf16[192,128]{1,0:T(8,128)(2,1)S(1)} %get-tuple-element.33.state_ref), channel_id=1, source_target_pairs={{0,4},{4,0},{1,5},{5,1},{2,6},{6,2},{3,7},{7,3},{8,12},{12,8},{9,1... | collective-permute-start | bytes 147464 | tf_op jit(solution)/shard_map/ppermute | solution.py:145
  10.7 2.5 %collective-permute-done.2.g2 = bf16[96,128]{1,0:T(8,128)(2,1)S(1)} collective-permute-done((bf16[96,128]{1,0:T(8,128)(2,1)S(1)}, bf16[96,128]{1,0:T(8,128)(2,1)S(1)}, u32[]{:S(2)}, u32[]{:S(2)}) %collective-permute-start.2) | collective-permute-done | bytes 24608 | tf_op jit(solution)/shard_map/ppermute | solution.py:151
  14.2 8.2 %all-to-all-start = ((bf16[8,96,128]{2,1,0:T(8,128)(2,1)}), bf16[8,96,128]{2,1,0:T(8,128)(2,1)S(1)}, u32[]{:S(2)}, u32[]{:S(2)}) async-start(bf16[8,96,128]{2,1,0:T(8,128)(2,1)} %shard_map.88), calls=%async_computation | async-start | bytes 393216 | tf_op jit(solution)/shard_map/all_to_all | solution.py:141
  22.4 2.8 %collective-permute-start.6 = (bf16[256,384]{1,0:T(8,128)(2,1)S(1)}, bf16[256,384]{1,0:T(8,128)(2,1)S(1)}, u32[]{:S(2)}, u32[]{:S(2)}) collective-permute-start(bf16[256,384]{1,0:T(8,128)(2,1)S(1)} %copy-done.2), channel_id=1, source_target_pairs={{0,2},{1,3},{2,0},{3,1},{4,6},{5,7},{6,4},{7,5},{8,10},{9,11},{10,... | collective-permute-start | bytes 589832 | tf_op jit(solution)/shard_map/ppermute | solution.py:521
  25.6 2.4 %collective-permute-start.7 = (bf16[256,384]{1,0:T(8,128)(2,1)S(1)}, bf16[256,384]{1,0:T(8,128)(2,1)S(1)}, u32[]{:S(2)}, u32[]{:S(2)}) collective-permute-start(bf16[256,384]{1,0:T(8,128)(2,1)S(1)} %copy-done.2), channel_id=1, source_target_pairs={{0,3},{1,0},{2,1},{3,2},{4,7},{5,4},{6,5},{7,6},{8,11},{9,8},{10,9... | collective-permute-start | bytes 589832 | tf_op jit(solution)/shard_map/ppermute | solution.py:521
  27.9 2.4 %shard_map.90 = (bf16[256,384]{1,0:T(8,128)(2,1)S(1)}, bf16[256,384]{1,0:T(8,128)(2,1)S(1)}) custom-call(bf16[256,1536]{1,0:T(8,128)(2,1)} %x_hbm.2, bf16[1536,384]{1,0:T(8,128)(2,1)S(1)} %copy-done, bf16[256,384]{1,0:T(8,128)(2,1)S(1)} %get-tuple-element.35.fk_ref, bf16[256,384]{1,0:T(8,128)(2,1)S(1)} %get-tuple-element.36.v_ref), custom_call_target="tpu_custom_call" | custom-call | flops 503316480 | bytes 3145728 | tf_op jit(solution)/shard_map/pallas_call | solution.py:253
  31.1 3.3 %collective-permute-start.4 = (bf16[96,128]{1,0:T(8,128)(2,1)S(1)}, bf16[96,128]{1,0:T(8,128)(2,1)S(1)}, u32[]{:S(2)}, u32[]{:S(2)}) collective-permute-start(bf16[96,128]{1,0:T(8,128)(2,1)S(1)} %shard_map.89.mine_ref), channel_id=1, source_target_pairs={{0,4},{4,0},{1,5},{5,1},{2,6},{6,2},{3,7},{7,3},{8,12},{12,8},{9,1... | collective-permute-start | bytes 73736 | tf_op jit(solution)/shard_map/ppermute | solution.py:145
  34.5 2.2 %shard_map.91.up_ref = bf16[256,384]{1,0:T(8,128)(2,1)S(1)} custom-call(bf16[256,384]{1,0:T(8,128)(2,1)S(1)} %copy-done.2, bf16[256,384]{1,0:T(8,128)(2,1)S(1)} %collective-permute-done.5.g1, bf16[256,384]{1,0:T(8,128)(2,1)S(1)} %collective-permute-done.6.g2, bf16[256,384]{1,0:T(8,128)(2,1)S(1)} %collective-permute-done.7.g3, bf16[384,1536]{1,0:T(8,128)(2,1)} %w_ref.1, ...), custom_call_target="tpu_custom_call" | custom-call | flops 301989888 | bytes 3145728 | tf_op jit(solution)/shard_map/pallas_call | solution.py:283
  37.7 1.5 %collective-permute-start.8 = (bf16[192,128]{1,0:T(8,128)(2,1)S(1)}, bf16[192,128]{1,0:T(8,128)(2,1)S(1)}, u32[]{:S(2)}, u32[]{:S(2)}) collective-permute-start(bf16[192,128]{1,0:T(8,128)(2,1)S(1)} %get-tuple-element.40.state_ref), channel_id=1, source_target_pairs={{0,4},{4,0},{1,5},{5,1},{2,6},{6,2},{3,7},{7,3},{8,12},{12,8},{9,1... | collective-permute-start | bytes 147464 | tf_op jit(solution)/shard_map/ppermute | solution.py:145
  40.1 1.6 %collective-permute-start.10 = (bf16[96,128]{1,0:T(8,128)(2,1)S(1)}, bf16[96,128]{1,0:T(8,128)(2,1)S(1)}, u32[]{:S(2)}, u32[]{:S(2)}) collective-permute-start(bf16[96,128]{1,0:T(8,128)(2,1)S(1)} %shard_map.93.chip_ref), channel_id=1, source_target_pairs={{0,16},{8,24},{16,0},{24,8},{1,17},{9,25},{17,1},{25,9},{2,18},{10... | collective-permute-start | bytes 73736 | tf_op jit(solution)/shard_map/ppermute | solution.py:151
  41.8 1.9 %collective-permute-start.9 = (bf16[96,128]{1,0:T(8,128)(2,1)S(1)}, bf16[96,128]{1,0:T(8,128)(2,1)S(1)}, u32[]{:S(2)}, u32[]{:S(2)}) collective-permute-start(bf16[96,128]{1,0:T(8,128)(2,1)S(1)} %shard_map.93.chip_ref), channel_id=1, source_target_pairs={{0,24},{8,0},{16,8},{24,16},{1,25},{9,1},{17,9},{25,17},{2,26},{10... | collective-permute-start | bytes 73736 | tf_op jit(solution)/shard_map/ppermute | solution.py:151
  45.8 6.6 %all-to-all-start.1 = ((bf16[8,96,128]{2,1,0:T(8,128)(2,1)}), bf16[8,96,128]{2,1,0:T(8,128)(2,1)S(1)}, u32[]{:S(2)}, u32[]{:S(2)}) async-start(bf16[8,96,128]{2,1,0:T(8,128)(2,1)} %shard_map.95), calls=%async_computation.1 | async-start | bytes 393216 | tf_op jit(solution)/shard_map/all_to_all | solution.py:141
  52.4 1.3 %shard_map.94 = (bf16[256,384]{1,0:T(8,128)(2,1)}, bf16[256,384]{1,0:T(8,128)(2,1)}, bf16[256,384]{1,0:T(8,128)(2,1)}, bf16[256,384]{1,0:T(8,128)(2,1)}) custom-call(bf16[256,384]{1,0:T(8,128)(2,1)S(1)} %get-tuple-element.41.attn_ref, bf16[384,1536]{1,0:T(8,128)(2,1)S(1)} %copy-done.1), custom_call_target="tpu_custom_call" | custom-call | flops 301989888 | bytes 2097152 | tf_op jit(solution)/shard_map/pallas_call | solution.py:48
  53.7 2.7 %collective-permute-start.14 = (bf16[256,384]{1,0:T(8,128)(2,1)}, bf16[256,384]{1,0:T(8,128)(2,1)S(1)}, u32[]{:S(2)}, u32[]{:S(2)}) collective-permute-start(bf16[256,384]{1,0:T(8,128)(2,1)} %get-tuple-element.48), channel_id=1, source_target_pairs={{0,3},{1,0},{2,1},{3,2},{4,7},{5,4},{6,5},{7,6},{8,11},{9,8},{10,9... | collective-permute-start | bytes 589832 | tf_op jit(solution)/shard_map/ppermute | solution.py:521
  56.4 1.2 %collective-permute-start.12 = (bf16[256,384]{1,0:T(8,128)(2,1)}, bf16[256,384]{1,0:T(8,128)(2,1)S(1)}, u32[]{:S(2)}, u32[]{:S(2)}) collective-permute-start(bf16[256,384]{1,0:T(8,128)(2,1)} %get-tuple-element.44), channel_id=1, source_target_pairs={{0,2},{1,3},{2,0},{3,1},{4,6},{5,7},{6,4},{7,5},{8,10},{9,11},{10,... | collective-permute-start | bytes 589832 | tf_op jit(solution)/shard_map/ppermute | solution.py:521
  59.7 1.4 %all-to-all-done.1.planes_ref = bf16[8,96,128]{2,1,0:T(8,128)(2,1)S(1)} async-done(((bf16[8,96,128]{2,1,0:T(8,128)(2,1)}), bf16[8,96,128]{2,1,0:T(8,128)(2,1)S(1)}, u32[]{:S(2)}, u32[]{:S(2)}) %all-to-all-start.1) | async-done | bytes 196640 | tf_op jit(solution)/shard_map/all_to_all | solution.py:141
  61.1 3.0 %collective-permute-start.15 = (bf16[96,128]{1,0:T(8,128)(2,1)S(1)}, bf16[96,128]{1,0:T(8,128)(2,1)S(1)}, u32[]{:S(2)}, u32[]{:S(2)}) collective-permute-start(bf16[96,128]{1,0:T(8,128)(2,1)S(1)} %shard_map.97.mine_ref), channel_id=1, source_target_pairs={{0,4},{4,0},{1,5},{5,1},{2,6},{6,2},{3,7},{7,3},{8,12},{12,8},{9,1... | collective-permute-start | bytes 73736 | tf_op jit(solution)/shard_map/ppermute | solution.py:145
  64.1 1.8 %shard_map.96 = (bf16[256,384]{1,0:T(8,128)(2,1)S(1)}, bf16[256,384]{1,0:T(8,128)(2,1)S(1)}, bf16[256,384]{1,0:T(8,128)(2,1)S(1)}) custom-call(bf16[256,384]{1,0:T(8,128)(2,1)S(1)} %get-tuple-element.37.fq_ref, bf16[256,384]{1,0:T(8,128)(2,1)S(1)} %get-tuple-element.35.fk_ref, bf16[256,384]{1,0:T(8,128)(2,1)S(1)} %get-tuple-element.36.v_ref, ...), custom_call_target="tpu_custom_call" | custom-call | flops 603979776 | bytes 3145728 | tf_op jit(solution)/shard_map/pallas_call | solution.py:48
  66.6 2.5 %shard_map.102 = (bf16[256,384]{1,0:T(8,128)(2,1)S(1)}, bf16[256,384]{1,0:T(8,128)(2,1)S(1)}) custom-call(bf16[256,384]{1,0:T(8,128)(2,1)S(1)} %get-tuple-element.52.dq_ref, bf16[256,384]{1,0:T(8,128)(2,1)S(1)} %get-tuple-element.59.dk_ref, bf16[256,384]{1,0:T(8,128)(2,1)S(1)} %get-tuple-element.60.dv_ref, bf16[1536,384]{1,0:T(8,128)(2,1)} %wq_hbm.3, ...), custom_call_target="tpu_custom_call" | custom-call | flops 452984832 | bytes 2097152 | tf_op jit(solution)/shard_map/pallas_call | solution.py:499
  70.2 1.8 %collective-permute-start.18 = (bf16[256,384]{1,0:T(8,128)(2,1)S(1)}, bf16[256,384]{1,0:T(8,128)(2,1)S(1)}, u32[]{:S(2)}, u32[]{:S(2)}) collective-permute-start(bf16[256,384]{1,0:T(8,128)(2,1)S(1)} %get-tuple-element.63), channel_id=1, source_target_pairs={{0,3},{1,0},{2,1},{3,2},{4,7},{5,4},{6,5},{7,6},{8,11},{9,8},{10,9... | collective-permute-start | bytes 589832 | tf_op jit(solution)/shard_map/ppermute | solution.py:521
  73.9 1.7 %shard_map.101 = bf16[256,384]{1,0:T(8,128)(2,1)S(1)} custom-call(bf16[256,384]{1,0:T(8,128)(2,1)S(1)} %get-tuple-element.52.dq_ref, bf16[256,384]{1,0:T(8,128)(2,1)S(1)} %get-tuple-element.59.dk_ref, bf16[256,384]{1,0:T(8,128)(2,1)S(1)} %get-tuple-element.60.dv_ref, bf16[1536,384]{1,0:T(8,128)(2,1)} %wq_hbm.3, bf16[1536,384]{1,0:T(8,128)(2,1)} %wk_hbm.5, ...), custom_call_target="tpu_custom_call" | custom-call | flops 226492416 | bytes 1048576 | tf_op jit(solution)/shard_map/pallas_call | solution.py:499
  75.6 1.3 %collective-permute-done.17 = bf16[256,384]{1,0:T(8,128)(2,1)S(1)} collective-permute-done((bf16[256,384]{1,0:T(8,128)(2,1)S(1)}, bf16[256,384]{1,0:T(8,128)(2,1)S(1)}, u32[]{:S(2)}, u32[]{:S(2)}) %collective-permute-start.17) | collective-permute-done | bytes 196640 | tf_op jit(solution)/shard_map/ppermute | solution.py:521
  76.9 5.4 %collective-permute-done.16 = bf16[256,384]{1,0:T(8,128)(2,1)S(1)} collective-permute-done((bf16[256,384]{1,0:T(8,128)(2,1)S(1)}, bf16[256,384]{1,0:T(8,128)(2,1)S(1)}, u32[]{:S(2)}, u32[]{:S(2)}) %collective-permute-start.16) | collective-permute-done | bytes 196640 | tf_op jit(solution)/shard_map/ppermute | solution.py:521
  (48 shorter events, 16.4 us)
Async XLA Ops:
  0.6 21.8 %copy-start.2 = (bf16[256,384]{1,0:T(8,128)(2,1)S(1)}, bf16[256,384]{1,0:T(8,128)(2,1)}, u32[]{:S(2)}) copy-start(bf16[256,384]{1,0:T(8,128)(2,1)} %g0.1) | copy-start | bytes 589828
  0.6 27.3 %copy-start.4 = (f32[384]{0:T(512)S(1)}, f32[384]{0:T(512)}, u32[]{:S(2)}) copy-start(f32[384]{0:T(512)} %param.12) | copy-start | bytes 4612
  0.6 27.3 %copy-start = (bf16[1536,384]{1,0:T(8,128)(2,1)S(1)}, bf16[1536,384]{1,0:T(8,128)(2,1)}, u32[]{:S(2)}) copy-start(bf16[1536,384]{1,0:T(8,128)(2,1)} %wq_hbm.3) | copy-start | bytes 3538948
  3.8 4.2 %collective-permute-start = (bf16[192,128]{1,0:T(8,128)(2,1)S(1)}, bf16[192,128]{1,0:T(8,128)(2,1)S(1)}, u32[]{:S(2)}, u32[]{:S(2)}) collective-permute-start(bf16[192,128]{1,0:T(8,128)(2,1)S(1)} %get-tuple-element.33.state_ref), channel_id=1, source_target_pairs={{0,4},{4,0},{1,5},{5,1},{2,6},{6,2},{3,7},{7,3},{8,12},{12,8},{9,1... | collective-permute-start | bytes 147464 | tf_op jit(solution)/shard_map/ppermute | solution.py:145
  8.0 2.8 %collective-permute-start.3 = (bf16[96,128]{1,0:T(8,128)(2,1)S(1)}, bf16[96,128]{1,0:T(8,128)(2,1)S(1)}, u32[]{:S(2)}, u32[]{:S(2)}) collective-permute-start(bf16[96,128]{1,0:T(8,128)(2,1)S(1)} %shard_map.87.chip_ref), channel_id=1, source_target_pairs={{0,24},{8,0},{16,8},{24,16},{1,25},{9,1},{17,9},{25,17},{2,26},{10... | collective-permute-start | bytes 73736 | tf_op jit(solution)/shard_map/ppermute | solution.py:151
  9.1 4.2 %collective-permute-start.2 = (bf16[96,128]{1,0:T(8,128)(2,1)S(1)}, bf16[96,128]{1,0:T(8,128)(2,1)S(1)}, u32[]{:S(2)}, u32[]{:S(2)}) collective-permute-start(bf16[96,128]{1,0:T(8,128)(2,1)S(1)} %shard_map.87.chip_ref), channel_id=1, source_target_pairs={{0,16},{8,24},{16,0},{24,8},{1,17},{9,25},{17,1},{25,9},{2,18},{10... | collective-permute-start | bytes 73736 | tf_op jit(solution)/shard_map/ppermute | solution.py:151
  9.4 4.1 %collective-permute-start.1 = (bf16[96,128]{1,0:T(8,128)(2,1)S(1)}, bf16[96,128]{1,0:T(8,128)(2,1)S(1)}, u32[]{:S(2)}, u32[]{:S(2)}) collective-permute-start(bf16[96,128]{1,0:T(8,128)(2,1)S(1)} %shard_map.87.chip_ref), channel_id=1, source_target_pairs={{0,8},{8,16},{16,24},{24,0},{1,9},{9,17},{17,25},{25,1},{2,10},{10... | collective-permute-start | bytes 73736 | tf_op jit(solution)/shard_map/ppermute | solution.py:151
  14.2 16.9 %all-to-all-start = ((bf16[8,96,128]{2,1,0:T(8,128)(2,1)}), bf16[8,96,128]{2,1,0:T(8,128)(2,1)S(1)}, u32[]{:S(2)}, u32[]{:S(2)}) async-start(bf16[8,96,128]{2,1,0:T(8,128)(2,1)} %shard_map.88), calls=%async_computation | async-start | bytes 393216 | tf_op jit(solution)/shard_map/all_to_all | solution.py:141
  22.4 12.1 %collective-permute-start.6 = (bf16[256,384]{1,0:T(8,128)(2,1)S(1)}, bf16[256,384]{1,0:T(8,128)(2,1)S(1)}, u32[]{:S(2)}, u32[]{:S(2)}) collective-permute-start(bf16[256,384]{1,0:T(8,128)(2,1)S(1)} %copy-done.2), channel_id=1, source_target_pairs={{0,2},{1,3},{2,0},{3,1},{4,6},{5,7},{6,4},{7,5},{8,10},{9,11},{10,... | collective-permute-start | bytes 589832 | tf_op jit(solution)/shard_map/ppermute | solution.py:521
  25.2 9.2 %collective-permute-start.5 = (bf16[256,384]{1,0:T(8,128)(2,1)S(1)}, bf16[256,384]{1,0:T(8,128)(2,1)S(1)}, u32[]{:S(2)}, u32[]{:S(2)}) collective-permute-start(bf16[256,384]{1,0:T(8,128)(2,1)S(1)} %copy-done.2), channel_id=1, source_target_pairs={{0,1},{1,2},{2,3},{3,0},{4,5},{5,6},{6,7},{7,4},{8,9},{9,10},{10,1... | collective-permute-start | bytes 589832 | tf_op jit(solution)/shard_map/ppermute | solution.py:521
  25.6 8.9 %collective-permute-start.7 = (bf16[256,384]{1,0:T(8,128)(2,1)S(1)}, bf16[256,384]{1,0:T(8,128)(2,1)S(1)}, u32[]{:S(2)}, u32[]{:S(2)}) collective-permute-start(bf16[256,384]{1,0:T(8,128)(2,1)S(1)} %copy-done.2), channel_id=1, source_target_pairs={{0,3},{1,0},{2,1},{3,2},{4,7},{5,4},{6,5},{7,6},{8,11},{9,8},{10,9... | collective-permute-start | bytes 589832 | tf_op jit(solution)/shard_map/ppermute | solution.py:521
  31.1 5.5 %collective-permute-start.4 = (bf16[96,128]{1,0:T(8,128)(2,1)S(1)}, bf16[96,128]{1,0:T(8,128)(2,1)S(1)}, u32[]{:S(2)}, u32[]{:S(2)}) collective-permute-start(bf16[96,128]{1,0:T(8,128)(2,1)S(1)} %shard_map.89.mine_ref), channel_id=1, source_target_pairs={{0,4},{4,0},{1,5},{5,1},{2,6},{6,2},{3,7},{7,3},{8,12},{12,8},{9,1... | collective-permute-start | bytes 73736 | tf_op jit(solution)/shard_map/ppermute | solution.py:145
  37.7 2.4 %collective-permute-start.8 = (bf16[192,128]{1,0:T(8,128)(2,1)S(1)}, bf16[192,128]{1,0:T(8,128)(2,1)S(1)}, u32[]{:S(2)}, u32[]{:S(2)}) collective-permute-start(bf16[192,128]{1,0:T(8,128)(2,1)S(1)} %get-tuple-element.40.state_ref), channel_id=1, source_target_pairs={{0,4},{4,0},{1,5},{5,1},{2,6},{6,2},{3,7},{7,3},{8,12},{12,8},{9,1... | collective-permute-start | bytes 147464 | tf_op jit(solution)/shard_map/ppermute | solution.py:145
  40.0 4.0 %collective-permute-start.11 = (bf16[96,128]{1,0:T(8,128)(2,1)S(1)}, bf16[96,128]{1,0:T(8,128)(2,1)S(1)}, u32[]{:S(2)}, u32[]{:S(2)}) collective-permute-start(bf16[96,128]{1,0:T(8,128)(2,1)S(1)} %shard_map.93.chip_ref), channel_id=1, source_target_pairs={{0,8},{8,16},{16,24},{24,0},{1,9},{9,17},{17,25},{25,1},{2,10},{10... | collective-permute-start | bytes 73736 | tf_op jit(solution)/shard_map/ppermute | solution.py:151
  40.1 4.3 %collective-permute-start.10 = (bf16[96,128]{1,0:T(8,128)(2,1)S(1)}, bf16[96,128]{1,0:T(8,128)(2,1)S(1)}, u32[]{:S(2)}, u32[]{:S(2)}) collective-permute-start(bf16[96,128]{1,0:T(8,128)(2,1)S(1)} %shard_map.93.chip_ref), channel_id=1, source_target_pairs={{0,16},{8,24},{16,0},{24,8},{1,17},{9,25},{17,1},{25,9},{2,18},{10... | collective-permute-start | bytes 73736 | tf_op jit(solution)/shard_map/ppermute | solution.py:151
  41.8 3.4 %collective-permute-start.9 = (bf16[96,128]{1,0:T(8,128)(2,1)S(1)}, bf16[96,128]{1,0:T(8,128)(2,1)S(1)}, u32[]{:S(2)}, u32[]{:S(2)}) collective-permute-start(bf16[96,128]{1,0:T(8,128)(2,1)S(1)} %shard_map.93.chip_ref), channel_id=1, source_target_pairs={{0,24},{8,0},{16,8},{24,16},{1,25},{9,1},{17,9},{25,17},{2,26},{10... | collective-permute-start | bytes 73736 | tf_op jit(solution)/shard_map/ppermute | solution.py:151
  45.8 15.2 %all-to-all-start.1 = ((bf16[8,96,128]{2,1,0:T(8,128)(2,1)}), bf16[8,96,128]{2,1,0:T(8,128)(2,1)S(1)}, u32[]{:S(2)}, u32[]{:S(2)}) async-start(bf16[8,96,128]{2,1,0:T(8,128)(2,1)} %shard_map.95), calls=%async_computation.1 | async-start | bytes 393216 | tf_op jit(solution)/shard_map/all_to_all | solution.py:141
  53.7 18.3 %collective-permute-start.14 = (bf16[256,384]{1,0:T(8,128)(2,1)}, bf16[256,384]{1,0:T(8,128)(2,1)S(1)}, u32[]{:S(2)}, u32[]{:S(2)}) collective-permute-start(bf16[256,384]{1,0:T(8,128)(2,1)} %get-tuple-element.48), channel_id=1, source_target_pairs={{0,3},{1,0},{2,1},{3,2},{4,7},{5,4},{6,5},{7,6},{8,11},{9,8},{10,9... | collective-permute-start | bytes 589832 | tf_op jit(solution)/shard_map/ppermute | solution.py:521
  56.4 16.7 %collective-permute-start.13 = (bf16[256,384]{1,0:T(8,128)(2,1)}, bf16[256,384]{1,0:T(8,128)(2,1)S(1)}, u32[]{:S(2)}, u32[]{:S(2)}) collective-permute-start(bf16[256,384]{1,0:T(8,128)(2,1)} %get-tuple-element.46), channel_id=1, source_target_pairs={{0,1},{1,2},{2,3},{3,0},{4,5},{5,6},{6,7},{7,4},{8,9},{9,10},{10,1... | collective-permute-start | bytes 589832 | tf_op jit(solution)/shard_map/ppermute | solution.py:521
  56.4 16.7 %collective-permute-start.12 = (bf16[256,384]{1,0:T(8,128)(2,1)}, bf16[256,384]{1,0:T(8,128)(2,1)S(1)}, u32[]{:S(2)}, u32[]{:S(2)}) collective-permute-start(bf16[256,384]{1,0:T(8,128)(2,1)} %get-tuple-element.44), channel_id=1, source_target_pairs={{0,2},{1,3},{2,0},{3,1},{4,6},{5,7},{6,4},{7,5},{8,10},{9,11},{10,... | collective-permute-start | bytes 589832 | tf_op jit(solution)/shard_map/ppermute | solution.py:521
  61.1 4.8 %collective-permute-start.15 = (bf16[96,128]{1,0:T(8,128)(2,1)S(1)}, bf16[96,128]{1,0:T(8,128)(2,1)S(1)}, u32[]{:S(2)}, u32[]{:S(2)}) collective-permute-start(bf16[96,128]{1,0:T(8,128)(2,1)S(1)} %shard_map.97.mine_ref), channel_id=1, source_target_pairs={{0,4},{4,0},{1,5},{5,1},{2,6},{6,2},{3,7},{7,3},{8,12},{12,8},{9,1... | collective-permute-start | bytes 73736 | tf_op jit(solution)/shard_map/ppermute | solution.py:145
  69.2 7.7 %collective-permute-start.17 = (bf16[256,384]{1,0:T(8,128)(2,1)S(1)}, bf16[256,384]{1,0:T(8,128)(2,1)S(1)}, u32[]{:S(2)}, u32[]{:S(2)}) collective-permute-start(bf16[256,384]{1,0:T(8,128)(2,1)S(1)} %get-tuple-element.62), channel_id=1, source_target_pairs={{0,1},{1,2},{2,3},{3,0},{4,5},{5,6},{6,7},{7,4},{8,9},{9,10},{10,1... | collective-permute-start | bytes 589832 | tf_op jit(solution)/shard_map/ppermute | solution.py:521
  70.2 6.7 %collective-permute-start.18 = (bf16[256,384]{1,0:T(8,128)(2,1)S(1)}, bf16[256,384]{1,0:T(8,128)(2,1)S(1)}, u32[]{:S(2)}, u32[]{:S(2)}) collective-permute-start(bf16[256,384]{1,0:T(8,128)(2,1)S(1)} %get-tuple-element.63), channel_id=1, source_target_pairs={{0,3},{1,0},{2,1},{3,2},{4,7},{5,4},{6,5},{7,6},{8,11},{9,8},{10,9... | collective-permute-start | bytes 589832 | tf_op jit(solution)/shard_map/ppermute | solution.py:521
  72.0 10.3 %collective-permute-start.16 = (bf16[256,384]{1,0:T(8,128)(2,1)S(1)}, bf16[256,384]{1,0:T(8,128)(2,1)S(1)}, u32[]{:S(2)}, u32[]{:S(2)}) collective-permute-start(bf16[256,384]{1,0:T(8,128)(2,1)S(1)} %get-tuple-element.61), channel_id=1, source_target_pairs={{0,2},{1,3},{2,0},{3,1},{4,6},{5,7},{6,4},{7,5},{8,10},{9,11},{10,... | collective-permute-start | bytes 589832 | tf_op jit(solution)/shard_map/ppermute | solution.py:521
  (2 other events, 22.3 us)

commit v8 on v7

--- a/solution.py
+++ b/solution.py
@@ -406,11 +406,16 @@
     ]
 
 
-def weight_blocks(k, weights):
+def weight_blocks(which, weights):
     width, count = (weights[0].shape[1], len(weights))
+    total = count * len(which)
 
     def body(*refs):
-        copies = block_copies(k, refs[:count], refs[count : 2 * count], refs[2 * count], 0)
+        sources, targets, sem = (refs[:count], refs[count : count + total], refs[count + total])
+        copies = []
+        for i, k in enumerate(which):
+            at = i * count
+            copies += block_copies(k, sources, targets[at : at + count], sem, at)
         for copy in copies:
             copy.start()
         for copy in copies:
@@ -418,12 +423,12 @@
 
     return call(
         body,
-        [((width, width), bf16)] * count,
+        [((width, width), bf16)] * total,
         1,
         1024 * 1024,
         in_specs=[pl.BlockSpec(memory_space=pltpu.HBM)] * count,
-        out_specs=[VMEM] * count,
-        scratch_shapes=[pltpu.SemaphoreType.DMA((count,))],
+        out_specs=[VMEM] * total,
+        scratch_shapes=[pltpu.SemaphoreType.DMA((total,))],
     )(*(in_hbm(w) for w in weights))
 
 
@@ -471,43 +476,56 @@
     )(mine, got, pair, fk, v, dq, dk, dv, *blocks)
 
 
-def other_parts(which, dq, dk, dv, weights):
+def other_parts(dq, dk, dv, *blocks):
     rows, width = dq.shape
-    count = len(which)
-
-    def body(dq_ref, dk_ref, dv_ref, wq_hbm, wk_hbm, wv_hbm, *refs):
-        outs, blocks, sem = (refs[:count], refs[count], refs[count + 1])
-        copies = [
-            block_copies(
-                k, (wq_hbm, wk_hbm, wv_hbm), [blocks.at[3 * i + j] for j in range(3)], sem, 3 * i
-            )
-            for i, k in enumerate(which)
-        ]
-        for group in copies:
-            for copy in group:
-                copy.start()
-        for i, (group, ref) in enumerate(zip(copies, outs)):
-            for copy in group:
-                copy.wait()
+
+    def body(dq_ref, dk_ref, dv_ref, *refs):
+        for i, out_ref in enumerate(refs[len(blocks) :]):
             total = None
             for j, grad_ref in enumerate((dq_ref, dk_ref, dv_ref)):
-                part = mm(grad_ref[...], blocks[3 * i + j], NT)
+                part = mm(grad_ref[...], refs[3 * i + j][...], NT)
                 total = part if total is None else total + part
-            ref[...] = total.astype(bf16)
-
-    hbm = pl.BlockSpec(memory_space=pltpu.HBM)
-    return call(
+            out_ref[...] = total.astype(bf16)
+
+    count = len(blocks) // 3
+    return plain(
         body,
         [((rows, width), bf16)] * count,
         6 * rows * width * width * count,
         1024 * 1024 * count,
+        dq,
+        dk,
+        dv,
+        *blocks,
+    )
+
+
+def own_part(dq, dk, dv, weights):
+    rows, width = dq.shape
+
+    def body(dq_ref, dk_ref, dv_ref, wq_hbm, wk_hbm, wv_hbm, out_ref, blocks, sem):
+        copies = block_copies(0, (wq_hbm, wk_hbm, wv_hbm), [blocks.at[j] for j in range(3)], sem, 0)
+        for copy in copies:
+            copy.start()
+        total = jnp.zeros((rows, width), f32)
+        for j, grad_ref in enumerate((dq_ref, dk_ref, dv_ref)):
+            copies[j].wait()
+            total = total + mm(grad_ref[...], blocks[j], NT)
+        out_ref[...] = total.astype(bf16)
+
+    hbm = pl.BlockSpec(memory_space=pltpu.HBM)
+    return call(
+        body,
+        [((rows, width), bf16)],
+        6 * rows * width * width,
+        1024 * 1024,
         in_specs=[VMEM] * 3 + [hbm] * 3,
-        out_specs=[VMEM] * count,
+        out_specs=[VMEM],
         scratch_shapes=[
-            pltpu.VMEM((3 * count, width, width), bf16),
-            pltpu.SemaphoreType.DMA((3 * count,)),
+            pltpu.VMEM((3, width, width), bf16),
+            pltpu.SemaphoreType.DMA((3,)),
         ],
-    )(dq, dk, dv, *(in_hbm(w) for w in weights))
+    )(dq, dk, dv, *(in_hbm(w) for w in weights))[0]
 
 
 def add_up(parts):
@@ -527,21 +545,23 @@
 
 def per_device(latents, w_query, w_key, w_value, w_out, head_gain, grad_out):
     gain = head_gain.reshape(1, -1)
-    grads = [grad_out] + [to_owner(grad_out, k) for k in (1, 2, 3)]
     fk, v, state = key_value(latents, w_key, w_value)
     pair = swap(state)
+    grad1 = to_owner(hold(grad_out, state), 1)
     chip = pair_sum(state, pair)
     got = y_gather(False, chip)
+    grad_held = hold(grad_out, chip)
+    grads = [grad_out, grad1] + [to_owner(grad_held, k) for k in (2, 3)]
     planes = plane_sums(False, chip, got)
     fq, raw_local = query_local(hold(latents, planes), w_query, fk, v)
     up = upstream_of(grads, w_out, gain)
     planes = plane_exchange(planes)
     mine = before_chip(False, planes)
     got = swap(mine)
-    blocks = weight_blocks(2, (hold(w_query, mine), w_key))
+    blocks = weight_blocks((2,), (hold(w_query, mine), w_key))
     attn, draw, before, state = normed(mine, got, pair, fq, raw_local, up, gain)
     weights = (w_query, w_key, w_value)
-    blocks = blocks + weight_blocks(2, (hold(w_value, state),))
+    blocks = blocks + weight_blocks((2,), (hold(w_value, state),))
     pair = swap(state)
     chip = pair_sum(state, pair)
     got = y_gather(True, chip)
@@ -553,11 +573,12 @@
     planes = plane_exchange(planes)
     mine = before_chip(True, planes)
     got = swap(mine)
+    others = weight_blocks((1, 3), (hold(w_query, mine), w_key, w_value))
     dk, dv, l2 = first_part(mine, got, pair, fk, v, dq, dk_local, dv_local, blocks)
     l2 = to_owner(l2, 2)
-    l1, l3 = other_parts((1, 3), dq, dk, dv, weights)
+    l1, l3 = other_parts(dq, dk, dv, *others)
     l1, l3 = (to_owner(l1, 1), to_owner(l3, 3))
-    (l0,) = other_parts((0,), dq, dk, dv, weights)
+    l0 = own_part(dq, dk, dv, weights)
     return (add_up(branch), add_up([l0, l2, l1, l3]))
 
 

time: 83.5 us -> 84.6 us (1.013)
    pallas_call x4, Pallas kernels: 6.29 us -> 5.35 us  [the longest x3 3.52 us: weight_blocks(): call(body, [((width, width), bf16)] * total, 1, 1024 * 1024, in_specs=[pl...]
    pallas_call x8 -> x9, Pallas kernels: 4.63 us -> 5.53 us  [plain(): call(body, outs, flops, moved, in_specs=[VMEM] * len(args), out_specs=[VM...]
  transfers between devices with their start and end apart: 21 -> 21, of which waited for: 12 -> 11; matrix products, arithmetic and copies ran while one was open for 1% -> 1% of each run, Pallas kernels for 18% -> 18%
where the time goes in v8:
time: 84.6 us; the launch traced here: 84.2 us
  starting transfers between devices  45.2 us (53%)
  Pallas kernels  20.3 us (24%)
  waiting for transfers between devices  16.3 us (19%)
  other arithmetic  1.56 us (2%)
    all_to_all x2, starting transfers between devices, plane_exchange(): return lax.all_to_all(planes, 'seq_0', 0, 0, tiled=True)  14.8 us
    ppermute x9, starting transfers between devices, to_owner(): return lax.ppermute(part, 'mp', shifts(4, k))  12.6 us
    ppermute x4, starting transfers between devices, swap(): return lax.ppermute(x, 'seq_2', SWAP)  11.7 us
    ppermute x9, waiting for transfers between devices, to_owner(): return lax.ppermute(part, 'mp', shifts(4, k))  6.32 us
    ppermute x6, starting transfers between devices, y_gather(): got.append(lax.ppermute(chip, 'seq_1', shifts(4, -k if later else k)))  6.11 us
    pallas_call x9, Pallas kernels, plain(): call(body, outs, flops, moved, in_specs=[VMEM] * len(args), out_specs=[VM...  5.53 us
    ppermute x6, waiting for transfers between devices, y_gather(): got.append(lax.ppermute(chip, 'seq_1', shifts(4, -k if later else k)))  5.41 us
    pallas_call x3, Pallas kernels, weight_blocks(): call(body, [((width, width), bf16)] * total, 1, 1024 * 1024, in_specs=[pl...  3.52 us
  transfers between devices with their start and end apart: 21, of which 11 were waited for; matrix products, arithmetic and copies ran while one was open for 1% of the time, Pallas kernels for 18%

profile of v8, /device:TPU:1, one launch (start us, length us, event | category | flops | bytes accessed | tf_op | source)
XLA Modules:
  0.0 84.2 jit_solution(11243704153935721885)
XLA Ops:
  0.7 3.1 %shard_map.86 = (bf16[256,384]{1,0:T(8,128)(2,1)S(1)}, bf16[256,384]{1,0:T(8,128)(2,1)S(1)}, bf16[192,128]{1,0:T(8,128)(2,1)S(1)}) custom-call(bf16[256,1536]{1,0:T(8,128)(2,1)} %x_hbm.2, bf16[1536,384]{1,0:T(8,128)(2,1)} %refs_1_.3, bf16[1536,384]{1,0:T(8,128)(2,1)} %refs_2_.1), custom_call_target="tpu_custom_call" | custom-call | flops 603979776 | bytes 3145728 | tf_op jit(solution)/shard_map/pallas_call | solution.py:195
  3.8 3.3 %collective-permute-start = (bf16[192,128]{1,0:T(8,128)(2,1)S(1)}, bf16[192,128]{1,0:T(8,128)(2,1)S(1)}, u32[]{:S(2)}, u32[]{:S(2)}) collective-permute-start(bf16[192,128]{1,0:T(8,128)(2,1)S(1)} %get-tuple-element.42.state_ref), channel_id=1, source_target_pairs={{0,4},{4,0},{1,5},{5,1},{2,6},{6,2},{3,7},{7,3},{8,12},{12,8},{9,1... | collective-permute-start | bytes 147464 | tf_op jit(solution)/shard_map/ppermute | solution.py:145
  8.0 2.2 %collective-permute-start.2 = (bf16[96,128]{1,0:T(8,128)(2,1)S(1)}, bf16[96,128]{1,0:T(8,128)(2,1)S(1)}, u32[]{:S(2)}, u32[]{:S(2)}) collective-permute-start(bf16[96,128]{1,0:T(8,128)(2,1)S(1)} %shard_map.87.chip_ref), channel_id=1, source_target_pairs={{0,16},{8,24},{16,0},{24,8},{1,17},{9,25},{17,1},{25,9},{2,18},{10... | collective-permute-start | bytes 73736 | tf_op jit(solution)/shard_map/ppermute | solution.py:151
  13.9 8.2 %all-to-all-start = ((bf16[8,96,128]{2,1,0:T(8,128)(2,1)}), bf16[8,96,128]{2,1,0:T(8,128)(2,1)S(1)}, u32[]{:S(2)}, u32[]{:S(2)}) async-start(bf16[8,96,128]{2,1,0:T(8,128)(2,1)} %shard_map.88), calls=%async_computation | async-start | bytes 393216 | tf_op jit(solution)/shard_map/all_to_all | solution.py:141
  23.4 2.5 %collective-permute-start.6 = (bf16[256,384]{1,0:T(8,128)(2,1)S(1)}, bf16[256,384]{1,0:T(8,128)(2,1)S(1)}, u32[]{:S(2)}, u32[]{:S(2)}) collective-permute-start(bf16[256,384]{1,0:T(8,128)(2,1)S(1)} %copy-done.2), channel_id=1, source_target_pairs={{0,2},{1,3},{2,0},{3,1},{4,6},{5,7},{6,4},{7,5},{8,10},{9,11},{10,... | collective-permute-start | bytes 589832 | tf_op jit(solution)/shard_map/ppermute | solution.py:539
  27.0 2.5 %shard_map.90 = (bf16[256,384]{1,0:T(8,128)(2,1)S(1)}, bf16[256,384]{1,0:T(8,128)(2,1)S(1)}) custom-call(bf16[256,1536]{1,0:T(8,128)(2,1)} %x_hbm.2, bf16[1536,384]{1,0:T(8,128)(2,1)S(1)} %copy-done, bf16[256,384]{1,0:T(8,128)(2,1)S(1)} %get-tuple-element.44.fk_ref, bf16[256,384]{1,0:T(8,128)(2,1)S(1)} %get-tuple-element.45.v_ref), custom_call_target="tpu_custom_call" | custom-call | flops 503316480 | bytes 3145728 | tf_op jit(solution)/shard_map/pallas_call | solution.py:253
  30.8 3.3 %collective-permute-start.4 = (bf16[96,128]{1,0:T(8,128)(2,1)S(1)}, bf16[96,128]{1,0:T(8,128)(2,1)S(1)}, u32[]{:S(2)}, u32[]{:S(2)}) collective-permute-start(bf16[96,128]{1,0:T(8,128)(2,1)S(1)} %shard_map.89.mine_ref), channel_id=1, source_target_pairs={{0,4},{4,0},{1,5},{5,1},{2,6},{6,2},{3,7},{7,3},{8,12},{12,8},{9,1... | collective-permute-start | bytes 73736 | tf_op jit(solution)/shard_map/ppermute | solution.py:145
  34.1 2.2 %shard_map.91.up_ref = bf16[256,384]{1,0:T(8,128)(2,1)S(1)} custom-call(bf16[256,384]{1,0:T(8,128)(2,1)S(1)} %copy-done.2, bf16[256,384]{1,0:T(8,128)(2,1)S(1)} %collective-permute-done.5.g1, bf16[256,384]{1,0:T(8,128)(2,1)S(1)} %collective-permute-done.6.g2, bf16[256,384]{1,0:T(8,128)(2,1)S(1)} %collective-permute-done.7.g3, bf16[384,1536]{1,0:T(8,128)(2,1)} %w_ref.1, ...), custom_call_target="tpu_custom_call" | custom-call | flops 301989888 | bytes 3145728 | tf_op jit(solution)/shard_map/pallas_call | solution.py:283
  37.3 1.9 %collective-permute-start.8 = (bf16[192,128]{1,0:T(8,128)(2,1)S(1)}, bf16[192,128]{1,0:T(8,128)(2,1)S(1)}, u32[]{:S(2)}, u32[]{:S(2)}) collective-permute-start(bf16[192,128]{1,0:T(8,128)(2,1)S(1)} %get-tuple-element.51.state_ref), channel_id=1, source_target_pairs={{0,4},{4,0},{1,5},{5,1},{2,6},{6,2},{3,7},{7,3},{8,12},{12,8},{9,1... | collective-permute-start | bytes 147464 | tf_op jit(solution)/shard_map/ppermute | solution.py:145
  40.1 2.1 %collective-permute-start.9 = (bf16[96,128]{1,0:T(8,128)(2,1)S(1)}, bf16[96,128]{1,0:T(8,128)(2,1)S(1)}, u32[]{:S(2)}, u32[]{:S(2)}) collective-permute-start(bf16[96,128]{1,0:T(8,128)(2,1)S(1)} %shard_map.93.chip_ref), channel_id=1, source_target_pairs={{0,24},{8,0},{16,8},{24,16},{1,25},{9,1},{17,9},{25,17},{2,26},{10... | collective-permute-start | bytes 73736 | tf_op jit(solution)/shard_map/ppermute | solution.py:151
  43.1 3.2 %collective-permute-done.10.g2 = bf16[96,128]{1,0:T(8,128)(2,1)S(1)} collective-permute-done((bf16[96,128]{1,0:T(8,128)(2,1)S(1)}, bf16[96,128]{1,0:T(8,128)(2,1)S(1)}, u32[]{:S(2)}, u32[]{:S(2)}) %collective-permute-start.10) | collective-permute-done | bytes 24608 | tf_op jit(solution)/shard_map/ppermute | solution.py:151
  47.0 6.6 %all-to-all-start.1 = ((bf16[8,96,128]{2,1,0:T(8,128)(2,1)}), bf16[8,96,128]{2,1,0:T(8,128)(2,1)S(1)}, u32[]{:S(2)}, u32[]{:S(2)}) async-start(bf16[8,96,128]{2,1,0:T(8,128)(2,1)} %shard_map.95), calls=%async_computation.1 | async-start | bytes 393216 | tf_op jit(solution)/shard_map/all_to_all | solution.py:141
  53.7 1.3 %shard_map.94 = (bf16[256,384]{1,0:T(8,128)(2,1)}, bf16[256,384]{1,0:T(8,128)(2,1)}, bf16[256,384]{1,0:T(8,128)(2,1)}, bf16[256,384]{1,0:T(8,128)(2,1)}) custom-call(bf16[256,384]{1,0:T(8,128)(2,1)S(1)} %get-tuple-element.52.attn_ref, bf16[384,1536]{1,0:T(8,128)(2,1)S(1)} %copy-done.1), custom_call_target="tpu_custom_call" | custom-call | flops 301989888 | bytes 2097152 | tf_op jit(solution)/shard_map/pallas_call | solution.py:48
  55.0 1.9 %collective-permute-start.14 = (bf16[256,384]{1,0:T(8,128)(2,1)}, bf16[256,384]{1,0:T(8,128)(2,1)S(1)}, u32[]{:S(2)}, u32[]{:S(2)}) collective-permute-start(bf16[256,384]{1,0:T(8,128)(2,1)} %get-tuple-element.59), channel_id=1, source_target_pairs={{0,3},{1,0},{2,1},{3,2},{4,7},{5,4},{6,5},{7,6},{8,11},{9,8},{10,9... | collective-permute-start | bytes 589832 | tf_op jit(solution)/shard_map/ppermute | solution.py:539
  56.9 1.9 %collective-permute-start.12 = (bf16[256,384]{1,0:T(8,128)(2,1)}, bf16[256,384]{1,0:T(8,128)(2,1)S(1)}, u32[]{:S(2)}, u32[]{:S(2)}) collective-permute-start(bf16[256,384]{1,0:T(8,128)(2,1)} %get-tuple-element.55), channel_id=1, source_target_pairs={{0,2},{1,3},{2,0},{3,1},{4,6},{5,7},{6,4},{7,5},{8,10},{9,11},{10,... | collective-permute-start | bytes 589832 | tf_op jit(solution)/shard_map/ppermute | solution.py:539
  60.9 1.4 %all-to-all-done.1.planes_ref = bf16[8,96,128]{2,1,0:T(8,128)(2,1)S(1)} async-done(((bf16[8,96,128]{2,1,0:T(8,128)(2,1)}), bf16[8,96,128]{2,1,0:T(8,128)(2,1)S(1)}, u32[]{:S(2)}, u32[]{:S(2)}) %all-to-all-start.1) | async-done | bytes 196640 | tf_op jit(solution)/shard_map/all_to_all | solution.py:141
  62.4 3.2 %collective-permute-start.15 = (bf16[96,128]{1,0:T(8,128)(2,1)S(1)}, bf16[96,128]{1,0:T(8,128)(2,1)S(1)}, u32[]{:S(2)}, u32[]{:S(2)}) collective-permute-start(bf16[96,128]{1,0:T(8,128)(2,1)S(1)} %shard_map.97.mine_ref), channel_id=1, source_target_pairs={{0,4},{4,0},{1,5},{5,1},{2,6},{6,2},{3,7},{7,3},{8,12},{12,8},{9,1... | collective-permute-start | bytes 73736 | tf_op jit(solution)/shard_map/ppermute | solution.py:145
  65.6 1.8 %shard_map.96 = (bf16[256,384]{1,0:T(8,128)(2,1)S(1)}, bf16[256,384]{1,0:T(8,128)(2,1)S(1)}, bf16[256,384]{1,0:T(8,128)(2,1)S(1)}) custom-call(bf16[256,384]{1,0:T(8,128)(2,1)S(1)} %get-tuple-element.46.fq_ref, bf16[256,384]{1,0:T(8,128)(2,1)S(1)} %get-tuple-element.44.fk_ref, bf16[256,384]{1,0:T(8,128)(2,1)S(1)} %get-tuple-element.45.v_ref, ...), custom_call_target="tpu_custom_call" | custom-call | flops 603979776 | bytes 3145728 | tf_op jit(solution)/shard_map/pallas_call | solution.py:48
  67.4 1.5 %shard_map.102 = (bf16[384,384]{1,0:T(8,128)(2,1)S(1)}, bf16[384,384]{1,0:T(8,128)(2,1)S(1)}, bf16[384,384]{1,0:T(8,128)(2,1)S(1)}, bf16[384,384]{1,0:T(8,128)(2...) custom-call(bf16[1536,384]{1,0:T(8,128)(2,1)} %refs_0_.2, bf16[1536,384]{1,0:T(8,128)(2,1)} %refs_1_.3, ...), custom_call_target="tpu_custom_call" | custom-call | flops 1 | bytes 1048576 | tf_op jit(solution)/shard_map/pallas_call | solution.py:424
  70.6 2.0 %collective-permute-start.18 = (bf16[256,384]{1,0:T(8,128)(2,1)S(1)}, bf16[256,384]{1,0:T(8,128)(2,1)S(1)}, u32[]{:S(2)}, u32[]{:S(2)}) collective-permute-start(bf16[256,384]{1,0:T(8,128)(2,1)S(1)} %get-tuple-element.81), channel_id=1, source_target_pairs={{0,3},{1,0},{2,1},{3,2},{4,7},{5,4},{6,5},{7,6},{8,11},{9,8},{10,9... | collective-permute-start | bytes 589832 | tf_op jit(solution)/shard_map/ppermute | solution.py:539
  72.6 1.9 %collective-permute-start.16 = (bf16[256,384]{1,0:T(8,128)(2,1)S(1)}, bf16[256,384]{1,0:T(8,128)(2,1)S(1)}, u32[]{:S(2)}, u32[]{:S(2)}) collective-permute-start(bf16[256,384]{1,0:T(8,128)(2,1)S(1)} %get-tuple-element.72), channel_id=1, source_target_pairs={{0,2},{1,3},{2,0},{3,1},{4,6},{5,7},{6,4},{7,5},{8,10},{9,11},{10,... | collective-permute-start | bytes 589832 | tf_op jit(solution)/shard_map/ppermute | solution.py:539
  75.3 1.8 %shard_map.101 = bf16[256,384]{1,0:T(8,128)(2,1)S(1)} custom-call(bf16[256,384]{1,0:T(8,128)(2,1)S(1)} %get-tuple-element.63.dq_ref, bf16[256,384]{1,0:T(8,128)(2,1)S(1)} %get-tuple-element.70.dk_ref, bf16[256,384]{1,0:T(8,128)(2,1)S(1)} %get-tuple-element.71.dv_ref, bf16[1536,384]{1,0:T(8,128)(2,1)} %refs_0_.2, bf16[1536,384]{1,0:T(8,128)(2,1)} %refs_1_.3, ...), custom_call_target="tpu_custom_call" | custom-call | flops 226492416 | bytes 1048576 | tf_op jit(solution)/shard_map/pallas_call | solution.py:517
  77.1 3.6 %collective-permute-done.17 = bf16[256,384]{1,0:T(8,128)(2,1)S(1)} collective-permute-done((bf16[256,384]{1,0:T(8,128)(2,1)S(1)}, bf16[256,384]{1,0:T(8,128)(2,1)S(1)}, u32[]{:S(2)}, u32[]{:S(2)}) %collective-permute-start.17) | collective-permute-done | bytes 196640 | tf_op jit(solution)/shard_map/ppermute | solution.py:539
  80.7 2.7 %collective-permute-done.16 = bf16[256,384]{1,0:T(8,128)(2,1)S(1)} collective-permute-done((bf16[256,384]{1,0:T(8,128)(2,1)S(1)}, bf16[256,384]{1,0:T(8,128)(2,1)S(1)}, u32[]{:S(2)}, u32[]{:S(2)}) %collective-permute-start.16) | collective-permute-done | bytes 196640 | tf_op jit(solution)/shard_map/ppermute | solution.py:539
  (49 shorter events, 17.3 us)
Async XLA Ops:
  0.6 21.5 %copy-start.2 = (bf16[256,384]{1,0:T(8,128)(2,1)S(1)}, bf16[256,384]{1,0:T(8,128)(2,1)}, u32[]{:S(2)}) copy-start(bf16[256,384]{1,0:T(8,128)(2,1)} %g0.1) | copy-start | bytes 589828
  0.6 26.3 %copy-start.4 = (f32[384]{0:T(512)S(1)}, f32[384]{0:T(512)}, u32[]{:S(2)}) copy-start(f32[384]{0:T(512)} %param.12) | copy-start | bytes 4612
  0.6 26.3 %copy-start = (bf16[1536,384]{1,0:T(8,128)(2,1)S(1)}, bf16[1536,384]{1,0:T(8,128)(2,1)}, u32[]{:S(2)}) copy-start(bf16[1536,384]{1,0:T(8,128)(2,1)} %refs_0_.2) | copy-start | bytes 3538948
  3.8 4.2 %collective-permute-start = (bf16[192,128]{1,0:T(8,128)(2,1)S(1)}, bf16[192,128]{1,0:T(8,128)(2,1)S(1)}, u32[]{:S(2)}, u32[]{:S(2)}) collective-permute-start(bf16[192,128]{1,0:T(8,128)(2,1)S(1)} %get-tuple-element.42.state_ref), channel_id=1, source_target_pairs={{0,4},{4,0},{1,5},{5,1},{2,6},{6,2},{3,7},{7,3},{8,12},{12,8},{9,1... | collective-permute-start | bytes 147464 | tf_op jit(solution)/shard_map/ppermute | solution.py:145
  8.0 4.0 %collective-permute-start.1 = (bf16[96,128]{1,0:T(8,128)(2,1)S(1)}, bf16[96,128]{1,0:T(8,128)(2,1)S(1)}, u32[]{:S(2)}, u32[]{:S(2)}) collective-permute-start(bf16[96,128]{1,0:T(8,128)(2,1)S(1)} %shard_map.87.chip_ref), channel_id=1, source_target_pairs={{0,8},{8,16},{16,24},{24,0},{1,9},{9,17},{17,25},{25,1},{2,10},{10... | collective-permute-start | bytes 73736 | tf_op jit(solution)/shard_map/ppermute | solution.py:151
  8.0 4.6 %collective-permute-start.2 = (bf16[96,128]{1,0:T(8,128)(2,1)S(1)}, bf16[96,128]{1,0:T(8,128)(2,1)S(1)}, u32[]{:S(2)}, u32[]{:S(2)}) collective-permute-start(bf16[96,128]{1,0:T(8,128)(2,1)S(1)} %shard_map.87.chip_ref), channel_id=1, source_target_pairs={{0,16},{8,24},{16,0},{24,8},{1,17},{9,25},{17,1},{25,9},{2,18},{10... | collective-permute-start | bytes 73736 | tf_op jit(solution)/shard_map/ppermute | solution.py:151
  10.2 3.0 %collective-permute-start.3 = (bf16[96,128]{1,0:T(8,128)(2,1)S(1)}, bf16[96,128]{1,0:T(8,128)(2,1)S(1)}, u32[]{:S(2)}, u32[]{:S(2)}) collective-permute-start(bf16[96,128]{1,0:T(8,128)(2,1)S(1)} %shard_map.87.chip_ref), channel_id=1, source_target_pairs={{0,24},{8,0},{16,8},{24,16},{1,25},{9,1},{17,9},{25,17},{2,26},{10... | collective-permute-start | bytes 73736 | tf_op jit(solution)/shard_map/ppermute | solution.py:151
  13.9 16.8 %all-to-all-start = ((bf16[8,96,128]{2,1,0:T(8,128)(2,1)}), bf16[8,96,128]{2,1,0:T(8,128)(2,1)S(1)}, u32[]{:S(2)}, u32[]{:S(2)}) async-start(bf16[8,96,128]{2,1,0:T(8,128)(2,1)} %shard_map.88), calls=%async_computation | async-start | bytes 393216 | tf_op jit(solution)/shard_map/all_to_all | solution.py:141
  22.1 12.0 %collective-permute-start.5 = (bf16[256,384]{1,0:T(8,128)(2,1)S(1)}, bf16[256,384]{1,0:T(8,128)(2,1)S(1)}, u32[]{:S(2)}, u32[]{:S(2)}) collective-permute-start(bf16[256,384]{1,0:T(8,128)(2,1)S(1)} %copy-done.2), channel_id=1, source_target_pairs={{0,1},{1,2},{2,3},{3,0},{4,5},{5,6},{6,7},{7,4},{8,9},{9,10},{10,1... | collective-permute-start | bytes 589832 | tf_op jit(solution)/shard_map/ppermute | solution.py:539
  23.4 10.7 %collective-permute-start.6 = (bf16[256,384]{1,0:T(8,128)(2,1)S(1)}, bf16[256,384]{1,0:T(8,128)(2,1)S(1)}, u32[]{:S(2)}, u32[]{:S(2)}) collective-permute-start(bf16[256,384]{1,0:T(8,128)(2,1)S(1)} %copy-done.2), channel_id=1, source_target_pairs={{0,2},{1,3},{2,0},{3,1},{4,6},{5,7},{6,4},{7,5},{8,10},{9,11},{10,... | collective-permute-start | bytes 589832 | tf_op jit(solution)/shard_map/ppermute | solution.py:539
  25.8 8.3 %collective-permute-start.7 = (bf16[256,384]{1,0:T(8,128)(2,1)S(1)}, bf16[256,384]{1,0:T(8,128)(2,1)S(1)}, u32[]{:S(2)}, u32[]{:S(2)}) collective-permute-start(bf16[256,384]{1,0:T(8,128)(2,1)S(1)} %copy-done.2), channel_id=1, source_target_pairs={{0,3},{1,0},{2,1},{3,2},{4,7},{5,4},{6,5},{7,6},{8,11},{9,8},{10,9... | collective-permute-start | bytes 589832 | tf_op jit(solution)/shard_map/ppermute | solution.py:539
  30.8 5.5 %collective-permute-start.4 = (bf16[96,128]{1,0:T(8,128)(2,1)S(1)}, bf16[96,128]{1,0:T(8,128)(2,1)S(1)}, u32[]{:S(2)}, u32[]{:S(2)}) collective-permute-start(bf16[96,128]{1,0:T(8,128)(2,1)S(1)} %shard_map.89.mine_ref), channel_id=1, source_target_pairs={{0,4},{4,0},{1,5},{5,1},{2,6},{6,2},{3,7},{7,3},{8,12},{12,8},{9,1... | collective-permute-start | bytes 73736 | tf_op jit(solution)/shard_map/ppermute | solution.py:145
  37.3 2.8 %collective-permute-start.8 = (bf16[192,128]{1,0:T(8,128)(2,1)S(1)}, bf16[192,128]{1,0:T(8,128)(2,1)S(1)}, u32[]{:S(2)}, u32[]{:S(2)}) collective-permute-start(bf16[192,128]{1,0:T(8,128)(2,1)S(1)} %get-tuple-element.51.state_ref), channel_id=1, source_target_pairs={{0,4},{4,0},{1,5},{5,1},{2,6},{6,2},{3,7},{7,3},{8,12},{12,8},{9,1... | collective-permute-start | bytes 147464 | tf_op jit(solution)/shard_map/ppermute | solution.py:145
  40.1 3.0 %collective-permute-start.9 = (bf16[96,128]{1,0:T(8,128)(2,1)S(1)}, bf16[96,128]{1,0:T(8,128)(2,1)S(1)}, u32[]{:S(2)}, u32[]{:S(2)}) collective-permute-start(bf16[96,128]{1,0:T(8,128)(2,1)S(1)} %shard_map.93.chip_ref), channel_id=1, source_target_pairs={{0,24},{8,0},{16,8},{24,16},{1,25},{9,1},{17,9},{25,17},{2,26},{10... | collective-permute-start | bytes 73736 | tf_op jit(solution)/shard_map/ppermute | solution.py:151
  42.1 4.2 %collective-permute-start.10 = (bf16[96,128]{1,0:T(8,128)(2,1)S(1)}, bf16[96,128]{1,0:T(8,128)(2,1)S(1)}, u32[]{:S(2)}, u32[]{:S(2)}) collective-permute-start(bf16[96,128]{1,0:T(8,128)(2,1)S(1)} %shard_map.93.chip_ref), channel_id=1, source_target_pairs={{0,16},{8,24},{16,0},{24,8},{1,17},{9,25},{17,1},{25,9},{2,18},{10... | collective-permute-start | bytes 73736 | tf_op jit(solution)/shard_map/ppermute | solution.py:151
  42.2 4.2 %collective-permute-start.11 = (bf16[96,128]{1,0:T(8,128)(2,1)S(1)}, bf16[96,128]{1,0:T(8,128)(2,1)S(1)}, u32[]{:S(2)}, u32[]{:S(2)}) collective-permute-start(bf16[96,128]{1,0:T(8,128)(2,1)S(1)} %shard_map.93.chip_ref), channel_id=1, source_target_pairs={{0,8},{8,16},{16,24},{24,0},{1,9},{9,17},{17,25},{25,1},{2,10},{10... | collective-permute-start | bytes 73736 | tf_op jit(solution)/shard_map/ppermute | solution.py:151
  47.0 15.3 %all-to-all-start.1 = ((bf16[8,96,128]{2,1,0:T(8,128)(2,1)}), bf16[8,96,128]{2,1,0:T(8,128)(2,1)S(1)}, u32[]{:S(2)}, u32[]{:S(2)}) async-start(bf16[8,96,128]{2,1,0:T(8,128)(2,1)} %shard_map.95), calls=%async_computation.1 | async-start | bytes 393216 | tf_op jit(solution)/shard_map/all_to_all | solution.py:141
  55.0 17.6 %collective-permute-start.14 = (bf16[256,384]{1,0:T(8,128)(2,1)}, bf16[256,384]{1,0:T(8,128)(2,1)S(1)}, u32[]{:S(2)}, u32[]{:S(2)}) collective-permute-start(bf16[256,384]{1,0:T(8,128)(2,1)} %get-tuple-element.59), channel_id=1, source_target_pairs={{0,3},{1,0},{2,1},{3,2},{4,7},{5,4},{6,5},{7,6},{8,11},{9,8},{10,9... | collective-permute-start | bytes 589832 | tf_op jit(solution)/shard_map/ppermute | solution.py:539
  56.9 17.6 %collective-permute-start.13 = (bf16[256,384]{1,0:T(8,128)(2,1)}, bf16[256,384]{1,0:T(8,128)(2,1)S(1)}, u32[]{:S(2)}, u32[]{:S(2)}) collective-permute-start(bf16[256,384]{1,0:T(8,128)(2,1)} %get-tuple-element.57), channel_id=1, source_target_pairs={{0,1},{1,2},{2,3},{3,0},{4,5},{5,6},{6,7},{7,4},{8,9},{9,10},{10,1... | collective-permute-start | bytes 589832 | tf_op jit(solution)/shard_map/ppermute | solution.py:539
  56.9 17.6 %collective-permute-start.12 = (bf16[256,384]{1,0:T(8,128)(2,1)}, bf16[256,384]{1,0:T(8,128)(2,1)S(1)}, u32[]{:S(2)}, u32[]{:S(2)}) collective-permute-start(bf16[256,384]{1,0:T(8,128)(2,1)} %get-tuple-element.55), channel_id=1, source_target_pairs={{0,2},{1,3},{2,0},{3,1},{4,6},{5,7},{6,4},{7,5},{8,10},{9,11},{10,... | collective-permute-start | bytes 589832 | tf_op jit(solution)/shard_map/ppermute | solution.py:539
  62.4 6.5 %collective-permute-start.15 = (bf16[96,128]{1,0:T(8,128)(2,1)S(1)}, bf16[96,128]{1,0:T(8,128)(2,1)S(1)}, u32[]{:S(2)}, u32[]{:S(2)}) collective-permute-start(bf16[96,128]{1,0:T(8,128)(2,1)S(1)} %shard_map.97.mine_ref), channel_id=1, source_target_pairs={{0,4},{4,0},{1,5},{5,1},{2,6},{6,2},{3,7},{7,3},{8,12},{12,8},{9,1... | collective-permute-start | bytes 73736 | tf_op jit(solution)/shard_map/ppermute | solution.py:145
  70.6 6.5 %collective-permute-start.18 = (bf16[256,384]{1,0:T(8,128)(2,1)S(1)}, bf16[256,384]{1,0:T(8,128)(2,1)S(1)}, u32[]{:S(2)}, u32[]{:S(2)}) collective-permute-start(bf16[256,384]{1,0:T(8,128)(2,1)S(1)} %get-tuple-element.81), channel_id=1, source_target_pairs={{0,3},{1,0},{2,1},{3,2},{4,7},{5,4},{6,5},{7,6},{8,11},{9,8},{10,9... | collective-permute-start | bytes 589832 | tf_op jit(solution)/shard_map/ppermute | solution.py:539
  72.6 8.1 %collective-permute-start.17 = (bf16[256,384]{1,0:T(8,128)(2,1)S(1)}, bf16[256,384]{1,0:T(8,128)(2,1)S(1)}, u32[]{:S(2)}, u32[]{:S(2)}) collective-permute-start(bf16[256,384]{1,0:T(8,128)(2,1)S(1)} %get-tuple-element.80), channel_id=1, source_target_pairs={{0,1},{1,2},{2,3},{3,0},{4,5},{5,6},{6,7},{7,4},{8,9},{9,10},{10,1... | collective-permute-start | bytes 589832 | tf_op jit(solution)/shard_map/ppermute | solution.py:539
  72.6 10.8 %collective-permute-start.16 = (bf16[256,384]{1,0:T(8,128)(2,1)S(1)}, bf16[256,384]{1,0:T(8,128)(2,1)S(1)}, u32[]{:S(2)}, u32[]{:S(2)}) collective-permute-start(bf16[256,384]{1,0:T(8,128)(2,1)S(1)} %get-tuple-element.72), channel_id=1, source_target_pairs={{0,2},{1,3},{2,0},{3,1},{4,6},{5,7},{6,4},{7,5},{8,10},{9,11},{10,... | collective-permute-start | bytes 589832 | tf_op jit(solution)/shard_map/ppermute | solution.py:539
  (2 other events, 22.2 us)

commit v9 on v5

--- a/solution.py
+++ b/solution.py
@@ -154,13 +154,13 @@
 
 def key_value(latents, w_key, w_value):
     rows, width = (latents.shape[0], w_key.shape[1])
-    steps = 4
-    depth = latents.shape[1] // steps
+    depths = [latents.shape[1] // 12 * part for part in (4, 4, 3, 1)]
+    steps = len(depths)
 
     def body(x_hbm, wk_hbm, wv_hbm, fk_ref, v_ref, state_ref, x_ref, w_ref, sem):
         copies = []
         for i in range(steps):
-            span = pl.ds(i * depth, depth)
+            span = pl.ds(sum(depths[:i]), depths[i])
             copies.append(
                 [
                     pltpu.make_async_copy(src, dst, sem.at[3 * i + j])
@@ -180,7 +180,7 @@
         for i, group in enumerate(copies):
             for copy in group:
                 copy.wait()
-            span = slice(i * depth, (i + 1) * depth)
+            span = slice(sum(depths[:i]), sum(depths[: i + 1]))
             part = mm(x_ref[:, span], w_ref[span, :])
             total = part if total is None else total + part
         fk_ref[...] = feature_map(total[:, :width]).astype(bf16)
@@ -529,10 +529,11 @@
     gain = head_gain.reshape(1, -1)
     fk, v, state = key_value(latents, w_key, w_value)
     pair = swap(state)
+    grad1 = to_owner(hold(grad_out, state), 1)
     chip = pair_sum(state, pair)
     got = y_gather(False, chip)
     grad_held = hold(grad_out, chip)
-    grads = [grad_out] + [to_owner(grad_held, k) for k in (1, 2, 3)]
+    grads = [grad_out, grad1] + [to_owner(grad_held, k) for k in (2, 3)]
     planes = plane_sums(False, chip, got)
     fq, raw_local = query_local(hold(latents, planes), w_query, fk, v)
     up = upstream_of(grads, w_out, gain)

time: 84.4 us -> 82.7 us (0.980)
  waiting for transfers between devices: 22.2 us -> 18.5 us
  starting transfers between devices: 40 us -> 42 us
    ppermute x9, waiting for transfers between devices: 8.82 us -> 6.71 us  [to_owner(): return lax.ppermute(part, 'mp', shifts(4, k))]
    ppermute x9, starting transfers between devices: 8.4 us -> 10.1 us  [to_owner(): return lax.ppermute(part, 'mp', shifts(4, k))]
    all_to_all x2, waiting for transfers between devices: 6.71 us -> 5.19 us  [plane_exchange(): return lax.all_to_all(planes, 'seq_0', 0, 0, tiled=True)]
where the time goes in v9:
time: 82.7 us; the launch traced here: 82.3 us
  starting transfers between devices  42 us (51%)
  Pallas kernels  19.4 us (23%)
  waiting for transfers between devices  18.5 us (22%)
  other arithmetic  1.56 us (2%)
    all_to_all x2, starting transfers between devices, plane_exchange(): return lax.all_to_all(planes, 'seq_0', 0, 0, tiled=True)  14.8 us
    ppermute x4, starting transfers between devices, swap(): return lax.ppermute(x, 'seq_2', SWAP)  11.4 us
    ppermute x9, starting transfers between devices, to_owner(): return lax.ppermute(part, 'mp', shifts(4, k))  10.1 us
    ppermute x9, waiting for transfers between devices, to_owner(): return lax.ppermute(part, 'mp', shifts(4, k))  6.71 us
    ppermute x6, starting transfers between devices, y_gather(): got.append(lax.ppermute(chip, 'seq_1', shifts(4, -k if later else k)))  5.75 us
    all_to_all x2, waiting for transfers between devices, plane_exchange(): return lax.all_to_all(planes, 'seq_0', 0, 0, tiled=True)  5.19 us
    ppermute x6, waiting for transfers between devices, y_gather(): got.append(lax.ppermute(chip, 'seq_1', shifts(4, -k if later else k)))  4.88 us
    pallas_call x8, Pallas kernels, plain(): call(body, outs, flops, moved, in_specs=[VMEM] * len(args), out_specs=[VM...  4.63 us
  transfers between devices with their start and end apart: 21, of which 12 were waited for; matrix products, arithmetic and copies ran while one was open for 1% of the time, Pallas kernels for 17%

profile of v9, /device:TPU:1, one launch (start us, length us, event | category | flops | bytes accessed | tf_op | source)
XLA Modules:
  0.0 82.3 jit_solution(5311227438908991605)
XLA Ops:
  0.7 3.0 %shard_map.86 = (bf16[256,384]{1,0:T(8,128)(2,1)S(1)}, bf16[256,384]{1,0:T(8,128)(2,1)S(1)}, bf16[192,128]{1,0:T(8,128)(2,1)S(1)}) custom-call(bf16[256,1536]{1,0:T(8,128)(2,1)} %x_hbm.2, bf16[1536,384]{1,0:T(8,128)(2,1)} %wk_hbm.5, bf16[1536,384]{1,0:T(8,128)(2,1)} %wv_hbm.5), custom_call_target="tpu_custom_call" | custom-call | flops 603979776 | bytes 3145728 | tf_op jit(solution)/shard_map/pallas_call | solution.py:195
  3.7 3.3 %collective-permute-start = (bf16[192,128]{1,0:T(8,128)(2,1)S(1)}, bf16[192,128]{1,0:T(8,128)(2,1)S(1)}, u32[]{:S(2)}, u32[]{:S(2)}) collective-permute-start(bf16[192,128]{1,0:T(8,128)(2,1)S(1)} %get-tuple-element.35.state_ref), channel_id=1, source_target_pairs={{0,4},{4,0},{1,5},{5,1},{2,6},{6,2},{3,7},{7,3},{8,12},{12,8},{9,1... | collective-permute-start | bytes 147464 | tf_op jit(solution)/shard_map/ppermute | solution.py:145
  10.6 2.6 %collective-permute-done.2.g2 = bf16[96,128]{1,0:T(8,128)(2,1)S(1)} collective-permute-done((bf16[96,128]{1,0:T(8,128)(2,1)S(1)}, bf16[96,128]{1,0:T(8,128)(2,1)S(1)}, u32[]{:S(2)}, u32[]{:S(2)}) %collective-permute-start.2) | collective-permute-done | bytes 24608 | tf_op jit(solution)/shard_map/ppermute | solution.py:151
  14.1 8.2 %all-to-all-start = ((bf16[8,96,128]{2,1,0:T(8,128)(2,1)}), bf16[8,96,128]{2,1,0:T(8,128)(2,1)S(1)}, u32[]{:S(2)}, u32[]{:S(2)}) async-start(bf16[8,96,128]{2,1,0:T(8,128)(2,1)} %shard_map.88), calls=%async_computation | async-start | bytes 393216 | tf_op jit(solution)/shard_map/all_to_all | solution.py:141
  23.6 1.5 %collective-permute-start.7 = (bf16[256,384]{1,0:T(8,128)(2,1)S(1)}, bf16[256,384]{1,0:T(8,128)(2,1)S(1)}, u32[]{:S(2)}, u32[]{:S(2)}) collective-permute-start(bf16[256,384]{1,0:T(8,128)(2,1)S(1)} %copy-done.2), channel_id=1, source_target_pairs={{0,3},{1,0},{2,1},{3,2},{4,7},{5,4},{6,5},{7,6},{8,11},{9,8},{10,9... | collective-permute-start | bytes 589832 | tf_op jit(solution)/shard_map/ppermute | solution.py:521
  25.1 1.5 %collective-permute-start.6 = (bf16[256,384]{1,0:T(8,128)(2,1)S(1)}, bf16[256,384]{1,0:T(8,128)(2,1)S(1)}, u32[]{:S(2)}, u32[]{:S(2)}) collective-permute-start(bf16[256,384]{1,0:T(8,128)(2,1)S(1)} %copy-done.2), channel_id=1, source_target_pairs={{0,2},{1,3},{2,0},{3,1},{4,6},{5,7},{6,4},{7,5},{8,10},{9,11},{10,... | collective-permute-start | bytes 589832 | tf_op jit(solution)/shard_map/ppermute | solution.py:521
  26.6 2.5 %shard_map.90 = (bf16[256,384]{1,0:T(8,128)(2,1)S(1)}, bf16[256,384]{1,0:T(8,128)(2,1)S(1)}) custom-call(bf16[256,1536]{1,0:T(8,128)(2,1)} %x_hbm.2, bf16[1536,384]{1,0:T(8,128)(2,1)S(1)} %copy-done, bf16[256,384]{1,0:T(8,128)(2,1)S(1)} %get-tuple-element.37.fk_ref, bf16[256,384]{1,0:T(8,128)(2,1)S(1)} %get-tuple-element.38.v_ref), custom_call_target="tpu_custom_call" | custom-call | flops 503316480 | bytes 3145728 | tf_op jit(solution)/shard_map/pallas_call | solution.py:253
  29.1 1.9 %all-to-all-done.planes_ref = bf16[8,96,128]{2,1,0:T(8,128)(2,1)S(1)} async-done(((bf16[8,96,128]{2,1,0:T(8,128)(2,1)}), bf16[8,96,128]{2,1,0:T(8,128)(2,1)S(1)}, u32[]{:S(2)}, u32[]{:S(2)}) %all-to-all-start) | async-done | bytes 196640 | tf_op jit(solution)/shard_map/all_to_all | solution.py:141
  31.0 3.3 %collective-permute-start.4 = (bf16[96,128]{1,0:T(8,128)(2,1)S(1)}, bf16[96,128]{1,0:T(8,128)(2,1)S(1)}, u32[]{:S(2)}, u32[]{:S(2)}) collective-permute-start(bf16[96,128]{1,0:T(8,128)(2,1)S(1)} %shard_map.89.mine_ref), channel_id=1, source_target_pairs={{0,4},{4,0},{1,5},{5,1},{2,6},{6,2},{3,7},{7,3},{8,12},{12,8},{9,1... | collective-permute-start | bytes 73736 | tf_op jit(solution)/shard_map/ppermute | solution.py:145
  34.4 2.2 %shard_map.91.up_ref = bf16[256,384]{1,0:T(8,128)(2,1)S(1)} custom-call(bf16[256,384]{1,0:T(8,128)(2,1)S(1)} %copy-done.2, bf16[256,384]{1,0:T(8,128)(2,1)S(1)} %collective-permute-done.5.g1, bf16[256,384]{1,0:T(8,128)(2,1)S(1)} %collective-permute-done.6.g2, bf16[256,384]{1,0:T(8,128)(2,1)S(1)} %collective-permute-done.7.g3, bf16[384,1536]{1,0:T(8,128)(2,1)} %w_ref.1, ...), custom_call_target="tpu_custom_call" | custom-call | flops 301989888 | bytes 3145728 | tf_op jit(solution)/shard_map/pallas_call | solution.py:283
  37.6 1.8 %collective-permute-start.8 = (bf16[192,128]{1,0:T(8,128)(2,1)S(1)}, bf16[192,128]{1,0:T(8,128)(2,1)S(1)}, u32[]{:S(2)}, u32[]{:S(2)}) collective-permute-start(bf16[192,128]{1,0:T(8,128)(2,1)S(1)} %get-tuple-element.44.state_ref), channel_id=1, source_target_pairs={{0,4},{4,0},{1,5},{5,1},{2,6},{6,2},{3,7},{7,3},{8,12},{12,8},{9,1... | collective-permute-start | bytes 147464 | tf_op jit(solution)/shard_map/ppermute | solution.py:145
  40.4 1.8 %collective-permute-start.10 = (bf16[96,128]{1,0:T(8,128)(2,1)S(1)}, bf16[96,128]{1,0:T(8,128)(2,1)S(1)}, u32[]{:S(2)}, u32[]{:S(2)}) collective-permute-start(bf16[96,128]{1,0:T(8,128)(2,1)S(1)} %shard_map.93.chip_ref), channel_id=1, source_target_pairs={{0,16},{8,24},{16,0},{24,8},{1,17},{9,25},{17,1},{25,9},{2,18},{10... | collective-permute-start | bytes 73736 | tf_op jit(solution)/shard_map/ppermute | solution.py:151
  42.1 1.8 %collective-permute-start.9 = (bf16[96,128]{1,0:T(8,128)(2,1)S(1)}, bf16[96,128]{1,0:T(8,128)(2,1)S(1)}, u32[]{:S(2)}, u32[]{:S(2)}) collective-permute-start(bf16[96,128]{1,0:T(8,128)(2,1)S(1)} %shard_map.93.chip_ref), channel_id=1, source_target_pairs={{0,24},{8,0},{16,8},{24,16},{1,25},{9,1},{17,9},{25,17},{2,26},{10... | collective-permute-start | bytes 73736 | tf_op jit(solution)/shard_map/ppermute | solution.py:151
  46.1 6.6 %all-to-all-start.1 = ((bf16[8,96,128]{2,1,0:T(8,128)(2,1)}), bf16[8,96,128]{2,1,0:T(8,128)(2,1)S(1)}, u32[]{:S(2)}, u32[]{:S(2)}) async-start(bf16[8,96,128]{2,1,0:T(8,128)(2,1)} %shard_map.95), calls=%async_computation.1 | async-start | bytes 393216 | tf_op jit(solution)/shard_map/all_to_all | solution.py:141
  52.7 1.3 %shard_map.94 = (bf16[256,384]{1,0:T(8,128)(2,1)}, bf16[256,384]{1,0:T(8,128)(2,1)}, bf16[256,384]{1,0:T(8,128)(2,1)}, bf16[256,384]{1,0:T(8,128)(2,1)}) custom-call(bf16[256,384]{1,0:T(8,128)(2,1)S(1)} %get-tuple-element.45.attn_ref, bf16[384,1536]{1,0:T(8,128)(2,1)S(1)} %copy-done.1), custom_call_target="tpu_custom_call" | custom-call | flops 301989888 | bytes 2097152 | tf_op jit(solution)/shard_map/pallas_call | solution.py:48
  54.0 1.7 %collective-permute-start.14 = (bf16[256,384]{1,0:T(8,128)(2,1)}, bf16[256,384]{1,0:T(8,128)(2,1)S(1)}, u32[]{:S(2)}, u32[]{:S(2)}) collective-permute-start(bf16[256,384]{1,0:T(8,128)(2,1)} %get-tuple-element.52), channel_id=1, source_target_pairs={{0,3},{1,0},{2,1},{3,2},{4,7},{5,4},{6,5},{7,6},{8,11},{9,8},{10,9... | collective-permute-start | bytes 589832 | tf_op jit(solution)/shard_map/ppermute | solution.py:521
  58.0 3.3 %all-to-all-done.1.planes_ref = bf16[8,96,128]{2,1,0:T(8,128)(2,1)S(1)} async-done(((bf16[8,96,128]{2,1,0:T(8,128)(2,1)}), bf16[8,96,128]{2,1,0:T(8,128)(2,1)S(1)}, u32[]{:S(2)}, u32[]{:S(2)}) %all-to-all-start.1) | async-done | bytes 196640 | tf_op jit(solution)/shard_map/all_to_all | solution.py:141
  61.4 3.0 %collective-permute-start.15 = (bf16[96,128]{1,0:T(8,128)(2,1)S(1)}, bf16[96,128]{1,0:T(8,128)(2,1)S(1)}, u32[]{:S(2)}, u32[]{:S(2)}) collective-permute-start(bf16[96,128]{1,0:T(8,128)(2,1)S(1)} %shard_map.97.mine_ref), channel_id=1, source_target_pairs={{0,4},{4,0},{1,5},{5,1},{2,6},{6,2},{3,7},{7,3},{8,12},{12,8},{9,1... | collective-permute-start | bytes 73736 | tf_op jit(solution)/shard_map/ppermute | solution.py:145
  64.3 1.8 %shard_map.96 = (bf16[256,384]{1,0:T(8,128)(2,1)S(1)}, bf16[256,384]{1,0:T(8,128)(2,1)S(1)}, bf16[256,384]{1,0:T(8,128)(2,1)S(1)}) custom-call(bf16[256,384]{1,0:T(8,128)(2,1)S(1)} %get-tuple-element.39.fq_ref, bf16[256,384]{1,0:T(8,128)(2,1)S(1)} %get-tuple-element.37.fk_ref, bf16[256,384]{1,0:T(8,128)(2,1)S(1)} %get-tuple-element.38.v_ref, ...), custom_call_target="tpu_custom_call" | custom-call | flops 603979776 | bytes 3145728 | tf_op jit(solution)/shard_map/pallas_call | solution.py:48
  66.9 2.5 %shard_map.101 = (bf16[256,384]{1,0:T(8,128)(2,1)S(1)}, bf16[256,384]{1,0:T(8,128)(2,1)S(1)}) custom-call(bf16[256,384]{1,0:T(8,128)(2,1)S(1)} %get-tuple-element.56.dq_ref, bf16[256,384]{1,0:T(8,128)(2,1)S(1)} %get-tuple-element.63.dk_ref, bf16[256,384]{1,0:T(8,128)(2,1)S(1)} %get-tuple-element.64.dv_ref, bf16[1536,384]{1,0:T(8,128)(2,1)} %wq_hbm.3, ...), custom_call_target="tpu_custom_call" | custom-call | flops 452984832 | bytes 2097152 | tf_op jit(solution)/shard_map/pallas_call | solution.py:499
  70.4 1.8 %collective-permute-start.18 = (bf16[256,384]{1,0:T(8,128)(2,1)S(1)}, bf16[256,384]{1,0:T(8,128)(2,1)S(1)}, u32[]{:S(2)}, u32[]{:S(2)}) collective-permute-start(bf16[256,384]{1,0:T(8,128)(2,1)S(1)} %get-tuple-element.67), channel_id=1, source_target_pairs={{0,3},{1,0},{2,1},{3,2},{4,7},{5,4},{6,5},{7,6},{8,11},{9,8},{10,9... | collective-permute-start | bytes 589832 | tf_op jit(solution)/shard_map/ppermute | solution.py:521
  73.2 1.7 %shard_map.100 = bf16[256,384]{1,0:T(8,128)(2,1)S(1)} custom-call(bf16[256,384]{1,0:T(8,128)(2,1)S(1)} %get-tuple-element.56.dq_ref, bf16[256,384]{1,0:T(8,128)(2,1)S(1)} %get-tuple-element.63.dk_ref, bf16[256,384]{1,0:T(8,128)(2,1)S(1)} %get-tuple-element.64.dv_ref, bf16[1536,384]{1,0:T(8,128)(2,1)} %wq_hbm.3, bf16[1536,384]{1,0:T(8,128)(2,1)} %wk_hbm.5, ...), custom_call_target="tpu_custom_call" | custom-call | flops 226492416 | bytes 1048576 | tf_op jit(solution)/shard_map/pallas_call | solution.py:499
  74.9 2.3 %collective-permute-done.17 = bf16[256,384]{1,0:T(8,128)(2,1)S(1)} collective-permute-done((bf16[256,384]{1,0:T(8,128)(2,1)S(1)}, bf16[256,384]{1,0:T(8,128)(2,1)S(1)}, u32[]{:S(2)}, u32[]{:S(2)}) %collective-permute-start.17) | collective-permute-done | bytes 196640 | tf_op jit(solution)/shard_map/ppermute | solution.py:521
  77.2 4.4 %collective-permute-done.16 = bf16[256,384]{1,0:T(8,128)(2,1)S(1)} collective-permute-done((bf16[256,384]{1,0:T(8,128)(2,1)S(1)}, bf16[256,384]{1,0:T(8,128)(2,1)S(1)}, u32[]{:S(2)}, u32[]{:S(2)}) %collective-permute-start.16) | collective-permute-done | bytes 196640 | tf_op jit(solution)/shard_map/ppermute | solution.py:521
  (47 shorter events, 16.0 us)
Async XLA Ops:
  0.6 21.7 %copy-start.2 = (bf16[256,384]{1,0:T(8,128)(2,1)S(1)}, bf16[256,384]{1,0:T(8,128)(2,1)}, u32[]{:S(2)}) copy-start(bf16[256,384]{1,0:T(8,128)(2,1)} %g0.1) | copy-start | bytes 589828
  0.6 26.0 %copy-start.4 = (f32[384]{0:T(512)S(1)}, f32[384]{0:T(512)}, u32[]{:S(2)}) copy-start(f32[384]{0:T(512)} %param.12) | copy-start | bytes 4612
  0.6 26.0 %copy-start = (bf16[1536,384]{1,0:T(8,128)(2,1)S(1)}, bf16[1536,384]{1,0:T(8,128)(2,1)}, u32[]{:S(2)}) copy-start(bf16[1536,384]{1,0:T(8,128)(2,1)} %wq_hbm.3) | copy-start | bytes 3538948
  3.7 4.2 %collective-permute-start = (bf16[192,128]{1,0:T(8,128)(2,1)S(1)}, bf16[192,128]{1,0:T(8,128)(2,1)S(1)}, u32[]{:S(2)}, u32[]{:S(2)}) collective-permute-start(bf16[192,128]{1,0:T(8,128)(2,1)S(1)} %get-tuple-element.35.state_ref), channel_id=1, source_target_pairs={{0,4},{4,0},{1,5},{5,1},{2,6},{6,2},{3,7},{7,3},{8,12},{12,8},{9,1... | collective-permute-start | bytes 147464 | tf_op jit(solution)/shard_map/ppermute | solution.py:145
  7.9 2.8 %collective-permute-start.3 = (bf16[96,128]{1,0:T(8,128)(2,1)S(1)}, bf16[96,128]{1,0:T(8,128)(2,1)S(1)}, u32[]{:S(2)}, u32[]{:S(2)}) collective-permute-start(bf16[96,128]{1,0:T(8,128)(2,1)S(1)} %shard_map.87.chip_ref), channel_id=1, source_target_pairs={{0,24},{8,0},{16,8},{24,16},{1,25},{9,1},{17,9},{25,17},{2,26},{10... | collective-permute-start | bytes 73736 | tf_op jit(solution)/shard_map/ppermute | solution.py:151
  9.0 4.2 %collective-permute-start.2 = (bf16[96,128]{1,0:T(8,128)(2,1)S(1)}, bf16[96,128]{1,0:T(8,128)(2,1)S(1)}, u32[]{:S(2)}, u32[]{:S(2)}) collective-permute-start(bf16[96,128]{1,0:T(8,128)(2,1)S(1)} %shard_map.87.chip_ref), channel_id=1, source_target_pairs={{0,16},{8,24},{16,0},{24,8},{1,17},{9,25},{17,1},{25,9},{2,18},{10... | collective-permute-start | bytes 73736 | tf_op jit(solution)/shard_map/ppermute | solution.py:151
  9.3 4.1 %collective-permute-start.1 = (bf16[96,128]{1,0:T(8,128)(2,1)S(1)}, bf16[96,128]{1,0:T(8,128)(2,1)S(1)}, u32[]{:S(2)}, u32[]{:S(2)}) collective-permute-start(bf16[96,128]{1,0:T(8,128)(2,1)S(1)} %shard_map.87.chip_ref), channel_id=1, source_target_pairs={{0,8},{8,16},{16,24},{24,0},{1,9},{9,17},{17,25},{25,1},{2,10},{10... | collective-permute-start | bytes 73736 | tf_op jit(solution)/shard_map/ppermute | solution.py:151
  14.1 16.9 %all-to-all-start = ((bf16[8,96,128]{2,1,0:T(8,128)(2,1)}), bf16[8,96,128]{2,1,0:T(8,128)(2,1)S(1)}, u32[]{:S(2)}, u32[]{:S(2)}) async-start(bf16[8,96,128]{2,1,0:T(8,128)(2,1)} %shard_map.88), calls=%async_computation | async-start | bytes 393216 | tf_op jit(solution)/shard_map/all_to_all | solution.py:141
  22.3 12.1 %collective-permute-start.5 = (bf16[256,384]{1,0:T(8,128)(2,1)S(1)}, bf16[256,384]{1,0:T(8,128)(2,1)S(1)}, u32[]{:S(2)}, u32[]{:S(2)}) collective-permute-start(bf16[256,384]{1,0:T(8,128)(2,1)S(1)} %copy-done.2), channel_id=1, source_target_pairs={{0,1},{1,2},{2,3},{3,0},{4,5},{5,6},{6,7},{7,4},{8,9},{9,10},{10,1... | collective-permute-start | bytes 589832 | tf_op jit(solution)/shard_map/ppermute | solution.py:521
  23.6 10.8 %collective-permute-start.7 = (bf16[256,384]{1,0:T(8,128)(2,1)S(1)}, bf16[256,384]{1,0:T(8,128)(2,1)S(1)}, u32[]{:S(2)}, u32[]{:S(2)}) collective-permute-start(bf16[256,384]{1,0:T(8,128)(2,1)S(1)} %copy-done.2), channel_id=1, source_target_pairs={{0,3},{1,0},{2,1},{3,2},{4,7},{5,4},{6,5},{7,6},{8,11},{9,8},{10,9... | collective-permute-start | bytes 589832 | tf_op jit(solution)/shard_map/ppermute | solution.py:521
  25.1 9.3 %collective-permute-start.6 = (bf16[256,384]{1,0:T(8,128)(2,1)S(1)}, bf16[256,384]{1,0:T(8,128)(2,1)S(1)}, u32[]{:S(2)}, u32[]{:S(2)}) collective-permute-start(bf16[256,384]{1,0:T(8,128)(2,1)S(1)} %copy-done.2), channel_id=1, source_target_pairs={{0,2},{1,3},{2,0},{3,1},{4,6},{5,7},{6,4},{7,5},{8,10},{9,11},{10,... | collective-permute-start | bytes 589832 | tf_op jit(solution)/shard_map/ppermute | solution.py:521
  31.0 5.5 %collective-permute-start.4 = (bf16[96,128]{1,0:T(8,128)(2,1)S(1)}, bf16[96,128]{1,0:T(8,128)(2,1)S(1)}, u32[]{:S(2)}, u32[]{:S(2)}) collective-permute-start(bf16[96,128]{1,0:T(8,128)(2,1)S(1)} %shard_map.89.mine_ref), channel_id=1, source_target_pairs={{0,4},{4,0},{1,5},{5,1},{2,6},{6,2},{3,7},{7,3},{8,12},{12,8},{9,1... | collective-permute-start | bytes 73736 | tf_op jit(solution)/shard_map/ppermute | solution.py:145
  37.6 2.7 %collective-permute-start.8 = (bf16[192,128]{1,0:T(8,128)(2,1)S(1)}, bf16[192,128]{1,0:T(8,128)(2,1)S(1)}, u32[]{:S(2)}, u32[]{:S(2)}) collective-permute-start(bf16[192,128]{1,0:T(8,128)(2,1)S(1)} %get-tuple-element.44.state_ref), channel_id=1, source_target_pairs={{0,4},{4,0},{1,5},{5,1},{2,6},{6,2},{3,7},{7,3},{8,12},{12,8},{9,1... | collective-permute-start | bytes 147464 | tf_op jit(solution)/shard_map/ppermute | solution.py:145
  40.3 4.0 %collective-permute-start.11 = (bf16[96,128]{1,0:T(8,128)(2,1)S(1)}, bf16[96,128]{1,0:T(8,128)(2,1)S(1)}, u32[]{:S(2)}, u32[]{:S(2)}) collective-permute-start(bf16[96,128]{1,0:T(8,128)(2,1)S(1)} %shard_map.93.chip_ref), channel_id=1, source_target_pairs={{0,8},{8,16},{16,24},{24,0},{1,9},{9,17},{17,25},{25,1},{2,10},{10... | collective-permute-start | bytes 73736 | tf_op jit(solution)/shard_map/ppermute | solution.py:151
  40.4 4.3 %collective-permute-start.10 = (bf16[96,128]{1,0:T(8,128)(2,1)S(1)}, bf16[96,128]{1,0:T(8,128)(2,1)S(1)}, u32[]{:S(2)}, u32[]{:S(2)}) collective-permute-start(bf16[96,128]{1,0:T(8,128)(2,1)S(1)} %shard_map.93.chip_ref), channel_id=1, source_target_pairs={{0,16},{8,24},{16,0},{24,8},{1,17},{9,25},{17,1},{25,9},{2,18},{10... | collective-permute-start | bytes 73736 | tf_op jit(solution)/shard_map/ppermute | solution.py:151
  42.1 3.3 %collective-permute-start.9 = (bf16[96,128]{1,0:T(8,128)(2,1)S(1)}, bf16[96,128]{1,0:T(8,128)(2,1)S(1)}, u32[]{:S(2)}, u32[]{:S(2)}) collective-permute-start(bf16[96,128]{1,0:T(8,128)(2,1)S(1)} %shard_map.93.chip_ref), channel_id=1, source_target_pairs={{0,24},{8,0},{16,8},{24,16},{1,25},{9,1},{17,9},{25,17},{2,26},{10... | collective-permute-start | bytes 73736 | tf_op jit(solution)/shard_map/ppermute | solution.py:151
  46.1 15.2 %all-to-all-start.1 = ((bf16[8,96,128]{2,1,0:T(8,128)(2,1)}), bf16[8,96,128]{2,1,0:T(8,128)(2,1)S(1)}, u32[]{:S(2)}, u32[]{:S(2)}) async-start(bf16[8,96,128]{2,1,0:T(8,128)(2,1)} %shard_map.95), calls=%async_computation.1 | async-start | bytes 393216 | tf_op jit(solution)/shard_map/all_to_all | solution.py:141
  54.0 18.2 %collective-permute-start.14 = (bf16[256,384]{1,0:T(8,128)(2,1)}, bf16[256,384]{1,0:T(8,128)(2,1)S(1)}, u32[]{:S(2)}, u32[]{:S(2)}) collective-permute-start(bf16[256,384]{1,0:T(8,128)(2,1)} %get-tuple-element.52), channel_id=1, source_target_pairs={{0,3},{1,0},{2,1},{3,2},{4,7},{5,4},{6,5},{7,6},{8,11},{9,8},{10,9... | collective-permute-start | bytes 589832 | tf_op jit(solution)/shard_map/ppermute | solution.py:521
  55.7 16.7 %collective-permute-start.13 = (bf16[256,384]{1,0:T(8,128)(2,1)}, bf16[256,384]{1,0:T(8,128)(2,1)S(1)}, u32[]{:S(2)}, u32[]{:S(2)}) collective-permute-start(bf16[256,384]{1,0:T(8,128)(2,1)} %get-tuple-element.50), channel_id=1, source_target_pairs={{0,1},{1,2},{2,3},{3,0},{4,5},{5,6},{6,7},{7,4},{8,9},{9,10},{10,1... | collective-permute-start | bytes 589832 | tf_op jit(solution)/shard_map/ppermute | solution.py:521
  55.7 16.7 %collective-permute-start.12 = (bf16[256,384]{1,0:T(8,128)(2,1)}, bf16[256,384]{1,0:T(8,128)(2,1)S(1)}, u32[]{:S(2)}, u32[]{:S(2)}) collective-permute-start(bf16[256,384]{1,0:T(8,128)(2,1)} %get-tuple-element.48), channel_id=1, source_target_pairs={{0,2},{1,3},{2,0},{3,1},{4,6},{5,7},{6,4},{7,5},{8,10},{9,11},{10,... | collective-permute-start | bytes 589832 | tf_op jit(solution)/shard_map/ppermute | solution.py:521
  61.4 4.8 %collective-permute-start.15 = (bf16[96,128]{1,0:T(8,128)(2,1)S(1)}, bf16[96,128]{1,0:T(8,128)(2,1)S(1)}, u32[]{:S(2)}, u32[]{:S(2)}) collective-permute-start(bf16[96,128]{1,0:T(8,128)(2,1)S(1)} %shard_map.97.mine_ref), channel_id=1, source_target_pairs={{0,4},{4,0},{1,5},{5,1},{2,6},{6,2},{3,7},{7,3},{8,12},{12,8},{9,1... | collective-permute-start | bytes 73736 | tf_op jit(solution)/shard_map/ppermute | solution.py:145
  69.4 7.7 %collective-permute-start.17 = (bf16[256,384]{1,0:T(8,128)(2,1)S(1)}, bf16[256,384]{1,0:T(8,128)(2,1)S(1)}, u32[]{:S(2)}, u32[]{:S(2)}) collective-permute-start(bf16[256,384]{1,0:T(8,128)(2,1)S(1)} %get-tuple-element.66), channel_id=1, source_target_pairs={{0,1},{1,2},{2,3},{3,0},{4,5},{5,6},{6,7},{7,4},{8,9},{9,10},{10,1... | collective-permute-start | bytes 589832 | tf_op jit(solution)/shard_map/ppermute | solution.py:521
  70.4 6.8 %collective-permute-start.18 = (bf16[256,384]{1,0:T(8,128)(2,1)S(1)}, bf16[256,384]{1,0:T(8,128)(2,1)S(1)}, u32[]{:S(2)}, u32[]{:S(2)}) collective-permute-start(bf16[256,384]{1,0:T(8,128)(2,1)S(1)} %get-tuple-element.67), channel_id=1, source_target_pairs={{0,3},{1,0},{2,1},{3,2},{4,7},{5,4},{6,5},{7,6},{8,11},{9,8},{10,9... | collective-permute-start | bytes 589832 | tf_op jit(solution)/shard_map/ppermute | solution.py:521
  72.2 9.4 %collective-permute-start.16 = (bf16[256,384]{1,0:T(8,128)(2,1)S(1)}, bf16[256,384]{1,0:T(8,128)(2,1)S(1)}, u32[]{:S(2)}, u32[]{:S(2)}) collective-permute-start(bf16[256,384]{1,0:T(8,128)(2,1)S(1)} %get-tuple-element.65), channel_id=1, source_target_pairs={{0,2},{1,3},{2,0},{3,1},{4,6},{5,7},{6,4},{7,5},{8,10},{9,11},{10,... | collective-permute-start | bytes 589832 | tf_op jit(solution)/shard_map/ppermute | solution.py:521
  (2 other events, 21.6 us)

commit v10 on v9

--- a/solution.py
+++ b/solution.py
@@ -342,49 +342,72 @@
     )(mine, got, pair, fq, raw_local, up, gain)
 
 
-def branch_parts(attn, w_out):
+def branch_parts(attn, w_out, weights):
     rows, width = attn.shape
 
-    def body(attn_ref, w_ref, *outs):
+    def body(attn_ref, w_ref, wq_hbm, wk_hbm, wv_hbm, *refs):
+        outs, blocks, sem = (refs[:4], refs[4:7], refs[7])
+        copies = block_copies(2, (wq_hbm, wk_hbm, wv_hbm), blocks, sem, 0)
+        for copy in copies:
+            copy.start()
         for k, ref in zip((2, 1, 3, 0), outs):
             ref[...] = mm(attn_ref[...], w_ref[:, block_rows(k, width)]).astype(bf16)
-
-    return plain(
-        body,
-        [((rows, width), bf16, pltpu.HBM)] * 4,
+        for copy in copies:
+            copy.wait()
+
+    hbm = pl.BlockSpec(memory_space=pltpu.HBM)
+    return call(
+        body,
+        [((rows, width), bf16, pltpu.HBM)] * 4 + [((width, width), bf16)] * 3,
         8 * rows * width * width,
-        2 * 1024 * 1024,
-        attn,
-        w_out,
-    )
+        3 * 1024 * 1024,
+        in_specs=[VMEM] * 2 + [hbm] * 3,
+        out_specs=[VMEM] * 7,
+        scratch_shapes=[pltpu.SemaphoreType.DMA((3,))],
+    )(attn, w_out, *(in_hbm(w) for w in weights))
+
+
+def local_values(fq, fk, draw):
+    rows, width = fq.shape
+
+    def body(fq_ref, fk_ref, draw_ref, dv_ref):
+        upper = tri(rows, True)
+        for p in range(width // LANES):
+            cols = slice(p * LANES, (p + 1) * LANES)
+            q, k, dr = (fq_ref[:, cols], fk_ref[:, cols], draw_ref[:, cols])
+            dv = None
+            for h in (0, 1):
+                part = mm(masked(mm(one_head(k, h), q, NT), upper), one_head(dr, h))
+                dv = part if dv is None else dv + part
+            dv_ref[:, cols] = dv.astype(bf16)
+
+    outs = [((rows, width), bf16)]
+    return plain(body, outs, 8 * rows * rows * width, 1024 * 1024, fq, fk, draw)[0]
 
 
 def local_grads(fq, fk, v, draw, before):
     rows, width = fq.shape
 
-    def body(fq_ref, fk_ref, v_ref, draw_ref, before_ref, dq_ref, dk_ref, dv_ref):
+    def body(fq_ref, fk_ref, v_ref, draw_ref, before_ref, dq_ref, dk_ref):
         lower, upper = (tri(rows, False), tri(rows, True))
         for p in range(width // LANES):
             cols = slice(p * LANES, (p + 1) * LANES)
             q, k, val, dr = (fq_ref[:, cols], fk_ref[:, cols], v_ref[:, cols], draw_ref[:, cols])
             dq = mm(dr, unpack(before_ref[p * HD : (p + 1) * HD, :]), NT)
-            dk, dv = (None, None)
+            dk = None
             for h in (0, 1):
-                val_h, k_h, q_h, dr_h = (one_head(a, h) for a in (val, k, q, dr))
+                val_h, k_h, q_h = (one_head(a, h) for a in (val, k, q))
                 dq = dq + mm(masked(mm(dr, val_h, NT), lower), k_h)
                 dk_h = mm(masked(mm(val_h, dr, NT), upper), q_h)
-                dv_h = mm(masked(mm(k_h, q, NT), upper), dr_h)
                 dk = dk_h if dk is None else dk + dk_h
-                dv = dv_h if dv is None else dv + dv_h
             dq_ref[:, cols] = (dq * jnp.minimum(q.astype(f32), 1.0)).astype(bf16)
             dk_ref[:, cols] = dk.astype(bf16)
-            dv_ref[:, cols] = dv.astype(bf16)
 
     return plain(
         body,
-        [((rows, width), bf16)] * 3,
-        24 * rows * rows * width,
-        3 * 1024 * 1024,
+        [((rows, width), bf16)] * 2,
+        16 * rows * rows * width,
+        2 * 1024 * 1024,
         fq,
         fk,
         v,
@@ -404,27 +427,6 @@
         pltpu.make_async_copy(src.at[block_rows(k, width), :], dst, sem.at[first + i])
         for i, (src, dst) in enumerate(zip(sources, targets))
     ]
-
-
-def weight_blocks(k, weights):
-    width = weights[0].shape[1]
-
-    def body(*refs):
-        copies = block_copies(k, refs[:3], refs[3:6], refs[6], 0)
-        for copy in copies:
-            copy.start()
-        for copy in copies:
-            copy.wait()
-
-    return call(
-        body,
-        [((width, width), bf16)] * 3,
-        1,
-        1024 * 1024,
-        in_specs=[pl.BlockSpec(memory_space=pltpu.HBM)] * 3,
-        out_specs=[VMEM] * 3,
-        scratch_shapes=[pltpu.SemaphoreType.DMA((3,))],
-    )(*(in_hbm(w) for w in weights))
 
 
 def first_part(mine, got, pair, fk, v, dq, dk, dv, blocks):
@@ -542,15 +544,15 @@
     got = swap(mine)
     attn, draw, before, state = normed(mine, got, pair, fq, raw_local, up, gain)
     weights = (w_query, w_key, w_value)
-    blocks = weight_blocks(2, (hold(w_query, state), w_key, w_value))
     pair = swap(state)
+    dv_local = local_values(fq, fk, draw)
     chip = pair_sum(state, pair)
     got = y_gather(True, chip)
-    b2, b1, b3, b0 = branch_parts(hold(attn, chip), w_out)
+    b2, b1, b3, b0, *blocks = branch_parts(hold(attn, chip), w_out, weights)
     planes = plane_sums(True, chip, got)
     b2, b1, b3 = (hold(b, planes) for b in (b2, b1, b3))
     branch = [b0, to_owner(b2, 2), to_owner(b1, 1), to_owner(b3, 3)]
-    dq, dk_local, dv_local = local_grads(fq, fk, v, hold(draw, planes), before)
+    dq, dk_local = local_grads(fq, fk, v, hold(draw, planes), before)
     planes = plane_exchange(planes)
     mine = before_chip(True, planes)
     got = swap(mine)

time: 82.7 us -> 84.4 us (1.021)
  starting transfers between devices: 42 us -> 45.3 us
  waiting for transfers between devices: 18.5 us -> 16.4 us
    ppermute x9, starting transfers between devices: 10.1 us -> 12.8 us  [to_owner(): return lax.ppermute(part, 'mp', shifts(4, k))]
    all_to_all x2, waiting for transfers between devices: 5.19 us -> 2.72 us  [plane_exchange(): return lax.all_to_all(planes, 'seq_0', 0, 0, tiled=True)]
    pallas_call x1, Pallas kernels: 1.16 us -> 2.55 us  [branch_parts(): call(body, [((rows, width), bf16, pltpu.HBM)] * 4 + [((width, width), bf1...]
    pallas_call x8, Pallas kernels: 4.63 us -> 3.75 us  [plain(): call(body, outs, flops, moved, in_specs=[VMEM] * len(args), out_specs=[VM...]
where the time goes in v10:
time: 84.4 us; the launch traced here: 84 us
  starting transfers between devices  45.3 us (54%)
  Pallas kernels  19.9 us (24%)
  waiting for transfers between devices  16.4 us (19%)
  other arithmetic  1.56 us (2%)
    all_to_all x2, starting transfers between devices, plane_exchange(): return lax.all_to_all(planes, 'seq_0', 0, 0, tiled=True)  14.8 us
    ppermute x9, starting transfers between devices, to_owner(): return lax.ppermute(part, 'mp', shifts(4, k))  12.8 us
    ppermute x4, starting transfers between devices, swap(): return lax.ppermute(x, 'seq_2', SWAP)  11.7 us
    ppermute x9, waiting for transfers between devices, to_owner(): return lax.ppermute(part, 'mp', shifts(4, k))  6.47 us
    ppermute x6, starting transfers between devices, y_gather(): got.append(lax.ppermute(chip, 'seq_1', shifts(4, -k if later else k)))  6.11 us
    ppermute x6, waiting for transfers between devices, y_gather(): got.append(lax.ppermute(chip, 'seq_1', shifts(4, -k if later else k)))  5.41 us
    pallas_call x2, Pallas kernels, other_parts(): call(body, [((rows, width), bf16)] * count, 6 * rows * width * width * co...  4.24 us
    pallas_call x8, Pallas kernels, plain(): call(body, outs, flops, moved, in_specs=[VMEM] * len(args), out_specs=[VM...  3.75 us
  transfers between devices with their start and end apart: 21, of which 12 were waited for; matrix products, arithmetic and copies ran while one was open for 1% of the time, Pallas kernels for 17%

profile of v10, /device:TPU:1, one launch (start us, length us, event | category | flops | bytes accessed | tf_op | source)
XLA Modules:
  0.0 84.0 jit_solution(8573232544236086673)
XLA Ops:
  0.7 3.0 %shard_map.86 = (bf16[256,384]{1,0:T(8,128)(2,1)S(1)}, bf16[256,384]{1,0:T(8,128)(2,1)S(1)}, bf16[192,128]{1,0:T(8,128)(2,1)S(1)}) custom-call(bf16[256,1536]{1,0:T(8,128)(2,1)} %x_hbm.2, bf16[1536,384]{1,0:T(8,128)(2,1)} %wk_hbm.7, bf16[1536,384]{1,0:T(8,128)(2,1)} %wv_hbm.7), custom_call_target="tpu_custom_call" | custom-call | flops 603979776 | bytes 3145728 | tf_op jit(solution)/shard_map/pallas_call | solution.py:195
  3.7 3.3 %collective-permute-start = (bf16[192,128]{1,0:T(8,128)(2,1)S(1)}, bf16[192,128]{1,0:T(8,128)(2,1)S(1)}, u32[]{:S(2)}, u32[]{:S(2)}) collective-permute-start(bf16[192,128]{1,0:T(8,128)(2,1)S(1)} %get-tuple-element.33.state_ref), channel_id=1, source_target_pairs={{0,4},{4,0},{1,5},{5,1},{2,6},{6,2},{3,7},{7,3},{8,12},{12,8},{9,1... | collective-permute-start | bytes 147464 | tf_op jit(solution)/shard_map/ppermute | solution.py:145
  8.0 2.2 %collective-permute-start.2 = (bf16[96,128]{1,0:T(8,128)(2,1)S(1)}, bf16[96,128]{1,0:T(8,128)(2,1)S(1)}, u32[]{:S(2)}, u32[]{:S(2)}) collective-permute-start(bf16[96,128]{1,0:T(8,128)(2,1)S(1)} %shard_map.87.chip_ref), channel_id=1, source_target_pairs={{0,16},{8,24},{16,0},{24,8},{1,17},{9,25},{17,1},{25,9},{2,18},{10... | collective-permute-start | bytes 73736 | tf_op jit(solution)/shard_map/ppermute | solution.py:151
  13.8 8.2 %all-to-all-start = ((bf16[8,96,128]{2,1,0:T(8,128)(2,1)}), bf16[8,96,128]{2,1,0:T(8,128)(2,1)S(1)}, u32[]{:S(2)}, u32[]{:S(2)}) async-start(bf16[8,96,128]{2,1,0:T(8,128)(2,1)} %shard_map.88), calls=%async_computation | async-start | bytes 393216 | tf_op jit(solution)/shard_map/all_to_all | solution.py:141
  23.3 2.4 %collective-permute-start.6 = (bf16[256,384]{1,0:T(8,128)(2,1)S(1)}, bf16[256,384]{1,0:T(8,128)(2,1)S(1)}, u32[]{:S(2)}, u32[]{:S(2)}) collective-permute-start(bf16[256,384]{1,0:T(8,128)(2,1)S(1)} %copy-done.2), channel_id=1, source_target_pairs={{0,2},{1,3},{2,0},{3,1},{4,6},{5,7},{6,4},{7,5},{8,10},{9,11},{10,... | collective-permute-start | bytes 589832 | tf_op jit(solution)/shard_map/ppermute | solution.py:523
  26.9 2.4 %shard_map.90 = (bf16[256,384]{1,0:T(8,128)(2,1)S(1)}, bf16[256,384]{1,0:T(8,128)(2,1)S(1)}) custom-call(bf16[256,1536]{1,0:T(8,128)(2,1)} %x_hbm.2, bf16[1536,384]{1,0:T(8,128)(2,1)S(1)} %copy-done, bf16[256,384]{1,0:T(8,128)(2,1)S(1)} %get-tuple-element.35.fk_ref, bf16[256,384]{1,0:T(8,128)(2,1)S(1)} %get-tuple-element.36.v_ref), custom_call_target="tpu_custom_call" | custom-call | flops 503316480 | bytes 3145728 | tf_op jit(solution)/shard_map/pallas_call | solution.py:253
  30.7 3.3 %collective-permute-start.4 = (bf16[96,128]{1,0:T(8,128)(2,1)S(1)}, bf16[96,128]{1,0:T(8,128)(2,1)S(1)}, u32[]{:S(2)}, u32[]{:S(2)}) collective-permute-start(bf16[96,128]{1,0:T(8,128)(2,1)S(1)} %shard_map.89.mine_ref), channel_id=1, source_target_pairs={{0,4},{4,0},{1,5},{5,1},{2,6},{6,2},{3,7},{7,3},{8,12},{12,8},{9,1... | collective-permute-start | bytes 73736 | tf_op jit(solution)/shard_map/ppermute | solution.py:145
  34.0 2.2 %shard_map.91.up_ref = bf16[256,384]{1,0:T(8,128)(2,1)S(1)} custom-call(bf16[256,384]{1,0:T(8,128)(2,1)S(1)} %copy-done.2, bf16[256,384]{1,0:T(8,128)(2,1)S(1)} %collective-permute-done.5.g1, bf16[256,384]{1,0:T(8,128)(2,1)S(1)} %collective-permute-done.6.g2, bf16[256,384]{1,0:T(8,128)(2,1)S(1)} %collective-permute-done.7.g3, bf16[384,1536]{1,0:T(8,128)(2,1)} %w_ref.1, ...), custom_call_target="tpu_custom_call" | custom-call | flops 301989888 | bytes 3145728 | tf_op jit(solution)/shard_map/pallas_call | solution.py:283
  37.2 1.9 %collective-permute-start.8 = (bf16[192,128]{1,0:T(8,128)(2,1)S(1)}, bf16[192,128]{1,0:T(8,128)(2,1)S(1)}, u32[]{:S(2)}, u32[]{:S(2)}) collective-permute-start(bf16[192,128]{1,0:T(8,128)(2,1)S(1)} %get-tuple-element.42.state_ref), channel_id=1, source_target_pairs={{0,4},{4,0},{1,5},{5,1},{2,6},{6,2},{3,7},{7,3},{8,12},{12,8},{9,1... | collective-permute-start | bytes 147464 | tf_op jit(solution)/shard_map/ppermute | solution.py:145
  40.0 2.1 %collective-permute-start.9 = (bf16[96,128]{1,0:T(8,128)(2,1)S(1)}, bf16[96,128]{1,0:T(8,128)(2,1)S(1)}, u32[]{:S(2)}, u32[]{:S(2)}) collective-permute-start(bf16[96,128]{1,0:T(8,128)(2,1)S(1)} %shard_map.93.chip_ref), channel_id=1, source_target_pairs={{0,24},{8,0},{16,8},{24,16},{1,25},{9,1},{17,9},{25,17},{2,26},{10... | collective-permute-start | bytes 73736 | tf_op jit(solution)/shard_map/ppermute | solution.py:151
  43.0 3.2 %collective-permute-done.10.g2 = bf16[96,128]{1,0:T(8,128)(2,1)S(1)} collective-permute-done((bf16[96,128]{1,0:T(8,128)(2,1)S(1)}, bf16[96,128]{1,0:T(8,128)(2,1)S(1)}, u32[]{:S(2)}, u32[]{:S(2)}) %collective-permute-start.10) | collective-permute-done | bytes 24608 | tf_op jit(solution)/shard_map/ppermute | solution.py:151
  47.0 6.6 %all-to-all-start.1 = ((bf16[8,96,128]{2,1,0:T(8,128)(2,1)}), bf16[8,96,128]{2,1,0:T(8,128)(2,1)S(1)}, u32[]{:S(2)}, u32[]{:S(2)}) async-start(bf16[8,96,128]{2,1,0:T(8,128)(2,1)} %shard_map.95), calls=%async_computation.1 | async-start | bytes 393216 | tf_op jit(solution)/shard_map/all_to_all | solution.py:141
  53.6 2.5 %shard_map.94 = (bf16[256,384]{1,0:T(8,128)(2,1)}, bf16[256,384]{1,0:T(8,128)(2,1)}, bf16[256,384]{1,0:T(8,128)(2,1)}, bf16[256,384]{1,0:T(8,128)(2,1)}, bf16[38...) custom-call(bf16[256,384]{1,0:T(8,128)(2,1)S(1)} %get-tuple-element.43.attn_ref, ...), custom_call_target="tpu_custom_call" | custom-call | flops 301989888 | bytes 3145728 | tf_op jit(solution)/shard_map/pallas_call | solution.py:359
  56.1 2.0 %collective-permute-start.14 = (bf16[256,384]{1,0:T(8,128)(2,1)}, bf16[256,384]{1,0:T(8,128)(2,1)S(1)}, u32[]{:S(2)}, u32[]{:S(2)}) collective-permute-start(bf16[256,384]{1,0:T(8,128)(2,1)} %get-tuple-element.50), channel_id=1, source_target_pairs={{0,3},{1,0},{2,1},{3,2},{4,7},{5,4},{6,5},{7,6},{8,11},{9,8},{10,9... | collective-permute-start | bytes 589832 | tf_op jit(solution)/shard_map/ppermute | solution.py:523
  58.1 1.9 %collective-permute-start.12 = (bf16[256,384]{1,0:T(8,128)(2,1)}, bf16[256,384]{1,0:T(8,128)(2,1)S(1)}, u32[]{:S(2)}, u32[]{:S(2)}) collective-permute-start(bf16[256,384]{1,0:T(8,128)(2,1)} %get-tuple-element.46), channel_id=1, source_target_pairs={{0,2},{1,3},{2,0},{3,1},{4,6},{5,7},{6,4},{7,5},{8,10},{9,11},{10,... | collective-permute-start | bytes 589832 | tf_op jit(solution)/shard_map/ppermute | solution.py:523
  60.8 1.4 %all-to-all-done.1.planes_ref = bf16[8,96,128]{2,1,0:T(8,128)(2,1)S(1)} async-done(((bf16[8,96,128]{2,1,0:T(8,128)(2,1)}), bf16[8,96,128]{2,1,0:T(8,128)(2,1)S(1)}, u32[]{:S(2)}, u32[]{:S(2)}) %all-to-all-start.1) | async-done | bytes 196640 | tf_op jit(solution)/shard_map/all_to_all | solution.py:141
  62.3 3.2 %collective-permute-start.15 = (bf16[96,128]{1,0:T(8,128)(2,1)S(1)}, bf16[96,128]{1,0:T(8,128)(2,1)S(1)}, u32[]{:S(2)}, u32[]{:S(2)}) collective-permute-start(bf16[96,128]{1,0:T(8,128)(2,1)S(1)} %shard_map.97.mine_ref), channel_id=1, source_target_pairs={{0,4},{4,0},{1,5},{5,1},{2,6},{6,2},{3,7},{7,3},{8,12},{12,8},{9,1... | collective-permute-start | bytes 73736 | tf_op jit(solution)/shard_map/ppermute | solution.py:145
  65.5 1.4 %shard_map.96 = (bf16[256,384]{1,0:T(8,128)(2,1)S(1)}, bf16[256,384]{1,0:T(8,128)(2,1)S(1)}) custom-call(bf16[256,384]{1,0:T(8,128)(2,1)S(1)} %get-tuple-element.37.fq_ref, bf16[256,384]{1,0:T(8,128)(2,1)S(1)} %get-tuple-element.35.fk_ref, bf16[256,384]{1,0:T(8,128)(2,1)S(1)} %get-tuple-element.36.v_ref, bf16[256,384]{1,0:T(8,128)(2,1)S(1)} %get-tuple-element.52.draw_ref, ...), custom_call_target="tpu_custom_call" | custom-call | flops 402653184 | bytes 2097152 | tf_op jit(solution)/shard_map/pallas_call | solution.py:48
  67.7 2.5 %shard_map.101 = (bf16[256,384]{1,0:T(8,128)(2,1)S(1)}, bf16[256,384]{1,0:T(8,128)(2,1)S(1)}) custom-call(bf16[256,384]{1,0:T(8,128)(2,1)S(1)} %get-tuple-element.54.dq_ref, bf16[256,384]{1,0:T(8,128)(2,1)S(1)} %get-tuple-element.59.dk_ref, bf16[256,384]{1,0:T(8,128)(2,1)S(1)} %get-tuple-element.60.dv_ref, bf16[1536,384]{1,0:T(8,128)(2,1)} %wq_hbm.5, ...), custom_call_target="tpu_custom_call" | custom-call | flops 452984832 | bytes 2097152 | tf_op jit(solution)/shard_map/pallas_call | solution.py:501
  70.3 2.0 %collective-permute-start.18 = (bf16[256,384]{1,0:T(8,128)(2,1)S(1)}, bf16[256,384]{1,0:T(8,128)(2,1)S(1)}, u32[]{:S(2)}, u32[]{:S(2)}) collective-permute-start(bf16[256,384]{1,0:T(8,128)(2,1)S(1)} %get-tuple-element.63), channel_id=1, source_target_pairs={{0,3},{1,0},{2,1},{3,2},{4,7},{5,4},{6,5},{7,6},{8,11},{9,8},{10,9... | collective-permute-start | bytes 589832 | tf_op jit(solution)/shard_map/ppermute | solution.py:523
  72.3 1.9 %collective-permute-start.16 = (bf16[256,384]{1,0:T(8,128)(2,1)S(1)}, bf16[256,384]{1,0:T(8,128)(2,1)S(1)}, u32[]{:S(2)}, u32[]{:S(2)}) collective-permute-start(bf16[256,384]{1,0:T(8,128)(2,1)S(1)} %get-tuple-element.61), channel_id=1, source_target_pairs={{0,2},{1,3},{2,0},{3,1},{4,6},{5,7},{6,4},{7,5},{8,10},{9,11},{10,... | collective-permute-start | bytes 589832 | tf_op jit(solution)/shard_map/ppermute | solution.py:523
  75.0 1.7 %shard_map.100 = bf16[256,384]{1,0:T(8,128)(2,1)S(1)} custom-call(bf16[256,384]{1,0:T(8,128)(2,1)S(1)} %get-tuple-element.54.dq_ref, bf16[256,384]{1,0:T(8,128)(2,1)S(1)} %get-tuple-element.59.dk_ref, bf16[256,384]{1,0:T(8,128)(2,1)S(1)} %get-tuple-element.60.dv_ref, bf16[1536,384]{1,0:T(8,128)(2,1)} %wq_hbm.5, bf16[1536,384]{1,0:T(8,128)(2,1)} %wk_hbm.7, ...), custom_call_target="tpu_custom_call" | custom-call | flops 226492416 | bytes 1048576 | tf_op jit(solution)/shard_map/pallas_call | solution.py:501
  76.8 3.6 %collective-permute-done.17 = bf16[256,384]{1,0:T(8,128)(2,1)S(1)} collective-permute-done((bf16[256,384]{1,0:T(8,128)(2,1)S(1)}, bf16[256,384]{1,0:T(8,128)(2,1)S(1)}, u32[]{:S(2)}, u32[]{:S(2)}) %collective-permute-start.17) | collective-permute-done | bytes 196640 | tf_op jit(solution)/shard_map/ppermute | solution.py:523
  80.4 2.7 %collective-permute-done.16 = bf16[256,384]{1,0:T(8,128)(2,1)S(1)} collective-permute-done((bf16[256,384]{1,0:T(8,128)(2,1)S(1)}, bf16[256,384]{1,0:T(8,128)(2,1)S(1)}, u32[]{:S(2)}, u32[]{:S(2)}) %collective-permute-start.16) | collective-permute-done | bytes 196640 | tf_op jit(solution)/shard_map/ppermute | solution.py:523
  (47 shorter events, 15.3 us)
Async XLA Ops:
  0.6 21.4 %copy-start.2 = (bf16[256,384]{1,0:T(8,128)(2,1)S(1)}, bf16[256,384]{1,0:T(8,128)(2,1)}, u32[]{:S(2)}) copy-start(bf16[256,384]{1,0:T(8,128)(2,1)} %g0.1) | copy-start | bytes 589828
  0.6 26.3 %copy-start.4 = (f32[384]{0:T(512)S(1)}, f32[384]{0:T(512)}, u32[]{:S(2)}) copy-start(f32[384]{0:T(512)} %param.12) | copy-start | bytes 4612
  0.6 26.2 %copy-start = (bf16[1536,384]{1,0:T(8,128)(2,1)S(1)}, bf16[1536,384]{1,0:T(8,128)(2,1)}, u32[]{:S(2)}) copy-start(bf16[1536,384]{1,0:T(8,128)(2,1)} %wq_hbm.5) | copy-start | bytes 3538948
  3.7 4.2 %collective-permute-start = (bf16[192,128]{1,0:T(8,128)(2,1)S(1)}, bf16[192,128]{1,0:T(8,128)(2,1)S(1)}, u32[]{:S(2)}, u32[]{:S(2)}) collective-permute-start(bf16[192,128]{1,0:T(8,128)(2,1)S(1)} %get-tuple-element.33.state_ref), channel_id=1, source_target_pairs={{0,4},{4,0},{1,5},{5,1},{2,6},{6,2},{3,7},{7,3},{8,12},{12,8},{9,1... | collective-permute-start | bytes 147464 | tf_op jit(solution)/shard_map/ppermute | solution.py:145
  7.9 4.0 %collective-permute-start.1 = (bf16[96,128]{1,0:T(8,128)(2,1)S(1)}, bf16[96,128]{1,0:T(8,128)(2,1)S(1)}, u32[]{:S(2)}, u32[]{:S(2)}) collective-permute-start(bf16[96,128]{1,0:T(8,128)(2,1)S(1)} %shard_map.87.chip_ref), channel_id=1, source_target_pairs={{0,8},{8,16},{16,24},{24,0},{1,9},{9,17},{17,25},{25,1},{2,10},{10... | collective-permute-start | bytes 73736 | tf_op jit(solution)/shard_map/ppermute | solution.py:151
  8.0 4.6 %collective-permute-start.2 = (bf16[96,128]{1,0:T(8,128)(2,1)S(1)}, bf16[96,128]{1,0:T(8,128)(2,1)S(1)}, u32[]{:S(2)}, u32[]{:S(2)}) collective-permute-start(bf16[96,128]{1,0:T(8,128)(2,1)S(1)} %shard_map.87.chip_ref), channel_id=1, source_target_pairs={{0,16},{8,24},{16,0},{24,8},{1,17},{9,25},{17,1},{25,9},{2,18},{10... | collective-permute-start | bytes 73736 | tf_op jit(solution)/shard_map/ppermute | solution.py:151
  10.2 3.0 %collective-permute-start.3 = (bf16[96,128]{1,0:T(8,128)(2,1)S(1)}, bf16[96,128]{1,0:T(8,128)(2,1)S(1)}, u32[]{:S(2)}, u32[]{:S(2)}) collective-permute-start(bf16[96,128]{1,0:T(8,128)(2,1)S(1)} %shard_map.87.chip_ref), channel_id=1, source_target_pairs={{0,24},{8,0},{16,8},{24,16},{1,25},{9,1},{17,9},{25,17},{2,26},{10... | collective-permute-start | bytes 73736 | tf_op jit(solution)/shard_map/ppermute | solution.py:151
  13.8 16.8 %all-to-all-start = ((bf16[8,96,128]{2,1,0:T(8,128)(2,1)}), bf16[8,96,128]{2,1,0:T(8,128)(2,1)S(1)}, u32[]{:S(2)}, u32[]{:S(2)}) async-start(bf16[8,96,128]{2,1,0:T(8,128)(2,1)} %shard_map.88), calls=%async_computation | async-start | bytes 393216 | tf_op jit(solution)/shard_map/all_to_all | solution.py:141
  22.0 12.0 %collective-permute-start.5 = (bf16[256,384]{1,0:T(8,128)(2,1)S(1)}, bf16[256,384]{1,0:T(8,128)(2,1)S(1)}, u32[]{:S(2)}, u32[]{:S(2)}) collective-permute-start(bf16[256,384]{1,0:T(8,128)(2,1)S(1)} %copy-done.2), channel_id=1, source_target_pairs={{0,1},{1,2},{2,3},{3,0},{4,5},{5,6},{6,7},{7,4},{8,9},{9,10},{10,1... | collective-permute-start | bytes 589832 | tf_op jit(solution)/shard_map/ppermute | solution.py:523
  23.3 10.7 %collective-permute-start.6 = (bf16[256,384]{1,0:T(8,128)(2,1)S(1)}, bf16[256,384]{1,0:T(8,128)(2,1)S(1)}, u32[]{:S(2)}, u32[]{:S(2)}) collective-permute-start(bf16[256,384]{1,0:T(8,128)(2,1)S(1)} %copy-done.2), channel_id=1, source_target_pairs={{0,2},{1,3},{2,0},{3,1},{4,6},{5,7},{6,4},{7,5},{8,10},{9,11},{10,... | collective-permute-start | bytes 589832 | tf_op jit(solution)/shard_map/ppermute | solution.py:523
  25.7 8.3 %collective-permute-start.7 = (bf16[256,384]{1,0:T(8,128)(2,1)S(1)}, bf16[256,384]{1,0:T(8,128)(2,1)S(1)}, u32[]{:S(2)}, u32[]{:S(2)}) collective-permute-start(bf16[256,384]{1,0:T(8,128)(2,1)S(1)} %copy-done.2), channel_id=1, source_target_pairs={{0,3},{1,0},{2,1},{3,2},{4,7},{5,4},{6,5},{7,6},{8,11},{9,8},{10,9... | collective-permute-start | bytes 589832 | tf_op jit(solution)/shard_map/ppermute | solution.py:523
  30.7 5.5 %collective-permute-start.4 = (bf16[96,128]{1,0:T(8,128)(2,1)S(1)}, bf16[96,128]{1,0:T(8,128)(2,1)S(1)}, u32[]{:S(2)}, u32[]{:S(2)}) collective-permute-start(bf16[96,128]{1,0:T(8,128)(2,1)S(1)} %shard_map.89.mine_ref), channel_id=1, source_target_pairs={{0,4},{4,0},{1,5},{5,1},{2,6},{6,2},{3,7},{7,3},{8,12},{12,8},{9,1... | collective-permute-start | bytes 73736 | tf_op jit(solution)/shard_map/ppermute | solution.py:145
  37.2 2.8 %collective-permute-start.8 = (bf16[192,128]{1,0:T(8,128)(2,1)S(1)}, bf16[192,128]{1,0:T(8,128)(2,1)S(1)}, u32[]{:S(2)}, u32[]{:S(2)}) collective-permute-start(bf16[192,128]{1,0:T(8,128)(2,1)S(1)} %get-tuple-element.42.state_ref), channel_id=1, source_target_pairs={{0,4},{4,0},{1,5},{5,1},{2,6},{6,2},{3,7},{7,3},{8,12},{12,8},{9,1... | collective-permute-start | bytes 147464 | tf_op jit(solution)/shard_map/ppermute | solution.py:145
  40.0 3.0 %collective-permute-start.9 = (bf16[96,128]{1,0:T(8,128)(2,1)S(1)}, bf16[96,128]{1,0:T(8,128)(2,1)S(1)}, u32[]{:S(2)}, u32[]{:S(2)}) collective-permute-start(bf16[96,128]{1,0:T(8,128)(2,1)S(1)} %shard_map.93.chip_ref), channel_id=1, source_target_pairs={{0,24},{8,0},{16,8},{24,16},{1,25},{9,1},{17,9},{25,17},{2,26},{10... | collective-permute-start | bytes 73736 | tf_op jit(solution)/shard_map/ppermute | solution.py:151
  42.1 4.2 %collective-permute-start.10 = (bf16[96,128]{1,0:T(8,128)(2,1)S(1)}, bf16[96,128]{1,0:T(8,128)(2,1)S(1)}, u32[]{:S(2)}, u32[]{:S(2)}) collective-permute-start(bf16[96,128]{1,0:T(8,128)(2,1)S(1)} %shard_map.93.chip_ref), channel_id=1, source_target_pairs={{0,16},{8,24},{16,0},{24,8},{1,17},{9,25},{17,1},{25,9},{2,18},{10... | collective-permute-start | bytes 73736 | tf_op jit(solution)/shard_map/ppermute | solution.py:151
  42.1 4.2 %collective-permute-start.11 = (bf16[96,128]{1,0:T(8,128)(2,1)S(1)}, bf16[96,128]{1,0:T(8,128)(2,1)S(1)}, u32[]{:S(2)}, u32[]{:S(2)}) collective-permute-start(bf16[96,128]{1,0:T(8,128)(2,1)S(1)} %shard_map.93.chip_ref), channel_id=1, source_target_pairs={{0,8},{8,16},{16,24},{24,0},{1,9},{9,17},{17,25},{25,1},{2,10},{10... | collective-permute-start | bytes 73736 | tf_op jit(solution)/shard_map/ppermute | solution.py:151
  47.0 15.3 %all-to-all-start.1 = ((bf16[8,96,128]{2,1,0:T(8,128)(2,1)}), bf16[8,96,128]{2,1,0:T(8,128)(2,1)S(1)}, u32[]{:S(2)}, u32[]{:S(2)}) async-start(bf16[8,96,128]{2,1,0:T(8,128)(2,1)} %shard_map.95), calls=%async_computation.1 | async-start | bytes 393216 | tf_op jit(solution)/shard_map/all_to_all | solution.py:141
  56.1 16.2 %collective-permute-start.14 = (bf16[256,384]{1,0:T(8,128)(2,1)}, bf16[256,384]{1,0:T(8,128)(2,1)S(1)}, u32[]{:S(2)}, u32[]{:S(2)}) collective-permute-start(bf16[256,384]{1,0:T(8,128)(2,1)} %get-tuple-element.50), channel_id=1, source_target_pairs={{0,3},{1,0},{2,1},{3,2},{4,7},{5,4},{6,5},{7,6},{8,11},{9,8},{10,9... | collective-permute-start | bytes 589832 | tf_op jit(solution)/shard_map/ppermute | solution.py:523
  58.1 16.1 %collective-permute-start.13 = (bf16[256,384]{1,0:T(8,128)(2,1)}, bf16[256,384]{1,0:T(8,128)(2,1)S(1)}, u32[]{:S(2)}, u32[]{:S(2)}) collective-permute-start(bf16[256,384]{1,0:T(8,128)(2,1)} %get-tuple-element.48), channel_id=1, source_target_pairs={{0,1},{1,2},{2,3},{3,0},{4,5},{5,6},{6,7},{7,4},{8,9},{9,10},{10,1... | collective-permute-start | bytes 589832 | tf_op jit(solution)/shard_map/ppermute | solution.py:523
  58.1 16.1 %collective-permute-start.12 = (bf16[256,384]{1,0:T(8,128)(2,1)}, bf16[256,384]{1,0:T(8,128)(2,1)S(1)}, u32[]{:S(2)}, u32[]{:S(2)}) collective-permute-start(bf16[256,384]{1,0:T(8,128)(2,1)} %get-tuple-element.46), channel_id=1, source_target_pairs={{0,2},{1,3},{2,0},{3,1},{4,6},{5,7},{6,4},{7,5},{8,10},{9,11},{10,... | collective-permute-start | bytes 589832 | tf_op jit(solution)/shard_map/ppermute | solution.py:523
  62.3 4.7 %collective-permute-start.15 = (bf16[96,128]{1,0:T(8,128)(2,1)S(1)}, bf16[96,128]{1,0:T(8,128)(2,1)S(1)}, u32[]{:S(2)}, u32[]{:S(2)}) collective-permute-start(bf16[96,128]{1,0:T(8,128)(2,1)S(1)} %shard_map.97.mine_ref), channel_id=1, source_target_pairs={{0,4},{4,0},{1,5},{5,1},{2,6},{6,2},{3,7},{7,3},{8,12},{12,8},{9,1... | collective-permute-start | bytes 73736 | tf_op jit(solution)/shard_map/ppermute | solution.py:145
  70.3 6.5 %collective-permute-start.18 = (bf16[256,384]{1,0:T(8,128)(2,1)S(1)}, bf16[256,384]{1,0:T(8,128)(2,1)S(1)}, u32[]{:S(2)}, u32[]{:S(2)}) collective-permute-start(bf16[256,384]{1,0:T(8,128)(2,1)S(1)} %get-tuple-element.63), channel_id=1, source_target_pairs={{0,3},{1,0},{2,1},{3,2},{4,7},{5,4},{6,5},{7,6},{8,11},{9,8},{10,9... | collective-permute-start | bytes 589832 | tf_op jit(solution)/shard_map/ppermute | solution.py:523
  72.3 8.1 %collective-permute-start.17 = (bf16[256,384]{1,0:T(8,128)(2,1)S(1)}, bf16[256,384]{1,0:T(8,128)(2,1)S(1)}, u32[]{:S(2)}, u32[]{:S(2)}) collective-permute-start(bf16[256,384]{1,0:T(8,128)(2,1)S(1)} %get-tuple-element.62), channel_id=1, source_target_pairs={{0,1},{1,2},{2,3},{3,0},{4,5},{5,6},{6,7},{7,4},{8,9},{9,10},{10,1... | collective-permute-start | bytes 589832 | tf_op jit(solution)/shard_map/ppermute | solution.py:523
  72.3 10.9 %collective-permute-start.16 = (bf16[256,384]{1,0:T(8,128)(2,1)S(1)}, bf16[256,384]{1,0:T(8,128)(2,1)S(1)}, u32[]{:S(2)}, u32[]{:S(2)}) collective-permute-start(bf16[256,384]{1,0:T(8,128)(2,1)S(1)} %get-tuple-element.61), channel_id=1, source_target_pairs={{0,2},{1,3},{2,0},{3,1},{4,6},{5,7},{6,4},{7,5},{8,10},{9,11},{10,... | collective-permute-start | bytes 589832 | tf_op jit(solution)/shard_map/ppermute | solution.py:523
  (2 other events, 23.9 us)

commit v11 on v6

--- a/solution.py
+++ b/solution.py
@@ -154,13 +154,13 @@
 
 def key_value(latents, w_key, w_value):
     rows, width = (latents.shape[0], w_key.shape[1])
-    steps = 4
-    depth = latents.shape[1] // steps
+    depths = [latents.shape[1] // 12 * part for part in (4, 4, 3, 1)]
+    steps = len(depths)
 
     def body(x_hbm, wk_hbm, wv_hbm, fk_ref, v_ref, state_ref, x_ref, w_ref, sem):
         copies = []
         for i in range(steps):
-            span = pl.ds(i * depth, depth)
+            span = pl.ds(sum(depths[:i]), depths[i])
             copies.append(
                 [
                     pltpu.make_async_copy(src, dst, sem.at[3 * i + j])
@@ -180,7 +180,7 @@
         for i, group in enumerate(copies):
             for copy in group:
                 copy.wait()
-            span = slice(i * depth, (i + 1) * depth)
+            span = slice(sum(depths[:i]), sum(depths[: i + 1]))
             part = mm(x_ref[:, span], w_ref[span, :])
             total = part if total is None else total + part
         fk_ref[...] = feature_map(total[:, :width]).astype(bf16)
@@ -359,32 +359,47 @@
     )
 
 
+def local_values(fq, fk, draw):
+    rows, width = fq.shape
+
+    def body(fq_ref, fk_ref, draw_ref, dv_ref):
+        upper = tri(rows, True)
+        for p in range(width // LANES):
+            cols = slice(p * LANES, (p + 1) * LANES)
+            q, k, dr = (fq_ref[:, cols], fk_ref[:, cols], draw_ref[:, cols])
+            dv = None
+            for h in (0, 1):
+                part = mm(masked(mm(one_head(k, h), q, NT), upper), one_head(dr, h))
+                dv = part if dv is None else dv + part
+            dv_ref[:, cols] = dv.astype(bf16)
+
+    outs = [((rows, width), bf16)]
+    return plain(body, outs, 8 * rows * rows * width, 1024 * 1024, fq, fk, draw)[0]
+
+
 def local_grads(fq, fk, v, draw, before):
     rows, width = fq.shape
 
-    def body(fq_ref, fk_ref, v_ref, draw_ref, before_ref, dq_ref, dk_ref, dv_ref):
+    def body(fq_ref, fk_ref, v_ref, draw_ref, before_ref, dq_ref, dk_ref):
         lower, upper = (tri(rows, False), tri(rows, True))
         for p in range(width // LANES):
             cols = slice(p * LANES, (p + 1) * LANES)
             q, k, val, dr = (fq_ref[:, cols], fk_ref[:, cols], v_ref[:, cols], draw_ref[:, cols])
             dq = mm(dr, unpack(before_ref[p * HD : (p + 1) * HD, :]), NT)
-            dk, dv = (None, None)
+            dk = None
             for h in (0, 1):
-                val_h, k_h, q_h, dr_h = (one_head(a, h) for a in (val, k, q, dr))
+                val_h, k_h, q_h = (one_head(a, h) for a in (val, k, q))
                 dq = dq + mm(masked(mm(dr, val_h, NT), lower), k_h)
                 dk_h = mm(masked(mm(val_h, dr, NT), upper), q_h)
-                dv_h = mm(masked(mm(k_h, q, NT), upper), dr_h)
                 dk = dk_h if dk is None else dk + dk_h
-                dv = dv_h if dv is None else dv + dv_h
             dq_ref[:, cols] = (dq * jnp.minimum(q.astype(f32), 1.0)).astype(bf16)
             dk_ref[:, cols] = dk.astype(bf16)
-            dv_ref[:, cols] = dv.astype(bf16)
 
     return plain(
         body,
-        [((rows, width), bf16)] * 3,
-        24 * rows * rows * width,
-        3 * 1024 * 1024,
+        [((rows, width), bf16)] * 2,
+        16 * rows * rows * width,
+        2 * 1024 * 1024,
         fq,
         fk,
         v,
@@ -566,13 +581,10 @@
 
 
 def add_up(parts):
-    def body(*refs):
-        total = refs[0][...].astype(f32)
-        for ref in refs[1:-1]:
-            total = total + ref[...].astype(f32)
-        refs[-1][...] = total.astype(bf16)
-
-    return plain(body, [(parts[0].shape, bf16, pltpu.HBM)], 1, 1024 * 1024, *map(in_hbm, parts))[0]
+    total = parts[0].astype(f32)
+    for part in parts[1:]:
+        total = total + part.astype(f32)
+    return total.astype(bf16)
 
 
 def to_owner(part, k):
@@ -587,27 +599,29 @@
     gain = head_gain.reshape(1, -1)
     fk, v, state = key_value(latents, w_key, w_value)
     pair = swap(state)
+    grad1 = to_owner(hold(grad_out, state), 1)
     chip = pair_sum(state, pair)
     got = y_gather(False, chip)
     grad_held = hold(grad_out, chip)
-    grads = [grad_out] + [to_owner(grad_held, k) for k in (1, 2, 3)]
+    grads = [grad_out, grad1] + [to_owner(grad_held, k) for k in (2, 3)]
     planes = plane_sums(False, chip, got)
     fq, raw_local = query_local(hold(latents, planes), w_query, fk, v)
     up = upstream_of(grads, w_out, gain)
     planes = plane_exchange(planes)
     mine = before_chip(False, planes)
     got = swap(mine)
+    weights = (w_query, w_key, w_value)
+    blocks = weight_blocks((2,), (hold(w_query, mine), w_key, w_value))
     attn, draw, before, state = normed(mine, got, pair, fq, raw_local, up, gain)
-    weights = (w_query, w_key, w_value)
-    blocks = weight_blocks((2,), (hold(w_query, state), w_key, w_value))
     pair = swap(state)
+    dv_local = local_values(fq, fk, draw)
     chip = pair_sum(state, pair)
     got = y_gather(True, chip)
     b2, b1, b3, b0 = branch_parts(hold(attn, chip), w_out)
     planes = plane_sums(True, chip, got)
     b2, b1, b3 = (hold(b, planes) for b in (b2, b1, b3))
     branch = [b0, to_owner(b2, 2), to_owner(b1, 1), to_owner(b3, 3)]
-    dq, dk_local, dv_local = local_grads(fq, fk, v, hold(draw, planes), before)
+    dq, dk_local = local_grads(fq, fk, v, hold(draw, planes), before)
     planes = plane_exchange(planes)
     mine = before_chip(True, planes)
     got = swap(mine)
@@ -619,9 +633,8 @@
     mark = marker(late1)
     late1, late3 = relayed(late1, late3, far1, far3, mark)
     late1, late3 = (to_owner(late1, 1), to_owner(late3, 3))
-    branch = add_up(branch)
     own = own_part(dq, dk, dv, weights)
-    return (branch, finished(own, soon3, late1, soon1, late3))
+    return (add_up(branch), finished(own, soon3, late1, soon1, late3))
 
 
 def solution(mesh):

time: 85.1 us -> 81.4 us (0.957)
  waiting for transfers between devices: 15.9 us -> 11.8 us
  starting transfers between devices: 44.3 us -> 46 us
  Pallas kernels: 22.2 us -> 20.6 us
    all_to_all x2, waiting for transfers between devices: 6.61 us -> 4.39 us  [plane_exchange(): return lax.all_to_all(planes, 'seq_0', 0, 0, tiled=True)]
    ppermute x12, waiting for transfers between devices: 2.64 us -> 0.71 us  [to_owner(): return lax.ppermute(part, 'mp', shifts(4, k))]
    pallas_call x13, Pallas kernels: 8.33 us -> 6.79 us  [plain(): call(body, outs, flops, moved, in_specs=[VMEM] * len(args), out_specs=[VM...]
    ppermute x12, starting transfers between devices: 12.7 us -> 14.1 us  [to_owner(): return lax.ppermute(part, 'mp', shifts(4, k))]
  transfers between devices with their start and end apart: 24 -> 24, of which waited for: 12 -> 12; matrix products, arithmetic and copies ran while one was open for 0% -> 1% of each run, Pallas kernels for 19% -> 18%
where the time goes in v11:
time: 81.4 us; the launch traced here: 80.1 us
  starting transfers between devices  46 us (57%)
  Pallas kernels  20.6 us (25%)
  waiting for transfers between devices  11.8 us (14%)
  between operations  0.88 us (1%)
    all_to_all x2, starting transfers between devices, plane_exchange(): return lax.all_to_all(planes, 'seq_0', 0, 0, tiled=True)  14.8 us
    ppermute x12, starting transfers between devices, to_owner(): return lax.ppermute(part, 'mp', shifts(4, k))  14.1 us
    ppermute x4, starting transfers between devices, swap(): return lax.ppermute(x, 'seq_2', SWAP)  11.4 us
    pallas_call x13, Pallas kernels, plain(): call(body, outs, flops, moved, in_specs=[VMEM] * len(args), out_specs=[VM...  6.79 us
    ppermute x6, starting transfers between devices, y_gather(): got.append(lax.ppermute(chip, 'seq_1', shifts(4, -k if later else k)))  5.76 us
    ppermute x6, waiting for transfers between devices, y_gather(): got.append(lax.ppermute(chip, 'seq_1', shifts(4, -k if later else k)))  4.88 us
    all_to_all x2, waiting for transfers between devices, plane_exchange(): return lax.all_to_all(planes, 'seq_0', 0, 0, tiled=True)  4.39 us
    pallas_call x1, Pallas kernels, key_value(): call(body, [((rows, width), bf16), ((rows, width), bf16), ((width * HD //...  3.02 us
  transfers between devices with their start and end apart: 24, of which 12 were waited for; matrix products, arithmetic and copies ran while one was open for 1% of the time, Pallas kernels for 18%

profile of v11, /device:TPU:1, one launch (start us, length us, event | category | flops | bytes accessed | tf_op | source)
XLA Modules:
  0.0 80.1 jit_solution(6740541676157243442)
XLA Ops:
  0.7 3.0 %shard_map.86 = (bf16[256,384]{1,0:T(8,128)(2,1)S(1)}, bf16[256,384]{1,0:T(8,128)(2,1)S(1)}, bf16[192,128]{1,0:T(8,128)(2,1)S(1)}) custom-call(bf16[256,1536]{1,0:T(8,128)(2,1)} %x_hbm.2, bf16[1536,384]{1,0:T(8,128)(2,1)} %refs_1_.3, bf16[1536,384]{1,0:T(8,128)(2,1)} %refs_2_.3), custom_call_target="tpu_custom_call" | custom-call | flops 603979776 | bytes 3145728 | tf_op jit(solution)/shard_map/pallas_call | solution.py:195
  3.7 3.3 %collective-permute-start = (bf16[192,128]{1,0:T(8,128)(2,1)S(1)}, bf16[192,128]{1,0:T(8,128)(2,1)S(1)}, u32[]{:S(2)}, u32[]{:S(2)}) collective-permute-start(bf16[192,128]{1,0:T(8,128)(2,1)S(1)} %get-tuple-element.46.state_ref), channel_id=1, source_target_pairs={{0,4},{4,0},{1,5},{5,1},{2,6},{6,2},{3,7},{7,3},{8,12},{12,8},{9,1... | collective-permute-start | bytes 147464 | tf_op jit(solution)/shard_map/ppermute | solution.py:145
  10.6 2.6 %collective-permute-done.2.g2 = bf16[96,128]{1,0:T(8,128)(2,1)S(1)} collective-permute-done((bf16[96,128]{1,0:T(8,128)(2,1)S(1)}, bf16[96,128]{1,0:T(8,128)(2,1)S(1)}, u32[]{:S(2)}, u32[]{:S(2)}) %collective-permute-start.2) | collective-permute-done | bytes 24608 | tf_op jit(solution)/shard_map/ppermute | solution.py:151
  14.1 8.2 %all-to-all-start = ((bf16[8,96,128]{2,1,0:T(8,128)(2,1)}), bf16[8,96,128]{2,1,0:T(8,128)(2,1)S(1)}, u32[]{:S(2)}, u32[]{:S(2)}) async-start(bf16[8,96,128]{2,1,0:T(8,128)(2,1)} %shard_map.88), calls=%async_computation | async-start | bytes 393216 | tf_op jit(solution)/shard_map/all_to_all | solution.py:141
  22.3 1.3 %collective-permute-start.5 = (bf16[256,384]{1,0:T(8,128)(2,1)S(1)}, bf16[256,384]{1,0:T(8,128)(2,1)S(1)}, u32[]{:S(2)}, u32[]{:S(2)}) collective-permute-start(bf16[256,384]{1,0:T(8,128)(2,1)S(1)} %copy-done.2), channel_id=1, source_target_pairs={{0,1},{1,2},{2,3},{3,0},{4,5},{5,6},{6,7},{7,4},{8,9},{9,10},{10,1... | collective-permute-start | bytes 589832 | tf_op jit(solution)/shard_map/ppermute | solution.py:591
  23.6 1.5 %collective-permute-start.7 = (bf16[256,384]{1,0:T(8,128)(2,1)S(1)}, bf16[256,384]{1,0:T(8,128)(2,1)S(1)}, u32[]{:S(2)}, u32[]{:S(2)}) collective-permute-start(bf16[256,384]{1,0:T(8,128)(2,1)S(1)} %copy-done.2), channel_id=1, source_target_pairs={{0,3},{1,0},{2,1},{3,2},{4,7},{5,4},{6,5},{7,6},{8,11},{9,8},{10,9... | collective-permute-start | bytes 589832 | tf_op jit(solution)/shard_map/ppermute | solution.py:591
  25.1 1.5 %collective-permute-start.6 = (bf16[256,384]{1,0:T(8,128)(2,1)S(1)}, bf16[256,384]{1,0:T(8,128)(2,1)S(1)}, u32[]{:S(2)}, u32[]{:S(2)}) collective-permute-start(bf16[256,384]{1,0:T(8,128)(2,1)S(1)} %copy-done.2), channel_id=1, source_target_pairs={{0,2},{1,3},{2,0},{3,1},{4,6},{5,7},{6,4},{7,5},{8,10},{9,11},{10,... | collective-permute-start | bytes 589832 | tf_op jit(solution)/shard_map/ppermute | solution.py:591
  26.6 2.4 %shard_map.90 = (bf16[256,384]{1,0:T(8,128)(2,1)S(1)}, bf16[256,384]{1,0:T(8,128)(2,1)S(1)}) custom-call(bf16[256,1536]{1,0:T(8,128)(2,1)} %x_hbm.2, bf16[1536,384]{1,0:T(8,128)(2,1)S(1)} %copy-done, bf16[256,384]{1,0:T(8,128)(2,1)S(1)} %get-tuple-element.48.fk_ref, bf16[256,384]{1,0:T(8,128)(2,1)S(1)} %get-tuple-element.49.v_ref), custom_call_target="tpu_custom_call" | custom-call | flops 503316480 | bytes 3145728 | tf_op jit(solution)/shard_map/pallas_call | solution.py:253
  29.1 1.9 %all-to-all-done.planes_ref = bf16[8,96,128]{2,1,0:T(8,128)(2,1)S(1)} async-done(((bf16[8,96,128]{2,1,0:T(8,128)(2,1)}), bf16[8,96,128]{2,1,0:T(8,128)(2,1)S(1)}, u32[]{:S(2)}, u32[]{:S(2)}) %all-to-all-start) | async-done | bytes 196640 | tf_op jit(solution)/shard_map/all_to_all | solution.py:141
  31.0 3.3 %collective-permute-start.4 = (bf16[96,128]{1,0:T(8,128)(2,1)S(1)}, bf16[96,128]{1,0:T(8,128)(2,1)S(1)}, u32[]{:S(2)}, u32[]{:S(2)}) collective-permute-start(bf16[96,128]{1,0:T(8,128)(2,1)S(1)} %shard_map.89.mine_ref), channel_id=1, source_target_pairs={{0,4},{4,0},{1,5},{5,1},{2,6},{6,2},{3,7},{7,3},{8,12},{12,8},{9,1... | collective-permute-start | bytes 73736 | tf_op jit(solution)/shard_map/ppermute | solution.py:145
  34.4 2.2 %shard_map.91.up_ref = bf16[256,384]{1,0:T(8,128)(2,1)S(1)} custom-call(bf16[256,384]{1,0:T(8,128)(2,1)S(1)} %copy-done.2, bf16[256,384]{1,0:T(8,128)(2,1)S(1)} %collective-permute-done.5.g1, bf16[256,384]{1,0:T(8,128)(2,1)S(1)} %collective-permute-done.6.g2, bf16[256,384]{1,0:T(8,128)(2,1)S(1)} %collective-permute-done.7.g3, bf16[384,1536]{1,0:T(8,128)(2,1)} %w_ref.1, ...), custom_call_target="tpu_custom_call" | custom-call | flops 301989888 | bytes 3145728 | tf_op jit(solution)/shard_map/pallas_call | solution.py:283
  37.6 1.8 %collective-permute-start.8 = (bf16[192,128]{1,0:T(8,128)(2,1)S(1)}, bf16[192,128]{1,0:T(8,128)(2,1)S(1)}, u32[]{:S(2)}, u32[]{:S(2)}) collective-permute-start(bf16[192,128]{1,0:T(8,128)(2,1)S(1)} %get-tuple-element.55.state_ref), channel_id=1, source_target_pairs={{0,4},{4,0},{1,5},{5,1},{2,6},{6,2},{3,7},{7,3},{8,12},{12,8},{9,1... | collective-permute-start | bytes 147464 | tf_op jit(solution)/shard_map/ppermute | solution.py:145
  40.4 1.8 %collective-permute-start.10 = (bf16[96,128]{1,0:T(8,128)(2,1)S(1)}, bf16[96,128]{1,0:T(8,128)(2,1)S(1)}, u32[]{:S(2)}, u32[]{:S(2)}) collective-permute-start(bf16[96,128]{1,0:T(8,128)(2,1)S(1)} %shard_map.93.chip_ref), channel_id=1, source_target_pairs={{0,16},{8,24},{16,0},{24,8},{1,17},{9,25},{17,1},{25,9},{2,18},{10... | collective-permute-start | bytes 73736 | tf_op jit(solution)/shard_map/ppermute | solution.py:151
  42.1 1.8 %collective-permute-start.9 = (bf16[96,128]{1,0:T(8,128)(2,1)S(1)}, bf16[96,128]{1,0:T(8,128)(2,1)S(1)}, u32[]{:S(2)}, u32[]{:S(2)}) collective-permute-start(bf16[96,128]{1,0:T(8,128)(2,1)S(1)} %shard_map.93.chip_ref), channel_id=1, source_target_pairs={{0,24},{8,0},{16,8},{24,16},{1,25},{9,1},{17,9},{25,17},{2,26},{10... | collective-permute-start | bytes 73736 | tf_op jit(solution)/shard_map/ppermute | solution.py:151
  46.1 6.6 %all-to-all-start.1 = ((bf16[8,96,128]{2,1,0:T(8,128)(2,1)}), bf16[8,96,128]{2,1,0:T(8,128)(2,1)S(1)}, u32[]{:S(2)}, u32[]{:S(2)}) async-start(bf16[8,96,128]{2,1,0:T(8,128)(2,1)} %shard_map.95), calls=%async_computation.1 | async-start | bytes 393216 | tf_op jit(solution)/shard_map/all_to_all | solution.py:141
  52.7 1.3 %shard_map.94 = (bf16[256,384]{1,0:T(8,128)(2,1)}, bf16[256,384]{1,0:T(8,128)(2,1)}, bf16[256,384]{1,0:T(8,128)(2,1)}, bf16[256,384]{1,0:T(8,128)(2,1)}) custom-call(bf16[256,384]{1,0:T(8,128)(2,1)S(1)} %get-tuple-element.56.attn_ref, bf16[384,1536]{1,0:T(8,128)(2,1)S(1)} %copy-done.1), custom_call_target="tpu_custom_call" | custom-call | flops 301989888 | bytes 2097152 | tf_op jit(solution)/shard_map/pallas_call | solution.py:48
  54.0 1.7 %collective-permute-start.14 = (bf16[256,384]{1,0:T(8,128)(2,1)}, bf16[256,384]{1,0:T(8,128)(2,1)S(1)}, u32[]{:S(2)}, u32[]{:S(2)}) collective-permute-start(bf16[256,384]{1,0:T(8,128)(2,1)} %get-tuple-element.63), channel_id=1, source_target_pairs={{0,3},{1,0},{2,1},{3,2},{4,7},{5,4},{6,5},{7,6},{8,11},{9,8},{10,9... | collective-permute-start | bytes 589832 | tf_op jit(solution)/shard_map/ppermute | solution.py:591
  58.8 2.5 %all-to-all-done.1.planes_ref = bf16[8,96,128]{2,1,0:T(8,128)(2,1)S(1)} async-done(((bf16[8,96,128]{2,1,0:T(8,128)(2,1)}), bf16[8,96,128]{2,1,0:T(8,128)(2,1)S(1)}, u32[]{:S(2)}, u32[]{:S(2)}) %all-to-all-start.1) | async-done | bytes 196640 | tf_op jit(solution)/shard_map/all_to_all | solution.py:141
  61.4 3.0 %collective-permute-start.15 = (bf16[96,128]{1,0:T(8,128)(2,1)S(1)}, bf16[96,128]{1,0:T(8,128)(2,1)S(1)}, u32[]{:S(2)}, u32[]{:S(2)}) collective-permute-start(bf16[96,128]{1,0:T(8,128)(2,1)S(1)} %shard_map.97.mine_ref), channel_id=1, source_target_pairs={{0,4},{4,0},{1,5},{5,1},{2,6},{6,2},{3,7},{7,3},{8,12},{12,8},{9,1... | collective-permute-start | bytes 73736 | tf_op jit(solution)/shard_map/ppermute | solution.py:145
  64.3 1.4 %shard_map.96 = (bf16[256,384]{1,0:T(8,128)(2,1)S(1)}, bf16[256,384]{1,0:T(8,128)(2,1)S(1)}) custom-call(bf16[256,384]{1,0:T(8,128)(2,1)S(1)} %get-tuple-element.50.fq_ref, bf16[256,384]{1,0:T(8,128)(2,1)S(1)} %get-tuple-element.48.fk_ref, bf16[256,384]{1,0:T(8,128)(2,1)S(1)} %get-tuple-element.49.v_ref, bf16[256,384]{1,0:T(8,128)(2,1)S(1)} %get-tuple-element.65.draw_ref, ...), custom_call_target="tpu_custom_call" | custom-call | flops 402653184 | bytes 2097152 | tf_op jit(solution)/shard_map/pallas_call | solution.py:48
  67.5 1.8 %collective-permute-start.18 = (bf16[128,384]{1,0:T(8,128)(2,1)S(1)}, bf16[128,384]{1,0:T(8,128)(2,1)S(1)}, u32[]{:S(2)}, u32[]{:S(2)}) collective-permute-start(bf16[128,384]{1,0:T(8,128)(2,1)S(1)} %get-tuple-element.86), channel_id=1, source_target_pairs={{0,3},{1,0},{2,1},{3,2},{4,7},{5,4},{6,5},{7,6},{8,11},{9,8},{10,9... | collective-permute-start | bytes 294920 | tf_op jit(solution)/shard_map/ppermute | solution.py:591
  69.3 1.5 %shard_map.102 = (bf16[384,384]{1,0:T(8,128)(2,1)S(1)}, bf16[384,384]{1,0:T(8,128)(2,1)S(1)}, bf16[384,384]{1,0:T(8,128)(2,1)S(1)}, bf16[384,384]{1,0:T(8,128)(2...) custom-call(bf16[1536,384]{1,0:T(8,128)(2,1)} %refs_0_.1, bf16[1536,384]{1,0:T(8,128)(2,1)} %refs_1_.3, ...), custom_call_target="tpu_custom_call" | custom-call | flops 1 | bytes 1048576 | tf_op jit(solution)/shard_map/pallas_call | solution.py:438
  73.8 2.7 %collective-permute-start.21 = (bf16[128,384]{1,0:T(8,128)(2,1)S(1)}, bf16[128,384]{1,0:T(8,128)(2,1)S(1)}, u32[]{:S(2)}, u32[]{:S(2)}) collective-permute-start(bf16[128,384]{1,0:T(8,128)(2,1)S(1)} %get-tuple-element.89), channel_id=1, source_target_pairs={{0,3},{1,0},{2,1},{3,2},{4,7},{5,4},{6,5},{7,6},{8,11},{9,8},{10,9... | collective-permute-start | bytes 294920 | tf_op jit(solution)/shard_map/ppermute | solution.py:591
  77.2 1.8 %shard_map.101.own_ref = bf16[256,384]{1,0:T(8,128)(2,1)S(1)} custom-call(bf16[256,384]{1,0:T(8,128)(2,1)S(1)} %get-tuple-element.67.dq_ref, bf16[256,384]{1,0:T(8,128)(2,1)S(1)} %get-tuple-element.73.dk_ref, bf16[256,384]{1,0:T(8,128)(2,1)S(1)} %get-tuple-element.74.dv_ref, bf16[1536,384]{1,0:T(8,128)(2,1)} %refs_0_.1, bf16[1536,384]{1,0:T(8,128)(2,1)} %refs_1_.3, ...), custom_call_target="tpu_custom_call" | custom-call | flops 226492416 | bytes 1048576 | tf_op jit(solution)/shard_map/pallas_call | solution.py:569
  (57 shorter events, 18.4 us)
Async XLA Ops:
  3.7 4.2 %collective-permute-start = (bf16[192,128]{1,0:T(8,128)(2,1)S(1)}, bf16[192,128]{1,0:T(8,128)(2,1)S(1)}, u32[]{:S(2)}, u32[]{:S(2)}) collective-permute-start(bf16[192,128]{1,0:T(8,128)(2,1)S(1)} %get-tuple-element.46.state_ref), channel_id=1, source_target_pairs={{0,4},{4,0},{1,5},{5,1},{2,6},{6,2},{3,7},{7,3},{8,12},{12,8},{9,1... | collective-permute-start | bytes 147464 | tf_op jit(solution)/shard_map/ppermute | solution.py:145
  7.9 2.8 %collective-permute-start.3 = (bf16[96,128]{1,0:T(8,128)(2,1)S(1)}, bf16[96,128]{1,0:T(8,128)(2,1)S(1)}, u32[]{:S(2)}, u32[]{:S(2)}) collective-permute-start(bf16[96,128]{1,0:T(8,128)(2,1)S(1)} %shard_map.87.chip_ref), channel_id=1, source_target_pairs={{0,24},{8,0},{16,8},{24,16},{1,25},{9,1},{17,9},{25,17},{2,26},{10... | collective-permute-start | bytes 73736 | tf_op jit(solution)/shard_map/ppermute | solution.py:151
  9.0 4.2 %collective-permute-start.2 = (bf16[96,128]{1,0:T(8,128)(2,1)S(1)}, bf16[96,128]{1,0:T(8,128)(2,1)S(1)}, u32[]{:S(2)}, u32[]{:S(2)}) collective-permute-start(bf16[96,128]{1,0:T(8,128)(2,1)S(1)} %shard_map.87.chip_ref), channel_id=1, source_target_pairs={{0,16},{8,24},{16,0},{24,8},{1,17},{9,25},{17,1},{25,9},{2,18},{10... | collective-permute-start | bytes 73736 | tf_op jit(solution)/shard_map/ppermute | solution.py:151
  9.3 4.1 %collective-permute-start.1 = (bf16[96,128]{1,0:T(8,128)(2,1)S(1)}, bf16[96,128]{1,0:T(8,128)(2,1)S(1)}, u32[]{:S(2)}, u32[]{:S(2)}) collective-permute-start(bf16[96,128]{1,0:T(8,128)(2,1)S(1)} %shard_map.87.chip_ref), channel_id=1, source_target_pairs={{0,8},{8,16},{16,24},{24,0},{1,9},{9,17},{17,25},{25,1},{2,10},{10... | collective-permute-start | bytes 73736 | tf_op jit(solution)/shard_map/ppermute | solution.py:151
  14.1 16.9 %all-to-all-start = ((bf16[8,96,128]{2,1,0:T(8,128)(2,1)}), bf16[8,96,128]{2,1,0:T(8,128)(2,1)S(1)}, u32[]{:S(2)}, u32[]{:S(2)}) async-start(bf16[8,96,128]{2,1,0:T(8,128)(2,1)} %shard_map.88), calls=%async_computation | async-start | bytes 393216 | tf_op jit(solution)/shard_map/all_to_all | solution.py:141
  22.3 12.1 %collective-permute-start.5 = (bf16[256,384]{1,0:T(8,128)(2,1)S(1)}, bf16[256,384]{1,0:T(8,128)(2,1)S(1)}, u32[]{:S(2)}, u32[]{:S(2)}) collective-permute-start(bf16[256,384]{1,0:T(8,128)(2,1)S(1)} %copy-done.2), channel_id=1, source_target_pairs={{0,1},{1,2},{2,3},{3,0},{4,5},{5,6},{6,7},{7,4},{8,9},{9,10},{10,1... | collective-permute-start | bytes 589832 | tf_op jit(solution)/shard_map/ppermute | solution.py:591
  23.6 10.8 %collective-permute-start.7 = (bf16[256,384]{1,0:T(8,128)(2,1)S(1)}, bf16[256,384]{1,0:T(8,128)(2,1)S(1)}, u32[]{:S(2)}, u32[]{:S(2)}) collective-permute-start(bf16[256,384]{1,0:T(8,128)(2,1)S(1)} %copy-done.2), channel_id=1, source_target_pairs={{0,3},{1,0},{2,1},{3,2},{4,7},{5,4},{6,5},{7,6},{8,11},{9,8},{10,9... | collective-permute-start | bytes 589832 | tf_op jit(solution)/shard_map/ppermute | solution.py:591
  25.1 9.3 %collective-permute-start.6 = (bf16[256,384]{1,0:T(8,128)(2,1)S(1)}, bf16[256,384]{1,0:T(8,128)(2,1)S(1)}, u32[]{:S(2)}, u32[]{:S(2)}) collective-permute-start(bf16[256,384]{1,0:T(8,128)(2,1)S(1)} %copy-done.2), channel_id=1, source_target_pairs={{0,2},{1,3},{2,0},{3,1},{4,6},{5,7},{6,4},{7,5},{8,10},{9,11},{10,... | collective-permute-start | bytes 589832 | tf_op jit(solution)/shard_map/ppermute | solution.py:591
  31.0 5.5 %collective-permute-start.4 = (bf16[96,128]{1,0:T(8,128)(2,1)S(1)}, bf16[96,128]{1,0:T(8,128)(2,1)S(1)}, u32[]{:S(2)}, u32[]{:S(2)}) collective-permute-start(bf16[96,128]{1,0:T(8,128)(2,1)S(1)} %shard_map.89.mine_ref), channel_id=1, source_target_pairs={{0,4},{4,0},{1,5},{5,1},{2,6},{6,2},{3,7},{7,3},{8,12},{12,8},{9,1... | collective-permute-start | bytes 73736 | tf_op jit(solution)/shard_map/ppermute | solution.py:145
  37.6 2.7 %collective-permute-start.8 = (bf16[192,128]{1,0:T(8,128)(2,1)S(1)}, bf16[192,128]{1,0:T(8,128)(2,1)S(1)}, u32[]{:S(2)}, u32[]{:S(2)}) collective-permute-start(bf16[192,128]{1,0:T(8,128)(2,1)S(1)} %get-tuple-element.55.state_ref), channel_id=1, source_target_pairs={{0,4},{4,0},{1,5},{5,1},{2,6},{6,2},{3,7},{7,3},{8,12},{12,8},{9,1... | collective-permute-start | bytes 147464 | tf_op jit(solution)/shard_map/ppermute | solution.py:145
  40.3 4.0 %collective-permute-start.11 = (bf16[96,128]{1,0:T(8,128)(2,1)S(1)}, bf16[96,128]{1,0:T(8,128)(2,1)S(1)}, u32[]{:S(2)}, u32[]{:S(2)}) collective-permute-start(bf16[96,128]{1,0:T(8,128)(2,1)S(1)} %shard_map.93.chip_ref), channel_id=1, source_target_pairs={{0,8},{8,16},{16,24},{24,0},{1,9},{9,17},{17,25},{25,1},{2,10},{10... | collective-permute-start | bytes 73736 | tf_op jit(solution)/shard_map/ppermute | solution.py:151
  40.4 4.3 %collective-permute-start.10 = (bf16[96,128]{1,0:T(8,128)(2,1)S(1)}, bf16[96,128]{1,0:T(8,128)(2,1)S(1)}, u32[]{:S(2)}, u32[]{:S(2)}) collective-permute-start(bf16[96,128]{1,0:T(8,128)(2,1)S(1)} %shard_map.93.chip_ref), channel_id=1, source_target_pairs={{0,16},{8,24},{16,0},{24,8},{1,17},{9,25},{17,1},{25,9},{2,18},{10... | collective-permute-start | bytes 73736 | tf_op jit(solution)/shard_map/ppermute | solution.py:151
  42.1 3.3 %collective-permute-start.9 = (bf16[96,128]{1,0:T(8,128)(2,1)S(1)}, bf16[96,128]{1,0:T(8,128)(2,1)S(1)}, u32[]{:S(2)}, u32[]{:S(2)}) collective-permute-start(bf16[96,128]{1,0:T(8,128)(2,1)S(1)} %shard_map.93.chip_ref), channel_id=1, source_target_pairs={{0,24},{8,0},{16,8},{24,16},{1,25},{9,1},{17,9},{25,17},{2,26},{10... | collective-permute-start | bytes 73736 | tf_op jit(solution)/shard_map/ppermute | solution.py:151
  46.1 15.2 %all-to-all-start.1 = ((bf16[8,96,128]{2,1,0:T(8,128)(2,1)}), bf16[8,96,128]{2,1,0:T(8,128)(2,1)S(1)}, u32[]{:S(2)}, u32[]{:S(2)}) async-start(bf16[8,96,128]{2,1,0:T(8,128)(2,1)} %shard_map.95), calls=%async_computation.1 | async-start | bytes 393216 | tf_op jit(solution)/shard_map/all_to_all | solution.py:141
  54.0 19.7 %collective-permute-start.14 = (bf16[256,384]{1,0:T(8,128)(2,1)}, bf16[256,384]{1,0:T(8,128)(2,1)S(1)}, u32[]{:S(2)}, u32[]{:S(2)}) collective-permute-start(bf16[256,384]{1,0:T(8,128)(2,1)} %get-tuple-element.63), channel_id=1, source_target_pairs={{0,3},{1,0},{2,1},{3,2},{4,7},{5,4},{6,5},{7,6},{8,11},{9,8},{10,9... | collective-permute-start | bytes 589832 | tf_op jit(solution)/shard_map/ppermute | solution.py:591
  55.7 18.1 %collective-permute-start.13 = (bf16[256,384]{1,0:T(8,128)(2,1)}, bf16[256,384]{1,0:T(8,128)(2,1)S(1)}, u32[]{:S(2)}, u32[]{:S(2)}) collective-permute-start(bf16[256,384]{1,0:T(8,128)(2,1)} %get-tuple-element.61), channel_id=1, source_target_pairs={{0,1},{1,2},{2,3},{3,0},{4,5},{5,6},{6,7},{7,4},{8,9},{9,10},{10,1... | collective-permute-start | bytes 589832 | tf_op jit(solution)/shard_map/ppermute | solution.py:591
  55.7 20.8 %collective-permute-start.12 = (bf16[256,384]{1,0:T(8,128)(2,1)}, bf16[256,384]{1,0:T(8,128)(2,1)S(1)}, u32[]{:S(2)}, u32[]{:S(2)}) collective-permute-start(bf16[256,384]{1,0:T(8,128)(2,1)} %get-tuple-element.59), channel_id=1, source_target_pairs={{0,2},{1,3},{2,0},{3,1},{4,6},{5,7},{6,4},{7,5},{8,10},{9,11},{10,... | collective-permute-start | bytes 589832 | tf_op jit(solution)/shard_map/ppermute | solution.py:591
  61.4 4.4 %collective-permute-start.15 = (bf16[96,128]{1,0:T(8,128)(2,1)S(1)}, bf16[96,128]{1,0:T(8,128)(2,1)S(1)}, u32[]{:S(2)}, u32[]{:S(2)}) collective-permute-start(bf16[96,128]{1,0:T(8,128)(2,1)S(1)} %shard_map.97.mine_ref), channel_id=1, source_target_pairs={{0,4},{4,0},{1,5},{5,1},{2,6},{6,2},{3,7},{7,3},{8,12},{12,8},{9,1... | collective-permute-start | bytes 73736 | tf_op jit(solution)/shard_map/ppermute | solution.py:145
  66.5 5.6 %collective-permute-start.17 = (bf16[128,384]{1,0:T(8,128)(2,1)S(1)}, bf16[128,384]{1,0:T(8,128)(2,1)S(1)}, u32[]{:S(2)}, u32[]{:S(2)}) collective-permute-start(bf16[128,384]{1,0:T(8,128)(2,1)S(1)} %get-tuple-element.85), channel_id=1, source_target_pairs={{0,1},{1,2},{2,3},{3,0},{4,5},{5,6},{6,7},{7,4},{8,9},{9,10},{10,1... | collective-permute-start | bytes 294920 | tf_op jit(solution)/shard_map/ppermute | solution.py:591
  67.5 5.2 %collective-permute-start.18 = (bf16[128,384]{1,0:T(8,128)(2,1)S(1)}, bf16[128,384]{1,0:T(8,128)(2,1)S(1)}, u32[]{:S(2)}, u32[]{:S(2)}) collective-permute-start(bf16[128,384]{1,0:T(8,128)(2,1)S(1)} %get-tuple-element.86), channel_id=1, source_target_pairs={{0,3},{1,0},{2,1},{3,2},{4,7},{5,4},{6,5},{7,6},{8,11},{9,8},{10,9... | collective-permute-start | bytes 294920 | tf_op jit(solution)/shard_map/ppermute | solution.py:591
  72.2 6.9 %collective-permute-start.16 = (bf16[128,384]{1,0:T(8,128)(2,1)S(1)}, bf16[128,384]{1,0:T(8,128)(2,1)S(1)}, u32[]{:S(2)}, u32[]{:S(2)}) collective-permute-start(bf16[128,384]{1,0:T(8,128)(2,1)S(1)} %get-tuple-element.82), channel_id=1, source_target_pairs={{0,3},{1,0},{2,1},{3,2},{4,7},{5,4},{6,5},{7,6},{8,11},{9,8},{10,9... | collective-permute-start | bytes 294920 | tf_op jit(solution)/shard_map/ppermute | solution.py:591
  72.7 6.4 %collective-permute-start.20 = (bf16[128,384]{1,0:T(8,128)(2,1)S(1)}, bf16[128,384]{1,0:T(8,128)(2,1)S(1)}, u32[]{:S(2)}, u32[]{:S(2)}) collective-permute-start(bf16[128,384]{1,0:T(8,128)(2,1)S(1)} %get-tuple-element.88), channel_id=1, source_target_pairs={{0,1},{1,2},{2,3},{3,0},{4,5},{5,6},{6,7},{7,4},{8,9},{9,10},{10,1... | collective-permute-start | bytes 294920 | tf_op jit(solution)/shard_map/ppermute | solution.py:591
  73.7 5.6 %collective-permute-start.19 = (bf16[128,384]{1,0:T(8,128)(2,1)S(1)}, bf16[128,384]{1,0:T(8,128)(2,1)S(1)}, u32[]{:S(2)}, u32[]{:S(2)}) collective-permute-start(bf16[128,384]{1,0:T(8,128)(2,1)S(1)} %get-tuple-element.87), channel_id=1, source_target_pairs={{0,1},{1,2},{2,3},{3,0},{4,5},{5,6},{6,7},{7,4},{8,9},{9,10},{10,1... | collective-permute-start | bytes 294920 | tf_op jit(solution)/shard_map/ppermute | solution.py:591
  73.8 5.5 %collective-permute-start.21 = (bf16[128,384]{1,0:T(8,128)(2,1)S(1)}, bf16[128,384]{1,0:T(8,128)(2,1)S(1)}, u32[]{:S(2)}, u32[]{:S(2)}) collective-permute-start(bf16[128,384]{1,0:T(8,128)(2,1)S(1)} %get-tuple-element.89), channel_id=1, source_target_pairs={{0,3},{1,0},{2,1},{3,2},{4,7},{5,4},{6,5},{7,6},{8,11},{9,8},{10,9... | collective-permute-start | bytes 294920 | tf_op jit(solution)/shard_map/ppermute | solution.py:591
  (5 other events, 95.4 us)

commit v12 on v9

--- a/solution.py
+++ b/solution.py
@@ -359,32 +359,47 @@
     )
 
 
+def local_values(fq, fk, draw):
+    rows, width = fq.shape
+
+    def body(fq_ref, fk_ref, draw_ref, dv_ref):
+        upper = tri(rows, True)
+        for p in range(width // LANES):
+            cols = slice(p * LANES, (p + 1) * LANES)
+            q, k, dr = (fq_ref[:, cols], fk_ref[:, cols], draw_ref[:, cols])
+            dv = None
+            for h in (0, 1):
+                part = mm(masked(mm(one_head(k, h), q, NT), upper), one_head(dr, h))
+                dv = part if dv is None else dv + part
+            dv_ref[:, cols] = dv.astype(bf16)
+
+    outs = [((rows, width), bf16)]
+    return plain(body, outs, 8 * rows * rows * width, 1024 * 1024, fq, fk, draw)[0]
+
+
 def local_grads(fq, fk, v, draw, before):
     rows, width = fq.shape
 
-    def body(fq_ref, fk_ref, v_ref, draw_ref, before_ref, dq_ref, dk_ref, dv_ref):
+    def body(fq_ref, fk_ref, v_ref, draw_ref, before_ref, dq_ref, dk_ref):
         lower, upper = (tri(rows, False), tri(rows, True))
         for p in range(width // LANES):
             cols = slice(p * LANES, (p + 1) * LANES)
             q, k, val, dr = (fq_ref[:, cols], fk_ref[:, cols], v_ref[:, cols], draw_ref[:, cols])
             dq = mm(dr, unpack(before_ref[p * HD : (p + 1) * HD, :]), NT)
-            dk, dv = (None, None)
+            dk = None
             for h in (0, 1):
-                val_h, k_h, q_h, dr_h = (one_head(a, h) for a in (val, k, q, dr))
+                val_h, k_h, q_h = (one_head(a, h) for a in (val, k, q))
                 dq = dq + mm(masked(mm(dr, val_h, NT), lower), k_h)
                 dk_h = mm(masked(mm(val_h, dr, NT), upper), q_h)
-                dv_h = mm(masked(mm(k_h, q, NT), upper), dr_h)
                 dk = dk_h if dk is None else dk + dk_h
-                dv = dv_h if dv is None else dv + dv_h
             dq_ref[:, cols] = (dq * jnp.minimum(q.astype(f32), 1.0)).astype(bf16)
             dk_ref[:, cols] = dk.astype(bf16)
-            dv_ref[:, cols] = dv.astype(bf16)
 
     return plain(
         body,
-        [((rows, width), bf16)] * 3,
-        24 * rows * rows * width,
-        3 * 1024 * 1024,
+        [((rows, width), bf16)] * 2,
+        16 * rows * rows * width,
+        2 * 1024 * 1024,
         fq,
         fk,
         v,
@@ -540,17 +555,18 @@
     planes = plane_exchange(planes)
     mine = before_chip(False, planes)
     got = swap(mine)
+    weights = (w_query, w_key, w_value)
+    blocks = weight_blocks(2, (hold(w_query, mine), w_key, w_value))
     attn, draw, before, state = normed(mine, got, pair, fq, raw_local, up, gain)
-    weights = (w_query, w_key, w_value)
-    blocks = weight_blocks(2, (hold(w_query, state), w_key, w_value))
     pair = swap(state)
+    dv_local = local_values(fq, fk, draw)
     chip = pair_sum(state, pair)
     got = y_gather(True, chip)
     b2, b1, b3, b0 = branch_parts(hold(attn, chip), w_out)
     planes = plane_sums(True, chip, got)
     b2, b1, b3 = (hold(b, planes) for b in (b2, b1, b3))
     branch = [b0, to_owner(b2, 2), to_owner(b1, 1), to_owner(b3, 3)]
-    dq, dk_local, dv_local = local_grads(fq, fk, v, hold(draw, planes), before)
+    dq, dk_local = local_grads(fq, fk, v, hold(draw, planes), before)
     planes = plane_exchange(planes)
     mine = before_chip(True, planes)
     got = swap(mine)

time: 82.7 us -> 82.4 us (level)
    pallas_call x8 -> x9, Pallas kernels: 4.63 us -> 5.07 us  [plain(): call(body, outs, flops, moved, in_specs=[VMEM] * len(args), out_specs=[VM...]
  transfers between devices with their start and end apart: 21 -> 21, of which waited for: 12 -> 12; matrix products, arithmetic and copies ran while one was open for 1% -> 1% of each run, Pallas kernels for 17% -> 18%
where the time goes in v12:
time: 82.4 us; the launch traced here: 82 us
  starting transfers between devices  42 us (51%)
  Pallas kernels  19.8 us (24%)
  waiting for transfers between devices  17.7 us (21%)
  other arithmetic  1.56 us (2%)
    all_to_all x2, starting transfers between devices, plane_exchange(): return lax.all_to_all(planes, 'seq_0', 0, 0, tiled=True)  14.8 us
    ppermute x4, starting transfers between devices, swap(): return lax.ppermute(x, 'seq_2', SWAP)  11.4 us
    ppermute x9, starting transfers between devices, to_owner(): return lax.ppermute(part, 'mp', shifts(4, k))  10.1 us
    ppermute x9, waiting for transfers between devices, to_owner(): return lax.ppermute(part, 'mp', shifts(4, k))  6.7 us
    ppermute x6, starting transfers between devices, y_gather(): got.append(lax.ppermute(chip, 'seq_1', shifts(4, -k if later else k)))  5.75 us
    pallas_call x9, Pallas kernels, plain(): call(body, outs, flops, moved, in_specs=[VMEM] * len(args), out_specs=[VM...  5.07 us
    ppermute x6, waiting for transfers between devices, y_gather(): got.append(lax.ppermute(chip, 'seq_1', shifts(4, -k if later else k)))  4.88 us
    all_to_all x2, waiting for transfers between devices, plane_exchange(): return lax.all_to_all(planes, 'seq_0', 0, 0, tiled=True)  4.39 us
  transfers between devices with their start and end apart: 21, of which 12 were waited for; matrix products, arithmetic and copies ran while one was open for 1% of the time, Pallas kernels for 18%

profile of v12, /device:TPU:1, one launch (start us, length us, event | category | flops | bytes accessed | tf_op | source)
XLA Modules:
  0.0 82.0 jit_solution(9322555042277172762)
XLA Ops:
  0.7 3.0 %shard_map.86 = (bf16[256,384]{1,0:T(8,128)(2,1)S(1)}, bf16[256,384]{1,0:T(8,128)(2,1)S(1)}, bf16[192,128]{1,0:T(8,128)(2,1)S(1)}) custom-call(bf16[256,1536]{1,0:T(8,128)(2,1)} %x_hbm.2, bf16[1536,384]{1,0:T(8,128)(2,1)} %wk_hbm.5, bf16[1536,384]{1,0:T(8,128)(2,1)} %wv_hbm.5), custom_call_target="tpu_custom_call" | custom-call | flops 603979776 | bytes 3145728 | tf_op jit(solution)/shard_map/pallas_call | solution.py:195
  3.7 3.3 %collective-permute-start = (bf16[192,128]{1,0:T(8,128)(2,1)S(1)}, bf16[192,128]{1,0:T(8,128)(2,1)S(1)}, u32[]{:S(2)}, u32[]{:S(2)}) collective-permute-start(bf16[192,128]{1,0:T(8,128)(2,1)S(1)} %get-tuple-element.34.state_ref), channel_id=1, source_target_pairs={{0,4},{4,0},{1,5},{5,1},{2,6},{6,2},{3,7},{7,3},{8,12},{12,8},{9,1... | collective-permute-start | bytes 147464 | tf_op jit(solution)/shard_map/ppermute | solution.py:145
  10.6 2.6 %collective-permute-done.2.g2 = bf16[96,128]{1,0:T(8,128)(2,1)S(1)} collective-permute-done((bf16[96,128]{1,0:T(8,128)(2,1)S(1)}, bf16[96,128]{1,0:T(8,128)(2,1)S(1)}, u32[]{:S(2)}, u32[]{:S(2)}) %collective-permute-start.2) | collective-permute-done | bytes 24608 | tf_op jit(solution)/shard_map/ppermute | solution.py:151
  14.1 8.2 %all-to-all-start = ((bf16[8,96,128]{2,1,0:T(8,128)(2,1)}), bf16[8,96,128]{2,1,0:T(8,128)(2,1)S(1)}, u32[]{:S(2)}, u32[]{:S(2)}) async-start(bf16[8,96,128]{2,1,0:T(8,128)(2,1)} %shard_map.88), calls=%async_computation | async-start | bytes 393216 | tf_op jit(solution)/shard_map/all_to_all | solution.py:141
  23.6 1.5 %collective-permute-start.7 = (bf16[256,384]{1,0:T(8,128)(2,1)S(1)}, bf16[256,384]{1,0:T(8,128)(2,1)S(1)}, u32[]{:S(2)}, u32[]{:S(2)}) collective-permute-start(bf16[256,384]{1,0:T(8,128)(2,1)S(1)} %copy-done.2), channel_id=1, source_target_pairs={{0,3},{1,0},{2,1},{3,2},{4,7},{5,4},{6,5},{7,6},{8,11},{9,8},{10,9... | collective-permute-start | bytes 589832 | tf_op jit(solution)/shard_map/ppermute | solution.py:536
  25.1 1.5 %collective-permute-start.6 = (bf16[256,384]{1,0:T(8,128)(2,1)S(1)}, bf16[256,384]{1,0:T(8,128)(2,1)S(1)}, u32[]{:S(2)}, u32[]{:S(2)}) collective-permute-start(bf16[256,384]{1,0:T(8,128)(2,1)S(1)} %copy-done.2), channel_id=1, source_target_pairs={{0,2},{1,3},{2,0},{3,1},{4,6},{5,7},{6,4},{7,5},{8,10},{9,11},{10,... | collective-permute-start | bytes 589832 | tf_op jit(solution)/shard_map/ppermute | solution.py:536
  26.6 2.5 %shard_map.90 = (bf16[256,384]{1,0:T(8,128)(2,1)S(1)}, bf16[256,384]{1,0:T(8,128)(2,1)S(1)}) custom-call(bf16[256,1536]{1,0:T(8,128)(2,1)} %x_hbm.2, bf16[1536,384]{1,0:T(8,128)(2,1)S(1)} %copy-done, bf16[256,384]{1,0:T(8,128)(2,1)S(1)} %get-tuple-element.36.fk_ref, bf16[256,384]{1,0:T(8,128)(2,1)S(1)} %get-tuple-element.37.v_ref), custom_call_target="tpu_custom_call" | custom-call | flops 503316480 | bytes 3145728 | tf_op jit(solution)/shard_map/pallas_call | solution.py:253
  29.1 1.9 %all-to-all-done.planes_ref = bf16[8,96,128]{2,1,0:T(8,128)(2,1)S(1)} async-done(((bf16[8,96,128]{2,1,0:T(8,128)(2,1)}), bf16[8,96,128]{2,1,0:T(8,128)(2,1)S(1)}, u32[]{:S(2)}, u32[]{:S(2)}) %all-to-all-start) | async-done | bytes 196640 | tf_op jit(solution)/shard_map/all_to_all | solution.py:141
  31.0 3.3 %collective-permute-start.4 = (bf16[96,128]{1,0:T(8,128)(2,1)S(1)}, bf16[96,128]{1,0:T(8,128)(2,1)S(1)}, u32[]{:S(2)}, u32[]{:S(2)}) collective-permute-start(bf16[96,128]{1,0:T(8,128)(2,1)S(1)} %shard_map.89.mine_ref), channel_id=1, source_target_pairs={{0,4},{4,0},{1,5},{5,1},{2,6},{6,2},{3,7},{7,3},{8,12},{12,8},{9,1... | collective-permute-start | bytes 73736 | tf_op jit(solution)/shard_map/ppermute | solution.py:145
  34.4 2.2 %shard_map.91.up_ref = bf16[256,384]{1,0:T(8,128)(2,1)S(1)} custom-call(bf16[256,384]{1,0:T(8,128)(2,1)S(1)} %copy-done.2, bf16[256,384]{1,0:T(8,128)(2,1)S(1)} %collective-permute-done.5.g1, bf16[256,384]{1,0:T(8,128)(2,1)S(1)} %collective-permute-done.6.g2, bf16[256,384]{1,0:T(8,128)(2,1)S(1)} %collective-permute-done.7.g3, bf16[384,1536]{1,0:T(8,128)(2,1)} %w_ref.1, ...), custom_call_target="tpu_custom_call" | custom-call | flops 301989888 | bytes 3145728 | tf_op jit(solution)/shard_map/pallas_call | solution.py:283
  37.6 1.8 %collective-permute-start.8 = (bf16[192,128]{1,0:T(8,128)(2,1)S(1)}, bf16[192,128]{1,0:T(8,128)(2,1)S(1)}, u32[]{:S(2)}, u32[]{:S(2)}) collective-permute-start(bf16[192,128]{1,0:T(8,128)(2,1)S(1)} %get-tuple-element.43.state_ref), channel_id=1, source_target_pairs={{0,4},{4,0},{1,5},{5,1},{2,6},{6,2},{3,7},{7,3},{8,12},{12,8},{9,1... | collective-permute-start | bytes 147464 | tf_op jit(solution)/shard_map/ppermute | solution.py:145
  40.4 1.8 %collective-permute-start.10 = (bf16[96,128]{1,0:T(8,128)(2,1)S(1)}, bf16[96,128]{1,0:T(8,128)(2,1)S(1)}, u32[]{:S(2)}, u32[]{:S(2)}) collective-permute-start(bf16[96,128]{1,0:T(8,128)(2,1)S(1)} %shard_map.93.chip_ref), channel_id=1, source_target_pairs={{0,16},{8,24},{16,0},{24,8},{1,17},{9,25},{17,1},{25,9},{2,18},{10... | collective-permute-start | bytes 73736 | tf_op jit(solution)/shard_map/ppermute | solution.py:151
  42.1 1.8 %collective-permute-start.9 = (bf16[96,128]{1,0:T(8,128)(2,1)S(1)}, bf16[96,128]{1,0:T(8,128)(2,1)S(1)}, u32[]{:S(2)}, u32[]{:S(2)}) collective-permute-start(bf16[96,128]{1,0:T(8,128)(2,1)S(1)} %shard_map.93.chip_ref), channel_id=1, source_target_pairs={{0,24},{8,0},{16,8},{24,16},{1,25},{9,1},{17,9},{25,17},{2,26},{10... | collective-permute-start | bytes 73736 | tf_op jit(solution)/shard_map/ppermute | solution.py:151
  46.1 6.6 %all-to-all-start.1 = ((bf16[8,96,128]{2,1,0:T(8,128)(2,1)}), bf16[8,96,128]{2,1,0:T(8,128)(2,1)S(1)}, u32[]{:S(2)}, u32[]{:S(2)}) async-start(bf16[8,96,128]{2,1,0:T(8,128)(2,1)} %shard_map.95), calls=%async_computation.1 | async-start | bytes 393216 | tf_op jit(solution)/shard_map/all_to_all | solution.py:141
  52.7 1.3 %shard_map.94 = (bf16[256,384]{1,0:T(8,128)(2,1)}, bf16[256,384]{1,0:T(8,128)(2,1)}, bf16[256,384]{1,0:T(8,128)(2,1)}, bf16[256,384]{1,0:T(8,128)(2,1)}) custom-call(bf16[256,384]{1,0:T(8,128)(2,1)S(1)} %get-tuple-element.44.attn_ref, bf16[384,1536]{1,0:T(8,128)(2,1)S(1)} %copy-done.1), custom_call_target="tpu_custom_call" | custom-call | flops 301989888 | bytes 2097152 | tf_op jit(solution)/shard_map/pallas_call | solution.py:48
  54.0 1.7 %collective-permute-start.14 = (bf16[256,384]{1,0:T(8,128)(2,1)}, bf16[256,384]{1,0:T(8,128)(2,1)S(1)}, u32[]{:S(2)}, u32[]{:S(2)}) collective-permute-start(bf16[256,384]{1,0:T(8,128)(2,1)} %get-tuple-element.51), channel_id=1, source_target_pairs={{0,3},{1,0},{2,1},{3,2},{4,7},{5,4},{6,5},{7,6},{8,11},{9,8},{10,9... | collective-permute-start | bytes 589832 | tf_op jit(solution)/shard_map/ppermute | solution.py:536
  58.8 2.5 %all-to-all-done.1.planes_ref = bf16[8,96,128]{2,1,0:T(8,128)(2,1)S(1)} async-done(((bf16[8,96,128]{2,1,0:T(8,128)(2,1)}), bf16[8,96,128]{2,1,0:T(8,128)(2,1)S(1)}, u32[]{:S(2)}, u32[]{:S(2)}) %all-to-all-start.1) | async-done | bytes 196640 | tf_op jit(solution)/shard_map/all_to_all | solution.py:141
  61.4 3.0 %collective-permute-start.15 = (bf16[96,128]{1,0:T(8,128)(2,1)S(1)}, bf16[96,128]{1,0:T(8,128)(2,1)S(1)}, u32[]{:S(2)}, u32[]{:S(2)}) collective-permute-start(bf16[96,128]{1,0:T(8,128)(2,1)S(1)} %shard_map.97.mine_ref), channel_id=1, source_target_pairs={{0,4},{4,0},{1,5},{5,1},{2,6},{6,2},{3,7},{7,3},{8,12},{12,8},{9,1... | collective-permute-start | bytes 73736 | tf_op jit(solution)/shard_map/ppermute | solution.py:145
  64.3 1.4 %shard_map.96 = (bf16[256,384]{1,0:T(8,128)(2,1)S(1)}, bf16[256,384]{1,0:T(8,128)(2,1)S(1)}) custom-call(bf16[256,384]{1,0:T(8,128)(2,1)S(1)} %get-tuple-element.38.fq_ref, bf16[256,384]{1,0:T(8,128)(2,1)S(1)} %get-tuple-element.36.fk_ref, bf16[256,384]{1,0:T(8,128)(2,1)S(1)} %get-tuple-element.37.v_ref, bf16[256,384]{1,0:T(8,128)(2,1)S(1)} %get-tuple-element.53.draw_ref, ...), custom_call_target="tpu_custom_call" | custom-call | flops 402653184 | bytes 2097152 | tf_op jit(solution)/shard_map/pallas_call | solution.py:48
  66.5 2.5 %shard_map.102 = (bf16[256,384]{1,0:T(8,128)(2,1)S(1)}, bf16[256,384]{1,0:T(8,128)(2,1)S(1)}) custom-call(bf16[256,384]{1,0:T(8,128)(2,1)S(1)} %get-tuple-element.55.dq_ref, bf16[256,384]{1,0:T(8,128)(2,1)S(1)} %get-tuple-element.61.dk_ref, bf16[256,384]{1,0:T(8,128)(2,1)S(1)} %get-tuple-element.62.dv_ref, bf16[1536,384]{1,0:T(8,128)(2,1)} %wq_hbm.3, ...), custom_call_target="tpu_custom_call" | custom-call | flops 452984832 | bytes 2097152 | tf_op jit(solution)/shard_map/pallas_call | solution.py:514
  70.0 1.8 %collective-permute-start.18 = (bf16[256,384]{1,0:T(8,128)(2,1)S(1)}, bf16[256,384]{1,0:T(8,128)(2,1)S(1)}, u32[]{:S(2)}, u32[]{:S(2)}) collective-permute-start(bf16[256,384]{1,0:T(8,128)(2,1)S(1)} %get-tuple-element.65), channel_id=1, source_target_pairs={{0,3},{1,0},{2,1},{3,2},{4,7},{5,4},{6,5},{7,6},{8,11},{9,8},{10,9... | collective-permute-start | bytes 589832 | tf_op jit(solution)/shard_map/ppermute | solution.py:536
  72.8 1.7 %shard_map.101 = bf16[256,384]{1,0:T(8,128)(2,1)S(1)} custom-call(bf16[256,384]{1,0:T(8,128)(2,1)S(1)} %get-tuple-element.55.dq_ref, bf16[256,384]{1,0:T(8,128)(2,1)S(1)} %get-tuple-element.61.dk_ref, bf16[256,384]{1,0:T(8,128)(2,1)S(1)} %get-tuple-element.62.dv_ref, bf16[1536,384]{1,0:T(8,128)(2,1)} %wq_hbm.3, bf16[1536,384]{1,0:T(8,128)(2,1)} %wk_hbm.5, ...), custom_call_target="tpu_custom_call" | custom-call | flops 226492416 | bytes 1048576 | tf_op jit(solution)/shard_map/pallas_call | solution.py:514
  74.5 2.3 %collective-permute-done.17 = bf16[256,384]{1,0:T(8,128)(2,1)S(1)} collective-permute-done((bf16[256,384]{1,0:T(8,128)(2,1)S(1)}, bf16[256,384]{1,0:T(8,128)(2,1)S(1)}, u32[]{:S(2)}, u32[]{:S(2)}) %collective-permute-start.17) | collective-permute-done | bytes 196640 | tf_op jit(solution)/shard_map/ppermute | solution.py:536
  76.8 4.4 %collective-permute-done.16 = bf16[256,384]{1,0:T(8,128)(2,1)S(1)} collective-permute-done((bf16[256,384]{1,0:T(8,128)(2,1)S(1)}, bf16[256,384]{1,0:T(8,128)(2,1)S(1)}, u32[]{:S(2)}, u32[]{:S(2)}) %collective-permute-start.16) | collective-permute-done | bytes 196640 | tf_op jit(solution)/shard_map/ppermute | solution.py:536
  (48 shorter events, 16.7 us)
Async XLA Ops:
  0.6 21.7 %copy-start.2 = (bf16[256,384]{1,0:T(8,128)(2,1)S(1)}, bf16[256,384]{1,0:T(8,128)(2,1)}, u32[]{:S(2)}) copy-start(bf16[256,384]{1,0:T(8,128)(2,1)} %g0.1) | copy-start | bytes 589828
  0.6 26.0 %copy-start.4 = (f32[384]{0:T(512)S(1)}, f32[384]{0:T(512)}, u32[]{:S(2)}) copy-start(f32[384]{0:T(512)} %param.12) | copy-start | bytes 4612
  0.6 26.0 %copy-start = (bf16[1536,384]{1,0:T(8,128)(2,1)S(1)}, bf16[1536,384]{1,0:T(8,128)(2,1)}, u32[]{:S(2)}) copy-start(bf16[1536,384]{1,0:T(8,128)(2,1)} %wq_hbm.3) | copy-start | bytes 3538948
  3.7 4.2 %collective-permute-start = (bf16[192,128]{1,0:T(8,128)(2,1)S(1)}, bf16[192,128]{1,0:T(8,128)(2,1)S(1)}, u32[]{:S(2)}, u32[]{:S(2)}) collective-permute-start(bf16[192,128]{1,0:T(8,128)(2,1)S(1)} %get-tuple-element.34.state_ref), channel_id=1, source_target_pairs={{0,4},{4,0},{1,5},{5,1},{2,6},{6,2},{3,7},{7,3},{8,12},{12,8},{9,1... | collective-permute-start | bytes 147464 | tf_op jit(solution)/shard_map/ppermute | solution.py:145
  7.9 2.8 %collective-permute-start.3 = (bf16[96,128]{1,0:T(8,128)(2,1)S(1)}, bf16[96,128]{1,0:T(8,128)(2,1)S(1)}, u32[]{:S(2)}, u32[]{:S(2)}) collective-permute-start(bf16[96,128]{1,0:T(8,128)(2,1)S(1)} %shard_map.87.chip_ref), channel_id=1, source_target_pairs={{0,24},{8,0},{16,8},{24,16},{1,25},{9,1},{17,9},{25,17},{2,26},{10... | collective-permute-start | bytes 73736 | tf_op jit(solution)/shard_map/ppermute | solution.py:151
  9.0 4.2 %collective-permute-start.2 = (bf16[96,128]{1,0:T(8,128)(2,1)S(1)}, bf16[96,128]{1,0:T(8,128)(2,1)S(1)}, u32[]{:S(2)}, u32[]{:S(2)}) collective-permute-start(bf16[96,128]{1,0:T(8,128)(2,1)S(1)} %shard_map.87.chip_ref), channel_id=1, source_target_pairs={{0,16},{8,24},{16,0},{24,8},{1,17},{9,25},{17,1},{25,9},{2,18},{10... | collective-permute-start | bytes 73736 | tf_op jit(solution)/shard_map/ppermute | solution.py:151
  9.3 4.1 %collective-permute-start.1 = (bf16[96,128]{1,0:T(8,128)(2,1)S(1)}, bf16[96,128]{1,0:T(8,128)(2,1)S(1)}, u32[]{:S(2)}, u32[]{:S(2)}) collective-permute-start(bf16[96,128]{1,0:T(8,128)(2,1)S(1)} %shard_map.87.chip_ref), channel_id=1, source_target_pairs={{0,8},{8,16},{16,24},{24,0},{1,9},{9,17},{17,25},{25,1},{2,10},{10... | collective-permute-start | bytes 73736 | tf_op jit(solution)/shard_map/ppermute | solution.py:151
  14.1 16.9 %all-to-all-start = ((bf16[8,96,128]{2,1,0:T(8,128)(2,1)}), bf16[8,96,128]{2,1,0:T(8,128)(2,1)S(1)}, u32[]{:S(2)}, u32[]{:S(2)}) async-start(bf16[8,96,128]{2,1,0:T(8,128)(2,1)} %shard_map.88), calls=%async_computation | async-start | bytes 393216 | tf_op jit(solution)/shard_map/all_to_all | solution.py:141
  22.3 12.1 %collective-permute-start.5 = (bf16[256,384]{1,0:T(8,128)(2,1)S(1)}, bf16[256,384]{1,0:T(8,128)(2,1)S(1)}, u32[]{:S(2)}, u32[]{:S(2)}) collective-permute-start(bf16[256,384]{1,0:T(8,128)(2,1)S(1)} %copy-done.2), channel_id=1, source_target_pairs={{0,1},{1,2},{2,3},{3,0},{4,5},{5,6},{6,7},{7,4},{8,9},{9,10},{10,1... | collective-permute-start | bytes 589832 | tf_op jit(solution)/shard_map/ppermute | solution.py:536
  23.6 10.8 %collective-permute-start.7 = (bf16[256,384]{1,0:T(8,128)(2,1)S(1)}, bf16[256,384]{1,0:T(8,128)(2,1)S(1)}, u32[]{:S(2)}, u32[]{:S(2)}) collective-permute-start(bf16[256,384]{1,0:T(8,128)(2,1)S(1)} %copy-done.2), channel_id=1, source_target_pairs={{0,3},{1,0},{2,1},{3,2},{4,7},{5,4},{6,5},{7,6},{8,11},{9,8},{10,9... | collective-permute-start | bytes 589832 | tf_op jit(solution)/shard_map/ppermute | solution.py:536
  25.1 9.3 %collective-permute-start.6 = (bf16[256,384]{1,0:T(8,128)(2,1)S(1)}, bf16[256,384]{1,0:T(8,128)(2,1)S(1)}, u32[]{:S(2)}, u32[]{:S(2)}) collective-permute-start(bf16[256,384]{1,0:T(8,128)(2,1)S(1)} %copy-done.2), channel_id=1, source_target_pairs={{0,2},{1,3},{2,0},{3,1},{4,6},{5,7},{6,4},{7,5},{8,10},{9,11},{10,... | collective-permute-start | bytes 589832 | tf_op jit(solution)/shard_map/ppermute | solution.py:536
  31.0 5.5 %collective-permute-start.4 = (bf16[96,128]{1,0:T(8,128)(2,1)S(1)}, bf16[96,128]{1,0:T(8,128)(2,1)S(1)}, u32[]{:S(2)}, u32[]{:S(2)}) collective-permute-start(bf16[96,128]{1,0:T(8,128)(2,1)S(1)} %shard_map.89.mine_ref), channel_id=1, source_target_pairs={{0,4},{4,0},{1,5},{5,1},{2,6},{6,2},{3,7},{7,3},{8,12},{12,8},{9,1... | collective-permute-start | bytes 73736 | tf_op jit(solution)/shard_map/ppermute | solution.py:145
  37.6 2.7 %collective-permute-start.8 = (bf16[192,128]{1,0:T(8,128)(2,1)S(1)}, bf16[192,128]{1,0:T(8,128)(2,1)S(1)}, u32[]{:S(2)}, u32[]{:S(2)}) collective-permute-start(bf16[192,128]{1,0:T(8,128)(2,1)S(1)} %get-tuple-element.43.state_ref), channel_id=1, source_target_pairs={{0,4},{4,0},{1,5},{5,1},{2,6},{6,2},{3,7},{7,3},{8,12},{12,8},{9,1... | collective-permute-start | bytes 147464 | tf_op jit(solution)/shard_map/ppermute | solution.py:145
  40.3 4.0 %collective-permute-start.11 = (bf16[96,128]{1,0:T(8,128)(2,1)S(1)}, bf16[96,128]{1,0:T(8,128)(2,1)S(1)}, u32[]{:S(2)}, u32[]{:S(2)}) collective-permute-start(bf16[96,128]{1,0:T(8,128)(2,1)S(1)} %shard_map.93.chip_ref), channel_id=1, source_target_pairs={{0,8},{8,16},{16,24},{24,0},{1,9},{9,17},{17,25},{25,1},{2,10},{10... | collective-permute-start | bytes 73736 | tf_op jit(solution)/shard_map/ppermute | solution.py:151
  40.4 4.3 %collective-permute-start.10 = (bf16[96,128]{1,0:T(8,128)(2,1)S(1)}, bf16[96,128]{1,0:T(8,128)(2,1)S(1)}, u32[]{:S(2)}, u32[]{:S(2)}) collective-permute-start(bf16[96,128]{1,0:T(8,128)(2,1)S(1)} %shard_map.93.chip_ref), channel_id=1, source_target_pairs={{0,16},{8,24},{16,0},{24,8},{1,17},{9,25},{17,1},{25,9},{2,18},{10... | collective-permute-start | bytes 73736 | tf_op jit(solution)/shard_map/ppermute | solution.py:151
  42.1 3.3 %collective-permute-start.9 = (bf16[96,128]{1,0:T(8,128)(2,1)S(1)}, bf16[96,128]{1,0:T(8,128)(2,1)S(1)}, u32[]{:S(2)}, u32[]{:S(2)}) collective-permute-start(bf16[96,128]{1,0:T(8,128)(2,1)S(1)} %shard_map.93.chip_ref), channel_id=1, source_target_pairs={{0,24},{8,0},{16,8},{24,16},{1,25},{9,1},{17,9},{25,17},{2,26},{10... | collective-permute-start | bytes 73736 | tf_op jit(solution)/shard_map/ppermute | solution.py:151
  46.1 15.2 %all-to-all-start.1 = ((bf16[8,96,128]{2,1,0:T(8,128)(2,1)}), bf16[8,96,128]{2,1,0:T(8,128)(2,1)S(1)}, u32[]{:S(2)}, u32[]{:S(2)}) async-start(bf16[8,96,128]{2,1,0:T(8,128)(2,1)} %shard_map.95), calls=%async_computation.1 | async-start | bytes 393216 | tf_op jit(solution)/shard_map/all_to_all | solution.py:141
  54.0 17.9 %collective-permute-start.14 = (bf16[256,384]{1,0:T(8,128)(2,1)}, bf16[256,384]{1,0:T(8,128)(2,1)S(1)}, u32[]{:S(2)}, u32[]{:S(2)}) collective-permute-start(bf16[256,384]{1,0:T(8,128)(2,1)} %get-tuple-element.51), channel_id=1, source_target_pairs={{0,3},{1,0},{2,1},{3,2},{4,7},{5,4},{6,5},{7,6},{8,11},{9,8},{10,9... | collective-permute-start | bytes 589832 | tf_op jit(solution)/shard_map/ppermute | solution.py:536
  55.7 16.4 %collective-permute-start.13 = (bf16[256,384]{1,0:T(8,128)(2,1)}, bf16[256,384]{1,0:T(8,128)(2,1)S(1)}, u32[]{:S(2)}, u32[]{:S(2)}) collective-permute-start(bf16[256,384]{1,0:T(8,128)(2,1)} %get-tuple-element.49), channel_id=1, source_target_pairs={{0,1},{1,2},{2,3},{3,0},{4,5},{5,6},{6,7},{7,4},{8,9},{9,10},{10,1... | collective-permute-start | bytes 589832 | tf_op jit(solution)/shard_map/ppermute | solution.py:536
  55.7 16.4 %collective-permute-start.12 = (bf16[256,384]{1,0:T(8,128)(2,1)}, bf16[256,384]{1,0:T(8,128)(2,1)S(1)}, u32[]{:S(2)}, u32[]{:S(2)}) collective-permute-start(bf16[256,384]{1,0:T(8,128)(2,1)} %get-tuple-element.47), channel_id=1, source_target_pairs={{0,2},{1,3},{2,0},{3,1},{4,6},{5,7},{6,4},{7,5},{8,10},{9,11},{10,... | collective-permute-start | bytes 589832 | tf_op jit(solution)/shard_map/ppermute | solution.py:536
  61.4 4.4 %collective-permute-start.15 = (bf16[96,128]{1,0:T(8,128)(2,1)S(1)}, bf16[96,128]{1,0:T(8,128)(2,1)S(1)}, u32[]{:S(2)}, u32[]{:S(2)}) collective-permute-start(bf16[96,128]{1,0:T(8,128)(2,1)S(1)} %shard_map.97.mine_ref), channel_id=1, source_target_pairs={{0,4},{4,0},{1,5},{5,1},{2,6},{6,2},{3,7},{7,3},{8,12},{12,8},{9,1... | collective-permute-start | bytes 73736 | tf_op jit(solution)/shard_map/ppermute | solution.py:145
  69.1 7.7 %collective-permute-start.17 = (bf16[256,384]{1,0:T(8,128)(2,1)S(1)}, bf16[256,384]{1,0:T(8,128)(2,1)S(1)}, u32[]{:S(2)}, u32[]{:S(2)}) collective-permute-start(bf16[256,384]{1,0:T(8,128)(2,1)S(1)} %get-tuple-element.64), channel_id=1, source_target_pairs={{0,1},{1,2},{2,3},{3,0},{4,5},{5,6},{6,7},{7,4},{8,9},{9,10},{10,1... | collective-permute-start | bytes 589832 | tf_op jit(solution)/shard_map/ppermute | solution.py:536
  70.0 6.8 %collective-permute-start.18 = (bf16[256,384]{1,0:T(8,128)(2,1)S(1)}, bf16[256,384]{1,0:T(8,128)(2,1)S(1)}, u32[]{:S(2)}, u32[]{:S(2)}) collective-permute-start(bf16[256,384]{1,0:T(8,128)(2,1)S(1)} %get-tuple-element.65), channel_id=1, source_target_pairs={{0,3},{1,0},{2,1},{3,2},{4,7},{5,4},{6,5},{7,6},{8,11},{9,8},{10,9... | collective-permute-start | bytes 589832 | tf_op jit(solution)/shard_map/ppermute | solution.py:536
  71.8 9.4 %collective-permute-start.16 = (bf16[256,384]{1,0:T(8,128)(2,1)S(1)}, bf16[256,384]{1,0:T(8,128)(2,1)S(1)}, u32[]{:S(2)}, u32[]{:S(2)}) collective-permute-start(bf16[256,384]{1,0:T(8,128)(2,1)S(1)} %get-tuple-element.63), channel_id=1, source_target_pairs={{0,2},{1,3},{2,0},{3,1},{4,6},{5,7},{6,4},{7,5},{8,10},{9,11},{10,... | collective-permute-start | bytes 589832 | tf_op jit(solution)/shard_map/ppermute | solution.py:536
  (2 other events, 21.6 us)
